TPU v7x, 32 devices: a whole 2x2x4 slice. The times are simulated.
32 devices in a mesh: tm: 16 (over z, y, core), grp: 2 (over x).
Axes of the slice: x: 2, y: 2, z: 4, core: 2. Of those that a mesh axis runs over, the one named last changes fastest.
Arguments:
- features: bfloat16 [4096, 512], P(('tm', 'grp')), may hold values from -6 to 6
- weight_five: bfloat16 [2, 512, 512], P(None, None, 'tm'), may hold values from -0.1875 to 0.1875
- weight_six: bfloat16 [2, 512, 512], P(None, None, 'tm'), may hold values from -0.1875 to 0.1875
- projection: bfloat16 [512, 960], P('tm'), may hold values from -0.25 to 0.25
- pos_weight: bfloat16 [128, 8, 120, 120], P(None, 'grp'), may hold values from -0.046875 to 0.046875
- pos_bias: bfloat16 [960], P('grp'), may hold values from -4 to 4
- cotangent: bfloat16 [1024, 960], P('tm', 'grp'), may hold values from -6 to 6
Outputs:
- encoded: bfloat16 [1024, 960], P('tm', 'grp')
- feature_grad: bfloat16 [1024, 512], P(('tm', 'grp'))
- projection_grad: float32 [512, 960], P('tm', 'grp')
All inputs are finite; a program needn't handle non-finite values.
Results may differ from a plain program's by a relative error of at most 0.0085.
Values may be sent and summed in bfloat16 or wider, within the bound.
No kernel may reach another device: no remote copies, remote signals or barrier semaphores. Data moves between devices by JAX's collectives and lax.ppermute only.
A program may use at most 192 MiB of HBM per device.

v0:
```python
import functools
import math

import jax
import jax.numpy as jnp
from jax import lax
from jax.experimental import pallas as pl
from jax.experimental.pallas import tpu as pltpu
from jax.sharding import PartitionSpec as P


EPS = 1e-05
F32 = jnp.float32
BF16 = jnp.bfloat16
VMEM_LIMIT = 56 * 1024 * 1024


def dot_nn(a, b):
    return lax.dot_general(a, b, (((1,), (0,)), ((), ())), preferred_element_type=F32)


def dot_nt(a, b):
    return lax.dot_general(a, b, (((1,), (1,)), ((), ())), preferred_element_type=F32)


def normalize(v):
    average = jnp.mean(v, axis=-1, keepdims=True)
    centred = v - average
    inv_dev = lax.rsqrt(jnp.mean(centred * centred, axis=-1, keepdims=True) + EPS)
    return centred * inv_dev, inv_dev


def phi_cdf(v):
    return 0.5 * (1.0 + lax.erf(v * 0.7071067811865476))


def pick_rows(rows, first):
    r = lax.broadcasted_iota(jnp.int32, (rows, 2 * rows), 0)
    c = lax.broadcasted_iota(jnp.int32, (rows, 2 * rows), 1)
    return jnp.where(c == 2 * r + first, 1.0, 0.0).astype(BF16)


def flip_rows(rows):
    r = lax.broadcasted_iota(jnp.int32, (rows, rows), 0)
    c = lax.broadcasted_iota(jnp.int32, (rows, rows), 1)
    return jnp.where(c == rows - 1 - r, 1.0, 0.0).astype(BF16)


def place_shards(idx, layout, stacks, first, taps, full, sems, base=0):
    copies = []
    for offs, ref in zip(layout, stacks):
        width = ref.shape[2]
        for q, off in enumerate(offs):
            at = pl.multiple_of((idx ^ off) * width, width)
            for tap in range(taps):
                copies.append(
                    pltpu.make_async_copy(
                        ref.at[q, first + tap],
                        full.at[tap, pl.ds(at, width), :],
                        sems.at[base + len(copies)],
                    )
                )
    for c in copies:
        c.start()
    return copies


def strided(blocks, full):
    rows = blocks[0].shape[0] // 2
    even = [dot_nn(pick_rows(rows, 0), b).astype(BF16) for b in blocks]
    odd = [dot_nn(pick_rows(rows, 1), b).astype(BF16) for b in blocks]
    even, odd = jnp.concatenate(even, 0), jnp.concatenate(odd, 0)
    mixed = dot_nt(even, full[0]) + dot_nt(odd, full[1])
    unit, _ = normalize(mixed)
    return (unit * phi_cdf(unit)).astype(BF16)


def five_body(where, *refs, layout, count):
    blocks, stacks = refs[:count], refs[count : count + len(layout)]
    out, full, sems = refs[count + len(layout) :]
    copies = place_shards(where[0], layout, stacks, 0, 2, full, sems)
    for c in copies:
        c.wait()
    out[...] = strided([b[...] for b in blocks], full)


def six_body(where, act, *refs, layout, count):
    stacks = refs[: len(layout)]
    normed, unit_own, inv_own, full, sems = refs[len(layout) :]
    copies = place_shards(where[0], layout, stacks, 0, 2, full, sems)
    for c in copies:
        c.wait()
    rows = act.shape[0] // count
    act_six = strided([act[e * rows : (e + 1) * rows] for e in range(count)], full)
    unit, inv_dev = normalize(act_six.astype(F32))
    own = rows // 2
    for e in range(count):
        at = pl.multiple_of((where[1] ^ e) * own, own)
        normed[pl.ds(at, own), :] = unit[e * own : (e + 1) * own].astype(BF16)
    unit_own[...] = unit[:own]
    inv_own[...] = jnp.broadcast_to(inv_dev[:own], inv_own.shape)


def swap_channels_body(w_ref, out_ref):
    out_ref[...] = jnp.swapaxes(w_ref[0], 0, 1)


def swap_channels(weights, group):
    a, b, taps = weights.shape[1:]
    size = 2 * a * b * taps
    return pl.pallas_call(
        swap_channels_body,
        grid=(1,),
        in_specs=[pl.BlockSpec((1, a, b, taps), lambda i: (group, 0, 0, 0))],
        out_specs=pl.BlockSpec((b, a, taps), lambda i: (0, 0, 0)),
        out_shape=jax.ShapeDtypeStruct((b, a, taps), weights.dtype),
        compiler_params=PARAMS,
        cost_estimate=pl.CostEstimate(flops=0, transcendentals=0, bytes_accessed=2 * size),
        name="swap_channels",
    )(weights)


def start_taps(w_anys, w_vmem, sems):
    per_group = sems.shape[0] // len(w_anys)
    size = w_vmem.shape[0] // sems.shape[0]
    for g, w_any in enumerate(w_anys):
        for c in range(per_group):
            at = g * per_group + c
            pltpu.make_async_copy(
                w_any.at[pl.ds(c * size, size)], w_vmem.at[pl.ds(at * size, size)], sems.at[at]
            ).start()


def conv_taps(w_vmem, sems, first, wrap, acc, chunk, sub):
    count = sems.shape[0]
    size = w_vmem.shape[0] // count
    groups = acc.shape[0]
    rows = acc.shape[1]
    taps = w_vmem.shape[2]
    per_group = count // groups
    s = lax.broadcasted_iota(jnp.int32, (rows, taps), 0)
    j = lax.broadcasted_iota(jnp.int32, (rows, taps), 1)
    mask = j < rows - 1 - s
    acc[...] = jnp.zeros_like(acc)

    def step(c, carry):
        if chunk == 0:
            here = w_vmem.at[pl.ds(c * size, size)]
            pltpu.make_async_copy(here, here, sems.at[c]).wait()
        total = acc[c // per_group]
        for b in range(0, size, sub):
            parts, weights = [], []
            at = pl.multiple_of(c * size + b, 8)
            f8, r8 = first[pl.ds(at, sub), :], wrap[pl.ds(at, sub), :]
            for i in range(sub):
                u = jnp.where(mask, r8[i : i + 1], f8[i : i + 1])
                u = pltpu.roll(u, taps - (rows - 1), 1, stride=1, stride_axis=0)
                parts.append(u.astype(BF16))
                weights.append(w_vmem[at + i])
            total = total + dot_nt(jnp.concatenate(parts, 1), jnp.concatenate(weights, 1))
        acc[c // per_group] = total
        return carry

    lax.fori_loop(0, count, step, 0)
    return jnp.concatenate([acc[g] for g in range(groups)], 1)


def forward_body(where, normed, got_a, got_b, *refs, layout, groups):
    stacks = refs[: len(layout)]
    w_any, cot, bias, encoded, slope_rev, proj = refs[len(layout) : len(layout) + 6]
    w_vmem, first, wrap, acc, full, sems, proj_sems = refs[len(layout) + 6 :]
    copies = place_shards(where[0], layout, stacks, 2, 1, full, proj_sems)
    start_taps([w_any.at[g] for g in range(groups)], w_vmem, sems)
    for c in copies:
        c.wait()
    proj[...] = full[0, :, : proj.shape[1]]
    odd = where[0] % 2 == 1
    low = jnp.where(odd, got_a[...], got_b[...])
    high = jnp.where(odd, got_b[...], got_a[...])
    rows = got_a.shape[0]
    chunks = normed.shape[0] // rows
    ext = jnp.concatenate([low, normed[...], high], 0)
    hidden = dot_nn(ext, proj[...]).astype(BF16).astype(F32)
    part = lambda c: hidden[c * rows : (c + 1) * rows]
    flip = flip_rows(rows)
    for c in range(chunks):
        first[...] = jnp.concatenate([part(c), part(c + 1)], 0).T
        wrap[...] = jnp.concatenate([part(c + 2), part(c + 1)], 0).T
        pos = conv_taps(w_vmem, sems, first, wrap, acc, c, 8)
        pos = pos + bias[...].astype(F32)
        cdf = phi_cdf(pos)
        here = slice(c * rows, (c + 1) * rows)
        cot_rev = dot_nn(flip, cot[here, :])
        hid_rev = dot_nn(flip, part(c + 1).astype(BF16))
        enc_rev = (hid_rev + pos * cdf).astype(BF16)
        encoded[here, :] = dot_nn(flip, enc_rev).astype(BF16)
        slope = cdf + pos * jnp.exp(-0.5 * pos * pos) * 0.3989422804014327
        slope_rev[here, :] = (cot_rev * slope).astype(BF16)


def backward_body(where, slope_rev, got_a, got_b, *refs, scale, order, groups):
    w_anys = refs[:groups]
    cot, normed, proj, kept, sent, unit_grad, w_vmem, first, wrap, acc, hid_grad, full, rows_f32, sems = refs[groups:]
    start_taps(w_anys, w_vmem, sems)
    odd = where[0] % 2 == 1
    low = jnp.where(odd, got_a[...], got_b[...])
    high = jnp.where(odd, got_b[...], got_a[...])
    rows = got_a.shape[0]
    chunks = slope_rev.shape[0] // rows
    ext = jnp.concatenate([low, slope_rev[...], high], 0).astype(F32)
    part = lambda c: ext[c * rows : (c + 1) * rows]
    for c in range(chunks):
        first[...] = jnp.concatenate([part(c + 2), part(c + 1)], 0).T
        wrap[...] = jnp.concatenate([part(c), part(c + 1)], 0).T
        back = conv_taps(w_vmem, sems, first, wrap, acc, c, 8)
        here = slice(c * rows, (c + 1) * rows)
        hid_grad[here, :] = (cot[here, :].astype(F32) + back).astype(BF16)
    grad = hid_grad[...]
    full[...] = (
        dot_nn(normed[...].astype(F32).T.astype(BF16), grad) * scale
    ).reshape(full.shape)
    for n, p in enumerate(order):
        kept[n] = full[where[0] ^ p].astype(BF16)
        sent[n] = full[where[0] ^ (p ^ 1)].astype(BF16)
    slots = unit_grad.shape[0]
    rows_f32[...] = dot_nt(grad, proj[...]).reshape(rows_f32.shape)
    for e in range(slots):
        unit_grad[e] = rows_f32[where[1] ^ e]


def vmem_specs(count):
    return [pl.BlockSpec(memory_space=pltpu.VMEM)] * count


SMEM_SPEC = pl.BlockSpec(memory_space=pltpu.SMEM)
ANY_SPEC = pl.BlockSpec(memory_space=pl.ANY)
PARAMS = pltpu.CompilerParams(vmem_limit_bytes=VMEM_LIMIT)


def swap(values, axis, mask):
    count = lax.axis_size(axis)
    return lax.ppermute(values, axis, [(i, i ^ mask) for i in range(count)])


def spread(shard, count):
    stack, offs = shard[None], [0]
    mask = count // 2
    while mask >= 4:
        got = swap(stack, "tm", mask)
        stack = jnp.concatenate([stack, got], 0)
        offs = offs + [o ^ mask for o in offs]
        mask //= 2
    stacks, layout = [stack], [offs]
    for mask in (2, 1):
        stacks = stacks + [swap(s, "tm", mask) for s in stacks]
        layout = layout + [[o ^ mask for o in offs] for offs in layout]
    return stacks, layout


def halo(tail, head, parity):
    count = lax.axis_size("tm")
    to_a = tail if tail is head else jnp.where(parity == 0, tail, head)
    to_b = tail if tail is head else jnp.where(parity == 0, head, tail)
    pairs = [(2 * i + 1, 2 * i + 2) for i in range(count // 2 - 1)]
    got_b = lax.ppermute(to_b, "tm", pairs + [(b, a) for a, b in pairs])
    return swap(to_a, "tm", 1), got_b


def on_device(features, weight_five, weight_six, projection, pos_weight, pos_bias, cotangent):
    members, slots = lax.axis_size("tm"), lax.axis_size("grp")
    me, slot = lax.axis_index("tm"), lax.axis_index("grp")
    where = jnp.stack([me, slot]).astype(jnp.int32)
    channels = features.shape[1]
    taps, groups, width = pos_weight.shape[0], pos_weight.shape[1], pos_weight.shape[2]
    columns = groups * width
    half = taps // 2
    own = features.shape[0] // 4
    block = own * slots

    w_taps = jnp.transpose(pos_weight, (1, 2, 3, 0))
    w_back = []
    for g in range(groups):
        w_back.append(swap_channels(w_taps, g))

    blocks = [features] + [swap(features, "grp", e) for e in range(1, slots)]
    five, layout = spread(jnp.transpose(weight_five, (0, 2, 1)), members)
    proj_half = lax.dynamic_slice_in_dim(projection, slot * columns, columns, 1)
    proj_half = jnp.pad(proj_half, ((0, 0), (0, channels - columns)))
    rest, _ = spread(
        jnp.concatenate([jnp.transpose(weight_six, (0, 2, 1)), proj_half[None]], 0), members
    )
    common = dict(layout=layout)
    taps_scratch = [
        pltpu.VMEM((2, channels, channels), BF16),
        pltpu.SemaphoreType.DMA((2 * members,)),
    ]
    act_five = pl.pallas_call(
        functools.partial(five_body, count=slots, **common),
        in_specs=[SMEM_SPEC] + vmem_specs(slots) + [ANY_SPEC] * len(five),
        out_specs=vmem_specs(1)[0],
        out_shape=jax.ShapeDtypeStruct((2 * block, channels), BF16),
        scratch_shapes=taps_scratch,
        compiler_params=PARAMS,
        name="five",
    )(where, *blocks, *five)
    normed, unit, inv_dev = pl.pallas_call(
        functools.partial(six_body, count=slots, **common),
        in_specs=[SMEM_SPEC] + vmem_specs(1) + [ANY_SPEC] * len(rest),
        out_specs=vmem_specs(3),
        out_shape=[
            jax.ShapeDtypeStruct((block, channels), BF16),
            jax.ShapeDtypeStruct((own, channels), F32),
            jax.ShapeDtypeStruct((own, 128), F32),
        ],
        scratch_shapes=taps_scratch,
        compiler_params=PARAMS,
        name="six",
    )(where, act_five, *rest)

    whole = block == half
    tail = normed if whole else normed[block - half :]
    head = normed if whole else normed[:half]
    got_a, got_b = halo(tail, head, me % 2)
    copies = 5 * groups
    conv_scratch = [
        pltpu.VMEM((groups * width, width, taps), BF16),
        pltpu.VMEM((columns, taps), F32),
        pltpu.VMEM((columns, taps), F32),
        pltpu.VMEM((groups, half, width), F32),
    ]
    sems = pltpu.SemaphoreType.DMA((copies,))
    encoded, slope_rev, proj = pl.pallas_call(
        functools.partial(forward_body, groups=groups, **common),
        in_specs=[SMEM_SPEC] + vmem_specs(3) + [ANY_SPEC] * (len(rest) + 1) + vmem_specs(2),
        out_specs=vmem_specs(3),
        out_shape=[
            jax.ShapeDtypeStruct((block, columns), BF16),
            jax.ShapeDtypeStruct((block, columns), BF16),
            jax.ShapeDtypeStruct((channels, columns), BF16),
        ],
        scratch_shapes=conv_scratch
        + [pltpu.VMEM((1, channels, channels), BF16), sems, pltpu.SemaphoreType.DMA((members,))],
        compiler_params=PARAMS,
        name="forward",
    )(
        where, normed, got_a, got_b, *rest, w_taps, cotangent, pos_bias.reshape(1, columns),
    )

    tail = slope_rev if whole else slope_rev[block - half :]
    head = slope_rev if whole else slope_rev[:half]
    got_a, got_b = halo(tail, head, me % 2)
    scale = 1.0 / math.sqrt(own * members * slots)
    share = channels // members
    finals = [0, members // 4, members // 2, 3 * (members // 4)]
    masks, mask = [], 2
    while mask < members // 4:
        masks.append(mask)
        mask *= 2
    order = finals
    for mask in reversed(masks):
        order = order + [p ^ mask for p in order]
    kept, sent, unit_grad = pl.pallas_call(
        functools.partial(backward_body, scale=scale, order=order, groups=groups),
        in_specs=[SMEM_SPEC] + vmem_specs(3) + [ANY_SPEC] * groups + vmem_specs(3),
        out_specs=vmem_specs(3),
        out_shape=[jax.ShapeDtypeStruct((members // 2, share, columns), BF16)] * 2
        + [jax.ShapeDtypeStruct((slots, own, channels), F32)],
        scratch_shapes=conv_scratch
        + [
            pltpu.VMEM((block, columns), BF16),
            pltpu.VMEM((members, share, columns), F32),
            pltpu.VMEM((slots, own, channels), F32),
            sems,
        ],
        compiler_params=PARAMS,
        name="backward",
    )(where, slope_rev, got_a, got_b, *w_back, cotangent, normed, proj)

    total = (kept.astype(F32) + swap(sent, "tm", 1).astype(F32)).astype(BF16)
    for mask in masks:
        middle = total.shape[0] // 2
        got = swap(total[middle:], "tm", mask)
        total = (total[:middle].astype(F32) + got.astype(F32)).astype(BF16)
    parts = [swap(total[n], "tm", p) for n, p in enumerate(finals) if p]
    projection_grad = total[0].astype(F32) + sum(p.astype(F32) for p in parts)

    grad_unit = unit_grad[0]
    for e in range(1, slots):
        grad_unit = grad_unit + swap(unit_grad[e].astype(BF16), "grp", e).astype(F32)
    first_mean = jnp.mean(grad_unit, axis=-1, keepdims=True)
    second_mean = jnp.mean(grad_unit * unit, axis=-1, keepdims=True)
    feature_grad = (inv_dev[:, :1] * (grad_unit - first_mean - unit * second_mean)).astype(BF16)
    return (encoded, feature_grad, projection_grad)


def solution(mesh):
    in_specs = (
        P(("tm", "grp"), None),
        P(None, None, "tm"),
        P(None, None, "tm"),
        P("tm", None),
        P(None, "grp", None, None),
        P("grp"),
        P("tm", "grp"),
    )
    out_specs = (P("tm", "grp"), P(("tm", "grp"), None), P("tm", "grp"))

    return jax.shard_map(
        on_device, mesh=mesh, in_specs=in_specs, out_specs=out_specs, check_vma=False
    )
```

profile of v0, /device:TPU:0, one launch (start us, length us, event | category | flops | bytes accessed | tf_op | source)
XLA Modules:
  0.0 131.5 jit_solution(8714419427200442979)
XLA Ops:
  0.7 0.8 copy-done
  1.6 0.9 maximum_bitcast_fusion
  2.4 4.1 %collective-permute-start.6 = (bf16[1,3,32,512]{3,2,1,0:T(8,128)(2,1)S(1)}, bf16[1,3,32,512]{3,2,1,0:T(8,128)(2,1)S(1)}, u32[]{:S(2)}, u32[]{:S(2)}) collective-permute-start(bf16[1,3,32,512]{3,2,1,0:T(8,128)(2,1)S(1)} %maximum_bitcast_fusion), channel_id=1, source_target_pairs={{0,16},{2,18},{4,20},{6,22},{8,24},{10,26},{12,28},{14,30},{16,0},... | collective-permute-start | bytes 294920 | tf_op jit(solution)/shard_map/ppermute | solution.py:242
  6.6 4.9 %collective-permute-done.6 = bf16[1,3,32,512]{3,2,1,0:T(8,128)(2,1)S(1)} collective-permute-done((bf16[1,3,32,512]{3,2,1,0:T(8,128)(2,1)S(1)}, bf16[1,3,32,512]{3,2,1,0:T(8,128)(2,1)S(1)}, u32[]{:S(2)}, u32[]{:S(2)}) %collective-permute-start.6) | collective-permute-done | bytes 98336 | tf_op jit(solution)/shard_map/ppermute | solution.py:242
  11.5 0.8 collective-permute-start.7
  12.3 3.4 %collective-permute-start.1 = (bf16[1,2,32,512]{3,2,1,0:T(8,128)(2,1)}, bf16[1,2,32,512]{3,2,1,0:T(8,128)(2,1)S(1)}, u32[]{:S(2)}, u32[]{:S(2)}) collective-permute-start(bf16[1,2,32,512]{3,2,1,0:T(8,128)(2,1)} %bitcast.37), channel_id=1, source_target_pairs={{0,16},{2,18},{4,20},{6,22},{8,24},{10,26},{12,28},{14,30},{16,0},... | collective-permute-start | bytes 196616 | tf_op jit(solution)/shard_map/ppermute | solution.py:242
  15.6 3.4 %collective-permute-done.7 = bf16[2,3,32,512]{3,2,1,0:T(8,128)(2,1)S(1)} collective-permute-done((bf16[2,3,32,512]{3,2,1,0:T(8,128)(2,1)S(1)}, bf16[2,3,32,512]{3,2,1,0:T(8,128)(2,1)S(1)}, u32[]{:S(2)}, u32[]{:S(2)}) %collective-permute-start.7) | collective-permute-done | bytes 196640 | tf_op jit(solution)/shard_map/ppermute | solution.py:242
  19.1 1.3 %collective-permute-start.8 = (bf16[4,3,32,512]{3,2,1,0:T(8,128)(2,1)S(1)}, bf16[4,3,32,512]{3,2,1,0:T(8,128)(2,1)S(1)}, u32[]{:S(2)}, u32[]{:S(2)}) collective-permute-start(bf16[4,3,32,512]{3,2,1,0:T(8,128)(2,1)S(1)} %pad_maximum_fusion.refs_0_), channel_id=1, source_target_pairs={{0,4},{2,6},{4,0},{6,2},{8,12},{10,14},{12,8},{14,10},{16,20},{18,... | collective-permute-start | bytes 1179656 | tf_op jit(solution)/shard_map/ppermute | solution.py:242
  20.4 0.9 pad_maximum_fusion.3
  21.3 1.8 %collective-permute-start.2 = (bf16[2,2,32,512]{3,2,1,0:T(8,128)(2,1)S(1)}, bf16[2,2,32,512]{3,2,1,0:T(8,128)(2,1)S(1)}, u32[]{:S(2)}, u32[]{:S(2)}) collective-permute-start(bf16[2,2,32,512]{3,2,1,0:T(8,128)(2,1)S(1)} %pad_maximum_fusion.3), channel_id=1, source_target_pairs={{0,8},{2,10},{4,12},{6,14},{8,0},{10,2},{12,4},{14,6},{16,24},{18,... | collective-permute-start | bytes 393224 | tf_op jit(solution)/shard_map/ppermute | solution.py:242
  23.1 3.2 %collective-permute-done.2 = bf16[2,2,32,512]{3,2,1,0:T(8,128)(2,1)S(1)} collective-permute-done((bf16[2,2,32,512]{3,2,1,0:T(8,128)(2,1)S(1)}, bf16[2,2,32,512]{3,2,1,0:T(8,128)(2,1)S(1)}, u32[]{:S(2)}, u32[]{:S(2)}) %collective-permute-start.2) | collective-permute-done | bytes 131104 | tf_op jit(solution)/shard_map/ppermute | solution.py:242
  26.3 0.9 pad_maximum_fusion.1.refs_2_
  27.2 1.5 %collective-permute-start.3 = (bf16[4,2,32,512]{3,2,1,0:T(8,128)(2,1)S(1)}, bf16[4,2,32,512]{3,2,1,0:T(8,128)(2,1)S(1)}, u32[]{:S(2)}, u32[]{:S(2)}) collective-permute-start(bf16[4,2,32,512]{3,2,1,0:T(8,128)(2,1)S(1)} %pad_maximum_fusion.1.refs_2_), channel_id=1, source_target_pairs={{0,4},{2,6},{4,0},{6,2},{8,12},{10,14},{12,8},{14,10},{16,20},{18,... | collective-permute-start | bytes 786440 | tf_op jit(solution)/shard_map/ppermute | solution.py:242
  29.2 4.8 %collective-permute-done.3.refs_3_ = bf16[4,2,32,512]{3,2,1,0:T(8,128)(2,1)S(1)} collective-permute-done((bf16[4,2,32,512]{3,2,1,0:T(8,128)(2,1)S(1)}, bf16[4,2,32,512]{3,2,1,0:T(8,128)(2,1)S(1)}, u32[]{:S(2)}, u32[]{:S(2)}) %collective-permute-start.3) | collective-permute-done | bytes 262176 | tf_op jit(solution)/shard_map/ppermute | solution.py:242
  34.0 1.5 %collective-permute-start = (bf16[128,512]{1,0:T(8,128)(2,1)}, bf16[128,512]{1,0:T(8,128)(2,1)S(1)}, u32[]{:S(2)}, u32[]{:S(2)}) collective-permute-start(bf16[128,512]{1,0:T(8,128)(2,1)} %refs_0_.1), channel_id=1, source_target_pairs={{0,1},{1,0},{2,3},{3,2},{4,5},{5,4},{6,7},{7,6},{8,9},{9,8},{10,11... | collective-permute-start | bytes 393224 | tf_op jit(solution)/shard_map/ppermute | solution.py:242
  35.5 0.6 pad_add_fusion.where
  36.1 4.0 %collective-permute-done.refs_1_ = bf16[128,512]{1,0:T(8,128)(2,1)S(1)} collective-permute-done((bf16[128,512]{1,0:T(8,128)(2,1)}, bf16[128,512]{1,0:T(8,128)(2,1)S(1)}, u32[]{:S(2)}, u32[]{:S(2)}) %collective-permute-start) | collective-permute-done | bytes 131104 | tf_op jit(solution)/shard_map/ppermute | solution.py:242
  40.2 0.6 copy-done.10
  40.9 0.7 copy-done.9
  41.6 3.9 %five.1.act = bf16[128,512]{1,0:T(8,128)(2,1)} custom-call(s32[2]{0:T(128)} %pad_add_fusion.where, bf16[128,512]{1,0:T(8,128)(2,1)} %refs_0_.1, bf16[128,512]{1,0:T(8,128)(2,1)} %copy-done.10, bf16[4,2,32,512]{3,2,1,0:T(8,128)(2,1)} %copy-done.5, bf16[4,2,32,512]{3,2,1,0:T(8,128)(2,1)} %copy-done.7, bf16[4,2,32,512]{3,2,1,0:T(8,128)(2,1)} %copy-done.8, ...), custom_call_target="tpu_custom_call" | custom-call | tf_op jit(solution)/shard_map/five/pallas_call | solution.py:297
  45.5 0.7 copy-done.3
  46.3 0.7 copy-done.4
  47.0 3.9 %six.1 = (bf16[64,512]{1,0:T(8,128)(2,1)}, f32[32,512]{1,0:T(8,128)}, f32[32,128]{1,0:T(8,128)}) custom-call(s32[2]{0:T(128)} %pad_add_fusion.where, bf16[128,512]{1,0:T(8,128)(2,1)} %five.1.act, bf16[4,3,32,512]{3,2,1,0:T(8,128)(2,1)} %copy-done.1, bf16[4,3,32,512]{3,2,1,0:T(8,128)(2,1)} %copy-done.2, bf16[4,3,32,512]{3,2,1,0:T(8,128)(2,1)} %copy-done.3, ...), custom_call_target="tpu_custom_call" | custom-call | tf_op jit(solution)/shard_map/six/pallas_call | solution.py:306
  50.9 0.7 collective-permute-start.12
  51.6 3.1 %collective-permute-start.11 = (bf16[64,512]{1,0:T(8,128)(2,1)}, bf16[64,512]{1,0:T(8,128)(2,1)S(1)}, u32[]{:S(2)}, u32[]{:S(2)}) collective-permute-start(bf16[64,512]{1,0:T(8,128)(2,1)} %get-tuple-element.12.normed.refs_5_), channel_id=1, source_target_pairs={{0,2},{2,0},{4,6},{6,4},{8,10},{10,8},{12,14},{14,12},{16,18},{18,... | collective-permute-start | bytes 196616 | tf_op jit(solution)/shard_map/ppermute | solution.py:242
  54.7 0.6 reshape.20.refs_6_
  56.4 16.2 %forward.1 = (bf16[64,480]{1,0:T(8,128)(2,1)}, bf16[64,480]{1,0:T(8,128)(2,1)}, bf16[512,480]{1,0:T(8,128)(2,1)}) custom-call(s32[2]{0:T(128)} %pad_add_fusion.where, bf16[64,512]{1,0:T(8,128)(2,1)} %get-tuple-element.12.normed.refs_5_, bf16[64,512]{1,0:T(8,128)(2,1)} %copy-done.14, bf16[64,512]{1,0:T(8,128)(2,1)} %copy-done.12, ...), custom_call_target="tpu_custom_call" | custom-call | tf_op jit(solution)/shard_map/forward/pallas_call | solution.py:332
  72.7 0.7 collective-permute-start.14
  73.4 4.0 %collective-permute-start.13 = (bf16[64,480]{1,0:T(8,128)(2,1)}, bf16[64,480]{1,0:T(8,128)(2,1)S(1)}, u32[]{:S(2)}, u32[]{:S(2)}) collective-permute-start(bf16[64,480]{1,0:T(8,128)(2,1)} %get-tuple-element.15.slope_rev), channel_id=1, source_target_pairs={{0,2},{2,0},{4,6},{6,4},{8,10},{10,8},{12,14},{14,12},{16,18},{18,... | collective-permute-start | bytes 184328 | tf_op jit(solution)/shard_map/ppermute | solution.py:242
  77.4 4.4 %swap_channels.7.refs_3_ = bf16[120,120,128]{2,1,0:T(8,128)(2,1)} custom-call(bf16[4,120,120,128]{3,2,1,0:T(8,128)(2,1)} %bitcast.33), custom_call_target="tpu_custom_call" | custom-call | bytes 7372800 | tf_op jit(solution)/shard_map/swap_channels/pallas_call | solution.py:111
  81.8 4.5 %swap_channels.6.refs_2_ = bf16[120,120,128]{2,1,0:T(8,128)(2,1)} custom-call(bf16[4,120,120,128]{3,2,1,0:T(8,128)(2,1)} %bitcast.34), custom_call_target="tpu_custom_call" | custom-call | bytes 7372800 | tf_op jit(solution)/shard_map/swap_channels/pallas_call | solution.py:111
  86.3 4.3 %swap_channels.5.refs_1_ = bf16[120,120,128]{2,1,0:T(8,128)(2,1)} custom-call(bf16[4,120,120,128]{3,2,1,0:T(8,128)(2,1)} %bitcast.35), custom_call_target="tpu_custom_call" | custom-call | bytes 7372800 | tf_op jit(solution)/shard_map/swap_channels/pallas_call | solution.py:111
  90.6 4.3 %swap_channels.4.refs_0_ = bf16[120,120,128]{2,1,0:T(8,128)(2,1)} custom-call(bf16[4,120,120,128]{3,2,1,0:T(8,128)(2,1)} %bitcast.36), custom_call_target="tpu_custom_call" | custom-call | bytes 7372800 | tf_op jit(solution)/shard_map/swap_channels/pallas_call | solution.py:111
  94.9 0.6 copy-done.11
  95.6 12.5 %backward.1 = (bf16[8,32,480]{2,1,0:T(8,128)(2,1)}, bf16[8,32,480]{2,1,0:T(8,128)(2,1)}, f32[2,32,512]{2,1,0:T(8,128)}) custom-call(s32[2]{0:T(128)} %pad_add_fusion.where, bf16[64,480]{1,0:T(8,128)(2,1)} %get-tuple-element.15.slope_rev, bf16[64,480]{1,0:T(8,128)(2,1)} %copy-done.13, bf16[64,480]{1,0:T(8,128)(2,1)} %copy-done.11, ...), custom_call_target="tpu_custom_call" | custom-call | tf_op jit(solution)/shard_map/backward/pallas_call | solution.py:362
  108.1 0.8 fusion
  109.0 1.5 %collective-permute-start.15 = (bf16[32,512]{1,0:T(8,128)(2,1)S(1)}, bf16[32,512]{1,0:T(8,128)(2,1)S(1)}, u32[]{:S(2)}, u32[]{:S(2)}) collective-permute-start(bf16[32,512]{1,0:T(8,128)(2,1)S(1)} %fusion), channel_id=1, source_target_pairs={{0,1},{1,0},{2,3},{3,2},{4,5},{5,4},{6,7},{7,6},{8,9},{9,8},{10,11... | collective-permute-start | bytes 98312 | tf_op jit(solution)/shard_map/ppermute | solution.py:242
  110.6 2.3 %collective-permute-done.15 = bf16[32,512]{1,0:T(8,128)(2,1)S(1)} collective-permute-done((bf16[32,512]{1,0:T(8,128)(2,1)S(1)}, bf16[32,512]{1,0:T(8,128)(2,1)S(1)}, u32[]{:S(2)}, u32[]{:S(2)}) %collective-permute-start.15) | collective-permute-done | bytes 32800 | tf_op jit(solution)/shard_map/ppermute | solution.py:242
  112.9 1.0 fusion.1
  113.8 1.0 add_convert_fusion
  114.9 2.5 %collective-permute-start.17 = (bf16[4,32,480]{2,1,0:T(8,128)(2,1)S(1)}, bf16[4,32,480]{2,1,0:T(8,128)(2,1)S(1)}, u32[]{:S(2)}, u32[]{:S(2)}) collective-permute-start(bf16[4,32,480]{2,1,0:T(8,128)(2,1)S(1)} %slice.39), channel_id=1, source_target_pairs={{0,4},{2,6},{4,0},{6,2},{8,12},{10,14},{12,8},{14,10},{16,20},{18,... | collective-permute-start | bytes 368648 | tf_op jit(solution)/shard_map/ppermute | solution.py:242
  117.4 3.0 %collective-permute-done.17 = bf16[4,32,480]{2,1,0:T(8,128)(2,1)S(1)} collective-permute-done((bf16[4,32,480]{2,1,0:T(8,128)(2,1)S(1)}, bf16[4,32,480]{2,1,0:T(8,128)(2,1)S(1)}, u32[]{:S(2)}, u32[]{:S(2)}) %collective-permute-start.17) | collective-permute-done | bytes 122912 | tf_op jit(solution)/shard_map/ppermute | solution.py:242
  120.4 2.2 %collective-permute-start.18 = (bf16[32,480]{1,0:T(8,128)(2,1)S(1)}, bf16[32,480]{1,0:T(8,128)(2,1)S(1)}, u32[]{:S(2)}, u32[]{:S(2)}) collective-permute-start(bf16[32,480]{1,0:T(8,128)(2,1)S(1)} %get-tuple-element.23), channel_id=1, source_target_pairs={{0,8},{2,10},{4,12},{6,14},{8,0},{10,2},{12,4},{14,6},{16,24},{18,... | collective-permute-start | bytes 92168 | tf_op jit(solution)/shard_map/ppermute | solution.py:242
  122.6 3.4 %collective-permute-start.20 = (bf16[32,480]{1,0:T(8,128)(2,1)S(1)}, bf16[32,480]{1,0:T(8,128)(2,1)S(1)}, u32[]{:S(2)}, u32[]{:S(2)}) collective-permute-start(bf16[32,480]{1,0:T(8,128)(2,1)S(1)} %get-tuple-element.24), channel_id=1, source_target_pairs={{0,24},{2,26},{4,28},{6,30},{8,16},{10,18},{12,20},{14,22},{16,8},... | collective-permute-start | bytes 92168 | tf_op jit(solution)/shard_map/ppermute | solution.py:242
  126.0 1.5 %multiply_convert_fusion = bf16[32,512]{1,0:T(8,128)(2,1)} fusion(f32[32,512]{1,0:T(8,128)S(1)} %copy-done.6, f32[32]{0:T(128)S(1)} %get-tuple-element.26, f32[32]{0:T(128)S(1)} %get-tuple-element.27, f32[32]{0:T(128)S(1)} %slice_reduce_fusion, bf16[32,512]{1,0:T(8,128)(2,1)S(1)} %collective-permute-done.15, f32[2,32,512]{2,1,0:T(8,128)} %get-tuple-element.17), kind=kLoop, calls=%fused_computation.10 | loop fusion | flops 114688 | bytes 196992 | tf_op jit(solution)/shard_map/convert_element_type | solution.py:392
  127.5 0.9 collective-permute-done.20
  128.4 2.4 %collective-permute-done.19 = bf16[32,480]{1,0:T(8,128)(2,1)S(1)} collective-permute-done((bf16[32,480]{1,0:T(8,128)(2,1)S(1)}, bf16[32,480]{1,0:T(8,128)(2,1)S(1)}, u32[]{:S(2)}, u32[]{:S(2)}) %collective-permute-start.19) | collective-permute-done | bytes 30752 | tf_op jit(solution)/shard_map/ppermute | solution.py:242
  130.8 0.6 convert_add_fusion
  (55 shorter events, 2.3 us)
Async XLA Ops:
  0.6 0.8 copy-start
  0.6 54.1 %copy-start.16 = (bf16[480]{0:T(512)(128)(2,1)S(1)}, bf16[480]{0:T(512)(128)(2,1)}, u32[]{:S(2)}) copy-start(bf16[480]{0:T(512)(128)(2,1)} %param.12) | copy-start | bytes 2884
  2.4 9.0 %collective-permute-start.6 = (bf16[1,3,32,512]{3,2,1,0:T(8,128)(2,1)S(1)}, bf16[1,3,32,512]{3,2,1,0:T(8,128)(2,1)S(1)}, u32[]{:S(2)}, u32[]{:S(2)}) collective-permute-start(bf16[1,3,32,512]{3,2,1,0:T(8,128)(2,1)S(1)} %maximum_bitcast_fusion), channel_id=1, source_target_pairs={{0,16},{2,18},{4,20},{6,22},{8,24},{10,26},{12,28},{14,30},{16,0},... | collective-permute-start | bytes 294920 | tf_op jit(solution)/shard_map/ppermute | solution.py:242
  11.5 7.5 %collective-permute-start.7 = (bf16[2,3,32,512]{3,2,1,0:T(8,128)(2,1)S(1)}, bf16[2,3,32,512]{3,2,1,0:T(8,128)(2,1)S(1)}, u32[]{:S(2)}, u32[]{:S(2)}) collective-permute-start(bf16[2,3,32,512]{3,2,1,0:T(8,128)(2,1)S(1)} %pad_maximum_fusion.2), channel_id=1, source_target_pairs={{0,8},{2,10},{4,12},{6,14},{8,0},{10,2},{12,4},{14,6},{16,24},{18,... | collective-permute-start | bytes 589832 | tf_op jit(solution)/shard_map/ppermute | solution.py:242
  12.3 8.1 %collective-permute-start.1 = (bf16[1,2,32,512]{3,2,1,0:T(8,128)(2,1)}, bf16[1,2,32,512]{3,2,1,0:T(8,128)(2,1)S(1)}, u32[]{:S(2)}, u32[]{:S(2)}) collective-permute-start(bf16[1,2,32,512]{3,2,1,0:T(8,128)(2,1)} %bitcast.37), channel_id=1, source_target_pairs={{0,16},{2,18},{4,20},{6,22},{8,24},{10,26},{12,28},{14,30},{16,0},... | collective-permute-start | bytes 196616 | tf_op jit(solution)/shard_map/ppermute | solution.py:242
  19.1 26.5 %copy-start.1 = (bf16[4,3,32,512]{3,2,1,0:T(8,128)(2,1)}, bf16[4,3,32,512]{3,2,1,0:T(8,128)(2,1)S(1)}, u32[]{:S(2)}) copy-start(bf16[4,3,32,512]{3,2,1,0:T(8,128)(2,1)S(1)} %pad_maximum_fusion.refs_0_) | copy-start | bytes 1179652
  19.1 9.6 %collective-permute-start.8 = (bf16[4,3,32,512]{3,2,1,0:T(8,128)(2,1)S(1)}, bf16[4,3,32,512]{3,2,1,0:T(8,128)(2,1)S(1)}, u32[]{:S(2)}, u32[]{:S(2)}) collective-permute-start(bf16[4,3,32,512]{3,2,1,0:T(8,128)(2,1)S(1)} %pad_maximum_fusion.refs_0_), channel_id=1, source_target_pairs={{0,4},{2,6},{4,0},{6,2},{8,12},{10,14},{12,8},{14,10},{16,20},{18,... | collective-permute-start | bytes 1179656 | tf_op jit(solution)/shard_map/ppermute | solution.py:242
  21.3 5.0 %collective-permute-start.2 = (bf16[2,2,32,512]{3,2,1,0:T(8,128)(2,1)S(1)}, bf16[2,2,32,512]{3,2,1,0:T(8,128)(2,1)S(1)}, u32[]{:S(2)}, u32[]{:S(2)}) collective-permute-start(bf16[2,2,32,512]{3,2,1,0:T(8,128)(2,1)S(1)} %pad_maximum_fusion.3), channel_id=1, source_target_pairs={{0,8},{2,10},{4,12},{6,14},{8,0},{10,2},{12,4},{14,6},{16,24},{18,... | collective-permute-start | bytes 393224 | tf_op jit(solution)/shard_map/ppermute | solution.py:242
  27.2 13.0 %copy-start.5 = (bf16[4,2,32,512]{3,2,1,0:T(8,128)(2,1)}, bf16[4,2,32,512]{3,2,1,0:T(8,128)(2,1)S(1)}, u32[]{:S(2)}) copy-start(bf16[4,2,32,512]{3,2,1,0:T(8,128)(2,1)S(1)} %pad_maximum_fusion.1.refs_2_) | copy-start | bytes 786436
  27.2 6.9 %collective-permute-start.3 = (bf16[4,2,32,512]{3,2,1,0:T(8,128)(2,1)S(1)}, bf16[4,2,32,512]{3,2,1,0:T(8,128)(2,1)S(1)}, u32[]{:S(2)}, u32[]{:S(2)}) collective-permute-start(bf16[4,2,32,512]{3,2,1,0:T(8,128)(2,1)S(1)} %pad_maximum_fusion.1.refs_2_), channel_id=1, source_target_pairs={{0,4},{2,6},{4,0},{6,2},{8,12},{10,14},{12,8},{14,10},{16,20},{18,... | collective-permute-start | bytes 786440 | tf_op jit(solution)/shard_map/ppermute | solution.py:242
  28.6 16.9 %collective-permute-start.9 = (bf16[4,3,32,512]{3,2,1,0:T(8,128)(2,1)S(1)}, bf16[4,3,32,512]{3,2,1,0:T(8,128)(2,1)S(1)}, u32[]{:S(2)}, u32[]{:S(2)}) collective-permute-start(bf16[4,3,32,512]{3,2,1,0:T(8,128)(2,1)S(1)} %pad_maximum_fusion.refs_0_), channel_id=1, source_target_pairs={{0,2},{2,0},{4,6},{6,4},{8,10},{10,8},{12,14},{14,12},{16,18},{18,... | collective-permute-start | bytes 1179656 | tf_op jit(solution)/shard_map/ppermute | solution.py:242
  28.6 16.9 %copy-start.2 = (bf16[4,3,32,512]{3,2,1,0:T(8,128)(2,1)}, bf16[4,3,32,512]{3,2,1,0:T(8,128)(2,1)S(1)}, u32[]{:S(2)}) copy-start(bf16[4,3,32,512]{3,2,1,0:T(8,128)(2,1)S(1)} %collective-permute-done.8.refs_1_) | copy-start | bytes 1179652
  28.6 16.9 %collective-permute-start.10 = (bf16[4,3,32,512]{3,2,1,0:T(8,128)(2,1)S(1)}, bf16[4,3,32,512]{3,2,1,0:T(8,128)(2,1)S(1)}, u32[]{:S(2)}, u32[]{:S(2)}) collective-permute-start(bf16[4,3,32,512]{3,2,1,0:T(8,128)(2,1)S(1)} %collective-permute-done.8.refs_1_), channel_id=1, source_target_pairs={{0,2},{2,0},{4,6},{6,4},{8,10},{10,8},{12,14},{14,12},{16,18},{18,... | collective-permute-start | bytes 1179656 | tf_op jit(solution)/shard_map/ppermute | solution.py:242
  29.1 11.0 %collective-permute-start.4 = (bf16[4,2,32,512]{3,2,1,0:T(8,128)(2,1)S(1)}, bf16[4,2,32,512]{3,2,1,0:T(8,128)(2,1)S(1)}, u32[]{:S(2)}, u32[]{:S(2)}) collective-permute-start(bf16[4,2,32,512]{3,2,1,0:T(8,128)(2,1)S(1)} %pad_maximum_fusion.1.refs_2_), channel_id=1, source_target_pairs={{0,2},{2,0},{4,6},{6,4},{8,10},{10,8},{12,14},{14,12},{16,18},{18,... | collective-permute-start | bytes 786440 | tf_op jit(solution)/shard_map/ppermute | solution.py:242
  34.0 6.2 %copy-start.7 = (bf16[4,2,32,512]{3,2,1,0:T(8,128)(2,1)}, bf16[4,2,32,512]{3,2,1,0:T(8,128)(2,1)S(1)}, u32[]{:S(2)}) copy-start(bf16[4,2,32,512]{3,2,1,0:T(8,128)(2,1)S(1)} %collective-permute-done.3.refs_3_) | copy-start | bytes 786436
  34.0 6.1 %collective-permute-start.5 = (bf16[4,2,32,512]{3,2,1,0:T(8,128)(2,1)S(1)}, bf16[4,2,32,512]{3,2,1,0:T(8,128)(2,1)S(1)}, u32[]{:S(2)}, u32[]{:S(2)}) collective-permute-start(bf16[4,2,32,512]{3,2,1,0:T(8,128)(2,1)S(1)} %collective-permute-done.3.refs_3_), channel_id=1, source_target_pairs={{0,2},{2,0},{4,6},{6,4},{8,10},{10,8},{12,14},{14,12},{16,18},{18,... | collective-permute-start | bytes 786440 | tf_op jit(solution)/shard_map/ppermute | solution.py:242
  34.0 6.1 %collective-permute-start = (bf16[128,512]{1,0:T(8,128)(2,1)}, bf16[128,512]{1,0:T(8,128)(2,1)S(1)}, u32[]{:S(2)}, u32[]{:S(2)}) collective-permute-start(bf16[128,512]{1,0:T(8,128)(2,1)} %refs_0_.1), channel_id=1, source_target_pairs={{0,1},{1,0},{2,3},{3,2},{4,5},{5,4},{6,7},{7,6},{8,9},{9,8},{10,11... | collective-permute-start | bytes 393224 | tf_op jit(solution)/shard_map/ppermute | solution.py:242
  40.2 0.6 copy-start.10
  40.2 0.7 copy-start.8
  40.9 0.7 copy-start.9
  45.5 0.8 copy-start.3
  46.3 0.7 copy-start.4
  50.9 4.4 %collective-permute-start.12 = (bf16[64,512]{1,0:T(8,128)(2,1)}, bf16[64,512]{1,0:T(8,128)(2,1)S(1)}, u32[]{:S(2)}, u32[]{:S(2)}) collective-permute-start(bf16[64,512]{1,0:T(8,128)(2,1)} %get-tuple-element.12.normed.refs_5_), channel_id=1, source_target_pairs={{2,4},{6,8},{10,12},{14,16},{18,20},{22,24},{26,28},{4,2},{8,6},{1... | collective-permute-start | bytes 196616 | tf_op jit(solution)/shard_map/ppermute | solution.py:265
  51.6 4.2 %collective-permute-start.11 = (bf16[64,512]{1,0:T(8,128)(2,1)}, bf16[64,512]{1,0:T(8,128)(2,1)S(1)}, u32[]{:S(2)}, u32[]{:S(2)}) collective-permute-start(bf16[64,512]{1,0:T(8,128)(2,1)} %get-tuple-element.12.normed.refs_5_), channel_id=1, source_target_pairs={{0,2},{2,0},{4,6},{6,4},{8,10},{10,8},{12,14},{14,12},{16,18},{18,... | collective-permute-start | bytes 196616 | tf_op jit(solution)/shard_map/ppermute | solution.py:242
  55.3 0.6 copy-start.12
  55.8 0.6 copy-start.14
  72.7 22.2 %collective-permute-start.14 = (bf16[64,480]{1,0:T(8,128)(2,1)}, bf16[64,480]{1,0:T(8,128)(2,1)S(1)}, u32[]{:S(2)}, u32[]{:S(2)}) collective-permute-start(bf16[64,480]{1,0:T(8,128)(2,1)} %get-tuple-element.15.slope_rev), channel_id=1, source_target_pairs={{2,4},{6,8},{10,12},{14,16},{18,20},{22,24},{26,28},{4,2},{8,6},{1... | collective-permute-start | bytes 184328 | tf_op jit(solution)/shard_map/ppermute | solution.py:265
  73.4 21.6 %collective-permute-start.13 = (bf16[64,480]{1,0:T(8,128)(2,1)}, bf16[64,480]{1,0:T(8,128)(2,1)S(1)}, u32[]{:S(2)}, u32[]{:S(2)}) collective-permute-start(bf16[64,480]{1,0:T(8,128)(2,1)} %get-tuple-element.15.slope_rev), channel_id=1, source_target_pairs={{0,2},{2,0},{4,6},{6,4},{8,10},{10,8},{12,14},{14,12},{16,18},{18,... | collective-permute-start | bytes 184328 | tf_op jit(solution)/shard_map/ppermute | solution.py:242
  94.9 0.6 copy-start.11
  94.9 0.6 copy-start.13
  95.6 14.9 %copy-start.15 = (f32[32,128]{1,0:T(8,128)S(1)}, f32[32,128]{1,0:T(8,128)}, u32[]{:S(2)}) copy-start(f32[32,128]{1,0:T(8,128)} %get-tuple-element.14) | copy-start | bytes 49156
  95.6 17.3 %copy-start.6 = (f32[32,512]{1,0:T(8,128)S(1)}, f32[32,512]{1,0:T(8,128)}, u32[]{:S(2)}) copy-start(f32[32,512]{1,0:T(8,128)} %get-tuple-element.18) | copy-start | bytes 196612
  108.0 5.8 %collective-permute-start.16 = (bf16[8,32,480]{2,1,0:T(8,128)(2,1)}, bf16[8,32,480]{2,1,0:T(8,128)(2,1)S(1)}, u32[]{:S(2)}, u32[]{:S(2)}) collective-permute-start(bf16[8,32,480]{2,1,0:T(8,128)(2,1)} %get-tuple-element.20), channel_id=1, source_target_pairs={{0,2},{2,0},{4,6},{6,4},{8,10},{10,8},{12,14},{14,12},{16,18},{18,... | collective-permute-start | bytes 737288 | tf_op jit(solution)/shard_map/ppermute | solution.py:242
  109.0 3.9 %collective-permute-start.15 = (bf16[32,512]{1,0:T(8,128)(2,1)S(1)}, bf16[32,512]{1,0:T(8,128)(2,1)S(1)}, u32[]{:S(2)}, u32[]{:S(2)}) collective-permute-start(bf16[32,512]{1,0:T(8,128)(2,1)S(1)} %fusion), channel_id=1, source_target_pairs={{0,1},{1,0},{2,3},{3,2},{4,5},{5,4},{6,7},{7,6},{8,9},{9,8},{10,11... | collective-permute-start | bytes 98312 | tf_op jit(solution)/shard_map/ppermute | solution.py:242
  114.9 5.5 %collective-permute-start.17 = (bf16[4,32,480]{2,1,0:T(8,128)(2,1)S(1)}, bf16[4,32,480]{2,1,0:T(8,128)(2,1)S(1)}, u32[]{:S(2)}, u32[]{:S(2)}) collective-permute-start(bf16[4,32,480]{2,1,0:T(8,128)(2,1)S(1)} %slice.39), channel_id=1, source_target_pairs={{0,4},{2,6},{4,0},{6,2},{8,12},{10,14},{12,8},{14,10},{16,20},{18,... | collective-permute-start | bytes 368648 | tf_op jit(solution)/shard_map/ppermute | solution.py:242
  120.4 7.1 %collective-permute-start.18 = (bf16[32,480]{1,0:T(8,128)(2,1)S(1)}, bf16[32,480]{1,0:T(8,128)(2,1)S(1)}, u32[]{:S(2)}, u32[]{:S(2)}) collective-permute-start(bf16[32,480]{1,0:T(8,128)(2,1)S(1)} %get-tuple-element.23), channel_id=1, source_target_pairs={{0,8},{2,10},{4,12},{6,14},{8,0},{10,2},{12,4},{14,6},{16,24},{18,... | collective-permute-start | bytes 92168 | tf_op jit(solution)/shard_map/ppermute | solution.py:242
  122.6 5.8 %collective-permute-start.20 = (bf16[32,480]{1,0:T(8,128)(2,1)S(1)}, bf16[32,480]{1,0:T(8,128)(2,1)S(1)}, u32[]{:S(2)}, u32[]{:S(2)}) collective-permute-start(bf16[32,480]{1,0:T(8,128)(2,1)S(1)} %get-tuple-element.24), channel_id=1, source_target_pairs={{0,24},{2,26},{4,28},{6,30},{8,16},{10,18},{12,20},{14,22},{16,8},... | collective-permute-start | bytes 92168 | tf_op jit(solution)/shard_map/ppermute | solution.py:242
  126.0 4.8 %collective-permute-start.19 = (bf16[32,480]{1,0:T(8,128)(2,1)S(1)}, bf16[32,480]{1,0:T(8,128)(2,1)S(1)}, u32[]{:S(2)}, u32[]{:S(2)}) collective-permute-start(bf16[32,480]{1,0:T(8,128)(2,1)S(1)} %get-tuple-element.25), channel_id=1, source_target_pairs={{0,16},{2,18},{4,20},{6,22},{8,24},{10,26},{12,28},{14,30},{16,0},... | collective-permute-start | bytes 92168 | tf_op jit(solution)/shard_map/ppermute | solution.py:242
where the time goes:
time: 132 us; the launch traced here: 131 us
  Pallas kernels  54 us (41%)
  starting transfers between devices  33 us (25%)
  waiting for transfers between devices  29.5 us (22%)
  other arithmetic  7.41 us (6%)
  local copies, waits for them, and re-layouts  6.68 us (5%)
    ppermute x19, starting transfers between devices, swap(): return lax.ppermute(values, axis, [(i, i ^ mask) for i in range(count)])  31.7 us
    ppermute x19, waiting for transfers between devices, swap(): return lax.ppermute(values, axis, [(i, i ^ mask) for i in range(count)])  29.5 us
    pallas_call x4, Pallas kernels, swap_channels(): pl.pallas_call(swap_channels_body, grid=(1,), in_specs=[pl.BlockSpec((1,...  17.5 us
    pallas_call x1, Pallas kernels, on_device(): pl.pallas_call(functools.partial(forward_body, groups=groups, **common),...  16.2 us
    pallas_call x1, Pallas kernels, on_device(): pl.pallas_call(functools.partial(backward_body, scale=scale, order=order,...  12.5 us
    unnamed x34, local copies, waits for them, and re-layouts  5.02 us
    pallas_call x1, Pallas kernels, on_device(): pl.pallas_call(functools.partial(six_body, count=slots, **common), in_spe...  3.9 us
    pallas_call x1, Pallas kernels, on_device(): pl.pallas_call(functools.partial(five_body, count=slots, **common), in_sp...  3.86 us
  transfers between devices with their start and end apart: 21, of which 10 were waited for; matrix products, arithmetic and copies ran while one was open for 5% of the time, Pallas kernels for 16%

commit v1 on v0

--- a/solution.py
+++ b/solution.py
@@ -13,6 +13,7 @@
 F32 = jnp.float32
 BF16 = jnp.bfloat16
 VMEM_LIMIT = 56 * 1024 * 1024
+SUB = 8
 
 
 def dot_nn(a, b):
@@ -46,23 +47,13 @@
     return jnp.where(c == rows - 1 - r, 1.0, 0.0).astype(BF16)
 
 
-def place_shards(idx, layout, stacks, first, taps, full, sems, base=0):
-    copies = []
+def place_shards(idx, layout, stacks, first, taps, full):
     for offs, ref in zip(layout, stacks):
         width = ref.shape[2]
         for q, off in enumerate(offs):
             at = pl.multiple_of((idx ^ off) * width, width)
             for tap in range(taps):
-                copies.append(
-                    pltpu.make_async_copy(
-                        ref.at[q, first + tap],
-                        full.at[tap, pl.ds(at, width), :],
-                        sems.at[base + len(copies)],
-                    )
-                )
-    for c in copies:
-        c.start()
-    return copies
+                full[tap, pl.ds(at, width), :] = ref[q, first + tap]
 
 
 def strided(blocks, full):
@@ -77,19 +68,15 @@
 
 def five_body(where, *refs, layout, count):
     blocks, stacks = refs[:count], refs[count : count + len(layout)]
-    out, full, sems = refs[count + len(layout) :]
-    copies = place_shards(where[0], layout, stacks, 0, 2, full, sems)
-    for c in copies:
-        c.wait()
+    out, full = refs[count + len(layout) :]
+    place_shards(where[0], layout, stacks, 0, 2, full)
     out[...] = strided([b[...] for b in blocks], full)
 
 
 def six_body(where, act, *refs, layout, count):
     stacks = refs[: len(layout)]
-    normed, unit_own, inv_own, full, sems = refs[len(layout) :]
-    copies = place_shards(where[0], layout, stacks, 0, 2, full, sems)
-    for c in copies:
-        c.wait()
+    normed, unit_own, inv_own, full = refs[len(layout) :]
+    place_shards(where[0], layout, stacks, 0, 2, full)
     rows = act.shape[0] // count
     act_six = strided([act[e * rows : (e + 1) * rows] for e in range(count)], full)
     unit, inv_dev = normalize(act_six.astype(F32))
@@ -101,79 +88,78 @@
     inv_own[...] = jnp.broadcast_to(inv_dev[:own], inv_own.shape)
 
 
-def swap_channels_body(w_ref, out_ref):
-    out_ref[...] = jnp.swapaxes(w_ref[0], 0, 1)
-
-
-def swap_channels(weights, group):
-    a, b, taps = weights.shape[1:]
-    size = 2 * a * b * taps
-    return pl.pallas_call(
-        swap_channels_body,
-        grid=(1,),
-        in_specs=[pl.BlockSpec((1, a, b, taps), lambda i: (group, 0, 0, 0))],
-        out_specs=pl.BlockSpec((b, a, taps), lambda i: (0, 0, 0)),
-        out_shape=jax.ShapeDtypeStruct((b, a, taps), weights.dtype),
-        compiler_params=PARAMS,
-        cost_estimate=pl.CostEstimate(flops=0, transcendentals=0, bytes_accessed=2 * size),
-        name="swap_channels",
-    )(weights)
-
-
-def start_taps(w_anys, w_vmem, sems):
-    per_group = sems.shape[0] // len(w_anys)
-    size = w_vmem.shape[0] // sems.shape[0]
-    for g, w_any in enumerate(w_anys):
-        for c in range(per_group):
-            at = g * per_group + c
-            pltpu.make_async_copy(
-                w_any.at[pl.ds(c * size, size)], w_vmem.at[pl.ds(at * size, size)], sems.at[at]
-            ).start()
-
-
-def conv_taps(w_vmem, sems, first, wrap, acc, chunk, sub):
-    count = sems.shape[0]
-    size = w_vmem.shape[0] // count
-    groups = acc.shape[0]
-    rows = acc.shape[1]
-    taps = w_vmem.shape[2]
-    per_group = count // groups
+def project_body(where, *refs, layout):
+    stacks = refs[: len(layout)]
+    proj, full, sems = refs[len(layout) :]
+    copies = []
+    for offs, ref in zip(layout, stacks):
+        width = ref.shape[2]
+        for q, off in enumerate(offs):
+            at = pl.multiple_of((where[0] ^ off) * width, width)
+            copies.append(
+                pltpu.make_async_copy(
+                    ref.at[q, 2], full.at[pl.ds(at, width), :], sems.at[len(copies)]
+                )
+            )
+    for c in copies:
+        c.start()
+    for c in copies:
+        c.wait()
+    proj[...] = full[:, : proj.shape[1]]
+
+
+def start_taps(w_any, w_vmem, sems):
+    def start(g, carry):
+        tap_copy(w_any, w_vmem, sems, g).start()
+        return carry
+
+    lax.fori_loop(0, w_vmem.shape[0], start, 0)
+
+
+def tap_copy(w_any, w_vmem, sems, g):
+    return pltpu.make_async_copy(w_any.at[g], w_vmem.at[g], sems.at[g])
+
+
+def conv_group(weights, first, wrap, rows):
+    size, _, taps = weights.shape
     s = lax.broadcasted_iota(jnp.int32, (rows, taps), 0)
     j = lax.broadcasted_iota(jnp.int32, (rows, taps), 1)
     mask = j < rows - 1 - s
-    acc[...] = jnp.zeros_like(acc)
-
-    def step(c, carry):
+    total = None
+    for b in range(0, size, SUB):
+        parts = []
+        for i in range(b, b + SUB):
+            u = jnp.where(mask, wrap[i : i + 1, :], first[i : i + 1, :])
+            u = pltpu.roll(u, taps - (rows - 1), 1, stride=1, stride_axis=0)
+            parts.append(u.astype(BF16))
+        tiles = [weights[i] for i in range(b, b + SUB)]
+        term = dot_nt(jnp.concatenate(parts, 1), jnp.concatenate(tiles, 1))
+        total = term if total is None else total + term
+    return total
+
+
+def conv(w_any, w_vmem, turned, sems, first, wrap, acc, chunk):
+    groups, width = w_vmem.shape[:2]
+    rows = acc.shape[1]
+
+    def step(g, carry):
         if chunk == 0:
-            here = w_vmem.at[pl.ds(c * size, size)]
-            pltpu.make_async_copy(here, here, sems.at[c]).wait()
-        total = acc[c // per_group]
-        for b in range(0, size, sub):
-            parts, weights = [], []
-            at = pl.multiple_of(c * size + b, 8)
-            f8, r8 = first[pl.ds(at, sub), :], wrap[pl.ds(at, sub), :]
-            for i in range(sub):
-                u = jnp.where(mask, r8[i : i + 1], f8[i : i + 1])
-                u = pltpu.roll(u, taps - (rows - 1), 1, stride=1, stride_axis=0)
-                parts.append(u.astype(BF16))
-                weights.append(w_vmem[at + i])
-            total = total + dot_nt(jnp.concatenate(parts, 1), jnp.concatenate(weights, 1))
-        acc[c // per_group] = total
+            tap_copy(w_any, w_vmem, sems, g).wait()
+        weights = w_vmem.at[g]
+        if turned is not None:
+            turned[...] = jnp.swapaxes(w_vmem[g], 0, 1)
+            weights = turned
+        here = pl.ds(pl.multiple_of(g * width, 8), width)
+        acc[g] = conv_group(weights, first.at[here], wrap.at[here], rows)
         return carry
 
-    lax.fori_loop(0, count, step, 0)
+    lax.fori_loop(0, groups, step, 0)
     return jnp.concatenate([acc[g] for g in range(groups)], 1)
 
 
-def forward_body(where, normed, got_a, got_b, *refs, layout, groups):
-    stacks = refs[: len(layout)]
-    w_any, cot, bias, encoded, slope_rev, proj = refs[len(layout) : len(layout) + 6]
-    w_vmem, first, wrap, acc, full, sems, proj_sems = refs[len(layout) + 6 :]
-    copies = place_shards(where[0], layout, stacks, 2, 1, full, proj_sems)
-    start_taps([w_any.at[g] for g in range(groups)], w_vmem, sems)
-    for c in copies:
-        c.wait()
-    proj[...] = full[0, :, : proj.shape[1]]
+def forward_body(where, normed, got_a, got_b, proj, w_any, cot, bias, *refs):
+    encoded, slope_rev, w_vmem, first, wrap, acc, sems = refs
+    start_taps(w_any, w_vmem, sems)
     odd = where[0] % 2 == 1
     low = jnp.where(odd, got_a[...], got_b[...])
     high = jnp.where(odd, got_b[...], got_a[...])
@@ -186,7 +172,7 @@
     for c in range(chunks):
         first[...] = jnp.concatenate([part(c), part(c + 1)], 0).T
         wrap[...] = jnp.concatenate([part(c + 2), part(c + 1)], 0).T
-        pos = conv_taps(w_vmem, sems, first, wrap, acc, c, 8)
+        pos = conv(w_any, w_vmem, None, sems, first, wrap, acc, c)
         pos = pos + bias[...].astype(F32)
         cdf = phi_cdf(pos)
         here = slice(c * rows, (c + 1) * rows)
@@ -198,10 +184,10 @@
         slope_rev[here, :] = (cot_rev * slope).astype(BF16)
 
 
-def backward_body(where, slope_rev, got_a, got_b, *refs, scale, order, groups):
-    w_anys = refs[:groups]
-    cot, normed, proj, kept, sent, unit_grad, w_vmem, first, wrap, acc, hid_grad, full, rows_f32, sems = refs[groups:]
-    start_taps(w_anys, w_vmem, sems)
+def backward_body(where, slope_rev, got_a, got_b, w_any, cot, normed, proj, *refs, scale, order):
+    kept, sent, unit_grad, w_vmem, first, wrap, acc, sems = refs[:8]
+    turned, hid_grad, full, rows_f32 = refs[8:]
+    start_taps(w_any, w_vmem, sems)
     odd = where[0] % 2 == 1
     low = jnp.where(odd, got_a[...], got_b[...])
     high = jnp.where(odd, got_b[...], got_a[...])
@@ -212,7 +198,7 @@
     for c in range(chunks):
         first[...] = jnp.concatenate([part(c + 2), part(c + 1)], 0).T
         wrap[...] = jnp.concatenate([part(c), part(c + 1)], 0).T
-        back = conv_taps(w_vmem, sems, first, wrap, acc, c, 8)
+        back = conv(w_any, w_vmem, turned, sems, first, wrap, acc, c)
         here = slice(c * rows, (c + 1) * rows)
         hid_grad[here, :] = (cot[here, :].astype(F32) + back).astype(BF16)
     grad = hid_grad[...]
@@ -278,10 +264,6 @@
     block = own * slots
 
     w_taps = jnp.transpose(pos_weight, (1, 2, 3, 0))
-    w_back = []
-    for g in range(groups):
-        w_back.append(swap_channels(w_taps, g))
-
     blocks = [features] + [swap(features, "grp", e) for e in range(1, slots)]
     five, layout = spread(jnp.transpose(weight_five, (0, 2, 1)), members)
     proj_half = lax.dynamic_slice_in_dim(projection, slot * columns, columns, 1)
@@ -290,13 +272,11 @@
         jnp.concatenate([jnp.transpose(weight_six, (0, 2, 1)), proj_half[None]], 0), members
     )
     common = dict(layout=layout)
-    taps_scratch = [
-        pltpu.VMEM((2, channels, channels), BF16),
-        pltpu.SemaphoreType.DMA((2 * members,)),
-    ]
+    taps_scratch = [pltpu.VMEM((2, channels, channels), BF16)]
+
     act_five = pl.pallas_call(
         functools.partial(five_body, count=slots, **common),
-        in_specs=[SMEM_SPEC] + vmem_specs(slots) + [ANY_SPEC] * len(five),
+        in_specs=[SMEM_SPEC] + vmem_specs(slots + len(five)),
         out_specs=vmem_specs(1)[0],
         out_shape=jax.ShapeDtypeStruct((2 * block, channels), BF16),
         scratch_shapes=taps_scratch,
@@ -305,7 +285,7 @@
     )(where, *blocks, *five)
     normed, unit, inv_dev = pl.pallas_call(
         functools.partial(six_body, count=slots, **common),
-        in_specs=[SMEM_SPEC] + vmem_specs(1) + [ANY_SPEC] * len(rest),
+        in_specs=[SMEM_SPEC] + vmem_specs(1 + len(rest)),
         out_specs=vmem_specs(3),
         out_shape=[
             jax.ShapeDtypeStruct((block, channels), BF16),
@@ -321,30 +301,34 @@
     tail = normed if whole else normed[block - half :]
     head = normed if whole else normed[:half]
     got_a, got_b = halo(tail, head, me % 2)
-    copies = 5 * groups
+    proj = pl.pallas_call(
+        functools.partial(project_body, **common),
+        in_specs=[SMEM_SPEC] + [ANY_SPEC] * len(rest),
+        out_specs=vmem_specs(1)[0],
+        out_shape=jax.ShapeDtypeStruct((channels, columns), BF16),
+        scratch_shapes=[
+            pltpu.VMEM((channels, channels), BF16),
+            pltpu.SemaphoreType.DMA((members,)),
+        ],
+        compiler_params=PARAMS,
+        name="project",
+    )(where, *rest)
     conv_scratch = [
-        pltpu.VMEM((groups * width, width, taps), BF16),
+        pltpu.VMEM((groups, width, width, taps), BF16),
         pltpu.VMEM((columns, taps), F32),
         pltpu.VMEM((columns, taps), F32),
         pltpu.VMEM((groups, half, width), F32),
+        pltpu.SemaphoreType.DMA((groups,)),
     ]
-    sems = pltpu.SemaphoreType.DMA((copies,))
-    encoded, slope_rev, proj = pl.pallas_call(
-        functools.partial(forward_body, groups=groups, **common),
-        in_specs=[SMEM_SPEC] + vmem_specs(3) + [ANY_SPEC] * (len(rest) + 1) + vmem_specs(2),
-        out_specs=vmem_specs(3),
-        out_shape=[
-            jax.ShapeDtypeStruct((block, columns), BF16),
-            jax.ShapeDtypeStruct((block, columns), BF16),
-            jax.ShapeDtypeStruct((channels, columns), BF16),
-        ],
-        scratch_shapes=conv_scratch
-        + [pltpu.VMEM((1, channels, channels), BF16), sems, pltpu.SemaphoreType.DMA((members,))],
+    encoded, slope_rev = pl.pallas_call(
+        forward_body,
+        in_specs=[SMEM_SPEC] + vmem_specs(4) + [ANY_SPEC] + vmem_specs(2),
+        out_specs=vmem_specs(2),
+        out_shape=[jax.ShapeDtypeStruct((block, columns), BF16)] * 2,
+        scratch_shapes=conv_scratch,
         compiler_params=PARAMS,
         name="forward",
-    )(
-        where, normed, got_a, got_b, *rest, w_taps, cotangent, pos_bias.reshape(1, columns),
-    )
+    )(where, normed, got_a, got_b, proj, w_taps, cotangent, pos_bias.reshape(1, columns))
 
     tail = slope_rev if whole else slope_rev[block - half :]
     head = slope_rev if whole else slope_rev[:half]
@@ -360,21 +344,21 @@
     for mask in reversed(masks):
         order = order + [p ^ mask for p in order]
     kept, sent, unit_grad = pl.pallas_call(
-        functools.partial(backward_body, scale=scale, order=order, groups=groups),
-        in_specs=[SMEM_SPEC] + vmem_specs(3) + [ANY_SPEC] * groups + vmem_specs(3),
+        functools.partial(backward_body, scale=scale, order=order),
+        in_specs=[SMEM_SPEC] + vmem_specs(3) + [ANY_SPEC] + vmem_specs(3),
         out_specs=vmem_specs(3),
         out_shape=[jax.ShapeDtypeStruct((members // 2, share, columns), BF16)] * 2
         + [jax.ShapeDtypeStruct((slots, own, channels), F32)],
         scratch_shapes=conv_scratch
         + [
+            pltpu.VMEM((width, width, taps), BF16),
             pltpu.VMEM((block, columns), BF16),
             pltpu.VMEM((members, share, columns), F32),
             pltpu.VMEM((slots, own, channels), F32),
-            sems,
         ],
         compiler_params=PARAMS,
         name="backward",
-    )(where, slope_rev, got_a, got_b, *w_back, cotangent, normed, proj)
+    )(where, slope_rev, got_a, got_b, w_taps, cotangent, normed, proj)
 
     total = (kept.astype(F32) + swap(sent, "tm", 1).astype(F32)).astype(BF16)
     for mask in masks:

time: 132 us -> 110 us (0.83)
  Pallas kernels: 54 us -> 29.5 us
    pallas_call x6 -> x3, Pallas kernels: 46.2 us -> 23.8 us  [the longest x1 10.7 us: on_device(): pl.pallas_call(functools.partial(backward_body, scale=scale, order=order)...]
    unnamed x34 -> x32, local copies, waits for them, and re-layouts: 5.02 us -> 5.04 us
  transfers between devices with their start and end apart: 21 -> 21, of which waited for: 10 -> 10; matrix products, arithmetic and copies ran while one was open for 5% -> 7% of each run, Pallas kernels for 16% -> 5%
where the time goes in v1:
time: 110 us; the launch traced here: 109 us
  starting transfers between devices  34.2 us (31%)
  waiting for transfers between devices  29.5 us (27%)
  Pallas kernels  29.5 us (27%)
  other arithmetic  7.45 us (7%)
  local copies, waits for them, and re-layouts  7.37 us (7%)
    ppermute x19, starting transfers between devices, swap(): return lax.ppermute(values, axis, [(i, i ^ mask) for i in range(count)])  32.9 us
    ppermute x19, waiting for transfers between devices, swap(): return lax.ppermute(values, axis, [(i, i ^ mask) for i in range(count)])  29.5 us
    pallas_call x1, Pallas kernels, on_device(): pl.pallas_call(functools.partial(backward_body, scale=scale, order=order)...  10.7 us
    pallas_call x1, Pallas kernels, on_device(): pl.pallas_call(forward_body, in_specs=[SMEM_SPEC] + vmem_specs(4) + [ANY_...  10.4 us
    unnamed x32, local copies, waits for them, and re-layouts  5.04 us
    pallas_call x1, Pallas kernels, on_device(): pl.pallas_call(functools.partial(six_body, count=slots, **common), in_spe...  2.94 us
    pallas_call x1, Pallas kernels, on_device(): pl.pallas_call(functools.partial(five_body, count=slots, **common), in_sp...  2.79 us
    pallas_call x1, Pallas kernels, on_device(): pl.pallas_call(functools.partial(project_body, **common), in_specs=[SMEM_...  2.64 us
  transfers between devices with their start and end apart: 21, of which 10 were waited for; matrix products, arithmetic and copies ran while one was open for 7% of the time, Pallas kernels for 5%

profile of v1, /device:TPU:0, one launch (start us, length us, event | category | flops | bytes accessed | tf_op | source)
XLA Modules:
  0.0 108.9 jit_solution(1201158116945475592)
XLA Ops:
  0.6 0.8 copy-done
  1.6 0.9 maximum_bitcast_fusion
  2.4 4.1 %collective-permute-start.6 = (bf16[1,3,32,512]{3,2,1,0:T(8,128)(2,1)S(1)}, bf16[1,3,32,512]{3,2,1,0:T(8,128)(2,1)S(1)}, u32[]{:S(2)}, u32[]{:S(2)}) collective-permute-start(bf16[1,3,32,512]{3,2,1,0:T(8,128)(2,1)S(1)} %maximum_bitcast_fusion), channel_id=1, source_target_pairs={{0,16},{2,18},{4,20},{6,22},{8,24},{10,26},{12,28},{14,30},{16,0},... | collective-permute-start | bytes 294920 | tf_op jit(solution)/shard_map/ppermute | solution.py:228
  6.6 4.9 %collective-permute-done.6 = bf16[1,3,32,512]{3,2,1,0:T(8,128)(2,1)S(1)} collective-permute-done((bf16[1,3,32,512]{3,2,1,0:T(8,128)(2,1)S(1)}, bf16[1,3,32,512]{3,2,1,0:T(8,128)(2,1)S(1)}, u32[]{:S(2)}, u32[]{:S(2)}) %collective-permute-start.6) | collective-permute-done | bytes 98336 | tf_op jit(solution)/shard_map/ppermute | solution.py:228
  11.5 0.8 collective-permute-start.7
  12.3 3.4 %collective-permute-start.1 = (bf16[1,2,32,512]{3,2,1,0:T(8,128)(2,1)}, bf16[1,2,32,512]{3,2,1,0:T(8,128)(2,1)S(1)}, u32[]{:S(2)}, u32[]{:S(2)}) collective-permute-start(bf16[1,2,32,512]{3,2,1,0:T(8,128)(2,1)} %bitcast.34), channel_id=1, source_target_pairs={{0,16},{2,18},{4,20},{6,22},{8,24},{10,26},{12,28},{14,30},{16,0},... | collective-permute-start | bytes 196616 | tf_op jit(solution)/shard_map/ppermute | solution.py:228
  15.6 3.4 %collective-permute-done.7 = bf16[2,3,32,512]{3,2,1,0:T(8,128)(2,1)S(1)} collective-permute-done((bf16[2,3,32,512]{3,2,1,0:T(8,128)(2,1)S(1)}, bf16[2,3,32,512]{3,2,1,0:T(8,128)(2,1)S(1)}, u32[]{:S(2)}, u32[]{:S(2)}) %collective-permute-start.7) | collective-permute-done | bytes 196640 | tf_op jit(solution)/shard_map/ppermute | solution.py:228
  19.1 1.3 %collective-permute-start.8 = (bf16[4,3,32,512]{3,2,1,0:T(8,128)(2,1)S(1)}, bf16[4,3,32,512]{3,2,1,0:T(8,128)(2,1)S(1)}, u32[]{:S(2)}, u32[]{:S(2)}) collective-permute-start(bf16[4,3,32,512]{3,2,1,0:T(8,128)(2,1)S(1)} %pad_maximum_fusion.refs_0_), channel_id=1, source_target_pairs={{0,4},{2,6},{4,0},{6,2},{8,12},{10,14},{12,8},{14,10},{16,20},{18,... | collective-permute-start | bytes 1179656 | tf_op jit(solution)/shard_map/ppermute | solution.py:228
  20.4 0.9 pad_maximum_fusion.3
  21.3 1.8 %collective-permute-start.2 = (bf16[2,2,32,512]{3,2,1,0:T(8,128)(2,1)S(1)}, bf16[2,2,32,512]{3,2,1,0:T(8,128)(2,1)S(1)}, u32[]{:S(2)}, u32[]{:S(2)}) collective-permute-start(bf16[2,2,32,512]{3,2,1,0:T(8,128)(2,1)S(1)} %pad_maximum_fusion.3), channel_id=1, source_target_pairs={{0,8},{2,10},{4,12},{6,14},{8,0},{10,2},{12,4},{14,6},{16,24},{18,... | collective-permute-start | bytes 393224 | tf_op jit(solution)/shard_map/ppermute | solution.py:228
  23.1 3.2 %collective-permute-done.2 = bf16[2,2,32,512]{3,2,1,0:T(8,128)(2,1)S(1)} collective-permute-done((bf16[2,2,32,512]{3,2,1,0:T(8,128)(2,1)S(1)}, bf16[2,2,32,512]{3,2,1,0:T(8,128)(2,1)S(1)}, u32[]{:S(2)}, u32[]{:S(2)}) %collective-permute-start.2) | collective-permute-done | bytes 131104 | tf_op jit(solution)/shard_map/ppermute | solution.py:228
  26.3 0.9 pad_maximum_fusion.1.refs_2_
  27.2 1.5 %collective-permute-start.3 = (bf16[4,2,32,512]{3,2,1,0:T(8,128)(2,1)S(1)}, bf16[4,2,32,512]{3,2,1,0:T(8,128)(2,1)S(1)}, u32[]{:S(2)}, u32[]{:S(2)}) collective-permute-start(bf16[4,2,32,512]{3,2,1,0:T(8,128)(2,1)S(1)} %pad_maximum_fusion.1.refs_2_), channel_id=1, source_target_pairs={{0,4},{2,6},{4,0},{6,2},{8,12},{10,14},{12,8},{14,10},{16,20},{18,... | collective-permute-start | bytes 786440 | tf_op jit(solution)/shard_map/ppermute | solution.py:228
  29.2 4.8 %collective-permute-done.3.refs_3_ = bf16[4,2,32,512]{3,2,1,0:T(8,128)(2,1)S(1)} collective-permute-done((bf16[4,2,32,512]{3,2,1,0:T(8,128)(2,1)S(1)}, bf16[4,2,32,512]{3,2,1,0:T(8,128)(2,1)S(1)}, u32[]{:S(2)}, u32[]{:S(2)}) %collective-permute-start.3) | collective-permute-done | bytes 262176 | tf_op jit(solution)/shard_map/ppermute | solution.py:228
  34.0 1.5 %collective-permute-start = (bf16[128,512]{1,0:T(8,128)(2,1)}, bf16[128,512]{1,0:T(8,128)(2,1)S(1)}, u32[]{:S(2)}, u32[]{:S(2)}) collective-permute-start(bf16[128,512]{1,0:T(8,128)(2,1)} %refs_0_.1), channel_id=1, source_target_pairs={{0,1},{1,0},{2,3},{3,2},{4,5},{5,4},{6,7},{7,6},{8,9},{9,8},{10,11... | collective-permute-start | bytes 393224 | tf_op jit(solution)/shard_map/ppermute | solution.py:228
  35.5 0.6 pad_add_fusion.where
  36.1 4.0 %collective-permute-done.refs_1_ = bf16[128,512]{1,0:T(8,128)(2,1)S(1)} collective-permute-done((bf16[128,512]{1,0:T(8,128)(2,1)}, bf16[128,512]{1,0:T(8,128)(2,1)S(1)}, u32[]{:S(2)}, u32[]{:S(2)}) %collective-permute-start) | collective-permute-done | bytes 131104 | tf_op jit(solution)/shard_map/ppermute | solution.py:228
  40.2 0.6 copy-done.10
  40.9 0.7 copy-done.9
  41.6 2.8 %five.1.act = bf16[128,512]{1,0:T(8,128)(2,1)} custom-call(s32[2]{0:T(128)} %pad_add_fusion.where, bf16[128,512]{1,0:T(8,128)(2,1)} %refs_0_.1, bf16[128,512]{1,0:T(8,128)(2,1)} %copy-done.10, bf16[4,2,32,512]{3,2,1,0:T(8,128)(2,1)} %copy-done.5, bf16[4,2,32,512]{3,2,1,0:T(8,128)(2,1)} %copy-done.7, bf16[4,2,32,512]{3,2,1,0:T(8,128)(2,1)} %copy-done.8, ...), custom_call_target="tpu_custom_call" | custom-call | tf_op jit(solution)/shard_map/five/pallas_call | solution.py:277
  44.4 0.8 copy-done.3
  45.2 0.7 copy-done.4
  45.9 2.9 %six.1 = (bf16[64,512]{1,0:T(8,128)(2,1)}, f32[32,512]{1,0:T(8,128)}, f32[32,128]{1,0:T(8,128)}) custom-call(s32[2]{0:T(128)} %pad_add_fusion.where, bf16[128,512]{1,0:T(8,128)(2,1)} %five.1.act, bf16[4,3,32,512]{3,2,1,0:T(8,128)(2,1)} %copy-done.1, bf16[4,3,32,512]{3,2,1,0:T(8,128)(2,1)} %copy-done.2, bf16[4,3,32,512]{3,2,1,0:T(8,128)(2,1)} %copy-done.3, ...), custom_call_target="tpu_custom_call" | custom-call | tf_op jit(solution)/shard_map/six/pallas_call | solution.py:286
  48.9 0.7 collective-permute-start.12
  49.5 3.1 %collective-permute-start.11 = (bf16[64,512]{1,0:T(8,128)(2,1)}, bf16[64,512]{1,0:T(8,128)(2,1)S(1)}, u32[]{:S(2)}, u32[]{:S(2)}) collective-permute-start(bf16[64,512]{1,0:T(8,128)(2,1)} %get-tuple-element.11.normed), channel_id=1, source_target_pairs={{0,2},{2,0},{4,6},{6,4},{8,10},{10,8},{12,14},{14,12},{16,18},{18,... | collective-permute-start | bytes 196616 | tf_op jit(solution)/shard_map/ppermute | solution.py:228
  52.7 1.3 %reshape.20.bias = bf16[1,480]{1,0:T(2,128)(2,1)} reshape(bf16[480]{0:T(512)(128)(2,1)} %param.12) | data formatting | bytes 1920 | tf_op jit(solution)/shard_map/reshape | solution.py:331
  53.9 2.6 %project.1.proj = bf16[512,480]{1,0:T(8,128)(2,1)} custom-call(s32[2]{0:T(128)} %pad_add_fusion.where, bf16[4,3,32,512]{3,2,1,0:T(8,128)(2,1)} %copy-done.1, bf16[4,3,32,512]{3,2,1,0:T(8,128)(2,1)} %copy-done.2, bf16[4,3,32,512]{3,2,1,0:T(8,128)(2,1)} %copy-done.3, bf16[4,3,32,512]{3,2,1,0:T(8,128)(2,1)} %copy-done.4), custom_call_target="tpu_custom_call" | custom-call | tf_op jit(solution)/shard_map/project/pallas_call | solution.py:304
  56.6 0.6 copy-done.11
  57.2 10.4 %forward.1 = (bf16[64,480]{1,0:T(8,128)(2,1)}, bf16[64,480]{1,0:T(8,128)(2,1)}) custom-call(s32[2]{0:T(128)} %pad_add_fusion.where, bf16[64,512]{1,0:T(8,128)(2,1)} %get-tuple-element.11.normed, bf16[64,512]{1,0:T(8,128)(2,1)} %copy-done.13, bf16[64,512]{1,0:T(8,128)(2,1)} %copy-done.11, bf16[512,480]{1,0:T(8,128)(2,1)} %project.1.proj, ...), custom_call_target="tpu_custom_call" | custom-call | tf_op jit(solution)/shard_map/forward/pallas_call | solution.py:323
  67.6 0.7 collective-permute-start.14
  68.3 2.9 %collective-permute-start.13 = (bf16[64,480]{1,0:T(8,128)(2,1)}, bf16[64,480]{1,0:T(8,128)(2,1)S(1)}, u32[]{:S(2)}, u32[]{:S(2)}) collective-permute-start(bf16[64,480]{1,0:T(8,128)(2,1)} %get-tuple-element.14.slope_rev), channel_id=1, source_target_pairs={{0,2},{2,0},{4,6},{6,4},{8,10},{10,8},{12,14},{14,12},{16,18},{18,... | collective-permute-start | bytes 184328 | tf_op jit(solution)/shard_map/ppermute | solution.py:228
  71.2 1.1 %collective-permute-done.13.got_a = bf16[64,480]{1,0:T(8,128)(2,1)S(1)} collective-permute-done((bf16[64,480]{1,0:T(8,128)(2,1)}, bf16[64,480]{1,0:T(8,128)(2,1)S(1)}, u32[]{:S(2)}, u32[]{:S(2)}) %collective-permute-start.13) | collective-permute-done | bytes 61472 | tf_op jit(solution)/shard_map/ppermute | solution.py:228
  72.3 0.6 copy-done.14
  73.0 10.7 %backward.1 = (bf16[8,32,480]{2,1,0:T(8,128)(2,1)}, bf16[8,32,480]{2,1,0:T(8,128)(2,1)}, f32[2,32,512]{2,1,0:T(8,128)}) custom-call(s32[2]{0:T(128)} %pad_add_fusion.where, bf16[64,480]{1,0:T(8,128)(2,1)} %get-tuple-element.14.slope_rev, bf16[64,480]{1,0:T(8,128)(2,1)} %copy-done.14, bf16[64,480]{1,0:T(8,128)(2,1)} %copy-done.12, ...), custom_call_target="tpu_custom_call" | custom-call | tf_op jit(solution)/shard_map/backward/pallas_call | solution.py:346
  83.7 1.8 %collective-permute-start.16 = (bf16[8,32,480]{2,1,0:T(8,128)(2,1)}, bf16[8,32,480]{2,1,0:T(8,128)(2,1)S(1)}, u32[]{:S(2)}, u32[]{:S(2)}) collective-permute-start(bf16[8,32,480]{2,1,0:T(8,128)(2,1)} %get-tuple-element.18), channel_id=1, source_target_pairs={{0,2},{2,0},{4,6},{6,4},{8,10},{10,8},{12,14},{14,12},{16,18},{18,... | collective-permute-start | bytes 737288 | tf_op jit(solution)/shard_map/ppermute | solution.py:228
  85.5 0.8 fusion
  86.3 1.5 %collective-permute-start.15 = (bf16[32,512]{1,0:T(8,128)(2,1)S(1)}, bf16[32,512]{1,0:T(8,128)(2,1)S(1)}, u32[]{:S(2)}, u32[]{:S(2)}) collective-permute-start(bf16[32,512]{1,0:T(8,128)(2,1)S(1)} %fusion), channel_id=1, source_target_pairs={{0,1},{1,0},{2,3},{3,2},{4,5},{5,4},{6,7},{7,6},{8,9},{9,8},{10,11... | collective-permute-start | bytes 98312 | tf_op jit(solution)/shard_map/ppermute | solution.py:228
  87.9 2.3 %collective-permute-done.15 = bf16[32,512]{1,0:T(8,128)(2,1)S(1)} collective-permute-done((bf16[32,512]{1,0:T(8,128)(2,1)S(1)}, bf16[32,512]{1,0:T(8,128)(2,1)S(1)}, u32[]{:S(2)}, u32[]{:S(2)}) %collective-permute-start.15) | collective-permute-done | bytes 32800 | tf_op jit(solution)/shard_map/ppermute | solution.py:228
  90.2 1.0 fusion.1
  91.2 1.0 add_convert_fusion
  92.3 2.5 %collective-permute-start.17 = (bf16[4,32,480]{2,1,0:T(8,128)(2,1)S(1)}, bf16[4,32,480]{2,1,0:T(8,128)(2,1)S(1)}, u32[]{:S(2)}, u32[]{:S(2)}) collective-permute-start(bf16[4,32,480]{2,1,0:T(8,128)(2,1)S(1)} %slice.39), channel_id=1, source_target_pairs={{0,4},{2,6},{4,0},{6,2},{8,12},{10,14},{12,8},{14,10},{16,20},{18,... | collective-permute-start | bytes 368648 | tf_op jit(solution)/shard_map/ppermute | solution.py:228
  94.7 2.9 %collective-permute-done.17 = bf16[4,32,480]{2,1,0:T(8,128)(2,1)S(1)} collective-permute-done((bf16[4,32,480]{2,1,0:T(8,128)(2,1)S(1)}, bf16[4,32,480]{2,1,0:T(8,128)(2,1)S(1)}, u32[]{:S(2)}, u32[]{:S(2)}) %collective-permute-start.17) | collective-permute-done | bytes 122912 | tf_op jit(solution)/shard_map/ppermute | solution.py:228
  97.7 2.4 %collective-permute-start.18 = (bf16[32,480]{1,0:T(8,128)(2,1)S(1)}, bf16[32,480]{1,0:T(8,128)(2,1)S(1)}, u32[]{:S(2)}, u32[]{:S(2)}) collective-permute-start(bf16[32,480]{1,0:T(8,128)(2,1)S(1)} %get-tuple-element.21), channel_id=1, source_target_pairs={{0,8},{2,10},{4,12},{6,14},{8,0},{10,2},{12,4},{14,6},{16,24},{18,... | collective-permute-start | bytes 92168 | tf_op jit(solution)/shard_map/ppermute | solution.py:228
  100.1 3.3 %collective-permute-start.20 = (bf16[32,480]{1,0:T(8,128)(2,1)S(1)}, bf16[32,480]{1,0:T(8,128)(2,1)S(1)}, u32[]{:S(2)}, u32[]{:S(2)}) collective-permute-start(bf16[32,480]{1,0:T(8,128)(2,1)S(1)} %get-tuple-element.22), channel_id=1, source_target_pairs={{0,24},{2,26},{4,28},{6,30},{8,16},{10,18},{12,20},{14,22},{16,8},... | collective-permute-start | bytes 92168 | tf_op jit(solution)/shard_map/ppermute | solution.py:228
  103.9 1.5 %multiply_convert_fusion = bf16[32,512]{1,0:T(8,128)(2,1)} fusion(f32[32,512]{1,0:T(8,128)S(1)} %copy-done.6, f32[32]{0:T(128)S(1)} %get-tuple-element.24, f32[32]{0:T(128)S(1)} %get-tuple-element.25, f32[32]{0:T(128)S(1)} %slice_reduce_fusion, bf16[32,512]{1,0:T(8,128)(2,1)S(1)} %collective-permute-done.15, f32[2,32,512]{2,1,0:T(8,128)} %get-tuple-element.15), kind=kLoop, calls=%fused_computation.10 | loop fusion | flops 114688 | bytes 196992 | tf_op jit(solution)/shard_map/convert_element_type | solution.py:376
  105.5 0.6 collective-permute-done.20
  106.1 2.1 %collective-permute-done.19 = bf16[32,480]{1,0:T(8,128)(2,1)S(1)} collective-permute-done((bf16[32,480]{1,0:T(8,128)(2,1)S(1)}, bf16[32,480]{1,0:T(8,128)(2,1)S(1)}, u32[]{:S(2)}, u32[]{:S(2)}) %collective-permute-start.19) | collective-permute-done | bytes 30752 | tf_op jit(solution)/shard_map/ppermute | solution.py:228
  108.2 0.6 convert_add_fusion
  (50 shorter events, 1.6 us)
Async XLA Ops:
  0.6 0.8 copy-start
  2.4 9.0 %collective-permute-start.6 = (bf16[1,3,32,512]{3,2,1,0:T(8,128)(2,1)S(1)}, bf16[1,3,32,512]{3,2,1,0:T(8,128)(2,1)S(1)}, u32[]{:S(2)}, u32[]{:S(2)}) collective-permute-start(bf16[1,3,32,512]{3,2,1,0:T(8,128)(2,1)S(1)} %maximum_bitcast_fusion), channel_id=1, source_target_pairs={{0,16},{2,18},{4,20},{6,22},{8,24},{10,26},{12,28},{14,30},{16,0},... | collective-permute-start | bytes 294920 | tf_op jit(solution)/shard_map/ppermute | solution.py:228
  11.5 7.5 %collective-permute-start.7 = (bf16[2,3,32,512]{3,2,1,0:T(8,128)(2,1)S(1)}, bf16[2,3,32,512]{3,2,1,0:T(8,128)(2,1)S(1)}, u32[]{:S(2)}, u32[]{:S(2)}) collective-permute-start(bf16[2,3,32,512]{3,2,1,0:T(8,128)(2,1)S(1)} %pad_maximum_fusion.2), channel_id=1, source_target_pairs={{0,8},{2,10},{4,12},{6,14},{8,0},{10,2},{12,4},{14,6},{16,24},{18,... | collective-permute-start | bytes 589832 | tf_op jit(solution)/shard_map/ppermute | solution.py:228
  12.3 8.1 %collective-permute-start.1 = (bf16[1,2,32,512]{3,2,1,0:T(8,128)(2,1)}, bf16[1,2,32,512]{3,2,1,0:T(8,128)(2,1)S(1)}, u32[]{:S(2)}, u32[]{:S(2)}) collective-permute-start(bf16[1,2,32,512]{3,2,1,0:T(8,128)(2,1)} %bitcast.34), channel_id=1, source_target_pairs={{0,16},{2,18},{4,20},{6,22},{8,24},{10,26},{12,28},{14,30},{16,0},... | collective-permute-start | bytes 196616 | tf_op jit(solution)/shard_map/ppermute | solution.py:228
  19.1 25.4 %copy-start.1 = (bf16[4,3,32,512]{3,2,1,0:T(8,128)(2,1)}, bf16[4,3,32,512]{3,2,1,0:T(8,128)(2,1)S(1)}, u32[]{:S(2)}) copy-start(bf16[4,3,32,512]{3,2,1,0:T(8,128)(2,1)S(1)} %pad_maximum_fusion.refs_0_) | copy-start | bytes 1179652
  19.1 9.6 %collective-permute-start.8 = (bf16[4,3,32,512]{3,2,1,0:T(8,128)(2,1)S(1)}, bf16[4,3,32,512]{3,2,1,0:T(8,128)(2,1)S(1)}, u32[]{:S(2)}, u32[]{:S(2)}) collective-permute-start(bf16[4,3,32,512]{3,2,1,0:T(8,128)(2,1)S(1)} %pad_maximum_fusion.refs_0_), channel_id=1, source_target_pairs={{0,4},{2,6},{4,0},{6,2},{8,12},{10,14},{12,8},{14,10},{16,20},{18,... | collective-permute-start | bytes 1179656 | tf_op jit(solution)/shard_map/ppermute | solution.py:228
  21.3 5.0 %collective-permute-start.2 = (bf16[2,2,32,512]{3,2,1,0:T(8,128)(2,1)S(1)}, bf16[2,2,32,512]{3,2,1,0:T(8,128)(2,1)S(1)}, u32[]{:S(2)}, u32[]{:S(2)}) collective-permute-start(bf16[2,2,32,512]{3,2,1,0:T(8,128)(2,1)S(1)} %pad_maximum_fusion.3), channel_id=1, source_target_pairs={{0,8},{2,10},{4,12},{6,14},{8,0},{10,2},{12,4},{14,6},{16,24},{18,... | collective-permute-start | bytes 393224 | tf_op jit(solution)/shard_map/ppermute | solution.py:228
  27.2 13.0 %copy-start.5 = (bf16[4,2,32,512]{3,2,1,0:T(8,128)(2,1)}, bf16[4,2,32,512]{3,2,1,0:T(8,128)(2,1)S(1)}, u32[]{:S(2)}) copy-start(bf16[4,2,32,512]{3,2,1,0:T(8,128)(2,1)S(1)} %pad_maximum_fusion.1.refs_2_) | copy-start | bytes 786436
  27.2 6.9 %collective-permute-start.3 = (bf16[4,2,32,512]{3,2,1,0:T(8,128)(2,1)S(1)}, bf16[4,2,32,512]{3,2,1,0:T(8,128)(2,1)S(1)}, u32[]{:S(2)}, u32[]{:S(2)}) collective-permute-start(bf16[4,2,32,512]{3,2,1,0:T(8,128)(2,1)S(1)} %pad_maximum_fusion.1.refs_2_), channel_id=1, source_target_pairs={{0,4},{2,6},{4,0},{6,2},{8,12},{10,14},{12,8},{14,10},{16,20},{18,... | collective-permute-start | bytes 786440 | tf_op jit(solution)/shard_map/ppermute | solution.py:228
  28.6 15.8 %collective-permute-start.9 = (bf16[4,3,32,512]{3,2,1,0:T(8,128)(2,1)S(1)}, bf16[4,3,32,512]{3,2,1,0:T(8,128)(2,1)S(1)}, u32[]{:S(2)}, u32[]{:S(2)}) collective-permute-start(bf16[4,3,32,512]{3,2,1,0:T(8,128)(2,1)S(1)} %pad_maximum_fusion.refs_0_), channel_id=1, source_target_pairs={{0,2},{2,0},{4,6},{6,4},{8,10},{10,8},{12,14},{14,12},{16,18},{18,... | collective-permute-start | bytes 1179656 | tf_op jit(solution)/shard_map/ppermute | solution.py:228
  28.6 15.8 %copy-start.2 = (bf16[4,3,32,512]{3,2,1,0:T(8,128)(2,1)}, bf16[4,3,32,512]{3,2,1,0:T(8,128)(2,1)S(1)}, u32[]{:S(2)}) copy-start(bf16[4,3,32,512]{3,2,1,0:T(8,128)(2,1)S(1)} %collective-permute-done.8.refs_1_) | copy-start | bytes 1179652
  28.6 15.8 %collective-permute-start.10 = (bf16[4,3,32,512]{3,2,1,0:T(8,128)(2,1)S(1)}, bf16[4,3,32,512]{3,2,1,0:T(8,128)(2,1)S(1)}, u32[]{:S(2)}, u32[]{:S(2)}) collective-permute-start(bf16[4,3,32,512]{3,2,1,0:T(8,128)(2,1)S(1)} %collective-permute-done.8.refs_1_), channel_id=1, source_target_pairs={{0,2},{2,0},{4,6},{6,4},{8,10},{10,8},{12,14},{14,12},{16,18},{18,... | collective-permute-start | bytes 1179656 | tf_op jit(solution)/shard_map/ppermute | solution.py:228
  29.1 11.0 %collective-permute-start.4 = (bf16[4,2,32,512]{3,2,1,0:T(8,128)(2,1)S(1)}, bf16[4,2,32,512]{3,2,1,0:T(8,128)(2,1)S(1)}, u32[]{:S(2)}, u32[]{:S(2)}) collective-permute-start(bf16[4,2,32,512]{3,2,1,0:T(8,128)(2,1)S(1)} %pad_maximum_fusion.1.refs_2_), channel_id=1, source_target_pairs={{0,2},{2,0},{4,6},{6,4},{8,10},{10,8},{12,14},{14,12},{16,18},{18,... | collective-permute-start | bytes 786440 | tf_op jit(solution)/shard_map/ppermute | solution.py:228
  34.0 6.2 %copy-start.7 = (bf16[4,2,32,512]{3,2,1,0:T(8,128)(2,1)}, bf16[4,2,32,512]{3,2,1,0:T(8,128)(2,1)S(1)}, u32[]{:S(2)}) copy-start(bf16[4,2,32,512]{3,2,1,0:T(8,128)(2,1)S(1)} %collective-permute-done.3.refs_3_) | copy-start | bytes 786436
  34.0 6.1 %collective-permute-start.5 = (bf16[4,2,32,512]{3,2,1,0:T(8,128)(2,1)S(1)}, bf16[4,2,32,512]{3,2,1,0:T(8,128)(2,1)S(1)}, u32[]{:S(2)}, u32[]{:S(2)}) collective-permute-start(bf16[4,2,32,512]{3,2,1,0:T(8,128)(2,1)S(1)} %collective-permute-done.3.refs_3_), channel_id=1, source_target_pairs={{0,2},{2,0},{4,6},{6,4},{8,10},{10,8},{12,14},{14,12},{16,18},{18,... | collective-permute-start | bytes 786440 | tf_op jit(solution)/shard_map/ppermute | solution.py:228
  34.0 6.1 %collective-permute-start = (bf16[128,512]{1,0:T(8,128)(2,1)}, bf16[128,512]{1,0:T(8,128)(2,1)S(1)}, u32[]{:S(2)}, u32[]{:S(2)}) collective-permute-start(bf16[128,512]{1,0:T(8,128)(2,1)} %refs_0_.1), channel_id=1, source_target_pairs={{0,1},{1,0},{2,3},{3,2},{4,5},{5,4},{6,7},{7,6},{8,9},{9,8},{10,11... | collective-permute-start | bytes 393224 | tf_op jit(solution)/shard_map/ppermute | solution.py:228
  40.2 0.6 copy-start.10
  40.2 0.8 copy-start.8
  40.9 0.7 copy-start.9
  44.4 0.8 copy-start.3
  45.2 0.7 copy-start.4
  48.9 7.7 %collective-permute-start.12 = (bf16[64,512]{1,0:T(8,128)(2,1)}, bf16[64,512]{1,0:T(8,128)(2,1)S(1)}, u32[]{:S(2)}, u32[]{:S(2)}) collective-permute-start(bf16[64,512]{1,0:T(8,128)(2,1)} %get-tuple-element.11.normed), channel_id=1, source_target_pairs={{2,4},{6,8},{10,12},{14,16},{18,20},{22,24},{26,28},{4,2},{8,6},{1... | collective-permute-start | bytes 196616 | tf_op jit(solution)/shard_map/ppermute | solution.py:251
  49.5 7.1 %collective-permute-start.11 = (bf16[64,512]{1,0:T(8,128)(2,1)}, bf16[64,512]{1,0:T(8,128)(2,1)S(1)}, u32[]{:S(2)}, u32[]{:S(2)}) collective-permute-start(bf16[64,512]{1,0:T(8,128)(2,1)} %get-tuple-element.11.normed), channel_id=1, source_target_pairs={{0,2},{2,0},{4,6},{6,4},{8,10},{10,8},{12,14},{14,12},{16,18},{18,... | collective-permute-start | bytes 196616 | tf_op jit(solution)/shard_map/ppermute | solution.py:228
  56.6 0.6 copy-start.11
  56.6 0.6 copy-start.13
  57.2 30.6 %copy-start.15 = (f32[32,128]{1,0:T(8,128)S(1)}, f32[32,128]{1,0:T(8,128)}, u32[]{:S(2)}) copy-start(f32[32,128]{1,0:T(8,128)} %get-tuple-element.13) | copy-start | bytes 49156
  57.2 33.0 %copy-start.6 = (f32[32,512]{1,0:T(8,128)S(1)}, f32[32,512]{1,0:T(8,128)}, u32[]{:S(2)}) copy-start(f32[32,512]{1,0:T(8,128)} %get-tuple-element.16) | copy-start | bytes 196612
  67.6 3.6 %collective-permute-start.14 = (bf16[64,480]{1,0:T(8,128)(2,1)}, bf16[64,480]{1,0:T(8,128)(2,1)S(1)}, u32[]{:S(2)}, u32[]{:S(2)}) collective-permute-start(bf16[64,480]{1,0:T(8,128)(2,1)} %get-tuple-element.14.slope_rev), channel_id=1, source_target_pairs={{2,4},{6,8},{10,12},{14,16},{18,20},{22,24},{26,28},{4,2},{8,6},{1... | collective-permute-start | bytes 184328 | tf_op jit(solution)/shard_map/ppermute | solution.py:251
  68.3 4.1 %collective-permute-start.13 = (bf16[64,480]{1,0:T(8,128)(2,1)}, bf16[64,480]{1,0:T(8,128)(2,1)S(1)}, u32[]{:S(2)}, u32[]{:S(2)}) collective-permute-start(bf16[64,480]{1,0:T(8,128)(2,1)} %get-tuple-element.14.slope_rev), channel_id=1, source_target_pairs={{0,2},{2,0},{4,6},{6,4},{8,10},{10,8},{12,14},{14,12},{16,18},{18,... | collective-permute-start | bytes 184328 | tf_op jit(solution)/shard_map/ppermute | solution.py:228
  71.2 1.1 %copy-start.12 = (bf16[64,480]{1,0:T(8,128)(2,1)}, bf16[64,480]{1,0:T(8,128)(2,1)S(1)}, u32[]{:S(2)}) copy-start(bf16[64,480]{1,0:T(8,128)(2,1)S(1)} %collective-permute-done.14.got_b) | copy-start | bytes 184324
  72.3 0.6 copy-start.14
  83.7 7.5 %collective-permute-start.16 = (bf16[8,32,480]{2,1,0:T(8,128)(2,1)}, bf16[8,32,480]{2,1,0:T(8,128)(2,1)S(1)}, u32[]{:S(2)}, u32[]{:S(2)}) collective-permute-start(bf16[8,32,480]{2,1,0:T(8,128)(2,1)} %get-tuple-element.18), channel_id=1, source_target_pairs={{0,2},{2,0},{4,6},{6,4},{8,10},{10,8},{12,14},{14,12},{16,18},{18,... | collective-permute-start | bytes 737288 | tf_op jit(solution)/shard_map/ppermute | solution.py:228
  86.3 3.9 %collective-permute-start.15 = (bf16[32,512]{1,0:T(8,128)(2,1)S(1)}, bf16[32,512]{1,0:T(8,128)(2,1)S(1)}, u32[]{:S(2)}, u32[]{:S(2)}) collective-permute-start(bf16[32,512]{1,0:T(8,128)(2,1)S(1)} %fusion), channel_id=1, source_target_pairs={{0,1},{1,0},{2,3},{3,2},{4,5},{5,4},{6,7},{7,6},{8,9},{9,8},{10,11... | collective-permute-start | bytes 98312 | tf_op jit(solution)/shard_map/ppermute | solution.py:228
  92.3 5.4 %collective-permute-start.17 = (bf16[4,32,480]{2,1,0:T(8,128)(2,1)S(1)}, bf16[4,32,480]{2,1,0:T(8,128)(2,1)S(1)}, u32[]{:S(2)}, u32[]{:S(2)}) collective-permute-start(bf16[4,32,480]{2,1,0:T(8,128)(2,1)S(1)} %slice.39), channel_id=1, source_target_pairs={{0,4},{2,6},{4,0},{6,2},{8,12},{10,14},{12,8},{14,10},{16,20},{18,... | collective-permute-start | bytes 368648 | tf_op jit(solution)/shard_map/ppermute | solution.py:228
  97.7 7.7 %collective-permute-start.18 = (bf16[32,480]{1,0:T(8,128)(2,1)S(1)}, bf16[32,480]{1,0:T(8,128)(2,1)S(1)}, u32[]{:S(2)}, u32[]{:S(2)}) collective-permute-start(bf16[32,480]{1,0:T(8,128)(2,1)S(1)} %get-tuple-element.21), channel_id=1, source_target_pairs={{0,8},{2,10},{4,12},{6,14},{8,0},{10,2},{12,4},{14,6},{16,24},{18,... | collective-permute-start | bytes 92168 | tf_op jit(solution)/shard_map/ppermute | solution.py:228
  100.1 6.0 %collective-permute-start.20 = (bf16[32,480]{1,0:T(8,128)(2,1)S(1)}, bf16[32,480]{1,0:T(8,128)(2,1)S(1)}, u32[]{:S(2)}, u32[]{:S(2)}) collective-permute-start(bf16[32,480]{1,0:T(8,128)(2,1)S(1)} %get-tuple-element.22), channel_id=1, source_target_pairs={{0,24},{2,26},{4,28},{6,30},{8,16},{10,18},{12,20},{14,22},{16,8},... | collective-permute-start | bytes 92168 | tf_op jit(solution)/shard_map/ppermute | solution.py:228
  103.4 4.8 %collective-permute-start.19 = (bf16[32,480]{1,0:T(8,128)(2,1)S(1)}, bf16[32,480]{1,0:T(8,128)(2,1)S(1)}, u32[]{:S(2)}, u32[]{:S(2)}) collective-permute-start(bf16[32,480]{1,0:T(8,128)(2,1)S(1)} %get-tuple-element.23), channel_id=1, source_target_pairs={{0,16},{2,18},{4,20},{6,22},{8,24},{10,26},{12,28},{14,30},{16,0},... | collective-permute-start | bytes 92168 | tf_op jit(solution)/shard_map/ppermute | solution.py:228

commit v2 on v1

--- a/solution.py
+++ b/solution.py
@@ -86,34 +86,6 @@
         normed[pl.ds(at, own), :] = unit[e * own : (e + 1) * own].astype(BF16)
     unit_own[...] = unit[:own]
     inv_own[...] = jnp.broadcast_to(inv_dev[:own], inv_own.shape)
-
-
-def project_body(where, *refs, layout):
-    stacks = refs[: len(layout)]
-    proj, full, sems = refs[len(layout) :]
-    copies = []
-    for offs, ref in zip(layout, stacks):
-        width = ref.shape[2]
-        for q, off in enumerate(offs):
-            at = pl.multiple_of((where[0] ^ off) * width, width)
-            copies.append(
-                pltpu.make_async_copy(
-                    ref.at[q, 2], full.at[pl.ds(at, width), :], sems.at[len(copies)]
-                )
-            )
-    for c in copies:
-        c.start()
-    for c in copies:
-        c.wait()
-    proj[...] = full[:, : proj.shape[1]]
-
-
-def start_taps(w_any, w_vmem, sems):
-    def start(g, carry):
-        tap_copy(w_any, w_vmem, sems, g).start()
-        return carry
-
-    lax.fori_loop(0, w_vmem.shape[0], start, 0)
 
 
 def tap_copy(w_any, w_vmem, sems, g):
@@ -145,6 +117,11 @@
     def step(g, carry):
         if chunk == 0:
             tap_copy(w_any, w_vmem, sems, g).wait()
+
+            @pl.when(g + 1 < groups)
+            def _():
+                tap_copy(w_any, w_vmem, sems, g + 1).start()
+
         weights = w_vmem.at[g]
         if turned is not None:
             turned[...] = jnp.swapaxes(w_vmem[g], 0, 1)
@@ -157,9 +134,13 @@
     return jnp.concatenate([acc[g] for g in range(groups)], 1)
 
 
-def forward_body(where, normed, got_a, got_b, proj, w_any, cot, bias, *refs):
-    encoded, slope_rev, w_vmem, first, wrap, acc, sems = refs
-    start_taps(w_any, w_vmem, sems)
+def forward_body(where, normed, got_a, got_b, *refs, layout):
+    stacks = refs[: len(layout)]
+    w_any, cot, bias, encoded, slope_rev, proj, full = refs[len(layout) : len(layout) + 7]
+    w_vmem, first, wrap, acc, sems = refs[len(layout) + 7 :]
+    tap_copy(w_any, w_vmem, sems, 0).start()
+    place_shards(where[0], layout, stacks, 0, 1, full)
+    proj[...] = full[0, :, : proj.shape[1]]
     odd = where[0] % 2 == 1
     low = jnp.where(odd, got_a[...], got_b[...])
     high = jnp.where(odd, got_b[...], got_a[...])
@@ -185,9 +166,9 @@
 
 
 def backward_body(where, slope_rev, got_a, got_b, w_any, cot, normed, proj, *refs, scale, order):
-    kept, sent, unit_grad, w_vmem, first, wrap, acc, sems = refs[:8]
-    turned, hid_grad, full, rows_f32 = refs[8:]
-    start_taps(w_any, w_vmem, sems)
+    kept, sent, unit_grad, unit_sent, w_vmem, first, wrap, acc, sems = refs[:9]
+    turned, hid_grad, full, rows_f32 = refs[9:]
+    tap_copy(w_any, w_vmem, sems, 0).start()
     odd = where[0] % 2 == 1
     low = jnp.where(odd, got_a[...], got_b[...])
     high = jnp.where(odd, got_b[...], got_a[...])
@@ -208,10 +189,11 @@
     for n, p in enumerate(order):
         kept[n] = full[where[0] ^ p].astype(BF16)
         sent[n] = full[where[0] ^ (p ^ 1)].astype(BF16)
-    slots = unit_grad.shape[0]
+    slots = rows_f32.shape[0]
     rows_f32[...] = dot_nt(grad, proj[...]).reshape(rows_f32.shape)
-    for e in range(slots):
-        unit_grad[e] = rows_f32[where[1] ^ e]
+    unit_grad[...] = rows_f32[where[1]]
+    for e in range(1, slots):
+        unit_sent[e - 1] = rows_f32[where[1] ^ e].astype(BF16)
 
 
 def vmem_specs(count):
@@ -228,18 +210,28 @@
     return lax.ppermute(values, axis, [(i, i ^ mask) for i in range(count)])
 
 
-def spread(shard, count):
-    stack, offs = shard[None], [0]
-    mask = count // 2
-    while mask >= 4:
-        got = swap(stack, "tm", mask)
-        stack = jnp.concatenate([stack, got], 0)
-        offs = offs + [o ^ mask for o in offs]
+def spread_near(shards, count):
+    offs = [0] + [n * (count // 4) for n in (1, 2, 3)]
+    joined = shards[0] if len(shards) == 1 else jnp.concatenate(shards, 0)
+    pieces = [joined] + [swap(joined, "tm", m) for m in offs[1:]]
+    stack = jnp.stack(pieces)
+    stacks, at = [], 0
+    for shard in shards:
+        stacks.append(stack[:, at : at + shard.shape[0]])
+        at += shard.shape[0]
+    return stacks, offs
+
+
+def spread_far(stack, offs, count):
+    stacks, layout = [stack], [offs]
+    mask = count // 8
+    while mask >= 1:
+        got = []
+        for part in stacks:
+            got.append(swap(part, "tm", mask))
+        stacks = stacks + got
+        layout = layout + [[o ^ mask for o in offs] for offs in layout]
         mask //= 2
-    stacks, layout = [stack], [offs]
-    for mask in (2, 1):
-        stacks = stacks + [swap(s, "tm", mask) for s in stacks]
-        layout = layout + [[o ^ mask for o in offs] for offs in layout]
     return stacks, layout
 
 
@@ -265,12 +257,16 @@
 
     w_taps = jnp.transpose(pos_weight, (1, 2, 3, 0))
     blocks = [features] + [swap(features, "grp", e) for e in range(1, slots)]
-    five, layout = spread(jnp.transpose(weight_five, (0, 2, 1)), members)
+    bias = pos_bias.reshape(1, columns)
     proj_half = lax.dynamic_slice_in_dim(projection, slot * columns, columns, 1)
     proj_half = jnp.pad(proj_half, ((0, 0), (0, channels - columns)))
-    rest, _ = spread(
-        jnp.concatenate([jnp.transpose(weight_six, (0, 2, 1)), proj_half[None]], 0), members
+    (five,), offs = spread_near([jnp.transpose(weight_five, (0, 2, 1))], members)
+    (six, last), _ = spread_near(
+        [jnp.transpose(weight_six, (0, 2, 1)), proj_half[None]], members
     )
+    five, layout = spread_far(five, offs, members)
+    six, _ = spread_far(six, offs, members)
+    last, _ = spread_far(last, offs, members)
     common = dict(layout=layout)
     taps_scratch = [pltpu.VMEM((2, channels, channels), BF16)]
 
@@ -285,7 +281,7 @@
     )(where, *blocks, *five)
     normed, unit, inv_dev = pl.pallas_call(
         functools.partial(six_body, count=slots, **common),
-        in_specs=[SMEM_SPEC] + vmem_specs(1 + len(rest)),
+        in_specs=[SMEM_SPEC] + vmem_specs(1 + len(six)),
         out_specs=vmem_specs(3),
         out_shape=[
             jax.ShapeDtypeStruct((block, channels), BF16),
@@ -295,24 +291,12 @@
         scratch_shapes=taps_scratch,
         compiler_params=PARAMS,
         name="six",
-    )(where, act_five, *rest)
+    )(where, act_five, *six)
 
     whole = block == half
     tail = normed if whole else normed[block - half :]
     head = normed if whole else normed[:half]
     got_a, got_b = halo(tail, head, me % 2)
-    proj = pl.pallas_call(
-        functools.partial(project_body, **common),
-        in_specs=[SMEM_SPEC] + [ANY_SPEC] * len(rest),
-        out_specs=vmem_specs(1)[0],
-        out_shape=jax.ShapeDtypeStruct((channels, columns), BF16),
-        scratch_shapes=[
-            pltpu.VMEM((channels, channels), BF16),
-            pltpu.SemaphoreType.DMA((members,)),
-        ],
-        compiler_params=PARAMS,
-        name="project",
-    )(where, *rest)
     conv_scratch = [
         pltpu.VMEM((groups, width, width, taps), BF16),
         pltpu.VMEM((columns, taps), F32),
@@ -320,15 +304,16 @@
         pltpu.VMEM((groups, half, width), F32),
         pltpu.SemaphoreType.DMA((groups,)),
     ]
-    encoded, slope_rev = pl.pallas_call(
-        forward_body,
-        in_specs=[SMEM_SPEC] + vmem_specs(4) + [ANY_SPEC] + vmem_specs(2),
-        out_specs=vmem_specs(2),
-        out_shape=[jax.ShapeDtypeStruct((block, columns), BF16)] * 2,
-        scratch_shapes=conv_scratch,
+    encoded, slope_rev, proj = pl.pallas_call(
+        functools.partial(forward_body, **common),
+        in_specs=[SMEM_SPEC] + vmem_specs(3 + len(last)) + [ANY_SPEC] + vmem_specs(2),
+        out_specs=vmem_specs(3),
+        out_shape=[jax.ShapeDtypeStruct((block, columns), BF16)] * 2
+        + [jax.ShapeDtypeStruct((channels, columns), BF16)],
+        scratch_shapes=[pltpu.VMEM((1, channels, channels), BF16)] + conv_scratch,
         compiler_params=PARAMS,
         name="forward",
-    )(where, normed, got_a, got_b, proj, w_taps, cotangent, pos_bias.reshape(1, columns))
+    )(where, normed, got_a, got_b, *last, w_taps, cotangent, bias)
 
     tail = slope_rev if whole else slope_rev[block - half :]
     head = slope_rev if whole else slope_rev[:half]
@@ -343,12 +328,15 @@
     order = finals
     for mask in reversed(masks):
         order = order + [p ^ mask for p in order]
-    kept, sent, unit_grad = pl.pallas_call(
+    kept, sent, unit_grad, unit_sent = pl.pallas_call(
         functools.partial(backward_body, scale=scale, order=order),
         in_specs=[SMEM_SPEC] + vmem_specs(3) + [ANY_SPEC] + vmem_specs(3),
-        out_specs=vmem_specs(3),
+        out_specs=vmem_specs(4),
         out_shape=[jax.ShapeDtypeStruct((members // 2, share, columns), BF16)] * 2
-        + [jax.ShapeDtypeStruct((slots, own, channels), F32)],
+        + [
+            jax.ShapeDtypeStruct((own, channels), F32),
+            jax.ShapeDtypeStruct((slots - 1, own, channels), BF16),
+        ],
         scratch_shapes=conv_scratch
         + [
             pltpu.VMEM((width, width, taps), BF16),
@@ -360,7 +348,8 @@
         name="backward",
     )(where, slope_rev, got_a, got_b, w_taps, cotangent, normed, proj)
 
-    total = (kept.astype(F32) + swap(sent, "tm", 1).astype(F32)).astype(BF16)
+    got = swap(sent, "tm", 1)
+    total = (kept.astype(F32) + got.astype(F32)).astype(BF16)
     for mask in masks:
         middle = total.shape[0] // 2
         got = swap(total[middle:], "tm", mask)
@@ -368,9 +357,10 @@
     parts = [swap(total[n], "tm", p) for n, p in enumerate(finals) if p]
     projection_grad = total[0].astype(F32) + sum(p.astype(F32) for p in parts)
 
-    grad_unit = unit_grad[0]
+    grad_unit = unit_grad
     for e in range(1, slots):
-        grad_unit = grad_unit + swap(unit_grad[e].astype(BF16), "grp", e).astype(F32)
+        got = swap(unit_sent[e - 1], "grp", e)
+        grad_unit = grad_unit + got.astype(F32)
     first_mean = jnp.mean(grad_unit, axis=-1, keepdims=True)
     second_mean = jnp.mean(grad_unit * unit, axis=-1, keepdims=True)
     feature_grad = (inv_dev[:, :1] * (grad_unit - first_mean - unit * second_mean)).astype(BF16)

time: 110 us -> 103 us (0.936)
  waiting for transfers between devices: 29.5 us -> 22.3 us
  starting transfers between devices: 34.2 us -> 37.3 us
  local copies, waits for them, and re-layouts: 7.37 us -> 5.01 us
    ppermute x19 -> x24, waiting for transfers between devices: 29.5 us -> 22.3 us  [swap(): return lax.ppermute(values, axis, [(i, i ^ mask) for i in range(count)])]
    ppermute x19 -> x24, starting transfers between devices: 32.9 us -> 36 us  [swap(): return lax.ppermute(values, axis, [(i, i ^ mask) for i in range(count)])]
    another operation x0 -> x3, other arithmetic: none -> 1.78 us  [spread_near(): stack = jnp.stack(pieces)]
    concatenate x4 -> x0, other arithmetic: 1.78 us -> none  [spread(): stack = jnp.concatenate([stack, got], 0)]
    unnamed x32 -> x40, local copies, waits for them, and re-layouts: 5.04 us -> 3.51 us
    pallas_call x1, Pallas kernels: 10.7 us -> 12.2 us  [on_device(): pl.pallas_call(functools.partial(backward_body, scale=scale, order=order)...]
    pallas_call x2 -> x1, Pallas kernels: 13 us -> 12 us  [on_device(): pl.pallas_call(functools.partial(forward_body, **common), in_specs=[SMEM_...]
  transfers between devices with their start and end apart: 21 -> 26, of which waited for: 10 -> 8; matrix products, arithmetic and copies ran while one was open for 7% -> 6% of each run, Pallas kernels for 5% -> 5%
where the time goes in v2:
time: 103 us; the launch traced here: 102 us
  starting transfers between devices  37.3 us (36%)
  Pallas kernels  29.8 us (29%)
  waiting for transfers between devices  22.3 us (22%)
  other arithmetic  6.58 us (6%)
  local copies, waits for them, and re-layouts  5.01 us (5%)
    ppermute x24, starting transfers between devices, swap(): return lax.ppermute(values, axis, [(i, i ^ mask) for i in range(count)])  36 us
    ppermute x24, waiting for transfers between devices, swap(): return lax.ppermute(values, axis, [(i, i ^ mask) for i in range(count)])  22.3 us
    pallas_call x1, Pallas kernels, on_device(): pl.pallas_call(functools.partial(backward_body, scale=scale, order=order)...  12.2 us
    pallas_call x1, Pallas kernels, on_device(): pl.pallas_call(functools.partial(forward_body, **common), in_specs=[SMEM_...  12 us
    unnamed x40, local copies, waits for them, and re-layouts  3.51 us
    pallas_call x1, Pallas kernels, on_device(): pl.pallas_call(functools.partial(five_body, count=slots, **common), in_sp...  2.78 us
    pallas_call x1, Pallas kernels, on_device(): pl.pallas_call(functools.partial(six_body, count=slots, **common), in_spe...  2.77 us
  transfers between devices with their start and end apart: 26, of which 8 were waited for; matrix products, arithmetic and copies ran while one was open for 6% of the time, Pallas kernels for 5%

profile of v2, /device:TPU:0, one launch (start us, length us, event | category | flops | bytes accessed | tf_op | source)
XLA Modules:
  0.0 101.9 jit_solution(4704222533722518946)
XLA Ops:
  0.6 5.1 %collective-permute-start.3 = (bf16[2,32,512]{2,1,0:T(8,128)(2,1)}, bf16[2,32,512]{2,1,0:T(8,128)(2,1)S(1)}, u32[]{:S(2)}, u32[]{:S(2)}) collective-permute-start(bf16[2,32,512]{2,1,0:T(8,128)(2,1)} %bitcast.38), channel_id=1, source_target_pairs={{0,24},{2,26},{4,28},{6,30},{8,16},{10,18},{12,20},{14,22},{16,8},... | collective-permute-start | bytes 196616 | tf_op jit(solution)/shard_map/ppermute | solution.py:210
  5.8 0.6 collective-permute-start.1
  6.4 0.1 constant_dynamic-slice_fusion
  6.5 0.9 fusion.1
  7.4 3.8 %collective-permute-start.9 = (bf16[3,32,512]{2,1,0:T(8,128)(2,1)S(1)}, bf16[3,32,512]{2,1,0:T(8,128)(2,1)S(1)}, u32[]{:S(2)}, u32[]{:S(2)}) collective-permute-start(bf16[3,32,512]{2,1,0:T(8,128)(2,1)S(1)} %get-tuple-element.29), channel_id=1, source_target_pairs={{0,24},{2,26},{4,28},{6,30},{8,16},{10,18},{12,20},{14,22},{16,8},... | collective-permute-start | bytes 294920 | tf_op jit(solution)/shard_map/ppermute | solution.py:210
  11.2 0.6 collective-permute-start.7
  11.8 3.2 %collective-permute-done.2 = bf16[2,32,512]{2,1,0:T(8,128)(2,1)S(1)} collective-permute-done((bf16[2,32,512]{2,1,0:T(8,128)(2,1)}, bf16[2,32,512]{2,1,0:T(8,128)(2,1)S(1)}, u32[]{:S(2)}, u32[]{:S(2)}) %collective-permute-start.2) | collective-permute-done | bytes 65568 | tf_op jit(solution)/shard_map/ppermute | solution.py:210
  15.0 0.9 pad_maximum_fusion.1.refs_2_
  15.9 1.4 %collective-permute-start.4 = (bf16[4,2,32,512]{3,2,1,0:T(8,128)(2,1)S(1)}, bf16[4,2,32,512]{3,2,1,0:T(8,128)(2,1)S(1)}, u32[]{:S(2)}, u32[]{:S(2)}) collective-permute-start(bf16[4,2,32,512]{3,2,1,0:T(8,128)(2,1)S(1)} %pad_maximum_fusion.1.refs_2_), channel_id=1, source_target_pairs={{0,4},{2,6},{4,0},{6,2},{8,12},{10,14},{12,8},{14,10},{16,20},{18,... | collective-permute-start | bytes 786440 | tf_op jit(solution)/shard_map/ppermute | solution.py:210
  17.4 2.6 %collective-permute-done.8 = bf16[3,32,512]{2,1,0:T(8,128)(2,1)S(1)} collective-permute-done((bf16[3,32,512]{2,1,0:T(8,128)(2,1)S(1)}, bf16[3,32,512]{2,1,0:T(8,128)(2,1)S(1)}, u32[]{:S(2)}, u32[]{:S(2)}) %collective-permute-start.8) | collective-permute-done | bytes 98336 | tf_op jit(solution)/shard_map/ppermute | solution.py:210
  20.1 1.6 %collective-permute-start.10 = (bf16[4,2,32,512]{3,2,1,0:T(8,128)(2,1)S(1)}, bf16[4,2,32,512]{3,2,1,0:T(8,128)(2,1)S(1)}, u32[]{:S(2)}, u32[]{:S(2)}) collective-permute-start(bf16[4,2,32,512]{3,2,1,0:T(8,128)(2,1)S(1)} %slice.36.refs_0_), channel_id=1, source_target_pairs={{0,4},{2,6},{4,0},{6,2},{8,12},{10,14},{12,8},{14,10},{16,20},{18,... | collective-permute-start | bytes 786440 | tf_op jit(solution)/shard_map/ppermute | solution.py:210
  21.7 1.5 %collective-permute-start = (bf16[128,512]{1,0:T(8,128)(2,1)}, bf16[128,512]{1,0:T(8,128)(2,1)S(1)}, u32[]{:S(2)}, u32[]{:S(2)}) collective-permute-start(bf16[128,512]{1,0:T(8,128)(2,1)} %refs_0_.1), channel_id=1, source_target_pairs={{0,1},{1,0},{2,3},{3,2},{4,5},{5,4},{6,7},{7,6},{8,9},{9,8},{10,11... | collective-permute-start | bytes 393224 | tf_op jit(solution)/shard_map/ppermute | solution.py:210
  23.2 0.5 collective-permute-start.11
  23.7 0.1 collective-permute-start.6
  23.8 4.3 %collective-permute-done.10.refs_1_ = bf16[4,2,32,512]{3,2,1,0:T(8,128)(2,1)S(1)} collective-permute-done((bf16[4,2,32,512]{3,2,1,0:T(8,128)(2,1)S(1)}, bf16[4,2,32,512]{3,2,1,0:T(8,128)(2,1)S(1)}, u32[]{:S(2)}, u32[]{:S(2)}) %collective-permute-start.10) | collective-permute-done | bytes 262176 | tf_op jit(solution)/shard_map/ppermute | solution.py:210
  28.1 1.7 %collective-permute-start.15 = (bf16[4,1,32,512]{3,2,1,0:T(8,128)(2,1)S(1)}, bf16[4,1,32,512]{3,2,1,0:T(8,128)(2,1)S(1)}, u32[]{:S(2)}, u32[]{:S(2)}) collective-permute-start(bf16[4,1,32,512]{3,2,1,0:T(8,128)(2,1)S(1)} %pad_maximum_fusion.2.refs_0_), channel_id=1, source_target_pairs={{0,4},{2,6},{4,0},{6,2},{8,12},{10,14},{12,8},{14,10},{16,20},{18,... | collective-permute-start | bytes 393224 | tf_op jit(solution)/shard_map/ppermute | solution.py:210
  29.8 4.3 %collective-permute-done.15.refs_1_ = bf16[4,1,32,512]{3,2,1,0:T(8,128)(2,1)S(1)} collective-permute-done((bf16[4,1,32,512]{3,2,1,0:T(8,128)(2,1)S(1)}, bf16[4,1,32,512]{3,2,1,0:T(8,128)(2,1)S(1)}, u32[]{:S(2)}, u32[]{:S(2)}) %collective-permute-start.15) | collective-permute-done | bytes 131104 | tf_op jit(solution)/shard_map/ppermute | solution.py:210
  34.1 0.5 collective-permute-start.17
  34.6 0.6 pad_add_fusion.where
  35.2 0.7 copy-done.10
  36.0 2.8 %five.1.act = bf16[128,512]{1,0:T(8,128)(2,1)} custom-call(s32[2]{0:T(128)} %pad_add_fusion.where, bf16[128,512]{1,0:T(8,128)(2,1)} %refs_0_.1, bf16[128,512]{1,0:T(8,128)(2,1)} %copy-done.14, bf16[4,2,32,512]{3,2,1,0:T(8,128)(2,1)} %copy-done.1, bf16[4,2,32,512]{3,2,1,0:T(8,128)(2,1)} %copy-done.5, bf16[4,2,32,512]{3,2,1,0:T(8,128)(2,1)} %copy-done.8, ...), custom_call_target="tpu_custom_call" | custom-call | tf_op jit(solution)/shard_map/five/pallas_call | solution.py:273
  38.8 0.7 copy-done.7
  39.5 0.7 copy-done.9
  40.2 2.8 %six.1 = (bf16[64,512]{1,0:T(8,128)(2,1)}, f32[32,512]{1,0:T(8,128)}, f32[32,128]{1,0:T(8,128)}) custom-call(s32[2]{0:T(128)} %pad_add_fusion.where, bf16[128,512]{1,0:T(8,128)(2,1)} %five.1.act, bf16[4,2,32,512]{3,2,1,0:T(8,128)(2,1)} %copy-done.2, bf16[4,2,32,512]{3,2,1,0:T(8,128)(2,1)} %copy-done.6, bf16[4,2,32,512]{3,2,1,0:T(8,128)(2,1)} %copy-done.7, ...), custom_call_target="tpu_custom_call" | custom-call | tf_op jit(solution)/shard_map/six/pallas_call | solution.py:282
  42.9 0.1 collective-permute-start.13
  43.0 0.7 collective-permute-start.14
  43.7 1.3 %reshape.19.refs_6_ = bf16[1,480]{1,0:T(2,128)(2,1)} reshape(bf16[480]{0:T(512)(128)(2,1)} %param.12) | data formatting | bytes 1920 | tf_op jit(solution)/shard_map/reshape | solution.py:260
  45.0 0.6 copy-done.12
  45.6 0.1 copy-done.13
  45.7 12.0 %forward.1 = (bf16[64,480]{1,0:T(8,128)(2,1)}, bf16[64,480]{1,0:T(8,128)(2,1)}, bf16[512,480]{1,0:T(8,128)(2,1)}) custom-call(s32[2]{0:T(128)} %pad_add_fusion.where, bf16[64,512]{1,0:T(8,128)(2,1)} %get-tuple-element.13.normed, bf16[64,512]{1,0:T(8,128)(2,1)} %copy-done.15, bf16[64,512]{1,0:T(8,128)(2,1)} %copy-done.16, bf16[4,1,32,512]{3,2,1,0:T(8,128)(2,1)} %copy-done.3, ...), custom_call_target="tpu_custom_call" | custom-call | tf_op jit(solution)/shard_map/forward/pallas_call | solution.py:307
  57.8 4.2 %collective-permute-start.18 = (bf16[64,480]{1,0:T(8,128)(2,1)}, bf16[64,480]{1,0:T(8,128)(2,1)S(1)}, u32[]{:S(2)}, u32[]{:S(2)}) collective-permute-start(bf16[64,480]{1,0:T(8,128)(2,1)} %get-tuple-element.16.slope_rev), channel_id=1, source_target_pairs={{0,2},{2,0},{4,6},{6,4},{8,10},{10,8},{12,14},{14,12},{16,18},{18,... | collective-permute-start | bytes 184328 | tf_op jit(solution)/shard_map/ppermute | solution.py:210
  62.0 0.7 collective-permute-start.19
  62.6 0.5 collective-permute-done.18.got_a
  63.1 0.6 copy-done.17
  63.7 12.2 %backward.1 = (bf16[8,32,480]{2,1,0:T(8,128)(2,1)}, bf16[8,32,480]{2,1,0:T(8,128)(2,1)}, f32[32,512]{1,0:T(8,128)}, bf16[1,32,512]{2,1,0:T(8,128)(2,1)}) custom-call(s32[2]{0:T(128)} %pad_add_fusion.where, bf16[64,480]{1,0:T(8,128)(2,1)} %get-tuple-element.16.slope_rev, bf16[64,480]{1,0:T(8,128)(2,1)} %copy-done.17, bf16[64,480]{1,0:T(8,128)(2,1)} %copy-done.18, ...), custom_call_target="tpu_custom_call" | custom-call | tf_op jit(solution)/shard_map/backward/pallas_call | solution.py:331
  76.0 5.6 %collective-permute-start.21 = (bf16[8,32,480]{2,1,0:T(8,128)(2,1)}, bf16[8,32,480]{2,1,0:T(8,128)(2,1)S(1)}, u32[]{:S(2)}, u32[]{:S(2)}) collective-permute-start(bf16[8,32,480]{2,1,0:T(8,128)(2,1)} %get-tuple-element.22), channel_id=1, source_target_pairs={{0,2},{2,0},{4,6},{6,4},{8,10},{10,8},{12,14},{14,12},{16,18},{18,... | collective-permute-start | bytes 737288 | tf_op jit(solution)/shard_map/ppermute | solution.py:210
  81.6 1.5 %collective-permute-start.20 = (bf16[32,512]{1,0:T(8,128)(2,1)}, bf16[32,512]{1,0:T(8,128)(2,1)S(1)}, u32[]{:S(2)}, u32[]{:S(2)}) collective-permute-start(bf16[32,512]{1,0:T(8,128)(2,1)} %bitcast.45), channel_id=1, source_target_pairs={{0,1},{1,0},{2,3},{3,2},{4,5},{5,4},{6,7},{7,6},{8,9},{9,8},{10,11... | collective-permute-start | bytes 98312 | tf_op jit(solution)/shard_map/ppermute | solution.py:210
  83.1 0.1 slice_reduce_fusion
  83.2 2.5 %collective-permute-done.20 = bf16[32,512]{1,0:T(8,128)(2,1)S(1)} collective-permute-done((bf16[32,512]{1,0:T(8,128)(2,1)}, bf16[32,512]{1,0:T(8,128)(2,1)S(1)}, u32[]{:S(2)}, u32[]{:S(2)}) %collective-permute-start.20) | collective-permute-done | bytes 32800 | tf_op jit(solution)/shard_map/ppermute | solution.py:210
  85.8 1.0 fusion
  86.7 1.0 %add_convert_fusion = bf16[8,32,480]{2,1,0:T(8,128)(2,1)S(1)} fusion(bf16[8,32,480]{2,1,0:T(8,128)(2,1)S(1)} %collective-permute-done.21, bf16[8,32,480]{2,1,0:T(8,128)(2,1)} %get-tuple-element.21), kind=kLoop, calls=%fused_computation | loop fusion | flops 491520 | bytes 737280 | tf_op jit(solution)/shard_map/convert_element_type | solution.py:352
  87.8 2.6 %collective-permute-start.22 = (bf16[4,32,480]{2,1,0:T(8,128)(2,1)S(1)}, bf16[4,32,480]{2,1,0:T(8,128)(2,1)S(1)}, u32[]{:S(2)}, u32[]{:S(2)}) collective-permute-start(bf16[4,32,480]{2,1,0:T(8,128)(2,1)S(1)} %slice.38), channel_id=1, source_target_pairs={{0,4},{2,6},{4,0},{6,2},{8,12},{10,14},{12,8},{14,10},{16,20},{18,... | collective-permute-start | bytes 368648 | tf_op jit(solution)/shard_map/ppermute | solution.py:210
  90.4 2.9 %collective-permute-done.22 = bf16[4,32,480]{2,1,0:T(8,128)(2,1)S(1)} collective-permute-done((bf16[4,32,480]{2,1,0:T(8,128)(2,1)S(1)}, bf16[4,32,480]{2,1,0:T(8,128)(2,1)S(1)}, u32[]{:S(2)}, u32[]{:S(2)}) %collective-permute-start.22) | collective-permute-done | bytes 122912 | tf_op jit(solution)/shard_map/ppermute | solution.py:210
  93.4 3.1 %collective-permute-start.25 = (bf16[32,480]{1,0:T(8,128)(2,1)S(1)}, bf16[32,480]{1,0:T(8,128)(2,1)S(1)}, u32[]{:S(2)}, u32[]{:S(2)}) collective-permute-start(bf16[32,480]{1,0:T(8,128)(2,1)S(1)} %get-tuple-element.26), channel_id=1, source_target_pairs={{0,24},{2,26},{4,28},{6,30},{8,16},{10,18},{12,20},{14,22},{16,8},... | collective-permute-start | bytes 92168 | tf_op jit(solution)/shard_map/ppermute | solution.py:210
  96.5 1.4 %collective-permute-start.23 = (bf16[32,480]{1,0:T(8,128)(2,1)S(1)}, bf16[32,480]{1,0:T(8,128)(2,1)S(1)}, u32[]{:S(2)}, u32[]{:S(2)}) collective-permute-start(bf16[32,480]{1,0:T(8,128)(2,1)S(1)} %get-tuple-element.25), channel_id=1, source_target_pairs={{0,8},{2,10},{4,12},{6,14},{8,0},{10,2},{12,4},{14,6},{16,24},{18,... | collective-permute-start | bytes 92168 | tf_op jit(solution)/shard_map/ppermute | solution.py:210
  97.8 1.5 %multiply_convert_fusion = bf16[32,512]{1,0:T(8,128)(2,1)} fusion(f32[32,512]{1,0:T(8,128)S(1)} %copy-done.4, f32[32]{0:T(128)S(1)} %get-tuple-element.30, f32[32]{0:T(128)S(1)} %get-tuple-element.31, f32[32]{0:T(128)S(1)} %slice_reduce_fusion, f32[32,512]{1,0:T(8,128)} %get-tuple-element.18, bf16[32,512]{1,0:T(8,128)(2,1)S(1)} %collective-permute-done.20), kind=kLoop, calls=%fused_computation.7 | loop fusion | flops 114688 | bytes 196992 | tf_op jit(solution)/shard_map/convert_element_type | solution.py:366
  99.4 1.9 %collective-permute-done.24 = bf16[32,480]{1,0:T(8,128)(2,1)S(1)} collective-permute-done((bf16[32,480]{1,0:T(8,128)(2,1)S(1)}, bf16[32,480]{1,0:T(8,128)(2,1)S(1)}, u32[]{:S(2)}, u32[]{:S(2)}) %collective-permute-start.24) | collective-permute-done | bytes 30752 | tf_op jit(solution)/shard_map/ppermute | solution.py:210
  101.3 0.6 convert_add_fusion
  (66 shorter events, 0.4 us)
Async XLA Ops:
  0.6 5.8 %copy-start = (bf16[32,960]{1,0:T(8,128)(2,1)S(1)}, bf16[32,960]{1,0:T(8,128)(2,1)}, u32[]{:S(2)}) copy-start(bf16[32,960]{1,0:T(8,128)(2,1)} %param.10) | copy-start | bytes 184324
  0.6 10.6 %collective-permute-start.3 = (bf16[2,32,512]{2,1,0:T(8,128)(2,1)}, bf16[2,32,512]{2,1,0:T(8,128)(2,1)S(1)}, u32[]{:S(2)}, u32[]{:S(2)}) collective-permute-start(bf16[2,32,512]{2,1,0:T(8,128)(2,1)} %bitcast.38), channel_id=1, source_target_pairs={{0,24},{2,26},{4,28},{6,30},{8,16},{10,18},{12,20},{14,22},{16,8},... | collective-permute-start | bytes 196616 | tf_op jit(solution)/shard_map/ppermute | solution.py:210
  5.8 9.3 %collective-permute-start.2 = (bf16[2,32,512]{2,1,0:T(8,128)(2,1)}, bf16[2,32,512]{2,1,0:T(8,128)(2,1)S(1)}, u32[]{:S(2)}, u32[]{:S(2)}) collective-permute-start(bf16[2,32,512]{2,1,0:T(8,128)(2,1)} %bitcast.39), channel_id=1, source_target_pairs={{0,16},{2,18},{4,20},{6,22},{8,24},{10,26},{12,28},{14,30},{16,0},... | collective-permute-start | bytes 196616 | tf_op jit(solution)/shard_map/ppermute | solution.py:210
  5.8 9.3 %collective-permute-start.1 = (bf16[2,32,512]{2,1,0:T(8,128)(2,1)}, bf16[2,32,512]{2,1,0:T(8,128)(2,1)S(1)}, u32[]{:S(2)}, u32[]{:S(2)}) collective-permute-start(bf16[2,32,512]{2,1,0:T(8,128)(2,1)} %bitcast.40), channel_id=1, source_target_pairs={{0,8},{2,10},{4,12},{6,14},{8,0},{10,2},{12,4},{14,6},{16,24},{18,... | collective-permute-start | bytes 196616 | tf_op jit(solution)/shard_map/ppermute | solution.py:210
  7.4 10.0 %collective-permute-start.9 = (bf16[3,32,512]{2,1,0:T(8,128)(2,1)S(1)}, bf16[3,32,512]{2,1,0:T(8,128)(2,1)S(1)}, u32[]{:S(2)}, u32[]{:S(2)}) collective-permute-start(bf16[3,32,512]{2,1,0:T(8,128)(2,1)S(1)} %get-tuple-element.29), channel_id=1, source_target_pairs={{0,24},{2,26},{4,28},{6,30},{8,16},{10,18},{12,20},{14,22},{16,8},... | collective-permute-start | bytes 294920 | tf_op jit(solution)/shard_map/ppermute | solution.py:210
  11.2 8.8 %collective-permute-start.8 = (bf16[3,32,512]{2,1,0:T(8,128)(2,1)S(1)}, bf16[3,32,512]{2,1,0:T(8,128)(2,1)S(1)}, u32[]{:S(2)}, u32[]{:S(2)}) collective-permute-start(bf16[3,32,512]{2,1,0:T(8,128)(2,1)S(1)} %get-tuple-element.29), channel_id=1, source_target_pairs={{0,16},{2,18},{4,20},{6,22},{8,24},{10,26},{12,28},{14,30},{16,0},... | collective-permute-start | bytes 294920 | tf_op jit(solution)/shard_map/ppermute | solution.py:210
  11.2 8.8 %collective-permute-start.7 = (bf16[3,32,512]{2,1,0:T(8,128)(2,1)S(1)}, bf16[3,32,512]{2,1,0:T(8,128)(2,1)S(1)}, u32[]{:S(2)}, u32[]{:S(2)}) collective-permute-start(bf16[3,32,512]{2,1,0:T(8,128)(2,1)S(1)} %get-tuple-element.29), channel_id=1, source_target_pairs={{0,8},{2,10},{4,12},{6,14},{8,0},{10,2},{12,4},{14,6},{16,24},{18,... | collective-permute-start | bytes 294920 | tf_op jit(solution)/shard_map/ppermute | solution.py:210
  15.9 19.3 %copy-start.1 = (bf16[4,2,32,512]{3,2,1,0:T(8,128)(2,1)}, bf16[4,2,32,512]{3,2,1,0:T(8,128)(2,1)S(1)}, u32[]{:S(2)}) copy-start(bf16[4,2,32,512]{3,2,1,0:T(8,128)(2,1)S(1)} %pad_maximum_fusion.1.refs_2_) | copy-start | bytes 786436
  15.9 7.8 %collective-permute-start.4 = (bf16[4,2,32,512]{3,2,1,0:T(8,128)(2,1)S(1)}, bf16[4,2,32,512]{3,2,1,0:T(8,128)(2,1)S(1)}, u32[]{:S(2)}, u32[]{:S(2)}) collective-permute-start(bf16[4,2,32,512]{3,2,1,0:T(8,128)(2,1)S(1)} %pad_maximum_fusion.1.refs_2_), channel_id=1, source_target_pairs={{0,4},{2,6},{4,0},{6,2},{8,12},{10,14},{12,8},{14,10},{16,20},{18,... | collective-permute-start | bytes 786440 | tf_op jit(solution)/shard_map/ppermute | solution.py:210
  20.1 18.6 %copy-start.2 = (bf16[4,2,32,512]{3,2,1,0:T(8,128)(2,1)}, bf16[4,2,32,512]{3,2,1,0:T(8,128)(2,1)S(1)}, u32[]{:S(2)}) copy-start(bf16[4,2,32,512]{3,2,1,0:T(8,128)(2,1)S(1)} %slice.36.refs_0_) | copy-start | bytes 786436
  20.1 7.9 %collective-permute-start.10 = (bf16[4,2,32,512]{3,2,1,0:T(8,128)(2,1)S(1)}, bf16[4,2,32,512]{3,2,1,0:T(8,128)(2,1)S(1)}, u32[]{:S(2)}, u32[]{:S(2)}) collective-permute-start(bf16[4,2,32,512]{3,2,1,0:T(8,128)(2,1)S(1)} %slice.36.refs_0_), channel_id=1, source_target_pairs={{0,4},{2,6},{4,0},{6,2},{8,12},{10,14},{12,8},{14,10},{16,20},{18,... | collective-permute-start | bytes 786440 | tf_op jit(solution)/shard_map/ppermute | solution.py:210
  21.7 6.4 %collective-permute-start = (bf16[128,512]{1,0:T(8,128)(2,1)}, bf16[128,512]{1,0:T(8,128)(2,1)S(1)}, u32[]{:S(2)}, u32[]{:S(2)}) collective-permute-start(bf16[128,512]{1,0:T(8,128)(2,1)} %refs_0_.1), channel_id=1, source_target_pairs={{0,1},{1,0},{2,3},{3,2},{4,5},{5,4},{6,7},{7,6},{8,9},{9,8},{10,11... | collective-permute-start | bytes 393224 | tf_op jit(solution)/shard_map/ppermute | solution.py:210
  23.2 10.9 %collective-permute-start.5 = (bf16[4,2,32,512]{3,2,1,0:T(8,128)(2,1)S(1)}, bf16[4,2,32,512]{3,2,1,0:T(8,128)(2,1)S(1)}, u32[]{:S(2)}, u32[]{:S(2)}) collective-permute-start(bf16[4,2,32,512]{3,2,1,0:T(8,128)(2,1)S(1)} %pad_maximum_fusion.1.refs_2_), channel_id=1, source_target_pairs={{0,2},{2,0},{4,6},{6,4},{8,10},{10,8},{12,14},{14,12},{16,18},{18,... | collective-permute-start | bytes 786440 | tf_op jit(solution)/shard_map/ppermute | solution.py:210
  23.2 15.5 %collective-permute-start.11 = (bf16[4,2,32,512]{3,2,1,0:T(8,128)(2,1)S(1)}, bf16[4,2,32,512]{3,2,1,0:T(8,128)(2,1)S(1)}, u32[]{:S(2)}, u32[]{:S(2)}) collective-permute-start(bf16[4,2,32,512]{3,2,1,0:T(8,128)(2,1)S(1)} %slice.36.refs_0_), channel_id=1, source_target_pairs={{0,2},{2,0},{4,6},{6,4},{8,10},{10,8},{12,14},{14,12},{16,18},{18,... | collective-permute-start | bytes 786440 | tf_op jit(solution)/shard_map/ppermute | solution.py:210
  23.7 11.5 %copy-start.5 = (bf16[4,2,32,512]{3,2,1,0:T(8,128)(2,1)}, bf16[4,2,32,512]{3,2,1,0:T(8,128)(2,1)S(1)}, u32[]{:S(2)}) copy-start(bf16[4,2,32,512]{3,2,1,0:T(8,128)(2,1)S(1)} %collective-permute-done.4.refs_3_) | copy-start | bytes 786436
  23.7 11.5 %collective-permute-start.6 = (bf16[4,2,32,512]{3,2,1,0:T(8,128)(2,1)S(1)}, bf16[4,2,32,512]{3,2,1,0:T(8,128)(2,1)S(1)}, u32[]{:S(2)}, u32[]{:S(2)}) collective-permute-start(bf16[4,2,32,512]{3,2,1,0:T(8,128)(2,1)S(1)} %collective-permute-done.4.refs_3_), channel_id=1, source_target_pairs={{0,2},{2,0},{4,6},{6,4},{8,10},{10,8},{12,14},{14,12},{16,18},{18,... | collective-permute-start | bytes 786440 | tf_op jit(solution)/shard_map/ppermute | solution.py:210
  28.1 10.7 %copy-start.6 = (bf16[4,2,32,512]{3,2,1,0:T(8,128)(2,1)}, bf16[4,2,32,512]{3,2,1,0:T(8,128)(2,1)S(1)}, u32[]{:S(2)}) copy-start(bf16[4,2,32,512]{3,2,1,0:T(8,128)(2,1)S(1)} %collective-permute-done.10.refs_1_) | copy-start | bytes 786436
  28.1 10.7 %collective-permute-start.12 = (bf16[4,2,32,512]{3,2,1,0:T(8,128)(2,1)S(1)}, bf16[4,2,32,512]{3,2,1,0:T(8,128)(2,1)S(1)}, u32[]{:S(2)}, u32[]{:S(2)}) collective-permute-start(bf16[4,2,32,512]{3,2,1,0:T(8,128)(2,1)S(1)} %collective-permute-done.10.refs_1_), channel_id=1, source_target_pairs={{0,2},{2,0},{4,6},{6,4},{8,10},{10,8},{12,14},{14,12},{16,18},{18,... | collective-permute-start | bytes 786440 | tf_op jit(solution)/shard_map/ppermute | solution.py:210
  28.1 16.9 %copy-start.3 = (bf16[4,1,32,512]{3,2,1,0:T(8,128)(2,1)}, bf16[4,1,32,512]{3,2,1,0:T(8,128)(2,1)S(1)}, u32[]{:S(2)}) copy-start(bf16[4,1,32,512]{3,2,1,0:T(8,128)(2,1)S(1)} %pad_maximum_fusion.2.refs_0_) | copy-start | bytes 393220
  28.1 7.1 %copy-start.14 = (bf16[128,512]{1,0:T(8,128)(2,1)}, bf16[128,512]{1,0:T(8,128)(2,1)S(1)}, u32[]{:S(2)}) copy-start(bf16[128,512]{1,0:T(8,128)(2,1)S(1)} %collective-permute-done.refs_1_) | copy-start | bytes 393220
  28.1 6.0 %collective-permute-start.15 = (bf16[4,1,32,512]{3,2,1,0:T(8,128)(2,1)S(1)}, bf16[4,1,32,512]{3,2,1,0:T(8,128)(2,1)S(1)}, u32[]{:S(2)}, u32[]{:S(2)}) collective-permute-start(bf16[4,1,32,512]{3,2,1,0:T(8,128)(2,1)S(1)} %pad_maximum_fusion.2.refs_0_), channel_id=1, source_target_pairs={{0,4},{2,6},{4,0},{6,2},{8,12},{10,14},{12,8},{14,10},{16,20},{18,... | collective-permute-start | bytes 393224 | tf_op jit(solution)/shard_map/ppermute | solution.py:210
  34.1 10.9 %copy-start.11 = (bf16[4,1,32,512]{3,2,1,0:T(8,128)(2,1)}, bf16[4,1,32,512]{3,2,1,0:T(8,128)(2,1)S(1)}, u32[]{:S(2)}) copy-start(bf16[4,1,32,512]{3,2,1,0:T(8,128)(2,1)S(1)} %collective-permute-done.15.refs_1_) | copy-start | bytes 393220
  34.1 10.9 %collective-permute-start.16 = (bf16[4,1,32,512]{3,2,1,0:T(8,128)(2,1)S(1)}, bf16[4,1,32,512]{3,2,1,0:T(8,128)(2,1)S(1)}, u32[]{:S(2)}, u32[]{:S(2)}) collective-permute-start(bf16[4,1,32,512]{3,2,1,0:T(8,128)(2,1)S(1)} %pad_maximum_fusion.2.refs_0_), channel_id=1, source_target_pairs={{0,2},{2,0},{4,6},{6,4},{8,10},{10,8},{12,14},{14,12},{16,18},{18,... | collective-permute-start | bytes 393224 | tf_op jit(solution)/shard_map/ppermute | solution.py:210
  34.1 1.1 %copy-start.8 = (bf16[4,2,32,512]{3,2,1,0:T(8,128)(2,1)}, bf16[4,2,32,512]{3,2,1,0:T(8,128)(2,1)S(1)}, u32[]{:S(2)}) copy-start(bf16[4,2,32,512]{3,2,1,0:T(8,128)(2,1)S(1)} %collective-permute-done.5.refs_4_) | copy-start | bytes 786436
  34.1 10.9 %collective-permute-start.17 = (bf16[4,1,32,512]{3,2,1,0:T(8,128)(2,1)S(1)}, bf16[4,1,32,512]{3,2,1,0:T(8,128)(2,1)S(1)}, u32[]{:S(2)}, u32[]{:S(2)}) collective-permute-start(bf16[4,1,32,512]{3,2,1,0:T(8,128)(2,1)S(1)} %collective-permute-done.15.refs_1_), channel_id=1, source_target_pairs={{0,2},{2,0},{4,6},{6,4},{8,10},{10,8},{12,14},{14,12},{16,18},{18,... | collective-permute-start | bytes 393224 | tf_op jit(solution)/shard_map/ppermute | solution.py:210
  35.2 0.7 copy-start.10
  38.7 0.7 copy-start.7
  39.5 0.7 copy-start.9
  42.9 2.0 %collective-permute-start.13 = (bf16[64,512]{1,0:T(8,128)(2,1)}, bf16[64,512]{1,0:T(8,128)(2,1)S(1)}, u32[]{:S(2)}, u32[]{:S(2)}) collective-permute-start(bf16[64,512]{1,0:T(8,128)(2,1)} %get-tuple-element.13.normed), channel_id=1, source_target_pairs={{0,2},{2,0},{4,6},{6,4},{8,10},{10,8},{12,14},{14,12},{16,18},{18,... | collective-permute-start | bytes 196616 | tf_op jit(solution)/shard_map/ppermute | solution.py:210
  43.0 2.0 %collective-permute-start.14 = (bf16[64,512]{1,0:T(8,128)(2,1)}, bf16[64,512]{1,0:T(8,128)(2,1)S(1)}, u32[]{:S(2)}, u32[]{:S(2)}) collective-permute-start(bf16[64,512]{1,0:T(8,128)(2,1)} %get-tuple-element.13.normed), channel_id=1, source_target_pairs={{2,4},{6,8},{10,12},{14,16},{18,20},{22,24},{26,28},{4,2},{8,6},{1... | collective-permute-start | bytes 196616 | tf_op jit(solution)/shard_map/ppermute | solution.py:243
  45.0 0.6 copy-start.12
  45.0 0.7 copy-start.13
  45.0 0.7 copy-start.15
  45.0 0.7 copy-start.16
  45.7 37.4 %copy-start.19 = (f32[32,128]{1,0:T(8,128)S(1)}, f32[32,128]{1,0:T(8,128)}, u32[]{:S(2)}) copy-start(f32[32,128]{1,0:T(8,128)} %get-tuple-element.15) | copy-start | bytes 49156
  45.7 40.0 %copy-start.4 = (f32[32,512]{1,0:T(8,128)S(1)}, f32[32,512]{1,0:T(8,128)}, u32[]{:S(2)}) copy-start(f32[32,512]{1,0:T(8,128)} %get-tuple-element.20) | copy-start | bytes 196612
  57.8 5.3 %collective-permute-start.18 = (bf16[64,480]{1,0:T(8,128)(2,1)}, bf16[64,480]{1,0:T(8,128)(2,1)S(1)}, u32[]{:S(2)}, u32[]{:S(2)}) collective-permute-start(bf16[64,480]{1,0:T(8,128)(2,1)} %get-tuple-element.16.slope_rev), channel_id=1, source_target_pairs={{0,2},{2,0},{4,6},{6,4},{8,10},{10,8},{12,14},{14,12},{16,18},{18,... | collective-permute-start | bytes 184328 | tf_op jit(solution)/shard_map/ppermute | solution.py:210
  62.0 1.1 %collective-permute-start.19 = (bf16[64,480]{1,0:T(8,128)(2,1)}, bf16[64,480]{1,0:T(8,128)(2,1)S(1)}, u32[]{:S(2)}, u32[]{:S(2)}) collective-permute-start(bf16[64,480]{1,0:T(8,128)(2,1)} %get-tuple-element.16.slope_rev), channel_id=1, source_target_pairs={{2,4},{6,8},{10,12},{14,16},{18,20},{22,24},{26,28},{4,2},{8,6},{1... | collective-permute-start | bytes 184328 | tf_op jit(solution)/shard_map/ppermute | solution.py:243
  63.1 0.6 copy-start.17
  63.1 0.6 copy-start.18
  76.0 10.7 %collective-permute-start.21 = (bf16[8,32,480]{2,1,0:T(8,128)(2,1)}, bf16[8,32,480]{2,1,0:T(8,128)(2,1)S(1)}, u32[]{:S(2)}, u32[]{:S(2)}) collective-permute-start(bf16[8,32,480]{2,1,0:T(8,128)(2,1)} %get-tuple-element.22), channel_id=1, source_target_pairs={{0,2},{2,0},{4,6},{6,4},{8,10},{10,8},{12,14},{14,12},{16,18},{18,... | collective-permute-start | bytes 737288 | tf_op jit(solution)/shard_map/ppermute | solution.py:210
  81.6 4.1 %collective-permute-start.20 = (bf16[32,512]{1,0:T(8,128)(2,1)}, bf16[32,512]{1,0:T(8,128)(2,1)S(1)}, u32[]{:S(2)}, u32[]{:S(2)}) collective-permute-start(bf16[32,512]{1,0:T(8,128)(2,1)} %bitcast.45), channel_id=1, source_target_pairs={{0,1},{1,0},{2,3},{3,2},{4,5},{5,4},{6,7},{7,6},{8,9},{9,8},{10,11... | collective-permute-start | bytes 98312 | tf_op jit(solution)/shard_map/ppermute | solution.py:210
  87.8 5.6 %collective-permute-start.22 = (bf16[4,32,480]{2,1,0:T(8,128)(2,1)S(1)}, bf16[4,32,480]{2,1,0:T(8,128)(2,1)S(1)}, u32[]{:S(2)}, u32[]{:S(2)}) collective-permute-start(bf16[4,32,480]{2,1,0:T(8,128)(2,1)S(1)} %slice.38), channel_id=1, source_target_pairs={{0,4},{2,6},{4,0},{6,2},{8,12},{10,14},{12,8},{14,10},{16,20},{18,... | collective-permute-start | bytes 368648 | tf_op jit(solution)/shard_map/ppermute | solution.py:210
  93.4 6.0 %collective-permute-start.25 = (bf16[32,480]{1,0:T(8,128)(2,1)S(1)}, bf16[32,480]{1,0:T(8,128)(2,1)S(1)}, u32[]{:S(2)}, u32[]{:S(2)}) collective-permute-start(bf16[32,480]{1,0:T(8,128)(2,1)S(1)} %get-tuple-element.26), channel_id=1, source_target_pairs={{0,24},{2,26},{4,28},{6,30},{8,16},{10,18},{12,20},{14,22},{16,8},... | collective-permute-start | bytes 92168 | tf_op jit(solution)/shard_map/ppermute | solution.py:210
  96.5 4.8 %collective-permute-start.24 = (bf16[32,480]{1,0:T(8,128)(2,1)S(1)}, bf16[32,480]{1,0:T(8,128)(2,1)S(1)}, u32[]{:S(2)}, u32[]{:S(2)}) collective-permute-start(bf16[32,480]{1,0:T(8,128)(2,1)S(1)} %get-tuple-element.27), channel_id=1, source_target_pairs={{0,16},{2,18},{4,20},{6,22},{8,24},{10,26},{12,28},{14,30},{16,0},... | collective-permute-start | bytes 92168 | tf_op jit(solution)/shard_map/ppermute | solution.py:210
  96.5 4.8 %collective-permute-start.23 = (bf16[32,480]{1,0:T(8,128)(2,1)S(1)}, bf16[32,480]{1,0:T(8,128)(2,1)S(1)}, u32[]{:S(2)}, u32[]{:S(2)}) collective-permute-start(bf16[32,480]{1,0:T(8,128)(2,1)S(1)} %get-tuple-element.25), channel_id=1, source_target_pairs={{0,8},{2,10},{4,12},{6,14},{8,0},{10,2},{12,4},{14,6},{16,24},{18,... | collective-permute-start | bytes 92168 | tf_op jit(solution)/shard_map/ppermute | solution.py:210

commit v3 on v2

--- a/solution.py
+++ b/solution.py
@@ -12,8 +12,8 @@
 EPS = 1e-05
 F32 = jnp.float32
 BF16 = jnp.bfloat16
-VMEM_LIMIT = 56 * 1024 * 1024
 SUB = 8
+CONV_MB = 16
 
 
 def dot_nn(a, b):
@@ -66,16 +66,41 @@
     return (unit * phi_cdf(unit)).astype(BF16)
 
 
+def tap_copies(w_any, w_out, sems, start):
+    count = sems.shape[1]
+    size = w_out.shape[1] // count
+    copies = []
+    for g in range(w_out.shape[0]):
+        for c in range(count):
+            part = pl.ds(c * size, size)
+            copies.append(
+                pltpu.make_async_copy(
+                    w_any.at[start + g, part], w_out.at[g, part], sems.at[g, c]
+                )
+            )
+    for copy in copies:
+        copy.start()
+    return copies
+
+
 def five_body(where, *refs, layout, count):
     blocks, stacks = refs[:count], refs[count : count + len(layout)]
-    out, full = refs[count + len(layout) :]
+    w_any, out, w_out, full, sems = refs[count + len(layout) :]
+    copies = tap_copies(w_any, w_out, sems, 0)
     place_shards(where[0], layout, stacks, 0, 2, full)
     out[...] = strided([b[...] for b in blocks], full)
-
-
-def six_body(where, act, *refs, layout, count):
+    for copy in copies:
+        copy.wait()
+
+
+def six_body(where, act, *refs, layout, count, start):
     stacks = refs[: len(layout)]
-    normed, unit_own, inv_own, full = refs[len(layout) :]
+    if start is None:
+        normed, unit_own, inv_own, full = refs[len(layout) :]
+        copies = []
+    else:
+        w_any, normed, unit_own, inv_own, w_out, full, sems = refs[len(layout) :]
+        copies = tap_copies(w_any, w_out, sems, start)
     place_shards(where[0], layout, stacks, 0, 2, full)
     rows = act.shape[0] // count
     act_six = strided([act[e * rows : (e + 1) * rows] for e in range(count)], full)
@@ -86,10 +111,8 @@
         normed[pl.ds(at, own), :] = unit[e * own : (e + 1) * own].astype(BF16)
     unit_own[...] = unit[:own]
     inv_own[...] = jnp.broadcast_to(inv_dev[:own], inv_own.shape)
-
-
-def tap_copy(w_any, w_vmem, sems, g):
-    return pltpu.make_async_copy(w_any.at[g], w_vmem.at[g], sems.at[g])
+    for copy in copies:
+        copy.wait()
 
 
 def conv_group(weights, first, wrap, rows):
@@ -110,35 +133,29 @@
     return total
 
 
-def conv(w_any, w_vmem, turned, sems, first, wrap, acc, chunk):
-    groups, width = w_vmem.shape[:2]
-    rows = acc.shape[1]
-
-    def step(g, carry):
-        if chunk == 0:
-            tap_copy(w_any, w_vmem, sems, g).wait()
-
-            @pl.when(g + 1 < groups)
-            def _():
-                tap_copy(w_any, w_vmem, sems, g + 1).start()
-
-        weights = w_vmem.at[g]
-        if turned is not None:
-            turned[...] = jnp.swapaxes(w_vmem[g], 0, 1)
-            weights = turned
-        here = pl.ds(pl.multiple_of(g * width, 8), width)
-        acc[g] = conv_group(weights, first.at[here], wrap.at[here], rows)
-        return carry
-
-    lax.fori_loop(0, groups, step, 0)
-    return jnp.concatenate([acc[g] for g in range(groups)], 1)
-
-
-def forward_body(where, normed, got_a, got_b, *refs, layout):
-    stacks = refs[: len(layout)]
-    w_any, cot, bias, encoded, slope_rev, proj, full = refs[len(layout) : len(layout) + 7]
-    w_vmem, first, wrap, acc, sems = refs[len(layout) + 7 :]
-    tap_copy(w_any, w_vmem, sems, 0).start()
+def conv(weights, turned, first, wrap, acc):
+    rows, width = acc.shape[1:]
+    start = 0
+    for held in weights:
+        def step(g, carry):
+            group = held.at[g]
+            if turned is not None:
+                turned[...] = jnp.swapaxes(held[g], 0, 1)
+                group = turned
+            here = pl.ds(pl.multiple_of((start + g) * width, 8), width)
+            acc[start + g] = conv_group(group, first.at[here], wrap.at[here], rows)
+            return carry
+
+        lax.fori_loop(0, held.shape[0], step, 0)
+        start += held.shape[0]
+    return jnp.concatenate([acc[g] for g in range(acc.shape[0])], 1)
+
+
+def forward_body(where, normed, got_a, got_b, *refs, layout, held):
+    stacks, refs = refs[: len(layout)], refs[len(layout) :]
+    weights, refs = refs[:held], refs[held:]
+    cot, bias, encoded, slope_rev, proj, full = refs[:6]
+    first, wrap, acc = refs[6:]
     place_shards(where[0], layout, stacks, 0, 1, full)
     proj[...] = full[0, :, : proj.shape[1]]
     odd = where[0] % 2 == 1
@@ -153,7 +170,7 @@
     for c in range(chunks):
         first[...] = jnp.concatenate([part(c), part(c + 1)], 0).T
         wrap[...] = jnp.concatenate([part(c + 2), part(c + 1)], 0).T
-        pos = conv(w_any, w_vmem, None, sems, first, wrap, acc, c)
+        pos = conv(weights, None, first, wrap, acc)
         pos = pos + bias[...].astype(F32)
         cdf = phi_cdf(pos)
         here = slice(c * rows, (c + 1) * rows)
@@ -165,10 +182,11 @@
         slope_rev[here, :] = (cot_rev * slope).astype(BF16)
 
 
-def backward_body(where, slope_rev, got_a, got_b, w_any, cot, normed, proj, *refs, scale, order):
-    kept, sent, unit_grad, unit_sent, w_vmem, first, wrap, acc, sems = refs[:9]
-    turned, hid_grad, full, rows_f32 = refs[9:]
-    tap_copy(w_any, w_vmem, sems, 0).start()
+def backward_body(where, slope_rev, got_a, got_b, *refs, scale, order, held):
+    weights, refs = refs[:held], refs[held:]
+    (cot, normed, proj), refs = refs[:3], refs[3:]
+    kept, sent, unit_grad, unit_sent, first, wrap, acc = refs[:7]
+    turned, hid_grad, full, rows_f32 = refs[7:]
     odd = where[0] % 2 == 1
     low = jnp.where(odd, got_a[...], got_b[...])
     high = jnp.where(odd, got_b[...], got_a[...])
@@ -179,7 +197,7 @@
     for c in range(chunks):
         first[...] = jnp.concatenate([part(c + 2), part(c + 1)], 0).T
         wrap[...] = jnp.concatenate([part(c), part(c + 1)], 0).T
-        back = conv(w_any, w_vmem, turned, sems, first, wrap, acc, c)
+        back = conv(weights, turned, first, wrap, acc)
         here = slice(c * rows, (c + 1) * rows)
         hid_grad[here, :] = (cot[here, :].astype(F32) + back).astype(BF16)
     grad = hid_grad[...]
@@ -196,13 +214,18 @@
         unit_sent[e - 1] = rows_f32[where[1] ^ e].astype(BF16)
 
 
+def on_chip(values):
+    return [pltpu.with_memory_space_constraint(v, pltpu.VMEM) for v in values]
+
+
 def vmem_specs(count):
     return [pl.BlockSpec(memory_space=pltpu.VMEM)] * count
 
 
 SMEM_SPEC = pl.BlockSpec(memory_space=pltpu.SMEM)
-ANY_SPEC = pl.BlockSpec(memory_space=pl.ANY)
-PARAMS = pltpu.CompilerParams(vmem_limit_bytes=VMEM_LIMIT)
+HBM_SPEC = pl.BlockSpec(memory_space=pltpu.HBM)
+PARAMS = pltpu.CompilerParams(vmem_limit_bytes=16 * 1024 * 1024)
+CONV_PARAMS = pltpu.CompilerParams(vmem_limit_bytes=CONV_MB * 1024 * 1024)
 
 
 def swap(values, axis, mask):
@@ -255,7 +278,9 @@
     own = features.shape[0] // 4
     block = own * slots
 
-    w_taps = jnp.transpose(pos_weight, (1, 2, 3, 0))
+    w_taps = pltpu.with_memory_space_constraint(
+        jnp.transpose(pos_weight, (1, 2, 3, 0)), pltpu.HBM
+    )
     blocks = [features] + [swap(features, "grp", e) for e in range(1, slots)]
     bias = pos_bias.reshape(1, columns)
     proj_half = lax.dynamic_slice_in_dim(projection, slot * columns, columns, 1)
@@ -270,50 +295,60 @@
     common = dict(layout=layout)
     taps_scratch = [pltpu.VMEM((2, channels, channels), BF16)]
 
-    act_five = pl.pallas_call(
+    cut = (groups + 1) // 2
+    tap_sems = lambda count: pltpu.SemaphoreType.DMA((count, 5))
+    act_five, w_low = pl.pallas_call(
         functools.partial(five_body, count=slots, **common),
-        in_specs=[SMEM_SPEC] + vmem_specs(slots + len(five)),
-        out_specs=vmem_specs(1)[0],
-        out_shape=jax.ShapeDtypeStruct((2 * block, channels), BF16),
-        scratch_shapes=taps_scratch,
+        in_specs=[SMEM_SPEC] + vmem_specs(slots + len(five)) + [HBM_SPEC],
+        out_specs=vmem_specs(2),
+        out_shape=[
+            pltpu.VMEM((2 * block, channels), BF16),
+            pltpu.VMEM((cut, width, width, taps), BF16),
+        ],
+        scratch_shapes=taps_scratch + [tap_sems(cut)],
         compiler_params=PARAMS,
         name="five",
-    )(where, *blocks, *five)
-    normed, unit, inv_dev = pl.pallas_call(
-        functools.partial(six_body, count=slots, **common),
-        in_specs=[SMEM_SPEC] + vmem_specs(1 + len(six)),
-        out_specs=vmem_specs(3),
+    )(where, blocks[0], *on_chip(blocks[1:] + five), w_taps)
+    rest = groups - cut
+    results = pl.pallas_call(
+        functools.partial(six_body, count=slots, start=cut if rest else None, **common),
+        in_specs=[SMEM_SPEC] + vmem_specs(1 + len(six)) + ([HBM_SPEC] if rest else []),
+        out_specs=vmem_specs(4 if rest else 3),
         out_shape=[
-            jax.ShapeDtypeStruct((block, channels), BF16),
-            jax.ShapeDtypeStruct((own, channels), F32),
-            jax.ShapeDtypeStruct((own, 128), F32),
-        ],
-        scratch_shapes=taps_scratch,
+            pltpu.VMEM((block, channels), BF16),
+            pltpu.VMEM((own, channels), F32),
+            pltpu.VMEM((own, 128), F32),
+        ]
+        + ([pltpu.VMEM((rest, width, width, taps), BF16)] if rest else []),
+        scratch_shapes=taps_scratch + ([tap_sems(rest)] if rest else []),
         compiler_params=PARAMS,
         name="six",
-    )(where, act_five, *six)
+    )(where, act_five, *on_chip(six), *([w_taps] if rest else []))
+    normed, unit, inv_dev = results[:3]
+    weights = [w_low] + list(results[3:])
 
     whole = block == half
     tail = normed if whole else normed[block - half :]
     head = normed if whole else normed[:half]
     got_a, got_b = halo(tail, head, me % 2)
     conv_scratch = [
-        pltpu.VMEM((groups, width, width, taps), BF16),
         pltpu.VMEM((columns, taps), F32),
         pltpu.VMEM((columns, taps), F32),
         pltpu.VMEM((groups, half, width), F32),
-        pltpu.SemaphoreType.DMA((groups,)),
     ]
     encoded, slope_rev, proj = pl.pallas_call(
-        functools.partial(forward_body, **common),
-        in_specs=[SMEM_SPEC] + vmem_specs(3 + len(last)) + [ANY_SPEC] + vmem_specs(2),
+        functools.partial(forward_body, held=len(weights), **common),
+        in_specs=[SMEM_SPEC] + vmem_specs(3 + len(last) + len(weights) + 2),
         out_specs=vmem_specs(3),
-        out_shape=[jax.ShapeDtypeStruct((block, columns), BF16)] * 2
-        + [jax.ShapeDtypeStruct((channels, columns), BF16)],
+        out_shape=[
+            jax.ShapeDtypeStruct((block, columns), BF16),
+            pltpu.VMEM((block, columns), BF16),
+            pltpu.VMEM((channels, columns), BF16),
+        ],
         scratch_shapes=[pltpu.VMEM((1, channels, channels), BF16)] + conv_scratch,
-        compiler_params=PARAMS,
+        compiler_params=CONV_PARAMS,
         name="forward",
-    )(where, normed, got_a, got_b, *last, w_taps, cotangent, bias)
+    )(where, normed, *on_chip([got_a, got_b] + last), *weights, cotangent, bias)
 
     tail = slope_rev if whole else slope_rev[block - half :]
     head = slope_rev if whole else slope_rev[:half]
@@ -329,13 +364,13 @@
     for mask in reversed(masks):
         order = order + [p ^ mask for p in order]
     kept, sent, unit_grad, unit_sent = pl.pallas_call(
-        functools.partial(backward_body, scale=scale, order=order),
-        in_specs=[SMEM_SPEC] + vmem_specs(3) + [ANY_SPEC] + vmem_specs(3),
+        functools.partial(backward_body, scale=scale, order=order, held=len(weights)),
+        in_specs=[SMEM_SPEC] + vmem_specs(6 + len(weights)),
         out_specs=vmem_specs(4),
-        out_shape=[jax.ShapeDtypeStruct((members // 2, share, columns), BF16)] * 2
+        out_shape=[pltpu.VMEM((members // 2, share, columns), BF16)] * 2
         + [
-            jax.ShapeDtypeStruct((own, channels), F32),
-            jax.ShapeDtypeStruct((slots - 1, own, channels), BF16),
+            pltpu.VMEM((own, channels), F32),
+            pltpu.VMEM((slots - 1, own, channels), BF16),
         ],
         scratch_shapes=conv_scratch
         + [
@@ -344,9 +379,9 @@
             pltpu.VMEM((members, share, columns), F32),
             pltpu.VMEM((slots, own, channels), F32),
         ],
-        compiler_params=PARAMS,
+        compiler_params=CONV_PARAMS,
         name="backward",
-    )(where, slope_rev, got_a, got_b, w_taps, cotangent, normed, proj)
+    )(where, slope_rev, *on_chip([got_a, got_b]), *weights, cotangent, normed, proj)
 
     got = swap(sent, "tm", 1)
     total = (kept.astype(F32) + got.astype(F32)).astype(BF16)

time: 103 us -> 93 us (0.903)
  Pallas kernels: 29.8 us -> 23.4 us
  local copies, waits for them, and re-layouts: 5.01 us -> 1.17 us
  starting transfers between devices: 37.3 us -> 40.7 us
  other arithmetic: 6.58 us -> 3.45 us
    pallas_call x3, Pallas kernels: 27.1 us -> 19.6 us  [the longest x1 8.04 us: on_device(): pl.pallas_call(functools.partial(forward_body, held=len(weights), **commo...]
    ppermute x24, starting transfers between devices: 36 us -> 39.4 us  [swap(): return lax.ppermute(values, axis, [(i, i ^ mask) for i in range(count)])]
    unnamed x40 -> x8, local copies, waits for them, and re-layouts: 3.51 us -> 0.93 us
    reshape x1, local copies, waits for them, and re-layouts: 1.26 us -> 0.01 us  [on_device(): bias = pos_bias.reshape(1, columns)]
    pallas_call x1, Pallas kernels: 2.78 us -> 3.83 us  [on_device(): pl.pallas_call(functools.partial(five_body, count=slots, **common), in_sp...]
  transfers between devices with their start and end apart: 26 -> 26, of which waited for: 8 -> 10; matrix products, arithmetic and copies ran while one was open for 6% -> 3% of each run, Pallas kernels for 5% -> 8%
where the time goes in v3:
time: 93 us; the launch traced here: 92.8 us
  starting transfers between devices  40.7 us (44%)
  Pallas kernels  23.4 us (25%)
  waiting for transfers between devices  23.2 us (25%)
  other arithmetic  3.45 us (4%)
  local copies, waits for them, and re-layouts  1.17 us (1%)
    ppermute x24, starting transfers between devices, swap(): return lax.ppermute(values, axis, [(i, i ^ mask) for i in range(count)])  39.4 us
    ppermute x24, waiting for transfers between devices, swap(): return lax.ppermute(values, axis, [(i, i ^ mask) for i in range(count)])  23.2 us
    pallas_call x1, Pallas kernels, on_device(): pl.pallas_call(functools.partial(forward_body, held=len(weights), **commo...  8.04 us
    pallas_call x1, Pallas kernels, on_device(): pl.pallas_call(functools.partial(backward_body, scale=scale, order=order,...  7.75 us
    pallas_call x1, Pallas kernels, on_device(): pl.pallas_call(functools.partial(five_body, count=slots, **common), in_sp...  3.83 us
    pallas_call x1, Pallas kernels, on_device(): pl.pallas_call(functools.partial(six_body, count=slots, start=cut if rest...  3.8 us
  transfers between devices with their start and end apart: 26, of which 10 were waited for; matrix products, arithmetic and copies ran while one was open for 3% of the time, Pallas kernels for 8%

profile of v3, /device:TPU:0, one launch (start us, length us, event | category | flops | bytes accessed | tf_op | source)
XLA Modules:
  0.0 92.8 jit_solution(5917032244199055449)
XLA Ops:
  0.6 0.0 copy-start
  0.6 3.1 %collective-permute-start.1 = (bf16[2,32,512]{2,1,0:T(8,128)(2,1)}, bf16[2,32,512]{2,1,0:T(8,128)(2,1)S(1)}, u32[]{:S(2)}, u32[]{:S(2)}) collective-permute-start(bf16[2,32,512]{2,1,0:T(8,128)(2,1)} %bitcast.39), channel_id=1, source_target_pairs={{0,8},{2,10},{4,12},{6,14},{8,0},{10,2},{12,4},{14,6},{16,24},{18,... | collective-permute-start | bytes 196616 | tf_op jit(solution)/shard_map/ppermute | solution.py:233
  3.8 2.6 %collective-permute-start.2 = (bf16[2,32,512]{2,1,0:T(8,128)(2,1)}, bf16[2,32,512]{2,1,0:T(8,128)(2,1)S(1)}, u32[]{:S(2)}, u32[]{:S(2)}) collective-permute-start(bf16[2,32,512]{2,1,0:T(8,128)(2,1)} %bitcast.40), channel_id=1, source_target_pairs={{0,16},{2,18},{4,20},{6,22},{8,24},{10,26},{12,28},{14,30},{16,0},... | collective-permute-start | bytes 196616 | tf_op jit(solution)/shard_map/ppermute | solution.py:233
  6.4 0.1 constant_dynamic-slice_fusion
  6.5 0.9 fusion.1
  7.3 1.0 %collective-permute-start.7 = (bf16[3,32,512]{2,1,0:T(8,128)(2,1)S(1)}, bf16[3,32,512]{2,1,0:T(8,128)(2,1)S(1)}, u32[]{:S(2)}, u32[]{:S(2)}) collective-permute-start(bf16[3,32,512]{2,1,0:T(8,128)(2,1)S(1)} %get-tuple-element.35), channel_id=1, source_target_pairs={{0,8},{2,10},{4,12},{6,14},{8,0},{10,2},{12,4},{14,6},{16,24},{18,... | collective-permute-start | bytes 294920 | tf_op jit(solution)/shard_map/ppermute | solution.py:233
  8.3 3.5 %collective-permute-start.8 = (bf16[3,32,512]{2,1,0:T(8,128)(2,1)S(1)}, bf16[3,32,512]{2,1,0:T(8,128)(2,1)S(1)}, u32[]{:S(2)}, u32[]{:S(2)}) collective-permute-start(bf16[3,32,512]{2,1,0:T(8,128)(2,1)S(1)} %get-tuple-element.35), channel_id=1, source_target_pairs={{0,16},{2,18},{4,20},{6,22},{8,24},{10,26},{12,28},{14,30},{16,0},... | collective-permute-start | bytes 294920 | tf_op jit(solution)/shard_map/ppermute | solution.py:233
  11.8 1.7 %collective-permute-done.3 = bf16[2,32,512]{2,1,0:T(8,128)(2,1)S(1)} collective-permute-done((bf16[2,32,512]{2,1,0:T(8,128)(2,1)}, bf16[2,32,512]{2,1,0:T(8,128)(2,1)S(1)}, u32[]{:S(2)}, u32[]{:S(2)}) %collective-permute-start.3) | collective-permute-done | bytes 65568 | tf_op jit(solution)/shard_map/ppermute | solution.py:233
  13.4 0.9 pad_maximum_fusion.1.refs_2_
  14.3 1.6 %collective-permute-start.4 = (bf16[4,2,32,512]{3,2,1,0:T(8,128)(2,1)S(1)}, bf16[4,2,32,512]{3,2,1,0:T(8,128)(2,1)S(1)}, u32[]{:S(2)}, u32[]{:S(2)}) collective-permute-start(bf16[4,2,32,512]{3,2,1,0:T(8,128)(2,1)S(1)} %pad_maximum_fusion.1.refs_2_), channel_id=1, source_target_pairs={{0,4},{2,6},{4,0},{6,2},{8,12},{10,14},{12,8},{14,10},{16,20},{18,... | collective-permute-start | bytes 786440 | tf_op jit(solution)/shard_map/ppermute | solution.py:233
  15.9 3.7 %collective-permute-done.8 = bf16[3,32,512]{2,1,0:T(8,128)(2,1)S(1)} collective-permute-done((bf16[3,32,512]{2,1,0:T(8,128)(2,1)S(1)}, bf16[3,32,512]{2,1,0:T(8,128)(2,1)S(1)}, u32[]{:S(2)}, u32[]{:S(2)}) %collective-permute-start.8) | collective-permute-done | bytes 98336 | tf_op jit(solution)/shard_map/ppermute | solution.py:233
  19.6 0.1 pad_maximum_fusion
  19.7 1.6 %collective-permute-start.10 = (bf16[4,2,32,512]{3,2,1,0:T(8,128)(2,1)S(1)}, bf16[4,2,32,512]{3,2,1,0:T(8,128)(2,1)S(1)}, u32[]{:S(2)}, u32[]{:S(2)}) collective-permute-start(bf16[4,2,32,512]{3,2,1,0:T(8,128)(2,1)S(1)} %slice.36.refs_0_), channel_id=1, source_target_pairs={{0,4},{2,6},{4,0},{6,2},{8,12},{10,14},{12,8},{14,10},{16,20},{18,... | collective-permute-start | bytes 786440 | tf_op jit(solution)/shard_map/ppermute | solution.py:233
  21.3 1.5 %collective-permute-start = (bf16[128,512]{1,0:T(8,128)(2,1)}, bf16[128,512]{1,0:T(8,128)(2,1)S(1)}, u32[]{:S(2)}, u32[]{:S(2)}) collective-permute-start(bf16[128,512]{1,0:T(8,128)(2,1)} %refs_0_.1), channel_id=1, source_target_pairs={{0,1},{1,0},{2,3},{3,2},{4,5},{5,4},{6,7},{7,6},{8,9},{9,8},{10,11... | collective-permute-start | bytes 393224 | tf_op jit(solution)/shard_map/ppermute | solution.py:233
  22.8 0.5 collective-permute-start.11
  23.3 3.5 %collective-permute-done.10.refs_1_ = bf16[4,2,32,512]{3,2,1,0:T(8,128)(2,1)S(1)} collective-permute-done((bf16[4,2,32,512]{3,2,1,0:T(8,128)(2,1)S(1)}, bf16[4,2,32,512]{3,2,1,0:T(8,128)(2,1)S(1)}, u32[]{:S(2)}, u32[]{:S(2)}) %collective-permute-start.10) | collective-permute-done | bytes 262176 | tf_op jit(solution)/shard_map/ppermute | solution.py:233
  26.9 1.6 %collective-permute-start.15 = (bf16[4,1,32,512]{3,2,1,0:T(8,128)(2,1)S(1)}, bf16[4,1,32,512]{3,2,1,0:T(8,128)(2,1)S(1)}, u32[]{:S(2)}, u32[]{:S(2)}) collective-permute-start(bf16[4,1,32,512]{3,2,1,0:T(8,128)(2,1)S(1)} %pad_maximum_fusion.2.refs_0_), channel_id=1, source_target_pairs={{0,4},{2,6},{4,0},{6,2},{8,12},{10,14},{12,8},{14,10},{16,20},{18,... | collective-permute-start | bytes 393224 | tf_op jit(solution)/shard_map/ppermute | solution.py:233
  28.4 4.4 %collective-permute-done.15.refs_1_ = bf16[4,1,32,512]{3,2,1,0:T(8,128)(2,1)S(1)} collective-permute-done((bf16[4,1,32,512]{3,2,1,0:T(8,128)(2,1)S(1)}, bf16[4,1,32,512]{3,2,1,0:T(8,128)(2,1)S(1)}, u32[]{:S(2)}, u32[]{:S(2)}) %collective-permute-start.15) | collective-permute-done | bytes 131104 | tf_op jit(solution)/shard_map/ppermute | solution.py:233
  32.8 0.5 collective-permute-start.17
  33.3 0.1 pad_add_fusion.where
  33.4 0.9 copy-done.2
  34.3 3.8 %five.1 = (bf16[128,512]{1,0:T(8,128)(2,1)S(1)}, bf16[2,120,120,128]{3,2,1,0:T(8,128)(2,1)S(1)}) custom-call(s32[2]{0:T(128)S(1)} %pad_add_fusion.where, bf16[128,512]{1,0:T(8,128)(2,1)S(1)} %copy-done.2, bf16[128,512]{1,0:T(8,128)(2,1)S(1)} %collective-permute-done.refs_1_, bf16[4,2,32,512]{3,2,1,0:T(8,128)(2,1)S(1)} %pad_maximum_fusion.1.refs_2_, ...), custom_call_target="tpu_custom_call" | custom-call | tf_op jit(solution)/shard_map/five/pallas_call | solution.py:300
  38.2 0.0 copy-start.3
  38.2 0.0 copy-start.1
  38.2 3.8 %six.1 = (bf16[64,512]{1,0:T(8,128)(2,1)S(1)}, f32[32,512]{1,0:T(8,128)S(1)}, f32[32,128]{1,0:T(8,128)S(1)}, bf16[2,120,120,128]{3,2,1,0:T(8,128)(2,1)S(1)}) custom-call(s32[2]{0:T(128)S(1)} %pad_add_fusion.where, bf16[128,512]{1,0:T(8,128)(2,1)S(1)} %get-tuple-element.16.act, bf16[4,2,32,512]{3,2,1,0:T(8,128)(2,1)S(1)} %slice.36.refs_0_, ...), custom_call_target="tpu_custom_call" | custom-call | tf_op jit(solution)/shard_map/six/pallas_call | solution.py:313
  42.0 0.1 collective-permute-start.13
  42.1 0.7 collective-permute-start.14
  42.8 0.5 collective-permute-done.13.got_a
  43.4 8.0 %forward.1 = (bf16[64,480]{1,0:T(8,128)(2,1)}, bf16[64,480]{1,0:T(8,128)(2,1)S(1)}, bf16[512,480]{1,0:T(8,128)(2,1)S(1)}) custom-call(s32[2]{0:T(128)S(1)} %pad_add_fusion.where, bf16[64,512]{1,0:T(8,128)(2,1)S(1)} %get-tuple-element.17.normed.refs_3_, bf16[64,512]{1,0:T(8,128)(2,1)S(1)} %collective-permute-done.13.got_a, ...), custom_call_target="tpu_custom_call" | custom-call | tf_op jit(solution)/shard_map/forward/pallas_call | solution.py:339
  51.4 4.8 %collective-permute-start.18 = (bf16[64,480]{1,0:T(8,128)(2,1)S(1)}, bf16[64,480]{1,0:T(8,128)(2,1)S(1)}, u32[]{:S(2)}, u32[]{:S(2)}) collective-permute-start(bf16[64,480]{1,0:T(8,128)(2,1)S(1)} %get-tuple-element.22.slope_rev), channel_id=1, source_target_pairs={{0,2},{2,0},{4,6},{6,4},{8,10},{10,8},{12,14},{14,12},{16,18},{18,... | collective-permute-start | bytes 184328 | tf_op jit(solution)/shard_map/ppermute | solution.py:233
  56.2 0.7 collective-permute-start.19
  56.9 0.2 collective-permute-done.18.got_a
  57.1 7.8 %backward.1 = (bf16[8,32,480]{2,1,0:T(8,128)(2,1)S(1)}, bf16[8,32,480]{2,1,0:T(8,128)(2,1)S(1)}, f32[32,512]{1,0:T(8,128)S(1)}, bf16[1,32,512]{2,1,0:T(8,128)(2,1)S(1)}) custom-call(s32[2]{0:T(128)S(1)} %pad_add_fusion.where, bf16[64,480]{1,0:T(8,128)(2,1)S(1)} %get-tuple-element.22.slope_rev, bf16[64,480]{1,0:T(8,128)(2,1)S(1)} %collective-permute-done.18.got_a, ...), custom_call_target="tpu_custom_call" | custom-call | tf_op jit(solution)/shard_map/backward/pallas_call | solution.py:366
  64.9 6.0 %collective-permute-start.21 = (bf16[8,32,480]{2,1,0:T(8,128)(2,1)S(1)}, bf16[8,32,480]{2,1,0:T(8,128)(2,1)S(1)}, u32[]{:S(2)}, u32[]{:S(2)}) collective-permute-start(bf16[8,32,480]{2,1,0:T(8,128)(2,1)S(1)} %get-tuple-element.28), channel_id=1, source_target_pairs={{0,2},{2,0},{4,6},{6,4},{8,10},{10,8},{12,14},{14,12},{16,18},{18,... | collective-permute-start | bytes 737288 | tf_op jit(solution)/shard_map/ppermute | solution.py:233
  70.8 1.5 %collective-permute-start.20 = (bf16[32,512]{1,0:T(8,128)(2,1)S(1)}, bf16[32,512]{1,0:T(8,128)(2,1)S(1)}, u32[]{:S(2)}, u32[]{:S(2)}) collective-permute-start(bf16[32,512]{1,0:T(8,128)(2,1)S(1)} %bitcast.29), channel_id=1, source_target_pairs={{0,1},{1,0},{2,3},{3,2},{4,5},{5,4},{6,7},{7,6},{8,9},{9,8},{10,11... | collective-permute-start | bytes 98312 | tf_op jit(solution)/shard_map/ppermute | solution.py:233
  72.3 0.1 slice_reduce_fusion
  72.4 2.3 %collective-permute-done.20 = bf16[32,512]{1,0:T(8,128)(2,1)S(1)} collective-permute-done((bf16[32,512]{1,0:T(8,128)(2,1)S(1)}, bf16[32,512]{1,0:T(8,128)(2,1)S(1)}, u32[]{:S(2)}, u32[]{:S(2)}) %collective-permute-start.20) | collective-permute-done | bytes 32800 | tf_op jit(solution)/shard_map/ppermute | solution.py:233
  74.8 0.1 fusion
  74.9 0.1 add_convert_fusion
  75.0 2.9 %collective-permute-start.22 = (bf16[4,32,480]{2,1,0:T(8,128)(2,1)S(1)}, bf16[4,32,480]{2,1,0:T(8,128)(2,1)S(1)}, u32[]{:S(2)}, u32[]{:S(2)}) collective-permute-start(bf16[4,32,480]{2,1,0:T(8,128)(2,1)S(1)} %slice.38), channel_id=1, source_target_pairs={{0,4},{2,6},{4,0},{6,2},{8,12},{10,14},{12,8},{14,10},{16,20},{18,... | collective-permute-start | bytes 368648 | tf_op jit(solution)/shard_map/ppermute | solution.py:233
  77.9 2.9 %collective-permute-done.22 = bf16[4,32,480]{2,1,0:T(8,128)(2,1)S(1)} collective-permute-done((bf16[4,32,480]{2,1,0:T(8,128)(2,1)S(1)}, bf16[4,32,480]{2,1,0:T(8,128)(2,1)S(1)}, u32[]{:S(2)}, u32[]{:S(2)}) %collective-permute-start.22) | collective-permute-done | bytes 122912 | tf_op jit(solution)/shard_map/ppermute | solution.py:233
  80.9 3.3 %collective-permute-start.23 = (bf16[32,480]{1,0:T(8,128)(2,1)S(1)}, bf16[32,480]{1,0:T(8,128)(2,1)S(1)}, u32[]{:S(2)}, u32[]{:S(2)}) collective-permute-start(bf16[32,480]{1,0:T(8,128)(2,1)S(1)} %get-tuple-element.31), channel_id=1, source_target_pairs={{0,8},{2,10},{4,12},{6,14},{8,0},{10,2},{12,4},{14,6},{16,24},{18,... | collective-permute-start | bytes 92168 | tf_op jit(solution)/shard_map/ppermute | solution.py:233
  84.2 2.2 %collective-permute-start.24 = (bf16[32,480]{1,0:T(8,128)(2,1)S(1)}, bf16[32,480]{1,0:T(8,128)(2,1)S(1)}, u32[]{:S(2)}, u32[]{:S(2)}) collective-permute-start(bf16[32,480]{1,0:T(8,128)(2,1)S(1)} %get-tuple-element.33), channel_id=1, source_target_pairs={{0,16},{2,18},{4,20},{6,22},{8,24},{10,26},{12,28},{14,30},{16,0},... | collective-permute-start | bytes 92168 | tf_op jit(solution)/shard_map/ppermute | solution.py:233
  86.4 1.2 %collective-permute-start.25 = (bf16[32,480]{1,0:T(8,128)(2,1)S(1)}, bf16[32,480]{1,0:T(8,128)(2,1)S(1)}, u32[]{:S(2)}, u32[]{:S(2)}) collective-permute-start(bf16[32,480]{1,0:T(8,128)(2,1)S(1)} %get-tuple-element.32), channel_id=1, source_target_pairs={{0,24},{2,26},{4,28},{6,30},{8,16},{10,18},{12,20},{14,22},{16,8},... | collective-permute-start | bytes 92168 | tf_op jit(solution)/shard_map/ppermute | solution.py:233
  87.6 0.7 multiply_convert_fusion
  88.3 0.9 collective-permute-done.24
  89.2 3.0 %collective-permute-done.25 = bf16[32,480]{1,0:T(8,128)(2,1)S(1)} collective-permute-done((bf16[32,480]{1,0:T(8,128)(2,1)S(1)}, bf16[32,480]{1,0:T(8,128)(2,1)S(1)}, u32[]{:S(2)}, u32[]{:S(2)}) %collective-permute-start.25) | collective-permute-done | bytes 30752 | tf_op jit(solution)/shard_map/ppermute | solution.py:233
  92.1 0.6 convert_add_fusion
  (34 shorter events, 0.2 us)
Async XLA Ops:
  0.6 5.7 %copy-start = (bf16[32,960]{1,0:T(8,128)(2,1)S(1)}, bf16[32,960]{1,0:T(8,128)(2,1)}, u32[]{:S(2)}) copy-start(bf16[32,960]{1,0:T(8,128)(2,1)} %param.10) | copy-start | bytes 184324
  0.6 11.1 %collective-permute-start.1 = (bf16[2,32,512]{2,1,0:T(8,128)(2,1)}, bf16[2,32,512]{2,1,0:T(8,128)(2,1)S(1)}, u32[]{:S(2)}, u32[]{:S(2)}) collective-permute-start(bf16[2,32,512]{2,1,0:T(8,128)(2,1)} %bitcast.39), channel_id=1, source_target_pairs={{0,8},{2,10},{4,12},{6,14},{8,0},{10,2},{12,4},{14,6},{16,24},{18,... | collective-permute-start | bytes 196616 | tf_op jit(solution)/shard_map/ppermute | solution.py:233
  3.8 8.0 %collective-permute-start.2 = (bf16[2,32,512]{2,1,0:T(8,128)(2,1)}, bf16[2,32,512]{2,1,0:T(8,128)(2,1)S(1)}, u32[]{:S(2)}, u32[]{:S(2)}) collective-permute-start(bf16[2,32,512]{2,1,0:T(8,128)(2,1)} %bitcast.40), channel_id=1, source_target_pairs={{0,16},{2,18},{4,20},{6,22},{8,24},{10,26},{12,28},{14,30},{16,0},... | collective-permute-start | bytes 196616 | tf_op jit(solution)/shard_map/ppermute | solution.py:233
  6.4 7.1 %collective-permute-start.3 = (bf16[2,32,512]{2,1,0:T(8,128)(2,1)}, bf16[2,32,512]{2,1,0:T(8,128)(2,1)S(1)}, u32[]{:S(2)}, u32[]{:S(2)}) collective-permute-start(bf16[2,32,512]{2,1,0:T(8,128)(2,1)} %bitcast.41), channel_id=1, source_target_pairs={{0,24},{2,26},{4,28},{6,30},{8,16},{10,18},{12,20},{14,22},{16,8},... | collective-permute-start | bytes 196616 | tf_op jit(solution)/shard_map/ppermute | solution.py:233
  7.3 8.6 %collective-permute-start.7 = (bf16[3,32,512]{2,1,0:T(8,128)(2,1)S(1)}, bf16[3,32,512]{2,1,0:T(8,128)(2,1)S(1)}, u32[]{:S(2)}, u32[]{:S(2)}) collective-permute-start(bf16[3,32,512]{2,1,0:T(8,128)(2,1)S(1)} %get-tuple-element.35), channel_id=1, source_target_pairs={{0,8},{2,10},{4,12},{6,14},{8,0},{10,2},{12,4},{14,6},{16,24},{18,... | collective-permute-start | bytes 294920 | tf_op jit(solution)/shard_map/ppermute | solution.py:233
  8.3 11.3 %collective-permute-start.8 = (bf16[3,32,512]{2,1,0:T(8,128)(2,1)S(1)}, bf16[3,32,512]{2,1,0:T(8,128)(2,1)S(1)}, u32[]{:S(2)}, u32[]{:S(2)}) collective-permute-start(bf16[3,32,512]{2,1,0:T(8,128)(2,1)S(1)} %get-tuple-element.35), channel_id=1, source_target_pairs={{0,16},{2,18},{4,20},{6,22},{8,24},{10,26},{12,28},{14,30},{16,0},... | collective-permute-start | bytes 294920 | tf_op jit(solution)/shard_map/ppermute | solution.py:233
  11.8 7.8 %collective-permute-start.9 = (bf16[3,32,512]{2,1,0:T(8,128)(2,1)S(1)}, bf16[3,32,512]{2,1,0:T(8,128)(2,1)S(1)}, u32[]{:S(2)}, u32[]{:S(2)}) collective-permute-start(bf16[3,32,512]{2,1,0:T(8,128)(2,1)S(1)} %get-tuple-element.35), channel_id=1, source_target_pairs={{0,24},{2,26},{4,28},{6,30},{8,16},{10,18},{12,20},{14,22},{16,8},... | collective-permute-start | bytes 294920 | tf_op jit(solution)/shard_map/ppermute | solution.py:233
  14.3 9.0 %collective-permute-start.4 = (bf16[4,2,32,512]{3,2,1,0:T(8,128)(2,1)S(1)}, bf16[4,2,32,512]{3,2,1,0:T(8,128)(2,1)S(1)}, u32[]{:S(2)}, u32[]{:S(2)}) collective-permute-start(bf16[4,2,32,512]{3,2,1,0:T(8,128)(2,1)S(1)} %pad_maximum_fusion.1.refs_2_), channel_id=1, source_target_pairs={{0,4},{2,6},{4,0},{6,2},{8,12},{10,14},{12,8},{14,10},{16,20},{18,... | collective-permute-start | bytes 786440 | tf_op jit(solution)/shard_map/ppermute | solution.py:233
  19.7 7.1 %collective-permute-start.10 = (bf16[4,2,32,512]{3,2,1,0:T(8,128)(2,1)S(1)}, bf16[4,2,32,512]{3,2,1,0:T(8,128)(2,1)S(1)}, u32[]{:S(2)}, u32[]{:S(2)}) collective-permute-start(bf16[4,2,32,512]{3,2,1,0:T(8,128)(2,1)S(1)} %slice.36.refs_0_), channel_id=1, source_target_pairs={{0,4},{2,6},{4,0},{6,2},{8,12},{10,14},{12,8},{14,10},{16,20},{18,... | collective-permute-start | bytes 786440 | tf_op jit(solution)/shard_map/ppermute | solution.py:233
  21.3 5.6 %collective-permute-start = (bf16[128,512]{1,0:T(8,128)(2,1)}, bf16[128,512]{1,0:T(8,128)(2,1)S(1)}, u32[]{:S(2)}, u32[]{:S(2)}) collective-permute-start(bf16[128,512]{1,0:T(8,128)(2,1)} %refs_0_.1), channel_id=1, source_target_pairs={{0,1},{1,0},{2,3},{3,2},{4,5},{5,4},{6,7},{7,6},{8,9},{9,8},{10,11... | collective-permute-start | bytes 393224 | tf_op jit(solution)/shard_map/ppermute | solution.py:233
  22.8 10.1 %collective-permute-start.5 = (bf16[4,2,32,512]{3,2,1,0:T(8,128)(2,1)S(1)}, bf16[4,2,32,512]{3,2,1,0:T(8,128)(2,1)S(1)}, u32[]{:S(2)}, u32[]{:S(2)}) collective-permute-start(bf16[4,2,32,512]{3,2,1,0:T(8,128)(2,1)S(1)} %pad_maximum_fusion.1.refs_2_), channel_id=1, source_target_pairs={{0,2},{2,0},{4,6},{6,4},{8,10},{10,8},{12,14},{14,12},{16,18},{18,... | collective-permute-start | bytes 786440 | tf_op jit(solution)/shard_map/ppermute | solution.py:233
  22.8 15.4 %collective-permute-start.11 = (bf16[4,2,32,512]{3,2,1,0:T(8,128)(2,1)S(1)}, bf16[4,2,32,512]{3,2,1,0:T(8,128)(2,1)S(1)}, u32[]{:S(2)}, u32[]{:S(2)}) collective-permute-start(bf16[4,2,32,512]{3,2,1,0:T(8,128)(2,1)S(1)} %slice.36.refs_0_), channel_id=1, source_target_pairs={{0,2},{2,0},{4,6},{6,4},{8,10},{10,8},{12,14},{14,12},{16,18},{18,... | collective-permute-start | bytes 786440 | tf_op jit(solution)/shard_map/ppermute | solution.py:233
  23.3 10.1 %collective-permute-start.6 = (bf16[4,2,32,512]{3,2,1,0:T(8,128)(2,1)S(1)}, bf16[4,2,32,512]{3,2,1,0:T(8,128)(2,1)S(1)}, u32[]{:S(2)}, u32[]{:S(2)}) collective-permute-start(bf16[4,2,32,512]{3,2,1,0:T(8,128)(2,1)S(1)} %collective-permute-done.4.refs_3_), channel_id=1, source_target_pairs={{0,2},{2,0},{4,6},{6,4},{8,10},{10,8},{12,14},{14,12},{16,18},{18,... | collective-permute-start | bytes 786440 | tf_op jit(solution)/shard_map/ppermute | solution.py:233
  26.8 11.4 %collective-permute-start.12 = (bf16[4,2,32,512]{3,2,1,0:T(8,128)(2,1)S(1)}, bf16[4,2,32,512]{3,2,1,0:T(8,128)(2,1)S(1)}, u32[]{:S(2)}, u32[]{:S(2)}) collective-permute-start(bf16[4,2,32,512]{3,2,1,0:T(8,128)(2,1)S(1)} %collective-permute-done.10.refs_1_), channel_id=1, source_target_pairs={{0,2},{2,0},{4,6},{6,4},{8,10},{10,8},{12,14},{14,12},{16,18},{18,... | collective-permute-start | bytes 786440 | tf_op jit(solution)/shard_map/ppermute | solution.py:233
  26.9 6.0 %collective-permute-start.15 = (bf16[4,1,32,512]{3,2,1,0:T(8,128)(2,1)S(1)}, bf16[4,1,32,512]{3,2,1,0:T(8,128)(2,1)S(1)}, u32[]{:S(2)}, u32[]{:S(2)}) collective-permute-start(bf16[4,1,32,512]{3,2,1,0:T(8,128)(2,1)S(1)} %pad_maximum_fusion.2.refs_0_), channel_id=1, source_target_pairs={{0,4},{2,6},{4,0},{6,2},{8,12},{10,14},{12,8},{14,10},{16,20},{18,... | collective-permute-start | bytes 393224 | tf_op jit(solution)/shard_map/ppermute | solution.py:233
  32.8 10.0 %collective-permute-start.16 = (bf16[4,1,32,512]{3,2,1,0:T(8,128)(2,1)S(1)}, bf16[4,1,32,512]{3,2,1,0:T(8,128)(2,1)S(1)}, u32[]{:S(2)}, u32[]{:S(2)}) collective-permute-start(bf16[4,1,32,512]{3,2,1,0:T(8,128)(2,1)S(1)} %pad_maximum_fusion.2.refs_0_), channel_id=1, source_target_pairs={{0,2},{2,0},{4,6},{6,4},{8,10},{10,8},{12,14},{14,12},{16,18},{18,... | collective-permute-start | bytes 393224 | tf_op jit(solution)/shard_map/ppermute | solution.py:233
  32.8 10.0 %collective-permute-start.17 = (bf16[4,1,32,512]{3,2,1,0:T(8,128)(2,1)S(1)}, bf16[4,1,32,512]{3,2,1,0:T(8,128)(2,1)S(1)}, u32[]{:S(2)}, u32[]{:S(2)}) collective-permute-start(bf16[4,1,32,512]{3,2,1,0:T(8,128)(2,1)S(1)} %collective-permute-done.15.refs_1_), channel_id=1, source_target_pairs={{0,2},{2,0},{4,6},{6,4},{8,10},{10,8},{12,14},{14,12},{16,18},{18,... | collective-permute-start | bytes 393224 | tf_op jit(solution)/shard_map/ppermute | solution.py:233
  33.4 0.9 copy-start.2
  38.2 4.6 %copy-start.3 = (bf16[480]{0:T(512)(128)(2,1)S(1)}, bf16[480]{0:T(512)(128)(2,1)}, u32[]{:S(2)}) copy-start(bf16[480]{0:T(512)(128)(2,1)} %param.12) | copy-start | bytes 2884
  38.2 5.1 %copy-start.1 = (bf16[64,480]{1,0:T(8,128)(2,1)S(1)}, bf16[64,480]{1,0:T(8,128)(2,1)}, u32[]{:S(2)}) copy-start(bf16[64,480]{1,0:T(8,128)(2,1)} %refs_2_.1) | copy-start | bytes 184324
  42.0 1.3 %collective-permute-start.13 = (bf16[64,512]{1,0:T(8,128)(2,1)S(1)}, bf16[64,512]{1,0:T(8,128)(2,1)S(1)}, u32[]{:S(2)}, u32[]{:S(2)}) collective-permute-start(bf16[64,512]{1,0:T(8,128)(2,1)S(1)} %get-tuple-element.17.normed.refs_3_), channel_id=1, source_target_pairs={{0,2},{2,0},{4,6},{6,4},{8,10},{10,8},{12,14},{14,12},{16,18},{18,... | collective-permute-start | bytes 196616 | tf_op jit(solution)/shard_map/ppermute | solution.py:233
  42.1 1.2 %collective-permute-start.14 = (bf16[64,512]{1,0:T(8,128)(2,1)S(1)}, bf16[64,512]{1,0:T(8,128)(2,1)S(1)}, u32[]{:S(2)}, u32[]{:S(2)}) collective-permute-start(bf16[64,512]{1,0:T(8,128)(2,1)S(1)} %get-tuple-element.17.normed.refs_3_), channel_id=1, source_target_pairs={{2,4},{6,8},{10,12},{14,16},{18,20},{22,24},{26,28},{4,2},{8,6},{1... | collective-permute-start | bytes 196616 | tf_op jit(solution)/shard_map/ppermute | solution.py:266
  51.4 5.7 %collective-permute-start.18 = (bf16[64,480]{1,0:T(8,128)(2,1)S(1)}, bf16[64,480]{1,0:T(8,128)(2,1)S(1)}, u32[]{:S(2)}, u32[]{:S(2)}) collective-permute-start(bf16[64,480]{1,0:T(8,128)(2,1)S(1)} %get-tuple-element.22.slope_rev), channel_id=1, source_target_pairs={{0,2},{2,0},{4,6},{6,4},{8,10},{10,8},{12,14},{14,12},{16,18},{18,... | collective-permute-start | bytes 184328 | tf_op jit(solution)/shard_map/ppermute | solution.py:233
  56.2 0.9 collective-permute-start.19
  64.9 10.0 %collective-permute-start.21 = (bf16[8,32,480]{2,1,0:T(8,128)(2,1)S(1)}, bf16[8,32,480]{2,1,0:T(8,128)(2,1)S(1)}, u32[]{:S(2)}, u32[]{:S(2)}) collective-permute-start(bf16[8,32,480]{2,1,0:T(8,128)(2,1)S(1)} %get-tuple-element.28), channel_id=1, source_target_pairs={{0,2},{2,0},{4,6},{6,4},{8,10},{10,8},{12,14},{14,12},{16,18},{18,... | collective-permute-start | bytes 737288 | tf_op jit(solution)/shard_map/ppermute | solution.py:233
  70.8 3.9 %collective-permute-start.20 = (bf16[32,512]{1,0:T(8,128)(2,1)S(1)}, bf16[32,512]{1,0:T(8,128)(2,1)S(1)}, u32[]{:S(2)}, u32[]{:S(2)}) collective-permute-start(bf16[32,512]{1,0:T(8,128)(2,1)S(1)} %bitcast.29), channel_id=1, source_target_pairs={{0,1},{1,0},{2,3},{3,2},{4,5},{5,4},{6,7},{7,6},{8,9},{9,8},{10,11... | collective-permute-start | bytes 98312 | tf_op jit(solution)/shard_map/ppermute | solution.py:233
  75.0 5.8 %collective-permute-start.22 = (bf16[4,32,480]{2,1,0:T(8,128)(2,1)S(1)}, bf16[4,32,480]{2,1,0:T(8,128)(2,1)S(1)}, u32[]{:S(2)}, u32[]{:S(2)}) collective-permute-start(bf16[4,32,480]{2,1,0:T(8,128)(2,1)S(1)} %slice.38), channel_id=1, source_target_pairs={{0,4},{2,6},{4,0},{6,2},{8,12},{10,14},{12,8},{14,10},{16,20},{18,... | collective-permute-start | bytes 368648 | tf_op jit(solution)/shard_map/ppermute | solution.py:233
  80.9 7.4 %collective-permute-start.23 = (bf16[32,480]{1,0:T(8,128)(2,1)S(1)}, bf16[32,480]{1,0:T(8,128)(2,1)S(1)}, u32[]{:S(2)}, u32[]{:S(2)}) collective-permute-start(bf16[32,480]{1,0:T(8,128)(2,1)S(1)} %get-tuple-element.31), channel_id=1, source_target_pairs={{0,8},{2,10},{4,12},{6,14},{8,0},{10,2},{12,4},{14,6},{16,24},{18,... | collective-permute-start | bytes 92168 | tf_op jit(solution)/shard_map/ppermute | solution.py:233
  84.2 5.0 %collective-permute-start.24 = (bf16[32,480]{1,0:T(8,128)(2,1)S(1)}, bf16[32,480]{1,0:T(8,128)(2,1)S(1)}, u32[]{:S(2)}, u32[]{:S(2)}) collective-permute-start(bf16[32,480]{1,0:T(8,128)(2,1)S(1)} %get-tuple-element.33), channel_id=1, source_target_pairs={{0,16},{2,18},{4,20},{6,22},{8,24},{10,26},{12,28},{14,30},{16,0},... | collective-permute-start | bytes 92168 | tf_op jit(solution)/shard_map/ppermute | solution.py:233
  86.4 5.7 %collective-permute-start.25 = (bf16[32,480]{1,0:T(8,128)(2,1)S(1)}, bf16[32,480]{1,0:T(8,128)(2,1)S(1)}, u32[]{:S(2)}, u32[]{:S(2)}) collective-permute-start(bf16[32,480]{1,0:T(8,128)(2,1)S(1)} %get-tuple-element.32), channel_id=1, source_target_pairs={{0,24},{2,26},{4,28},{6,30},{8,16},{10,18},{12,20},{14,22},{16,8},... | collective-permute-start | bytes 92168 | tf_op jit(solution)/shard_map/ppermute | solution.py:233

commit v4 on v3

--- a/solution.py
+++ b/solution.py
@@ -85,10 +85,13 @@
 
 def five_body(where, *refs, layout, count):
     blocks, stacks = refs[:count], refs[count : count + len(layout)]
-    w_any, out, w_out, full, sems = refs[count + len(layout) :]
+    w_any, out, w_out, full, sems, mine, mine_sem = refs[count + len(layout) :]
+    own = pltpu.make_async_copy(blocks[0], mine, mine_sem)
+    own.start()
     copies = tap_copies(w_any, w_out, sems, 0)
     place_shards(where[0], layout, stacks, 0, 2, full)
-    out[...] = strided([b[...] for b in blocks], full)
+    own.wait()
+    out[...] = strided([mine[...]] + [b[...] for b in blocks[1:]], full)
     for copy in copies:
         copy.wait()
 
@@ -218,6 +221,10 @@
     return [pltpu.with_memory_space_constraint(v, pltpu.VMEM) for v in values]
 
 
+def in_hbm(value):
+    return pltpu.with_memory_space_constraint(value, pltpu.HBM)
+
+
 def vmem_specs(count):
     return [pl.BlockSpec(memory_space=pltpu.VMEM)] * count
 
@@ -233,16 +240,12 @@
     return lax.ppermute(values, axis, [(i, i ^ mask) for i in range(count)])
 
 
-def spread_near(shards, count):
-    offs = [0] + [n * (count // 4) for n in (1, 2, 3)]
-    joined = shards[0] if len(shards) == 1 else jnp.concatenate(shards, 0)
-    pieces = [joined] + [swap(joined, "tm", m) for m in offs[1:]]
-    stack = jnp.stack(pieces)
-    stacks, at = [], 0
-    for shard in shards:
-        stacks.append(stack[:, at : at + shard.shape[0]])
-        at += shard.shape[0]
-    return stacks, offs
+def spread_near(shard, count):
+    offs = [n * (count // 4) for n in range(4)]
+    pieces = [shard]
+    for n in (1, 2, 3):
+        pieces.append(swap(shard, "tm", offs[n]))
+    return jnp.stack(pieces), offs
 
 
 def spread_far(stack, offs, count):
@@ -278,17 +281,14 @@
     own = features.shape[0] // 4
     block = own * slots
 
-    w_taps = pltpu.with_memory_space_constraint(
-        jnp.transpose(pos_weight, (1, 2, 3, 0)), pltpu.HBM
-    )
+    w_taps = in_hbm(jnp.transpose(pos_weight, (1, 2, 3, 0)))
     blocks = [features] + [swap(features, "grp", e) for e in range(1, slots)]
     bias = pos_bias.reshape(1, columns)
     proj_half = lax.dynamic_slice_in_dim(projection, slot * columns, columns, 1)
     proj_half = jnp.pad(proj_half, ((0, 0), (0, channels - columns)))
-    (five,), offs = spread_near([jnp.transpose(weight_five, (0, 2, 1))], members)
-    (six, last), _ = spread_near(
-        [jnp.transpose(weight_six, (0, 2, 1)), proj_half[None]], members
-    )
+    five, offs = spread_near(jnp.transpose(weight_five, (0, 2, 1)), members)
+    six, _ = spread_near(jnp.transpose(weight_six, (0, 2, 1)), members)
+    last, _ = spread_near(proj_half[None], members)
     five, layout = spread_far(five, offs, members)
     six, _ = spread_far(six, offs, members)
     last, _ = spread_far(last, offs, members)
@@ -299,16 +299,17 @@
     tap_sems = lambda count: pltpu.SemaphoreType.DMA((count, 5))
     act_five, w_low = pl.pallas_call(
         functools.partial(five_body, count=slots, **common),
-        in_specs=[SMEM_SPEC] + vmem_specs(slots + len(five)) + [HBM_SPEC],
+        in_specs=[SMEM_SPEC, HBM_SPEC] + vmem_specs(slots - 1 + len(five)) + [HBM_SPEC],
         out_specs=vmem_specs(2),
         out_shape=[
             pltpu.VMEM((2 * block, channels), BF16),
             pltpu.VMEM((cut, width, width, taps), BF16),
         ],
-        scratch_shapes=taps_scratch + [tap_sems(cut)],
+        scratch_shapes=taps_scratch
+        + [tap_sems(cut), pltpu.VMEM(features.shape, BF16), pltpu.SemaphoreType.DMA(())],
         compiler_params=PARAMS,
         name="five",
-    )(where, blocks[0], *on_chip(blocks[1:] + five), w_taps)
+    )(where, in_hbm(blocks[0]), *on_chip(blocks[1:] + five), w_taps)
     rest = groups - cut
     results = pl.pallas_call(
         functools.partial(six_body, count=slots, start=cut if rest else None, **common),
@@ -389,7 +390,9 @@
         middle = total.shape[0] // 2
         got = swap(total[middle:], "tm", mask)
         total = (total[:middle].astype(F32) + got.astype(F32)).astype(BF16)
-    parts = [swap(total[n], "tm", p) for n, p in enumerate(finals) if p]
+    parts = []
+    for n in (1, 2, 3):
+        parts.append(swap(total[n], "tm", finals[n]))
     projection_grad = total[0].astype(F32) + sum(p.astype(F32) for p in parts)
 
     grad_unit = unit_grad

time: 93 us -> 91.6 us (0.985)
  waiting for transfers between devices: 23.2 us -> 21.7 us
    ppermute x24 -> x27, waiting for transfers between devices: 23.2 us -> 21.7 us  [swap(): return lax.ppermute(values, axis, [(i, i ^ mask) for i in range(count)])]
    ppermute x24 -> x27, starting transfers between devices: 39.4 us -> 39.9 us  [swap(): return lax.ppermute(values, axis, [(i, i ^ mask) for i in range(count)])]
  transfers between devices with their start and end apart: 26 -> 29, of which waited for: 10 -> 12; matrix products, arithmetic and copies ran while one was open for 3% -> 3% of each run, Pallas kernels for 8% -> 9%
where the time goes in v4:
time: 91.6 us; the launch traced here: 91.4 us
  starting transfers between devices  41.2 us (45%)
  Pallas kernels  23.9 us (26%)
  waiting for transfers between devices  21.7 us (24%)
  other arithmetic  3.42 us (4%)
    ppermute x27, starting transfers between devices, swap(): return lax.ppermute(values, axis, [(i, i ^ mask) for i in range(count)])  39.9 us
    ppermute x27, waiting for transfers between devices, swap(): return lax.ppermute(values, axis, [(i, i ^ mask) for i in range(count)])  21.7 us
    pallas_call x1, Pallas kernels, on_device(): pl.pallas_call(functools.partial(forward_body, held=len(weights), **commo...  8.04 us
    pallas_call x1, Pallas kernels, on_device(): pl.pallas_call(functools.partial(backward_body, scale=scale, order=order,...  7.75 us
    pallas_call x1, Pallas kernels, on_device(): pl.pallas_call(functools.partial(five_body, count=slots, **common), in_sp...  4.34 us
    pallas_call x1, Pallas kernels, on_device(): pl.pallas_call(functools.partial(six_body, count=slots, start=cut if rest...  3.8 us
  transfers between devices with their start and end apart: 29, of which 12 were waited for; matrix products, arithmetic and copies ran while one was open for 3% of the time, Pallas kernels for 9%

profile of v4, /device:TPU:0, one launch (start us, length us, event | category | flops | bytes accessed | tf_op | source)
XLA Modules:
  0.0 91.4 jit_solution(1711190171420013861)
XLA Ops:
  0.6 5.1 %collective-permute-start.3 = (bf16[2,32,512]{2,1,0:T(8,128)(2,1)}, bf16[2,32,512]{2,1,0:T(8,128)(2,1)S(1)}, u32[]{:S(2)}, u32[]{:S(2)}) collective-permute-start(bf16[2,32,512]{2,1,0:T(8,128)(2,1)} %bitcast.37), channel_id=1, source_target_pairs={{0,24},{2,26},{4,28},{6,30},{8,16},{10,18},{12,20},{14,22},{16,8},... | collective-permute-start | bytes 196616 | tf_op jit(solution)/shard_map/ppermute | solution.py:240
  5.8 0.6 collective-permute-start.1
  6.4 3.7 %collective-permute-start.9 = (bf16[2,32,512]{2,1,0:T(8,128)(2,1)}, bf16[2,32,512]{2,1,0:T(8,128)(2,1)S(1)}, u32[]{:S(2)}, u32[]{:S(2)}) collective-permute-start(bf16[2,32,512]{2,1,0:T(8,128)(2,1)} %bitcast.41), channel_id=1, source_target_pairs={{0,24},{2,26},{4,28},{6,30},{8,16},{10,18},{12,20},{14,22},{16,8},... | collective-permute-start | bytes 196616 | tf_op jit(solution)/shard_map/ppermute | solution.py:240
  10.2 1.0 %collective-permute-start.7 = (bf16[2,32,512]{2,1,0:T(8,128)(2,1)}, bf16[2,32,512]{2,1,0:T(8,128)(2,1)S(1)}, u32[]{:S(2)}, u32[]{:S(2)}) collective-permute-start(bf16[2,32,512]{2,1,0:T(8,128)(2,1)} %bitcast.43), channel_id=1, source_target_pairs={{0,8},{2,10},{4,12},{6,14},{8,0},{10,2},{12,4},{14,6},{16,24},{18,... | collective-permute-start | bytes 196616 | tf_op jit(solution)/shard_map/ppermute | solution.py:240
  11.2 3.3 %collective-permute-done.2 = bf16[2,32,512]{2,1,0:T(8,128)(2,1)S(1)} collective-permute-done((bf16[2,32,512]{2,1,0:T(8,128)(2,1)}, bf16[2,32,512]{2,1,0:T(8,128)(2,1)S(1)}, u32[]{:S(2)}, u32[]{:S(2)}) %collective-permute-start.2) | collective-permute-done | bytes 65568 | tf_op jit(solution)/shard_map/ppermute | solution.py:240
  14.5 0.9 pad_maximum_fusion.refs_2_
  15.4 1.4 %collective-permute-start.4 = (bf16[4,2,32,512]{3,2,1,0:T(8,128)(2,1)S(1)}, bf16[4,2,32,512]{3,2,1,0:T(8,128)(2,1)S(1)}, u32[]{:S(2)}, u32[]{:S(2)}) collective-permute-start(bf16[4,2,32,512]{3,2,1,0:T(8,128)(2,1)S(1)} %pad_maximum_fusion.refs_2_), channel_id=1, source_target_pairs={{0,4},{2,6},{4,0},{6,2},{8,12},{10,14},{12,8},{14,10},{16,20},{18,... | collective-permute-start | bytes 786440 | tf_op jit(solution)/shard_map/ppermute | solution.py:240
  16.8 0.5 collective-permute-done.8
  17.2 0.9 pad_maximum_fusion.1.refs_0_
  18.1 1.6 %collective-permute-start.10 = (bf16[4,2,32,512]{3,2,1,0:T(8,128)(2,1)S(1)}, bf16[4,2,32,512]{3,2,1,0:T(8,128)(2,1)S(1)}, u32[]{:S(2)}, u32[]{:S(2)}) collective-permute-start(bf16[4,2,32,512]{3,2,1,0:T(8,128)(2,1)S(1)} %pad_maximum_fusion.1.refs_0_), channel_id=1, source_target_pairs={{0,4},{2,6},{4,0},{6,2},{8,12},{10,14},{12,8},{14,10},{16,20},{18,... | collective-permute-start | bytes 786440 | tf_op jit(solution)/shard_map/ppermute | solution.py:240
  19.7 0.1 constant_dynamic-slice_fusion
  19.8 2.8 %collective-permute-start.17 = (bf16[1,32,512]{2,1,0:T(8,128)(2,1)S(1)}, bf16[1,32,512]{2,1,0:T(8,128)(2,1)S(1)}, u32[]{:S(2)}, u32[]{:S(2)}) collective-permute-start(bf16[1,32,512]{2,1,0:T(8,128)(2,1)S(1)} %get-tuple-element.35), channel_id=1, source_target_pairs={{0,24},{2,26},{4,28},{6,30},{8,16},{10,18},{12,20},{14,22},{16,8},... | collective-permute-start | bytes 98312 | tf_op jit(solution)/shard_map/ppermute | solution.py:240
  22.6 1.7 %collective-permute-start.15 = (bf16[1,32,512]{2,1,0:T(8,128)(2,1)S(1)}, bf16[1,32,512]{2,1,0:T(8,128)(2,1)S(1)}, u32[]{:S(2)}, u32[]{:S(2)}) collective-permute-start(bf16[1,32,512]{2,1,0:T(8,128)(2,1)S(1)} %get-tuple-element.35), channel_id=1, source_target_pairs={{0,8},{2,10},{4,12},{6,14},{8,0},{10,2},{12,4},{14,6},{16,24},{18,... | collective-permute-start | bytes 98312 | tf_op jit(solution)/shard_map/ppermute | solution.py:240
  24.2 1.3 %collective-permute-done.17 = bf16[1,32,512]{2,1,0:T(8,128)(2,1)S(1)} collective-permute-done((bf16[1,32,512]{2,1,0:T(8,128)(2,1)S(1)}, bf16[1,32,512]{2,1,0:T(8,128)(2,1)S(1)}, u32[]{:S(2)}, u32[]{:S(2)}) %collective-permute-start.17) | collective-permute-done | bytes 32800 | tf_op jit(solution)/shard_map/ppermute | solution.py:240
  25.6 1.5 %collective-permute-start = (bf16[128,512]{1,0:T(8,128)(2,1)}, bf16[128,512]{1,0:T(8,128)(2,1)S(1)}, u32[]{:S(2)}, u32[]{:S(2)}) collective-permute-start(bf16[128,512]{1,0:T(8,128)(2,1)} %refs_0_.1), channel_id=1, source_target_pairs={{0,1},{1,0},{2,3},{3,2},{4,5},{5,4},{6,7},{7,6},{8,9},{9,8},{10,11... | collective-permute-start | bytes 393224 | tf_op jit(solution)/shard_map/ppermute | solution.py:240
  27.1 0.3 collective-permute-done.16
  27.4 0.5 collective-permute-start.11
  27.9 0.1 collective-permute-start.6
  28.0 0.4 collective-permute-start.12
  28.4 2.3 %collective-permute-done.refs_1_ = bf16[128,512]{1,0:T(8,128)(2,1)S(1)} collective-permute-done((bf16[128,512]{1,0:T(8,128)(2,1)}, bf16[128,512]{1,0:T(8,128)(2,1)S(1)}, u32[]{:S(2)}, u32[]{:S(2)}) %collective-permute-start) | collective-permute-done | bytes 131104 | tf_op jit(solution)/shard_map/ppermute | solution.py:240
  30.7 0.5 collective-permute-start.18
  31.2 4.5 %collective-permute-done.18.refs_1_ = bf16[4,1,32,512]{3,2,1,0:T(8,128)(2,1)S(1)} collective-permute-done((bf16[4,1,32,512]{3,2,1,0:T(8,128)(2,1)S(1)}, bf16[4,1,32,512]{3,2,1,0:T(8,128)(2,1)S(1)}, u32[]{:S(2)}, u32[]{:S(2)}) %collective-permute-start.18) | collective-permute-done | bytes 131104 | tf_op jit(solution)/shard_map/ppermute | solution.py:240
  35.7 0.5 collective-permute-start.20
  36.2 0.1 pad_add_fusion.where
  36.3 4.3 %five.1 = (bf16[128,512]{1,0:T(8,128)(2,1)S(1)}, bf16[2,120,120,128]{3,2,1,0:T(8,128)(2,1)S(1)}) custom-call(s32[2]{0:T(128)S(1)} %pad_add_fusion.where, bf16[128,512]{1,0:T(8,128)(2,1)} %refs_0_.1, bf16[128,512]{1,0:T(8,128)(2,1)S(1)} %collective-permute-done.refs_1_, bf16[4,2,32,512]{3,2,1,0:T(8,128)(2,1)S(1)} %pad_maximum_fusion.refs_2_, ...), custom_call_target="tpu_custom_call" | custom-call | tf_op jit(solution)/shard_map/five/pallas_call | solution.py:300
  40.7 3.8 %six.1 = (bf16[64,512]{1,0:T(8,128)(2,1)S(1)}, f32[32,512]{1,0:T(8,128)S(1)}, f32[32,128]{1,0:T(8,128)S(1)}, bf16[2,120,120,128]{3,2,1,0:T(8,128)(2,1)S(1)}) custom-call(s32[2]{0:T(128)S(1)} %pad_add_fusion.where, bf16[128,512]{1,0:T(8,128)(2,1)S(1)} %get-tuple-element.16.act, bf16[4,2,32,512]{3,2,1,0:T(8,128)(2,1)S(1)} %pad_maximum_fusion.1.refs_0_, ...), custom_call_target="tpu_custom_call" | custom-call | tf_op jit(solution)/shard_map/six/pallas_call | solution.py:314
  44.5 0.1 collective-permute-start.13
  44.6 0.7 collective-permute-start.14
  45.3 0.5 collective-permute-done.13.got_a
  45.8 8.0 %forward.1 = (bf16[64,480]{1,0:T(8,128)(2,1)}, bf16[64,480]{1,0:T(8,128)(2,1)S(1)}, bf16[512,480]{1,0:T(8,128)(2,1)S(1)}) custom-call(s32[2]{0:T(128)S(1)} %pad_add_fusion.where, bf16[64,512]{1,0:T(8,128)(2,1)S(1)} %get-tuple-element.17.normed.refs_3_, bf16[64,512]{1,0:T(8,128)(2,1)S(1)} %collective-permute-done.13.got_a, ...), custom_call_target="tpu_custom_call" | custom-call | tf_op jit(solution)/shard_map/forward/pallas_call | solution.py:340
  53.9 4.8 %collective-permute-start.21 = (bf16[64,480]{1,0:T(8,128)(2,1)S(1)}, bf16[64,480]{1,0:T(8,128)(2,1)S(1)}, u32[]{:S(2)}, u32[]{:S(2)}) collective-permute-start(bf16[64,480]{1,0:T(8,128)(2,1)S(1)} %get-tuple-element.22.slope_rev), channel_id=1, source_target_pairs={{0,2},{2,0},{4,6},{6,4},{8,10},{10,8},{12,14},{14,12},{16,18},{18,... | collective-permute-start | bytes 184328 | tf_op jit(solution)/shard_map/ppermute | solution.py:240
  58.7 0.7 collective-permute-start.22
  59.4 0.2 collective-permute-done.21.got_a
  59.6 7.8 %backward.1 = (bf16[8,32,480]{2,1,0:T(8,128)(2,1)S(1)}, bf16[8,32,480]{2,1,0:T(8,128)(2,1)S(1)}, f32[32,512]{1,0:T(8,128)S(1)}, bf16[1,32,512]{2,1,0:T(8,128)(2,1)S(1)}) custom-call(s32[2]{0:T(128)S(1)} %pad_add_fusion.where, bf16[64,480]{1,0:T(8,128)(2,1)S(1)} %get-tuple-element.22.slope_rev, bf16[64,480]{1,0:T(8,128)(2,1)S(1)} %collective-permute-done.21.got_a, ...), custom_call_target="tpu_custom_call" | custom-call | tf_op jit(solution)/shard_map/backward/pallas_call | solution.py:367
  67.4 4.7 %collective-permute-start.24 = (bf16[8,32,480]{2,1,0:T(8,128)(2,1)S(1)}, bf16[8,32,480]{2,1,0:T(8,128)(2,1)S(1)}, u32[]{:S(2)}, u32[]{:S(2)}) collective-permute-start(bf16[8,32,480]{2,1,0:T(8,128)(2,1)S(1)} %get-tuple-element.28), channel_id=1, source_target_pairs={{0,2},{2,0},{4,6},{6,4},{8,10},{10,8},{12,14},{14,12},{16,18},{18,... | collective-permute-start | bytes 737288 | tf_op jit(solution)/shard_map/ppermute | solution.py:240
  72.1 1.5 %collective-permute-start.23 = (bf16[32,512]{1,0:T(8,128)(2,1)S(1)}, bf16[32,512]{1,0:T(8,128)(2,1)S(1)}, u32[]{:S(2)}, u32[]{:S(2)}) collective-permute-start(bf16[32,512]{1,0:T(8,128)(2,1)S(1)} %bitcast.34), channel_id=1, source_target_pairs={{0,1},{1,0},{2,3},{3,2},{4,5},{5,4},{6,7},{7,6},{8,9},{9,8},{10,11... | collective-permute-start | bytes 98312 | tf_op jit(solution)/shard_map/ppermute | solution.py:240
  73.6 0.1 slice_reduce_fusion
  73.7 2.3 %collective-permute-done.23 = bf16[32,512]{1,0:T(8,128)(2,1)S(1)} collective-permute-done((bf16[32,512]{1,0:T(8,128)(2,1)S(1)}, bf16[32,512]{1,0:T(8,128)(2,1)S(1)}, u32[]{:S(2)}, u32[]{:S(2)}) %collective-permute-start.23) | collective-permute-done | bytes 32800 | tf_op jit(solution)/shard_map/ppermute | solution.py:240
  76.0 0.1 fusion
  76.1 0.1 add_convert_fusion
  76.2 2.4 %collective-permute-start.25 = (bf16[4,32,480]{2,1,0:T(8,128)(2,1)S(1)}, bf16[4,32,480]{2,1,0:T(8,128)(2,1)S(1)}, u32[]{:S(2)}, u32[]{:S(2)}) collective-permute-start(bf16[4,32,480]{2,1,0:T(8,128)(2,1)S(1)} %slice.29), channel_id=1, source_target_pairs={{0,4},{2,6},{4,0},{6,2},{8,12},{10,14},{12,8},{14,10},{16,20},{18,... | collective-permute-start | bytes 368648 | tf_op jit(solution)/shard_map/ppermute | solution.py:240
  78.6 2.9 %collective-permute-done.25 = bf16[4,32,480]{2,1,0:T(8,128)(2,1)S(1)} collective-permute-done((bf16[4,32,480]{2,1,0:T(8,128)(2,1)S(1)}, bf16[4,32,480]{2,1,0:T(8,128)(2,1)S(1)}, u32[]{:S(2)}, u32[]{:S(2)}) %collective-permute-start.25) | collective-permute-done | bytes 122912 | tf_op jit(solution)/shard_map/ppermute | solution.py:240
  81.6 4.3 %collective-permute-start.28 = (bf16[32,480]{1,0:T(8,128)(2,1)S(1)}, bf16[32,480]{1,0:T(8,128)(2,1)S(1)}, u32[]{:S(2)}, u32[]{:S(2)}) collective-permute-start(bf16[32,480]{1,0:T(8,128)(2,1)S(1)} %get-tuple-element.32), channel_id=1, source_target_pairs={{0,24},{2,26},{4,28},{6,30},{8,16},{10,18},{12,20},{14,22},{16,8},... | collective-permute-start | bytes 92168 | tf_op jit(solution)/shard_map/ppermute | solution.py:240
  85.9 0.6 collective-permute-start.26
  86.5 0.7 multiply_convert_fusion
  87.2 0.7 collective-permute-done.28
  87.9 2.8 %collective-permute-done.27 = bf16[32,480]{1,0:T(8,128)(2,1)S(1)} collective-permute-done((bf16[32,480]{1,0:T(8,128)(2,1)S(1)}, bf16[32,480]{1,0:T(8,128)(2,1)S(1)}, u32[]{:S(2)}, u32[]{:S(2)}) %collective-permute-start.27) | collective-permute-done | bytes 30752 | tf_op jit(solution)/shard_map/ppermute | solution.py:240
  90.7 0.6 convert_add_fusion
  (36 shorter events, 0.2 us)
Async XLA Ops:
  0.6 19.1 %copy-start = (bf16[32,960]{1,0:T(8,128)(2,1)S(1)}, bf16[32,960]{1,0:T(8,128)(2,1)}, u32[]{:S(2)}) copy-start(bf16[32,960]{1,0:T(8,128)(2,1)} %param.10) | copy-start | bytes 184324
  0.6 9.5 %collective-permute-start.3 = (bf16[2,32,512]{2,1,0:T(8,128)(2,1)}, bf16[2,32,512]{2,1,0:T(8,128)(2,1)S(1)}, u32[]{:S(2)}, u32[]{:S(2)}) collective-permute-start(bf16[2,32,512]{2,1,0:T(8,128)(2,1)} %bitcast.37), channel_id=1, source_target_pairs={{0,24},{2,26},{4,28},{6,30},{8,16},{10,18},{12,20},{14,22},{16,8},... | collective-permute-start | bytes 196616 | tf_op jit(solution)/shard_map/ppermute | solution.py:240
  5.8 8.7 %collective-permute-start.2 = (bf16[2,32,512]{2,1,0:T(8,128)(2,1)}, bf16[2,32,512]{2,1,0:T(8,128)(2,1)S(1)}, u32[]{:S(2)}, u32[]{:S(2)}) collective-permute-start(bf16[2,32,512]{2,1,0:T(8,128)(2,1)} %bitcast.38), channel_id=1, source_target_pairs={{0,16},{2,18},{4,20},{6,22},{8,24},{10,26},{12,28},{14,30},{16,0},... | collective-permute-start | bytes 196616 | tf_op jit(solution)/shard_map/ppermute | solution.py:240
  5.8 8.7 %collective-permute-start.1 = (bf16[2,32,512]{2,1,0:T(8,128)(2,1)}, bf16[2,32,512]{2,1,0:T(8,128)(2,1)S(1)}, u32[]{:S(2)}, u32[]{:S(2)}) collective-permute-start(bf16[2,32,512]{2,1,0:T(8,128)(2,1)} %bitcast.39), channel_id=1, source_target_pairs={{0,8},{2,10},{4,12},{6,14},{8,0},{10,2},{12,4},{14,6},{16,24},{18,... | collective-permute-start | bytes 196616 | tf_op jit(solution)/shard_map/ppermute | solution.py:240
  6.4 10.3 %collective-permute-start.9 = (bf16[2,32,512]{2,1,0:T(8,128)(2,1)}, bf16[2,32,512]{2,1,0:T(8,128)(2,1)S(1)}, u32[]{:S(2)}, u32[]{:S(2)}) collective-permute-start(bf16[2,32,512]{2,1,0:T(8,128)(2,1)} %bitcast.41), channel_id=1, source_target_pairs={{0,24},{2,26},{4,28},{6,30},{8,16},{10,18},{12,20},{14,22},{16,8},... | collective-permute-start | bytes 196616 | tf_op jit(solution)/shard_map/ppermute | solution.py:240
  10.2 7.0 %collective-permute-start.8 = (bf16[2,32,512]{2,1,0:T(8,128)(2,1)}, bf16[2,32,512]{2,1,0:T(8,128)(2,1)S(1)}, u32[]{:S(2)}, u32[]{:S(2)}) collective-permute-start(bf16[2,32,512]{2,1,0:T(8,128)(2,1)} %bitcast.42), channel_id=1, source_target_pairs={{0,16},{2,18},{4,20},{6,22},{8,24},{10,26},{12,28},{14,30},{16,0},... | collective-permute-start | bytes 196616 | tf_op jit(solution)/shard_map/ppermute | solution.py:240
  10.2 7.0 %collective-permute-start.7 = (bf16[2,32,512]{2,1,0:T(8,128)(2,1)}, bf16[2,32,512]{2,1,0:T(8,128)(2,1)S(1)}, u32[]{:S(2)}, u32[]{:S(2)}) collective-permute-start(bf16[2,32,512]{2,1,0:T(8,128)(2,1)} %bitcast.43), channel_id=1, source_target_pairs={{0,8},{2,10},{4,12},{6,14},{8,0},{10,2},{12,4},{14,6},{16,24},{18,... | collective-permute-start | bytes 196616 | tf_op jit(solution)/shard_map/ppermute | solution.py:240
  15.4 12.5 %collective-permute-start.4 = (bf16[4,2,32,512]{3,2,1,0:T(8,128)(2,1)S(1)}, bf16[4,2,32,512]{3,2,1,0:T(8,128)(2,1)S(1)}, u32[]{:S(2)}, u32[]{:S(2)}) collective-permute-start(bf16[4,2,32,512]{3,2,1,0:T(8,128)(2,1)S(1)} %pad_maximum_fusion.refs_2_), channel_id=1, source_target_pairs={{0,4},{2,6},{4,0},{6,2},{8,12},{10,14},{12,8},{14,10},{16,20},{18,... | collective-permute-start | bytes 786440 | tf_op jit(solution)/shard_map/ppermute | solution.py:240
  18.1 9.9 %collective-permute-start.10 = (bf16[4,2,32,512]{3,2,1,0:T(8,128)(2,1)S(1)}, bf16[4,2,32,512]{3,2,1,0:T(8,128)(2,1)S(1)}, u32[]{:S(2)}, u32[]{:S(2)}) collective-permute-start(bf16[4,2,32,512]{3,2,1,0:T(8,128)(2,1)S(1)} %pad_maximum_fusion.1.refs_0_), channel_id=1, source_target_pairs={{0,4},{2,6},{4,0},{6,2},{8,12},{10,14},{12,8},{14,10},{16,20},{18,... | collective-permute-start | bytes 786440 | tf_op jit(solution)/shard_map/ppermute | solution.py:240
  19.8 5.8 %collective-permute-start.17 = (bf16[1,32,512]{2,1,0:T(8,128)(2,1)S(1)}, bf16[1,32,512]{2,1,0:T(8,128)(2,1)S(1)}, u32[]{:S(2)}, u32[]{:S(2)}) collective-permute-start(bf16[1,32,512]{2,1,0:T(8,128)(2,1)S(1)} %get-tuple-element.35), channel_id=1, source_target_pairs={{0,24},{2,26},{4,28},{6,30},{8,16},{10,18},{12,20},{14,22},{16,8},... | collective-permute-start | bytes 98312 | tf_op jit(solution)/shard_map/ppermute | solution.py:240
  22.6 4.8 %collective-permute-start.16 = (bf16[1,32,512]{2,1,0:T(8,128)(2,1)S(1)}, bf16[1,32,512]{2,1,0:T(8,128)(2,1)S(1)}, u32[]{:S(2)}, u32[]{:S(2)}) collective-permute-start(bf16[1,32,512]{2,1,0:T(8,128)(2,1)S(1)} %get-tuple-element.35), channel_id=1, source_target_pairs={{0,16},{2,18},{4,20},{6,22},{8,24},{10,26},{12,28},{14,30},{16,0},... | collective-permute-start | bytes 98312 | tf_op jit(solution)/shard_map/ppermute | solution.py:240
  22.6 4.8 %collective-permute-start.15 = (bf16[1,32,512]{2,1,0:T(8,128)(2,1)S(1)}, bf16[1,32,512]{2,1,0:T(8,128)(2,1)S(1)}, u32[]{:S(2)}, u32[]{:S(2)}) collective-permute-start(bf16[1,32,512]{2,1,0:T(8,128)(2,1)S(1)} %get-tuple-element.35), channel_id=1, source_target_pairs={{0,8},{2,10},{4,12},{6,14},{8,0},{10,2},{12,4},{14,6},{16,24},{18,... | collective-permute-start | bytes 98312 | tf_op jit(solution)/shard_map/ppermute | solution.py:240
  25.6 5.2 %collective-permute-start = (bf16[128,512]{1,0:T(8,128)(2,1)}, bf16[128,512]{1,0:T(8,128)(2,1)S(1)}, u32[]{:S(2)}, u32[]{:S(2)}) collective-permute-start(bf16[128,512]{1,0:T(8,128)(2,1)} %refs_0_.1), channel_id=1, source_target_pairs={{0,1},{1,0},{2,3},{3,2},{4,5},{5,4},{6,7},{7,6},{8,9},{9,8},{10,11... | collective-permute-start | bytes 393224 | tf_op jit(solution)/shard_map/ppermute | solution.py:240
  27.4 8.3 %collective-permute-start.5 = (bf16[4,2,32,512]{3,2,1,0:T(8,128)(2,1)S(1)}, bf16[4,2,32,512]{3,2,1,0:T(8,128)(2,1)S(1)}, u32[]{:S(2)}, u32[]{:S(2)}) collective-permute-start(bf16[4,2,32,512]{3,2,1,0:T(8,128)(2,1)S(1)} %pad_maximum_fusion.refs_2_), channel_id=1, source_target_pairs={{0,2},{2,0},{4,6},{6,4},{8,10},{10,8},{12,14},{14,12},{16,18},{18,... | collective-permute-start | bytes 786440 | tf_op jit(solution)/shard_map/ppermute | solution.py:240
  27.4 13.3 %collective-permute-start.11 = (bf16[4,2,32,512]{3,2,1,0:T(8,128)(2,1)S(1)}, bf16[4,2,32,512]{3,2,1,0:T(8,128)(2,1)S(1)}, u32[]{:S(2)}, u32[]{:S(2)}) collective-permute-start(bf16[4,2,32,512]{3,2,1,0:T(8,128)(2,1)S(1)} %pad_maximum_fusion.1.refs_0_), channel_id=1, source_target_pairs={{0,2},{2,0},{4,6},{6,4},{8,10},{10,8},{12,14},{14,12},{16,18},{18,... | collective-permute-start | bytes 786440 | tf_op jit(solution)/shard_map/ppermute | solution.py:240
  27.9 8.4 %collective-permute-start.6 = (bf16[4,2,32,512]{3,2,1,0:T(8,128)(2,1)S(1)}, bf16[4,2,32,512]{3,2,1,0:T(8,128)(2,1)S(1)}, u32[]{:S(2)}, u32[]{:S(2)}) collective-permute-start(bf16[4,2,32,512]{3,2,1,0:T(8,128)(2,1)S(1)} %collective-permute-done.4.refs_3_), channel_id=1, source_target_pairs={{0,2},{2,0},{4,6},{6,4},{8,10},{10,8},{12,14},{14,12},{16,18},{18,... | collective-permute-start | bytes 786440 | tf_op jit(solution)/shard_map/ppermute | solution.py:240
  28.0 12.7 %collective-permute-start.12 = (bf16[4,2,32,512]{3,2,1,0:T(8,128)(2,1)S(1)}, bf16[4,2,32,512]{3,2,1,0:T(8,128)(2,1)S(1)}, u32[]{:S(2)}, u32[]{:S(2)}) collective-permute-start(bf16[4,2,32,512]{3,2,1,0:T(8,128)(2,1)S(1)} %collective-permute-done.10.refs_1_), channel_id=1, source_target_pairs={{0,2},{2,0},{4,6},{6,4},{8,10},{10,8},{12,14},{14,12},{16,18},{18,... | collective-permute-start | bytes 786440 | tf_op jit(solution)/shard_map/ppermute | solution.py:240
  30.7 5.0 %collective-permute-start.18 = (bf16[4,1,32,512]{3,2,1,0:T(8,128)(2,1)S(1)}, bf16[4,1,32,512]{3,2,1,0:T(8,128)(2,1)S(1)}, u32[]{:S(2)}, u32[]{:S(2)}) collective-permute-start(bf16[4,1,32,512]{3,2,1,0:T(8,128)(2,1)S(1)} %pad_maximum_fusion.2.refs_0_), channel_id=1, source_target_pairs={{0,4},{2,6},{4,0},{6,2},{8,12},{10,14},{12,8},{14,10},{16,20},{18,... | collective-permute-start | bytes 393224 | tf_op jit(solution)/shard_map/ppermute | solution.py:240
  35.7 9.6 %collective-permute-start.19 = (bf16[4,1,32,512]{3,2,1,0:T(8,128)(2,1)S(1)}, bf16[4,1,32,512]{3,2,1,0:T(8,128)(2,1)S(1)}, u32[]{:S(2)}, u32[]{:S(2)}) collective-permute-start(bf16[4,1,32,512]{3,2,1,0:T(8,128)(2,1)S(1)} %pad_maximum_fusion.2.refs_0_), channel_id=1, source_target_pairs={{0,2},{2,0},{4,6},{6,4},{8,10},{10,8},{12,14},{14,12},{16,18},{18,... | collective-permute-start | bytes 393224 | tf_op jit(solution)/shard_map/ppermute | solution.py:240
  35.7 9.6 %collective-permute-start.20 = (bf16[4,1,32,512]{3,2,1,0:T(8,128)(2,1)S(1)}, bf16[4,1,32,512]{3,2,1,0:T(8,128)(2,1)S(1)}, u32[]{:S(2)}, u32[]{:S(2)}) collective-permute-start(bf16[4,1,32,512]{3,2,1,0:T(8,128)(2,1)S(1)} %collective-permute-done.18.refs_1_), channel_id=1, source_target_pairs={{0,2},{2,0},{4,6},{6,4},{8,10},{10,8},{12,14},{14,12},{16,18},{18,... | collective-permute-start | bytes 393224 | tf_op jit(solution)/shard_map/ppermute | solution.py:240
  40.7 4.6 %copy-start.2 = (bf16[480]{0:T(512)(128)(2,1)S(1)}, bf16[480]{0:T(512)(128)(2,1)}, u32[]{:S(2)}) copy-start(bf16[480]{0:T(512)(128)(2,1)} %param.12) | copy-start | bytes 2884
  40.7 5.1 %copy-start.1 = (bf16[64,480]{1,0:T(8,128)(2,1)S(1)}, bf16[64,480]{1,0:T(8,128)(2,1)}, u32[]{:S(2)}) copy-start(bf16[64,480]{1,0:T(8,128)(2,1)} %refs_2_.1) | copy-start | bytes 184324
  44.5 1.3 %collective-permute-start.13 = (bf16[64,512]{1,0:T(8,128)(2,1)S(1)}, bf16[64,512]{1,0:T(8,128)(2,1)S(1)}, u32[]{:S(2)}, u32[]{:S(2)}) collective-permute-start(bf16[64,512]{1,0:T(8,128)(2,1)S(1)} %get-tuple-element.17.normed.refs_3_), channel_id=1, source_target_pairs={{0,2},{2,0},{4,6},{6,4},{8,10},{10,8},{12,14},{14,12},{16,18},{18,... | collective-permute-start | bytes 196616 | tf_op jit(solution)/shard_map/ppermute | solution.py:240
  44.6 1.2 %collective-permute-start.14 = (bf16[64,512]{1,0:T(8,128)(2,1)S(1)}, bf16[64,512]{1,0:T(8,128)(2,1)S(1)}, u32[]{:S(2)}, u32[]{:S(2)}) collective-permute-start(bf16[64,512]{1,0:T(8,128)(2,1)S(1)} %get-tuple-element.17.normed.refs_3_), channel_id=1, source_target_pairs={{2,4},{6,8},{10,12},{14,16},{18,20},{22,24},{26,28},{4,2},{8,6},{1... | collective-permute-start | bytes 196616 | tf_op jit(solution)/shard_map/ppermute | solution.py:269
  53.9 5.7 %collective-permute-start.21 = (bf16[64,480]{1,0:T(8,128)(2,1)S(1)}, bf16[64,480]{1,0:T(8,128)(2,1)S(1)}, u32[]{:S(2)}, u32[]{:S(2)}) collective-permute-start(bf16[64,480]{1,0:T(8,128)(2,1)S(1)} %get-tuple-element.22.slope_rev), channel_id=1, source_target_pairs={{0,2},{2,0},{4,6},{6,4},{8,10},{10,8},{12,14},{14,12},{16,18},{18,... | collective-permute-start | bytes 184328 | tf_op jit(solution)/shard_map/ppermute | solution.py:240
  58.7 0.9 collective-permute-start.22
  67.4 8.8 %collective-permute-start.24 = (bf16[8,32,480]{2,1,0:T(8,128)(2,1)S(1)}, bf16[8,32,480]{2,1,0:T(8,128)(2,1)S(1)}, u32[]{:S(2)}, u32[]{:S(2)}) collective-permute-start(bf16[8,32,480]{2,1,0:T(8,128)(2,1)S(1)} %get-tuple-element.28), channel_id=1, source_target_pairs={{0,2},{2,0},{4,6},{6,4},{8,10},{10,8},{12,14},{14,12},{16,18},{18,... | collective-permute-start | bytes 737288 | tf_op jit(solution)/shard_map/ppermute | solution.py:240
  72.1 3.9 %collective-permute-start.23 = (bf16[32,512]{1,0:T(8,128)(2,1)S(1)}, bf16[32,512]{1,0:T(8,128)(2,1)S(1)}, u32[]{:S(2)}, u32[]{:S(2)}) collective-permute-start(bf16[32,512]{1,0:T(8,128)(2,1)S(1)} %bitcast.34), channel_id=1, source_target_pairs={{0,1},{1,0},{2,3},{3,2},{4,5},{5,4},{6,7},{7,6},{8,9},{9,8},{10,11... | collective-permute-start | bytes 98312 | tf_op jit(solution)/shard_map/ppermute | solution.py:240
  76.2 5.3 %collective-permute-start.25 = (bf16[4,32,480]{2,1,0:T(8,128)(2,1)S(1)}, bf16[4,32,480]{2,1,0:T(8,128)(2,1)S(1)}, u32[]{:S(2)}, u32[]{:S(2)}) collective-permute-start(bf16[4,32,480]{2,1,0:T(8,128)(2,1)S(1)} %slice.29), channel_id=1, source_target_pairs={{0,4},{2,6},{4,0},{6,2},{8,12},{10,14},{12,8},{14,10},{16,20},{18,... | collective-permute-start | bytes 368648 | tf_op jit(solution)/shard_map/ppermute | solution.py:240
  81.6 6.3 %collective-permute-start.28 = (bf16[32,480]{1,0:T(8,128)(2,1)S(1)}, bf16[32,480]{1,0:T(8,128)(2,1)S(1)}, u32[]{:S(2)}, u32[]{:S(2)}) collective-permute-start(bf16[32,480]{1,0:T(8,128)(2,1)S(1)} %get-tuple-element.32), channel_id=1, source_target_pairs={{0,24},{2,26},{4,28},{6,30},{8,16},{10,18},{12,20},{14,22},{16,8},... | collective-permute-start | bytes 92168 | tf_op jit(solution)/shard_map/ppermute | solution.py:240
  85.9 4.8 %collective-permute-start.27 = (bf16[32,480]{1,0:T(8,128)(2,1)S(1)}, bf16[32,480]{1,0:T(8,128)(2,1)S(1)}, u32[]{:S(2)}, u32[]{:S(2)}) collective-permute-start(bf16[32,480]{1,0:T(8,128)(2,1)S(1)} %get-tuple-element.33), channel_id=1, source_target_pairs={{0,16},{2,18},{4,20},{6,22},{8,24},{10,26},{12,28},{14,30},{16,0},... | collective-permute-start | bytes 92168 | tf_op jit(solution)/shard_map/ppermute | solution.py:240
  85.9 4.8 %collective-permute-start.26 = (bf16[32,480]{1,0:T(8,128)(2,1)S(1)}, bf16[32,480]{1,0:T(8,128)(2,1)S(1)}, u32[]{:S(2)}, u32[]{:S(2)}) collective-permute-start(bf16[32,480]{1,0:T(8,128)(2,1)S(1)} %get-tuple-element.31), channel_id=1, source_target_pairs={{0,8},{2,10},{4,12},{6,14},{8,0},{10,2},{12,4},{14,6},{16,24},{18,... | collective-permute-start | bytes 92168 | tf_op jit(solution)/shard_map/ppermute | solution.py:240

commit v5 on v4

--- a/solution.py
+++ b/solution.py
@@ -136,10 +136,14 @@
     return total
 
 
-def conv(weights, turned, first, wrap, acc):
+def conv(weights, turned, first, wrap, acc, copies=()):
     rows, width = acc.shape[1:]
     start = 0
     for held in weights:
+        if held is weights[-1]:
+            for copy in copies:
+                copy.wait()
+
         def step(g, carry):
             group = held.at[g]
             if turned is not None:
@@ -154,11 +158,16 @@
     return jnp.concatenate([acc[g] for g in range(acc.shape[0])], 1)
 
 
-def forward_body(where, normed, got_a, got_b, *refs, layout, held):
+def forward_body(where, normed, got_a, got_b, *refs, layout, held, late):
     stacks, refs = refs[: len(layout)], refs[len(layout) :]
-    weights, refs = refs[:held], refs[held:]
-    cot, bias, encoded, slope_rev, proj, full = refs[:6]
-    first, wrap, acc = refs[6:]
+    weights, refs = list(refs[:held]), refs[held:]
+    copies = []
+    if late:
+        w_any, cot, bias, encoded, slope_rev, proj, w_out, full, first, wrap, acc, sems = refs
+        copies = tap_copies(w_any, w_out, sems, acc.shape[0] - late)
+        weights.append(w_out)
+    else:
+        cot, bias, encoded, slope_rev, proj, full, first, wrap, acc = refs
     place_shards(where[0], layout, stacks, 0, 1, full)
     proj[...] = full[0, :, : proj.shape[1]]
     odd = where[0] % 2 == 1
@@ -173,7 +182,7 @@
     for c in range(chunks):
         first[...] = jnp.concatenate([part(c), part(c + 1)], 0).T
         wrap[...] = jnp.concatenate([part(c + 2), part(c + 1)], 0).T
-        pos = conv(weights, None, first, wrap, acc)
+        pos = conv(weights, None, first, wrap, acc, copies if c == 0 else ())
         pos = pos + bias[...].astype(F32)
         cdf = phi_cdf(pos)
         here = slice(c * rows, (c + 1) * rows)
@@ -267,7 +276,8 @@
     to_b = tail if tail is head else jnp.where(parity == 0, head, tail)
     pairs = [(2 * i + 1, 2 * i + 2) for i in range(count // 2 - 1)]
     got_b = lax.ppermute(to_b, "tm", pairs + [(b, a) for a, b in pairs])
-    return swap(to_a, "tm", 1), got_b
+    got_a = swap(to_a, "tm", 1)
+    return got_a, got_b
 
 
 def on_device(features, weight_five, weight_six, projection, pos_weight, pos_bias, cotangent):
@@ -295,7 +305,7 @@
     common = dict(layout=layout)
     taps_scratch = [pltpu.VMEM((2, channels, channels), BF16)]
 
-    cut = (groups + 1) // 2
+    cut = 1
     tap_sems = lambda count: pltpu.SemaphoreType.DMA((count, 5))
     act_five, w_low = pl.pallas_call(
         functools.partial(five_body, count=slots, **common),
@@ -310,7 +320,8 @@
         compiler_params=PARAMS,
         name="five",
     )(where, in_hbm(blocks[0]), *on_chip(blocks[1:] + five), w_taps)
-    rest = groups - cut
+    rest = min(1, groups - cut)
+    late = groups - cut - rest
     results = pl.pallas_call(
         functools.partial(six_body, count=slots, start=cut if rest else None, **common),
         in_specs=[SMEM_SPEC] + vmem_specs(1 + len(six)) + ([HBM_SPEC] if rest else []),
@@ -337,19 +348,30 @@
         pltpu.VMEM((columns, taps), F32),
         pltpu.VMEM((groups, half, width), F32),
     ]
-    encoded, slope_rev, proj = pl.pallas_call(
-        functools.partial(forward_body, held=len(weights), **common),
-        in_specs=[SMEM_SPEC] + vmem_specs(3 + len(last) + len(weights) + 2),
-        out_specs=vmem_specs(3),
+    results = pl.pallas_call(
+        functools.partial(forward_body, held=len(weights), late=late, **common),
+        in_specs=[SMEM_SPEC]
+        + vmem_specs(3 + len(last) + len(weights))
+        + ([HBM_SPEC] if late else [])
+        + vmem_specs(2),
+        out_specs=vmem_specs(4 if late else 3),
         out_shape=[
             jax.ShapeDtypeStruct((block, columns), BF16),
             pltpu.VMEM((block, columns), BF16),
             pltpu.VMEM((channels, columns), BF16),
-        ],
-        scratch_shapes=[pltpu.VMEM((1, channels, channels), BF16)] + conv_scratch,
+        ]
+        + ([pltpu.VMEM((late, width, width, taps), BF16)] if late else []),
+        scratch_shapes=[pltpu.VMEM((1, channels, channels), BF16)]
+        + conv_scratch
+        + ([tap_sems(late)] if late else []),
         compiler_params=CONV_PARAMS,
         name="forward",
-    )(where, normed, *on_chip([got_a, got_b] + last), *weights, cotangent, bias)
+    )(
+        where, normed, *on_chip([got_a, got_b] + last), *weights,
+        *([w_taps] if late else []), cotangent, bias,
+    )
+    encoded, slope_rev, proj = results[:3]
+    weights = weights + list(results[3:])
 
     tail = slope_rev if whole else slope_rev[block - half :]
     head = slope_rev if whole else slope_rev[:half]

time: 91.6 us -> 91.6 us (level)
    pallas_call x1, Pallas kernels: 8.04 us -> 10.3 us  [on_device(): pl.pallas_call(functools.partial(forward_body, held=len(weights), late=la...]
    pallas_call x1, Pallas kernels: 3.8 us -> 2.67 us  [on_device(): pl.pallas_call(functools.partial(six_body, count=slots, start=cut if rest...]
    ppermute x27, waiting for transfers between devices: 21.7 us -> 20.8 us  [swap(): return lax.ppermute(values, axis, [(i, i ^ mask) for i in range(count)])]
    pallas_call x1, Pallas kernels: 4.34 us -> 3.41 us  [on_device(): pl.pallas_call(functools.partial(five_body, count=slots, **common), in_sp...]
  transfers between devices with their start and end apart: 29 -> 29, of which waited for: 12 -> 10; matrix products, arithmetic and copies ran while one was open for 3% -> 3% of each run, Pallas kernels for 9% -> 7%
where the time goes in v5:
time: 91.6 us; the launch traced here: 91.3 us
  starting transfers between devices  41.6 us (45%)
  Pallas kernels  24.5 us (27%)
  waiting for transfers between devices  20.8 us (23%)
  other arithmetic  3.41 us (4%)
    ppermute x27, starting transfers between devices, swap(): return lax.ppermute(values, axis, [(i, i ^ mask) for i in range(count)])  40.2 us
    ppermute x27, waiting for transfers between devices, swap(): return lax.ppermute(values, axis, [(i, i ^ mask) for i in range(count)])  20.8 us
    pallas_call x1, Pallas kernels, on_device(): pl.pallas_call(functools.partial(forward_body, held=len(weights), late=la...  10.3 us
    pallas_call x1, Pallas kernels, on_device(): pl.pallas_call(functools.partial(backward_body, scale=scale, order=order,...  8.08 us
    pallas_call x1, Pallas kernels, on_device(): pl.pallas_call(functools.partial(five_body, count=slots, **common), in_sp...  3.41 us
    pallas_call x1, Pallas kernels, on_device(): pl.pallas_call(functools.partial(six_body, count=slots, start=cut if rest...  2.67 us
  transfers between devices with their start and end apart: 29, of which 10 were waited for; matrix products, arithmetic and copies ran while one was open for 3% of the time, Pallas kernels for 7%

profile of v5, /device:TPU:0, one launch (start us, length us, event | category | flops | bytes accessed | tf_op | source)
XLA Modules:
  0.0 91.3 jit_solution(446103185822413349)
XLA Ops:
  0.6 4.1 %collective-permute-start.8 = (bf16[2,32,512]{2,1,0:T(8,128)(2,1)}, bf16[2,32,512]{2,1,0:T(8,128)(2,1)S(1)}, u32[]{:S(2)}, u32[]{:S(2)}) collective-permute-start(bf16[2,32,512]{2,1,0:T(8,128)(2,1)} %bitcast.38), channel_id=1, source_target_pairs={{0,16},{2,18},{4,20},{6,22},{8,24},{10,26},{12,28},{14,30},{16,0},... | collective-permute-start | bytes 196616 | tf_op jit(solution)/shard_map/ppermute | solution.py:249
  4.8 1.6 %collective-permute-start.7 = (bf16[2,32,512]{2,1,0:T(8,128)(2,1)}, bf16[2,32,512]{2,1,0:T(8,128)(2,1)S(1)}, u32[]{:S(2)}, u32[]{:S(2)}) collective-permute-start(bf16[2,32,512]{2,1,0:T(8,128)(2,1)} %bitcast.39), channel_id=1, source_target_pairs={{0,8},{2,10},{4,12},{6,14},{8,0},{10,2},{12,4},{14,6},{16,24},{18,... | collective-permute-start | bytes 196616 | tf_op jit(solution)/shard_map/ppermute | solution.py:249
  6.4 1.9 %collective-permute-start.2 = (bf16[2,32,512]{2,1,0:T(8,128)(2,1)}, bf16[2,32,512]{2,1,0:T(8,128)(2,1)S(1)}, u32[]{:S(2)}, u32[]{:S(2)}) collective-permute-start(bf16[2,32,512]{2,1,0:T(8,128)(2,1)} %bitcast.42), channel_id=1, source_target_pairs={{0,16},{2,18},{4,20},{6,22},{8,24},{10,26},{12,28},{14,30},{16,0},... | collective-permute-start | bytes 196616 | tf_op jit(solution)/shard_map/ppermute | solution.py:249
  8.3 2.5 %collective-permute-start.1 = (bf16[2,32,512]{2,1,0:T(8,128)(2,1)}, bf16[2,32,512]{2,1,0:T(8,128)(2,1)S(1)}, u32[]{:S(2)}, u32[]{:S(2)}) collective-permute-start(bf16[2,32,512]{2,1,0:T(8,128)(2,1)} %bitcast.43), channel_id=1, source_target_pairs={{0,8},{2,10},{4,12},{6,14},{8,0},{10,2},{12,4},{14,6},{16,24},{18,... | collective-permute-start | bytes 196616 | tf_op jit(solution)/shard_map/ppermute | solution.py:249
  10.7 2.6 %collective-permute-start.3 = (bf16[2,32,512]{2,1,0:T(8,128)(2,1)}, bf16[2,32,512]{2,1,0:T(8,128)(2,1)S(1)}, u32[]{:S(2)}, u32[]{:S(2)}) collective-permute-start(bf16[2,32,512]{2,1,0:T(8,128)(2,1)} %bitcast.44), channel_id=1, source_target_pairs={{0,24},{2,26},{4,28},{6,30},{8,16},{10,18},{12,20},{14,22},{16,8},... | collective-permute-start | bytes 196616 | tf_op jit(solution)/shard_map/ppermute | solution.py:249
  13.3 0.9 pad_maximum_fusion.1.refs_0_
  14.2 1.6 %collective-permute-start.10 = (bf16[4,2,32,512]{3,2,1,0:T(8,128)(2,1)S(1)}, bf16[4,2,32,512]{3,2,1,0:T(8,128)(2,1)S(1)}, u32[]{:S(2)}, u32[]{:S(2)}) collective-permute-start(bf16[4,2,32,512]{3,2,1,0:T(8,128)(2,1)S(1)} %pad_maximum_fusion.1.refs_0_), channel_id=1, source_target_pairs={{0,4},{2,6},{4,0},{6,2},{8,12},{10,14},{12,8},{14,10},{16,20},{18,... | collective-permute-start | bytes 786440 | tf_op jit(solution)/shard_map/ppermute | solution.py:249
  15.8 1.3 %collective-permute-done.3 = bf16[2,32,512]{2,1,0:T(8,128)(2,1)S(1)} collective-permute-done((bf16[2,32,512]{2,1,0:T(8,128)(2,1)}, bf16[2,32,512]{2,1,0:T(8,128)(2,1)S(1)}, u32[]{:S(2)}, u32[]{:S(2)}) %collective-permute-start.3) | collective-permute-done | bytes 65568 | tf_op jit(solution)/shard_map/ppermute | solution.py:249
  17.1 0.9 pad_maximum_fusion.refs_2_
  18.0 1.6 %collective-permute-start.4 = (bf16[4,2,32,512]{3,2,1,0:T(8,128)(2,1)S(1)}, bf16[4,2,32,512]{3,2,1,0:T(8,128)(2,1)S(1)}, u32[]{:S(2)}, u32[]{:S(2)}) collective-permute-start(bf16[4,2,32,512]{3,2,1,0:T(8,128)(2,1)S(1)} %pad_maximum_fusion.refs_2_), channel_id=1, source_target_pairs={{0,4},{2,6},{4,0},{6,2},{8,12},{10,14},{12,8},{14,10},{16,20},{18,... | collective-permute-start | bytes 786440 | tf_op jit(solution)/shard_map/ppermute | solution.py:249
  19.6 0.1 constant_dynamic-slice_fusion
  19.7 2.6 %collective-permute-start.17 = (bf16[1,32,512]{2,1,0:T(8,128)(2,1)S(1)}, bf16[1,32,512]{2,1,0:T(8,128)(2,1)S(1)}, u32[]{:S(2)}, u32[]{:S(2)}) collective-permute-start(bf16[1,32,512]{2,1,0:T(8,128)(2,1)S(1)} %get-tuple-element.37), channel_id=1, source_target_pairs={{0,24},{2,26},{4,28},{6,30},{8,16},{10,18},{12,20},{14,22},{16,8},... | collective-permute-start | bytes 98312 | tf_op jit(solution)/shard_map/ppermute | solution.py:249
  22.3 1.8 %collective-permute-start.15 = (bf16[1,32,512]{2,1,0:T(8,128)(2,1)S(1)}, bf16[1,32,512]{2,1,0:T(8,128)(2,1)S(1)}, u32[]{:S(2)}, u32[]{:S(2)}) collective-permute-start(bf16[1,32,512]{2,1,0:T(8,128)(2,1)S(1)} %get-tuple-element.37), channel_id=1, source_target_pairs={{0,8},{2,10},{4,12},{6,14},{8,0},{10,2},{12,4},{14,6},{16,24},{18,... | collective-permute-start | bytes 98312 | tf_op jit(solution)/shard_map/ppermute | solution.py:249
  24.1 1.7 %collective-permute-done.17 = bf16[1,32,512]{2,1,0:T(8,128)(2,1)S(1)} collective-permute-done((bf16[1,32,512]{2,1,0:T(8,128)(2,1)S(1)}, bf16[1,32,512]{2,1,0:T(8,128)(2,1)S(1)}, u32[]{:S(2)}, u32[]{:S(2)}) %collective-permute-start.17) | collective-permute-done | bytes 32800 | tf_op jit(solution)/shard_map/ppermute | solution.py:249
  25.8 1.5 %collective-permute-start = (bf16[128,512]{1,0:T(8,128)(2,1)}, bf16[128,512]{1,0:T(8,128)(2,1)S(1)}, u32[]{:S(2)}, u32[]{:S(2)}) collective-permute-start(bf16[128,512]{1,0:T(8,128)(2,1)} %refs_0_.1), channel_id=1, source_target_pairs={{0,1},{1,0},{2,3},{3,2},{4,5},{5,4},{6,7},{7,6},{8,9},{9,8},{10,11... | collective-permute-start | bytes 393224 | tf_op jit(solution)/shard_map/ppermute | solution.py:249
  27.3 0.5 collective-permute-start.11
  27.9 0.1 collective-permute-start.12
  27.9 0.4 collective-permute-start.6
  28.4 2.6 %collective-permute-done.refs_1_ = bf16[128,512]{1,0:T(8,128)(2,1)S(1)} collective-permute-done((bf16[128,512]{1,0:T(8,128)(2,1)}, bf16[128,512]{1,0:T(8,128)(2,1)S(1)}, u32[]{:S(2)}, u32[]{:S(2)}) %collective-permute-start) | collective-permute-done | bytes 131104 | tf_op jit(solution)/shard_map/ppermute | solution.py:249
  31.0 0.5 collective-permute-start.18
  31.5 4.5 %collective-permute-done.18.refs_1_ = bf16[4,1,32,512]{3,2,1,0:T(8,128)(2,1)S(1)} collective-permute-done((bf16[4,1,32,512]{3,2,1,0:T(8,128)(2,1)S(1)}, bf16[4,1,32,512]{3,2,1,0:T(8,128)(2,1)S(1)}, u32[]{:S(2)}, u32[]{:S(2)}) %collective-permute-start.18) | collective-permute-done | bytes 131104 | tf_op jit(solution)/shard_map/ppermute | solution.py:249
  36.0 0.5 collective-permute-start.20
  36.5 0.1 pad_add_fusion.where
  36.5 3.4 %five.1 = (bf16[128,512]{1,0:T(8,128)(2,1)S(1)}, bf16[1,120,120,128]{3,2,1,0:T(8,128)(2,1)S(1)}) custom-call(s32[2]{0:T(128)S(1)} %pad_add_fusion.where, bf16[128,512]{1,0:T(8,128)(2,1)} %refs_0_.1, bf16[128,512]{1,0:T(8,128)(2,1)S(1)} %collective-permute-done.refs_1_, bf16[4,2,32,512]{3,2,1,0:T(8,128)(2,1)S(1)} %pad_maximum_fusion.refs_2_, ...), custom_call_target="tpu_custom_call" | custom-call | tf_op jit(solution)/shard_map/five/pallas_call | solution.py:310
  40.0 2.7 %six.1 = (bf16[64,512]{1,0:T(8,128)(2,1)S(1)}, f32[32,512]{1,0:T(8,128)S(1)}, f32[32,128]{1,0:T(8,128)S(1)}, bf16[1,120,120,128]{3,2,1,0:T(8,128)(2,1)S(1)}) custom-call(s32[2]{0:T(128)S(1)} %pad_add_fusion.where, bf16[128,512]{1,0:T(8,128)(2,1)S(1)} %get-tuple-element.17.act, bf16[4,2,32,512]{3,2,1,0:T(8,128)(2,1)S(1)} %pad_maximum_fusion.1.refs_0_, ...), custom_call_target="tpu_custom_call" | custom-call | tf_op jit(solution)/shard_map/six/pallas_call | solution.py:325
  42.7 0.7 collective-permute-start.14
  43.4 1.9 %collective-permute-start.13 = (bf16[64,512]{1,0:T(8,128)(2,1)S(1)}, bf16[64,512]{1,0:T(8,128)(2,1)S(1)}, u32[]{:S(2)}, u32[]{:S(2)}) collective-permute-start(bf16[64,512]{1,0:T(8,128)(2,1)S(1)} %get-tuple-element.18.normed.refs_4_), channel_id=1, source_target_pairs={{0,2},{2,0},{4,6},{6,4},{8,10},{10,8},{12,14},{14,12},{16,18},{18,... | collective-permute-start | bytes 196616 | tf_op jit(solution)/shard_map/ppermute | solution.py:249
  45.3 0.9 collective-permute-done.13.got_a
  46.2 10.3 %forward.1 = (bf16[64,480]{1,0:T(8,128)(2,1)}, bf16[64,480]{1,0:T(8,128)(2,1)S(1)}, bf16[512,480]{1,0:T(8,128)(2,1)S(1)}, bf16[2,120,120,128]{3,2,1,0:T(8,128)(2,1)S(1)}) custom-call(s32[2]{0:T(128)S(1)} %pad_add_fusion.where, bf16[64,512]{1,0:T(8,128)(2,1)S(1)} %get-tuple-element.18.normed.refs_4_, bf16[64,512]{1,0:T(8,128)(2,1)S(1)} %collective-permute-done.13.got_a, ...), custom_call_target="tpu_custom_call" | custom-call | tf_op jit(solution)/shard_map/forward/pallas_call | solution.py:351
  56.5 0.7 collective-permute-start.22
  57.2 4.0 %collective-permute-start.21 = (bf16[64,480]{1,0:T(8,128)(2,1)S(1)}, bf16[64,480]{1,0:T(8,128)(2,1)S(1)}, u32[]{:S(2)}, u32[]{:S(2)}) collective-permute-start(bf16[64,480]{1,0:T(8,128)(2,1)S(1)} %get-tuple-element.23.slope_rev), channel_id=1, source_target_pairs={{0,2},{2,0},{4,6},{6,4},{8,10},{10,8},{12,14},{14,12},{16,18},{18,... | collective-permute-start | bytes 184328 | tf_op jit(solution)/shard_map/ppermute | solution.py:249
  61.2 0.9 collective-permute-done.21.got_a
  62.1 8.1 %backward.1 = (bf16[8,32,480]{2,1,0:T(8,128)(2,1)S(1)}, bf16[8,32,480]{2,1,0:T(8,128)(2,1)S(1)}, f32[32,512]{1,0:T(8,128)S(1)}, bf16[1,32,512]{2,1,0:T(8,128)(2,1)S(1)}) custom-call(s32[2]{0:T(128)S(1)} %pad_add_fusion.where, bf16[64,480]{1,0:T(8,128)(2,1)S(1)} %get-tuple-element.23.slope_rev, bf16[64,480]{1,0:T(8,128)(2,1)S(1)} %collective-permute-done.21.got_a, ...), custom_call_target="tpu_custom_call" | custom-call | tf_op jit(solution)/shard_map/backward/pallas_call | solution.py:389
  70.2 2.1 %collective-permute-start.24 = (bf16[8,32,480]{2,1,0:T(8,128)(2,1)S(1)}, bf16[8,32,480]{2,1,0:T(8,128)(2,1)S(1)}, u32[]{:S(2)}, u32[]{:S(2)}) collective-permute-start(bf16[8,32,480]{2,1,0:T(8,128)(2,1)S(1)} %get-tuple-element.30), channel_id=1, source_target_pairs={{0,2},{2,0},{4,6},{6,4},{8,10},{10,8},{12,14},{14,12},{16,18},{18,... | collective-permute-start | bytes 737288 | tf_op jit(solution)/shard_map/ppermute | solution.py:249
  72.3 1.5 %collective-permute-start.23 = (bf16[32,512]{1,0:T(8,128)(2,1)S(1)}, bf16[32,512]{1,0:T(8,128)(2,1)S(1)}, u32[]{:S(2)}, u32[]{:S(2)}) collective-permute-start(bf16[32,512]{1,0:T(8,128)(2,1)S(1)} %bitcast.34), channel_id=1, source_target_pairs={{0,1},{1,0},{2,3},{3,2},{4,5},{5,4},{6,7},{7,6},{8,9},{9,8},{10,11... | collective-permute-start | bytes 98312 | tf_op jit(solution)/shard_map/ppermute | solution.py:249
  73.9 0.1 slice_reduce_fusion
  74.0 2.3 %collective-permute-done.23 = bf16[32,512]{1,0:T(8,128)(2,1)S(1)} collective-permute-done((bf16[32,512]{1,0:T(8,128)(2,1)S(1)}, bf16[32,512]{1,0:T(8,128)(2,1)S(1)}, u32[]{:S(2)}, u32[]{:S(2)}) %collective-permute-start.23) | collective-permute-done | bytes 32800 | tf_op jit(solution)/shard_map/ppermute | solution.py:249
  76.3 0.1 fusion
  76.4 0.1 add_convert_fusion
  76.5 2.4 %collective-permute-start.25 = (bf16[4,32,480]{2,1,0:T(8,128)(2,1)S(1)}, bf16[4,32,480]{2,1,0:T(8,128)(2,1)S(1)}, u32[]{:S(2)}, u32[]{:S(2)}) collective-permute-start(bf16[4,32,480]{2,1,0:T(8,128)(2,1)S(1)} %slice.29), channel_id=1, source_target_pairs={{0,4},{2,6},{4,0},{6,2},{8,12},{10,14},{12,8},{14,10},{16,20},{18,... | collective-permute-start | bytes 368648 | tf_op jit(solution)/shard_map/ppermute | solution.py:249
  78.9 2.9 %collective-permute-done.25 = bf16[4,32,480]{2,1,0:T(8,128)(2,1)S(1)} collective-permute-done((bf16[4,32,480]{2,1,0:T(8,128)(2,1)S(1)}, bf16[4,32,480]{2,1,0:T(8,128)(2,1)S(1)}, u32[]{:S(2)}, u32[]{:S(2)}) %collective-permute-start.25) | collective-permute-done | bytes 122912 | tf_op jit(solution)/shard_map/ppermute | solution.py:249
  81.9 0.7 collective-permute-start.26
  82.6 3.3 %collective-permute-start.28 = (bf16[32,480]{1,0:T(8,128)(2,1)S(1)}, bf16[32,480]{1,0:T(8,128)(2,1)S(1)}, u32[]{:S(2)}, u32[]{:S(2)}) collective-permute-start(bf16[32,480]{1,0:T(8,128)(2,1)S(1)} %get-tuple-element.34), channel_id=1, source_target_pairs={{0,24},{2,26},{4,28},{6,30},{8,16},{10,18},{12,20},{14,22},{16,8},... | collective-permute-start | bytes 92168 | tf_op jit(solution)/shard_map/ppermute | solution.py:249
  85.8 0.5 collective-permute-start.27
  86.3 0.7 multiply_convert_fusion
  87.0 1.4 %collective-permute-done.28 = bf16[32,480]{1,0:T(8,128)(2,1)S(1)} collective-permute-done((bf16[32,480]{1,0:T(8,128)(2,1)S(1)}, bf16[32,480]{1,0:T(8,128)(2,1)S(1)}, u32[]{:S(2)}, u32[]{:S(2)}) %collective-permute-start.28) | collective-permute-done | bytes 30752 | tf_op jit(solution)/shard_map/ppermute | solution.py:249
  88.4 2.2 %collective-permute-done.27 = bf16[32,480]{1,0:T(8,128)(2,1)S(1)} collective-permute-done((bf16[32,480]{1,0:T(8,128)(2,1)S(1)}, bf16[32,480]{1,0:T(8,128)(2,1)S(1)}, u32[]{:S(2)}, u32[]{:S(2)}) %collective-permute-start.27) | collective-permute-done | bytes 30752 | tf_op jit(solution)/shard_map/ppermute | solution.py:249
  90.6 0.6 convert_add_fusion
  (36 shorter events, 0.2 us)
Async XLA Ops:
  0.6 19.0 %copy-start = (bf16[32,960]{1,0:T(8,128)(2,1)S(1)}, bf16[32,960]{1,0:T(8,128)(2,1)}, u32[]{:S(2)}) copy-start(bf16[32,960]{1,0:T(8,128)(2,1)} %param.10) | copy-start | bytes 184324
  0.6 10.1 %collective-permute-start.8 = (bf16[2,32,512]{2,1,0:T(8,128)(2,1)}, bf16[2,32,512]{2,1,0:T(8,128)(2,1)S(1)}, u32[]{:S(2)}, u32[]{:S(2)}) collective-permute-start(bf16[2,32,512]{2,1,0:T(8,128)(2,1)} %bitcast.38), channel_id=1, source_target_pairs={{0,16},{2,18},{4,20},{6,22},{8,24},{10,26},{12,28},{14,30},{16,0},... | collective-permute-start | bytes 196616 | tf_op jit(solution)/shard_map/ppermute | solution.py:249
  4.8 8.5 %collective-permute-start.7 = (bf16[2,32,512]{2,1,0:T(8,128)(2,1)}, bf16[2,32,512]{2,1,0:T(8,128)(2,1)S(1)}, u32[]{:S(2)}, u32[]{:S(2)}) collective-permute-start(bf16[2,32,512]{2,1,0:T(8,128)(2,1)} %bitcast.39), channel_id=1, source_target_pairs={{0,8},{2,10},{4,12},{6,14},{8,0},{10,2},{12,4},{14,6},{16,24},{18,... | collective-permute-start | bytes 196616 | tf_op jit(solution)/shard_map/ppermute | solution.py:249
  6.4 7.0 %collective-permute-start.9 = (bf16[2,32,512]{2,1,0:T(8,128)(2,1)}, bf16[2,32,512]{2,1,0:T(8,128)(2,1)S(1)}, u32[]{:S(2)}, u32[]{:S(2)}) collective-permute-start(bf16[2,32,512]{2,1,0:T(8,128)(2,1)} %bitcast.40), channel_id=1, source_target_pairs={{0,24},{2,26},{4,28},{6,30},{8,16},{10,18},{12,20},{14,22},{16,8},... | collective-permute-start | bytes 196616 | tf_op jit(solution)/shard_map/ppermute | solution.py:249
  6.4 9.5 %collective-permute-start.2 = (bf16[2,32,512]{2,1,0:T(8,128)(2,1)}, bf16[2,32,512]{2,1,0:T(8,128)(2,1)S(1)}, u32[]{:S(2)}, u32[]{:S(2)}) collective-permute-start(bf16[2,32,512]{2,1,0:T(8,128)(2,1)} %bitcast.42), channel_id=1, source_target_pairs={{0,16},{2,18},{4,20},{6,22},{8,24},{10,26},{12,28},{14,30},{16,0},... | collective-permute-start | bytes 196616 | tf_op jit(solution)/shard_map/ppermute | solution.py:249
  8.3 7.6 %collective-permute-start.1 = (bf16[2,32,512]{2,1,0:T(8,128)(2,1)}, bf16[2,32,512]{2,1,0:T(8,128)(2,1)S(1)}, u32[]{:S(2)}, u32[]{:S(2)}) collective-permute-start(bf16[2,32,512]{2,1,0:T(8,128)(2,1)} %bitcast.43), channel_id=1, source_target_pairs={{0,8},{2,10},{4,12},{6,14},{8,0},{10,2},{12,4},{14,6},{16,24},{18,... | collective-permute-start | bytes 196616 | tf_op jit(solution)/shard_map/ppermute | solution.py:249
  10.7 6.4 %collective-permute-start.3 = (bf16[2,32,512]{2,1,0:T(8,128)(2,1)}, bf16[2,32,512]{2,1,0:T(8,128)(2,1)S(1)}, u32[]{:S(2)}, u32[]{:S(2)}) collective-permute-start(bf16[2,32,512]{2,1,0:T(8,128)(2,1)} %bitcast.44), channel_id=1, source_target_pairs={{0,24},{2,26},{4,28},{6,30},{8,16},{10,18},{12,20},{14,22},{16,8},... | collective-permute-start | bytes 196616 | tf_op jit(solution)/shard_map/ppermute | solution.py:249
  14.2 13.7 %collective-permute-start.10 = (bf16[4,2,32,512]{3,2,1,0:T(8,128)(2,1)S(1)}, bf16[4,2,32,512]{3,2,1,0:T(8,128)(2,1)S(1)}, u32[]{:S(2)}, u32[]{:S(2)}) collective-permute-start(bf16[4,2,32,512]{3,2,1,0:T(8,128)(2,1)S(1)} %pad_maximum_fusion.1.refs_0_), channel_id=1, source_target_pairs={{0,4},{2,6},{4,0},{6,2},{8,12},{10,14},{12,8},{14,10},{16,20},{18,... | collective-permute-start | bytes 786440 | tf_op jit(solution)/shard_map/ppermute | solution.py:249
  18.0 9.9 %collective-permute-start.4 = (bf16[4,2,32,512]{3,2,1,0:T(8,128)(2,1)S(1)}, bf16[4,2,32,512]{3,2,1,0:T(8,128)(2,1)S(1)}, u32[]{:S(2)}, u32[]{:S(2)}) collective-permute-start(bf16[4,2,32,512]{3,2,1,0:T(8,128)(2,1)S(1)} %pad_maximum_fusion.refs_2_), channel_id=1, source_target_pairs={{0,4},{2,6},{4,0},{6,2},{8,12},{10,14},{12,8},{14,10},{16,20},{18,... | collective-permute-start | bytes 786440 | tf_op jit(solution)/shard_map/ppermute | solution.py:249
  19.7 6.1 %collective-permute-start.17 = (bf16[1,32,512]{2,1,0:T(8,128)(2,1)S(1)}, bf16[1,32,512]{2,1,0:T(8,128)(2,1)S(1)}, u32[]{:S(2)}, u32[]{:S(2)}) collective-permute-start(bf16[1,32,512]{2,1,0:T(8,128)(2,1)S(1)} %get-tuple-element.37), channel_id=1, source_target_pairs={{0,24},{2,26},{4,28},{6,30},{8,16},{10,18},{12,20},{14,22},{16,8},... | collective-permute-start | bytes 98312 | tf_op jit(solution)/shard_map/ppermute | solution.py:249
  22.3 5.0 %collective-permute-start.16 = (bf16[1,32,512]{2,1,0:T(8,128)(2,1)S(1)}, bf16[1,32,512]{2,1,0:T(8,128)(2,1)S(1)}, u32[]{:S(2)}, u32[]{:S(2)}) collective-permute-start(bf16[1,32,512]{2,1,0:T(8,128)(2,1)S(1)} %get-tuple-element.37), channel_id=1, source_target_pairs={{0,16},{2,18},{4,20},{6,22},{8,24},{10,26},{12,28},{14,30},{16,0},... | collective-permute-start | bytes 98312 | tf_op jit(solution)/shard_map/ppermute | solution.py:249
  22.3 5.0 %collective-permute-start.15 = (bf16[1,32,512]{2,1,0:T(8,128)(2,1)S(1)}, bf16[1,32,512]{2,1,0:T(8,128)(2,1)S(1)}, u32[]{:S(2)}, u32[]{:S(2)}) collective-permute-start(bf16[1,32,512]{2,1,0:T(8,128)(2,1)S(1)} %get-tuple-element.37), channel_id=1, source_target_pairs={{0,8},{2,10},{4,12},{6,14},{8,0},{10,2},{12,4},{14,6},{16,24},{18,... | collective-permute-start | bytes 98312 | tf_op jit(solution)/shard_map/ppermute | solution.py:249
  25.8 5.2 %collective-permute-start = (bf16[128,512]{1,0:T(8,128)(2,1)}, bf16[128,512]{1,0:T(8,128)(2,1)S(1)}, u32[]{:S(2)}, u32[]{:S(2)}) collective-permute-start(bf16[128,512]{1,0:T(8,128)(2,1)} %refs_0_.1), channel_id=1, source_target_pairs={{0,1},{1,0},{2,3},{3,2},{4,5},{5,4},{6,7},{7,6},{8,9},{9,8},{10,11... | collective-permute-start | bytes 393224 | tf_op jit(solution)/shard_map/ppermute | solution.py:249
  27.3 8.6 %collective-permute-start.5 = (bf16[4,2,32,512]{3,2,1,0:T(8,128)(2,1)S(1)}, bf16[4,2,32,512]{3,2,1,0:T(8,128)(2,1)S(1)}, u32[]{:S(2)}, u32[]{:S(2)}) collective-permute-start(bf16[4,2,32,512]{3,2,1,0:T(8,128)(2,1)S(1)} %pad_maximum_fusion.refs_2_), channel_id=1, source_target_pairs={{0,2},{2,0},{4,6},{6,4},{8,10},{10,8},{12,14},{14,12},{16,18},{18,... | collective-permute-start | bytes 786440 | tf_op jit(solution)/shard_map/ppermute | solution.py:249
  27.3 12.6 %collective-permute-start.11 = (bf16[4,2,32,512]{3,2,1,0:T(8,128)(2,1)S(1)}, bf16[4,2,32,512]{3,2,1,0:T(8,128)(2,1)S(1)}, u32[]{:S(2)}, u32[]{:S(2)}) collective-permute-start(bf16[4,2,32,512]{3,2,1,0:T(8,128)(2,1)S(1)} %pad_maximum_fusion.1.refs_0_), channel_id=1, source_target_pairs={{0,2},{2,0},{4,6},{6,4},{8,10},{10,8},{12,14},{14,12},{16,18},{18,... | collective-permute-start | bytes 786440 | tf_op jit(solution)/shard_map/ppermute | solution.py:249
  27.9 12.1 %collective-permute-start.12 = (bf16[4,2,32,512]{3,2,1,0:T(8,128)(2,1)S(1)}, bf16[4,2,32,512]{3,2,1,0:T(8,128)(2,1)S(1)}, u32[]{:S(2)}, u32[]{:S(2)}) collective-permute-start(bf16[4,2,32,512]{3,2,1,0:T(8,128)(2,1)S(1)} %collective-permute-done.10.refs_1_), channel_id=1, source_target_pairs={{0,2},{2,0},{4,6},{6,4},{8,10},{10,8},{12,14},{14,12},{16,18},{18,... | collective-permute-start | bytes 786440 | tf_op jit(solution)/shard_map/ppermute | solution.py:249
  27.9 8.6 %collective-permute-start.6 = (bf16[4,2,32,512]{3,2,1,0:T(8,128)(2,1)S(1)}, bf16[4,2,32,512]{3,2,1,0:T(8,128)(2,1)S(1)}, u32[]{:S(2)}, u32[]{:S(2)}) collective-permute-start(bf16[4,2,32,512]{3,2,1,0:T(8,128)(2,1)S(1)} %collective-permute-done.4.refs_3_), channel_id=1, source_target_pairs={{0,2},{2,0},{4,6},{6,4},{8,10},{10,8},{12,14},{14,12},{16,18},{18,... | collective-permute-start | bytes 786440 | tf_op jit(solution)/shard_map/ppermute | solution.py:249
  31.0 5.0 %collective-permute-start.18 = (bf16[4,1,32,512]{3,2,1,0:T(8,128)(2,1)S(1)}, bf16[4,1,32,512]{3,2,1,0:T(8,128)(2,1)S(1)}, u32[]{:S(2)}, u32[]{:S(2)}) collective-permute-start(bf16[4,1,32,512]{3,2,1,0:T(8,128)(2,1)S(1)} %pad_maximum_fusion.2.refs_0_), channel_id=1, source_target_pairs={{0,4},{2,6},{4,0},{6,2},{8,12},{10,14},{12,8},{14,10},{16,20},{18,... | collective-permute-start | bytes 393224 | tf_op jit(solution)/shard_map/ppermute | solution.py:249
  36.0 9.3 %collective-permute-start.19 = (bf16[4,1,32,512]{3,2,1,0:T(8,128)(2,1)S(1)}, bf16[4,1,32,512]{3,2,1,0:T(8,128)(2,1)S(1)}, u32[]{:S(2)}, u32[]{:S(2)}) collective-permute-start(bf16[4,1,32,512]{3,2,1,0:T(8,128)(2,1)S(1)} %pad_maximum_fusion.2.refs_0_), channel_id=1, source_target_pairs={{0,2},{2,0},{4,6},{6,4},{8,10},{10,8},{12,14},{14,12},{16,18},{18,... | collective-permute-start | bytes 393224 | tf_op jit(solution)/shard_map/ppermute | solution.py:249
  36.0 9.3 %collective-permute-start.20 = (bf16[4,1,32,512]{3,2,1,0:T(8,128)(2,1)S(1)}, bf16[4,1,32,512]{3,2,1,0:T(8,128)(2,1)S(1)}, u32[]{:S(2)}, u32[]{:S(2)}) collective-permute-start(bf16[4,1,32,512]{3,2,1,0:T(8,128)(2,1)S(1)} %collective-permute-done.18.refs_1_), channel_id=1, source_target_pairs={{0,2},{2,0},{4,6},{6,4},{8,10},{10,8},{12,14},{14,12},{16,18},{18,... | collective-permute-start | bytes 393224 | tf_op jit(solution)/shard_map/ppermute | solution.py:249
  40.0 5.3 %copy-start.2 = (bf16[480]{0:T(512)(128)(2,1)S(1)}, bf16[480]{0:T(512)(128)(2,1)}, u32[]{:S(2)}) copy-start(bf16[480]{0:T(512)(128)(2,1)} %param.12) | copy-start | bytes 2884
  40.0 6.2 %copy-start.1 = (bf16[64,480]{1,0:T(8,128)(2,1)S(1)}, bf16[64,480]{1,0:T(8,128)(2,1)}, u32[]{:S(2)}) copy-start(bf16[64,480]{1,0:T(8,128)(2,1)} %refs_3_.1) | copy-start | bytes 184324
  42.7 2.6 %collective-permute-start.14 = (bf16[64,512]{1,0:T(8,128)(2,1)S(1)}, bf16[64,512]{1,0:T(8,128)(2,1)S(1)}, u32[]{:S(2)}, u32[]{:S(2)}) collective-permute-start(bf16[64,512]{1,0:T(8,128)(2,1)S(1)} %get-tuple-element.18.normed.refs_4_), channel_id=1, source_target_pairs={{2,4},{6,8},{10,12},{14,16},{18,20},{22,24},{26,28},{4,2},{8,6},{1... | collective-permute-start | bytes 196616 | tf_op jit(solution)/shard_map/ppermute | solution.py:278
  43.4 2.8 %collective-permute-start.13 = (bf16[64,512]{1,0:T(8,128)(2,1)S(1)}, bf16[64,512]{1,0:T(8,128)(2,1)S(1)}, u32[]{:S(2)}, u32[]{:S(2)}) collective-permute-start(bf16[64,512]{1,0:T(8,128)(2,1)S(1)} %get-tuple-element.18.normed.refs_4_), channel_id=1, source_target_pairs={{0,2},{2,0},{4,6},{6,4},{8,10},{10,8},{12,14},{14,12},{16,18},{18,... | collective-permute-start | bytes 196616 | tf_op jit(solution)/shard_map/ppermute | solution.py:249
  56.5 4.7 %collective-permute-start.22 = (bf16[64,480]{1,0:T(8,128)(2,1)S(1)}, bf16[64,480]{1,0:T(8,128)(2,1)S(1)}, u32[]{:S(2)}, u32[]{:S(2)}) collective-permute-start(bf16[64,480]{1,0:T(8,128)(2,1)S(1)} %get-tuple-element.23.slope_rev), channel_id=1, source_target_pairs={{2,4},{6,8},{10,12},{14,16},{18,20},{22,24},{26,28},{4,2},{8,6},{1... | collective-permute-start | bytes 184328 | tf_op jit(solution)/shard_map/ppermute | solution.py:278
  57.2 4.9 %collective-permute-start.21 = (bf16[64,480]{1,0:T(8,128)(2,1)S(1)}, bf16[64,480]{1,0:T(8,128)(2,1)S(1)}, u32[]{:S(2)}, u32[]{:S(2)}) collective-permute-start(bf16[64,480]{1,0:T(8,128)(2,1)S(1)} %get-tuple-element.23.slope_rev), channel_id=1, source_target_pairs={{0,2},{2,0},{4,6},{6,4},{8,10},{10,8},{12,14},{14,12},{16,18},{18,... | collective-permute-start | bytes 184328 | tf_op jit(solution)/shard_map/ppermute | solution.py:249
  70.2 6.2 %collective-permute-start.24 = (bf16[8,32,480]{2,1,0:T(8,128)(2,1)S(1)}, bf16[8,32,480]{2,1,0:T(8,128)(2,1)S(1)}, u32[]{:S(2)}, u32[]{:S(2)}) collective-permute-start(bf16[8,32,480]{2,1,0:T(8,128)(2,1)S(1)} %get-tuple-element.30), channel_id=1, source_target_pairs={{0,2},{2,0},{4,6},{6,4},{8,10},{10,8},{12,14},{14,12},{16,18},{18,... | collective-permute-start | bytes 737288 | tf_op jit(solution)/shard_map/ppermute | solution.py:249
  72.3 3.9 %collective-permute-start.23 = (bf16[32,512]{1,0:T(8,128)(2,1)S(1)}, bf16[32,512]{1,0:T(8,128)(2,1)S(1)}, u32[]{:S(2)}, u32[]{:S(2)}) collective-permute-start(bf16[32,512]{1,0:T(8,128)(2,1)S(1)} %bitcast.34), channel_id=1, source_target_pairs={{0,1},{1,0},{2,3},{3,2},{4,5},{5,4},{6,7},{7,6},{8,9},{9,8},{10,11... | collective-permute-start | bytes 98312 | tf_op jit(solution)/shard_map/ppermute | solution.py:249
  76.5 5.3 %collective-permute-start.25 = (bf16[4,32,480]{2,1,0:T(8,128)(2,1)S(1)}, bf16[4,32,480]{2,1,0:T(8,128)(2,1)S(1)}, u32[]{:S(2)}, u32[]{:S(2)}) collective-permute-start(bf16[4,32,480]{2,1,0:T(8,128)(2,1)S(1)} %slice.29), channel_id=1, source_target_pairs={{0,4},{2,6},{4,0},{6,2},{8,12},{10,14},{12,8},{14,10},{16,20},{18,... | collective-permute-start | bytes 368648 | tf_op jit(solution)/shard_map/ppermute | solution.py:249
  81.9 5.1 %collective-permute-start.26 = (bf16[32,480]{1,0:T(8,128)(2,1)S(1)}, bf16[32,480]{1,0:T(8,128)(2,1)S(1)}, u32[]{:S(2)}, u32[]{:S(2)}) collective-permute-start(bf16[32,480]{1,0:T(8,128)(2,1)S(1)} %get-tuple-element.33), channel_id=1, source_target_pairs={{0,8},{2,10},{4,12},{6,14},{8,0},{10,2},{12,4},{14,6},{16,24},{18,... | collective-permute-start | bytes 92168 | tf_op jit(solution)/shard_map/ppermute | solution.py:249
  82.6 5.9 %collective-permute-start.28 = (bf16[32,480]{1,0:T(8,128)(2,1)S(1)}, bf16[32,480]{1,0:T(8,128)(2,1)S(1)}, u32[]{:S(2)}, u32[]{:S(2)}) collective-permute-start(bf16[32,480]{1,0:T(8,128)(2,1)S(1)} %get-tuple-element.34), channel_id=1, source_target_pairs={{0,24},{2,26},{4,28},{6,30},{8,16},{10,18},{12,20},{14,22},{16,8},... | collective-permute-start | bytes 92168 | tf_op jit(solution)/shard_map/ppermute | solution.py:249
  85.8 4.8 %collective-permute-start.27 = (bf16[32,480]{1,0:T(8,128)(2,1)S(1)}, bf16[32,480]{1,0:T(8,128)(2,1)S(1)}, u32[]{:S(2)}, u32[]{:S(2)}) collective-permute-start(bf16[32,480]{1,0:T(8,128)(2,1)S(1)} %get-tuple-element.35), channel_id=1, source_target_pairs={{0,16},{2,18},{4,20},{6,22},{8,24},{10,26},{12,28},{14,30},{16,0},... | collective-permute-start | bytes 92168 | tf_op jit(solution)/shard_map/ppermute | solution.py:249

commit v6 on v4

--- a/solution.py
+++ b/solution.py
@@ -66,7 +66,7 @@
     return (unit * phi_cdf(unit)).astype(BF16)
 
 
-def tap_copies(w_any, w_out, sems, start):
+def hold_body(w_any, w_out, sems):
     count = sems.shape[1]
     size = w_out.shape[1] // count
     copies = []
@@ -74,36 +74,27 @@
         for c in range(count):
             part = pl.ds(c * size, size)
             copies.append(
-                pltpu.make_async_copy(
-                    w_any.at[start + g, part], w_out.at[g, part], sems.at[g, c]
-                )
+                pltpu.make_async_copy(w_any.at[g, part], w_out.at[g, part], sems.at[g, c])
             )
     for copy in copies:
         copy.start()
-    return copies
+    for copy in copies:
+        copy.wait()
 
 
 def five_body(where, *refs, layout, count):
     blocks, stacks = refs[:count], refs[count : count + len(layout)]
-    w_any, out, w_out, full, sems, mine, mine_sem = refs[count + len(layout) :]
+    out, full, mine, mine_sem = refs[count + len(layout) :]
     own = pltpu.make_async_copy(blocks[0], mine, mine_sem)
     own.start()
-    copies = tap_copies(w_any, w_out, sems, 0)
     place_shards(where[0], layout, stacks, 0, 2, full)
     own.wait()
     out[...] = strided([mine[...]] + [b[...] for b in blocks[1:]], full)
-    for copy in copies:
-        copy.wait()
-
-
-def six_body(where, act, *refs, layout, count, start):
+
+
+def six_body(where, act, *refs, layout, count):
     stacks = refs[: len(layout)]
-    if start is None:
-        normed, unit_own, inv_own, full = refs[len(layout) :]
-        copies = []
-    else:
-        w_any, normed, unit_own, inv_own, w_out, full, sems = refs[len(layout) :]
-        copies = tap_copies(w_any, w_out, sems, start)
+    normed, unit_own, inv_own, full = refs[len(layout) :]
     place_shards(where[0], layout, stacks, 0, 2, full)
     rows = act.shape[0] // count
     act_six = strided([act[e * rows : (e + 1) * rows] for e in range(count)], full)
@@ -114,8 +105,6 @@
         normed[pl.ds(at, own), :] = unit[e * own : (e + 1) * own].astype(BF16)
     unit_own[...] = unit[:own]
     inv_own[...] = jnp.broadcast_to(inv_dev[:own], inv_own.shape)
-    for copy in copies:
-        copy.wait()
 
 
 def conv_group(weights, first, wrap, rows):
@@ -138,28 +127,26 @@
 
 def conv(weights, turned, first, wrap, acc):
     rows, width = acc.shape[1:]
-    start = 0
-    for held in weights:
-        def step(g, carry):
-            group = held.at[g]
-            if turned is not None:
-                turned[...] = jnp.swapaxes(held[g], 0, 1)
-                group = turned
-            here = pl.ds(pl.multiple_of((start + g) * width, 8), width)
-            acc[start + g] = conv_group(group, first.at[here], wrap.at[here], rows)
-            return carry
-
-        lax.fori_loop(0, held.shape[0], step, 0)
-        start += held.shape[0]
+
+    def step(g, carry):
+        group = weights.at[g]
+        if turned is not None:
+            turned[...] = jnp.swapaxes(weights[g], 0, 1)
+            group = turned
+        here = pl.ds(pl.multiple_of(g * width, 8), width)
+        acc[g] = conv_group(group, first.at[here], wrap.at[here], rows)
+        return carry
+
+    lax.fori_loop(0, acc.shape[0], step, 0)
     return jnp.concatenate([acc[g] for g in range(acc.shape[0])], 1)
 
 
-def forward_body(where, normed, got_a, got_b, *refs, layout, held):
+def forward_body(where, normed, got_a, got_b, *refs, layout):
     stacks, refs = refs[: len(layout)], refs[len(layout) :]
-    weights, refs = refs[:held], refs[held:]
+    weights, refs = refs[0], refs[1:]
     cot, bias, encoded, slope_rev, proj, full = refs[:6]
     first, wrap, acc = refs[6:]
-    place_shards(where[0], layout, stacks, 0, 1, full)
+    place_shards(where[0], layout, stacks, 2, 1, full)
     proj[...] = full[0, :, : proj.shape[1]]
     odd = where[0] % 2 == 1
     low = jnp.where(odd, got_a[...], got_b[...])
@@ -185,8 +172,8 @@
         slope_rev[here, :] = (cot_rev * slope).astype(BF16)
 
 
-def backward_body(where, slope_rev, got_a, got_b, *refs, scale, order, held):
-    weights, refs = refs[:held], refs[held:]
+def backward_body(where, slope_rev, got_a, got_b, *refs, scale, order):
+    weights, refs = refs[0], refs[1:]
     (cot, normed, proj), refs = refs[:3], refs[3:]
     kept, sent, unit_grad, unit_sent, first, wrap, acc = refs[:7]
     turned, hid_grad, full, rows_f32 = refs[7:]
@@ -267,7 +254,8 @@
     to_b = tail if tail is head else jnp.where(parity == 0, head, tail)
     pairs = [(2 * i + 1, 2 * i + 2) for i in range(count // 2 - 1)]
     got_b = lax.ppermute(to_b, "tm", pairs + [(b, a) for a, b in pairs])
-    return swap(to_a, "tm", 1), got_b
+    got_a = swap(to_a, "tm", 1)
+    return got_a, got_b
 
 
 def on_device(features, weight_five, weight_six, projection, pos_weight, pos_bias, cotangent):
@@ -286,47 +274,47 @@
     bias = pos_bias.reshape(1, columns)
     proj_half = lax.dynamic_slice_in_dim(projection, slot * columns, columns, 1)
     proj_half = jnp.pad(proj_half, ((0, 0), (0, channels - columns)))
+    rest = jnp.concatenate([jnp.transpose(weight_six, (0, 2, 1)), proj_half[None]], 0)
     five, offs = spread_near(jnp.transpose(weight_five, (0, 2, 1)), members)
-    six, _ = spread_near(jnp.transpose(weight_six, (0, 2, 1)), members)
-    last, _ = spread_near(proj_half[None], members)
+    rest, _ = spread_near(rest, members)
     five, layout = spread_far(five, offs, members)
-    six, _ = spread_far(six, offs, members)
-    last, _ = spread_far(last, offs, members)
+    rest, _ = spread_far(rest, offs, members)
+    rest = on_chip(rest)
     common = dict(layout=layout)
     taps_scratch = [pltpu.VMEM((2, channels, channels), BF16)]
 
-    cut = (groups + 1) // 2
-    tap_sems = lambda count: pltpu.SemaphoreType.DMA((count, 5))
-    act_five, w_low = pl.pallas_call(
+    weights = pl.pallas_call(
+        hold_body,
+        in_specs=[HBM_SPEC],
+        out_specs=vmem_specs(1)[0],
+        out_shape=pltpu.VMEM((groups, width, width, taps), BF16),
+        scratch_shapes=[pltpu.SemaphoreType.DMA((groups, 5))],
+        compiler_params=PARAMS,
+        name="hold",
+    )(w_taps)
+    act_five = pl.pallas_call(
         functools.partial(five_body, count=slots, **common),
-        in_specs=[SMEM_SPEC, HBM_SPEC] + vmem_specs(slots - 1 + len(five)) + [HBM_SPEC],
-        out_specs=vmem_specs(2),
-        out_shape=[
-            pltpu.VMEM((2 * block, channels), BF16),
-            pltpu.VMEM((cut, width, width, taps), BF16),
-        ],
+        in_specs=[SMEM_SPEC, HBM_SPEC] + vmem_specs(slots - 1 + len(five)),
+        out_specs=vmem_specs(1)[0],
+        out_shape=pltpu.VMEM((2 * block, channels), BF16),
         scratch_shapes=taps_scratch
-        + [tap_sems(cut), pltpu.VMEM(features.shape, BF16), pltpu.SemaphoreType.DMA(())],
+        + [pltpu.VMEM(features.shape, BF16), pltpu.SemaphoreType.DMA(())],
         compiler_params=PARAMS,
         name="five",
-    )(where, in_hbm(blocks[0]), *on_chip(blocks[1:] + five), w_taps)
-    rest = groups - cut
-    results = pl.pallas_call(
-        functools.partial(six_body, count=slots, start=cut if rest else None, **common),
-        in_specs=[SMEM_SPEC] + vmem_specs(1 + len(six)) + ([HBM_SPEC] if rest else []),
-        out_specs=vmem_specs(4 if rest else 3),
+    )(where, in_hbm(blocks[0]), *on_chip(blocks[1:] + five))
+    normed, unit, inv_dev = pl.pallas_call(
+        functools.partial(six_body, count=slots, **common),
+        in_specs=[SMEM_SPEC] + vmem_specs(1 + len(rest)),
+        out_specs=vmem_specs(3),
         out_shape=[
             pltpu.VMEM((block, channels), BF16),
             pltpu.VMEM((own, channels), F32),
             pltpu.VMEM((own, 128), F32),
-        ]
-        + ([pltpu.VMEM((rest, width, width, taps), BF16)] if rest else []),
-        scratch_shapes=taps_scratch + ([tap_sems(rest)] if rest else []),
+        ],
+        scratch_shapes=taps_scratch,
         compiler_params=PARAMS,
         name="six",
-    )(where, act_five, *on_chip(six), *([w_taps] if rest else []))
-    normed, unit, inv_dev = results[:3]
-    weights = [w_low] + list(results[3:])
+    )(where, act_five, *rest)
 
     whole = block == half
     tail = normed if whole else normed[block - half :]
@@ -338,8 +326,8 @@
         pltpu.VMEM((groups, half, width), F32),
     ]
     encoded, slope_rev, proj = pl.pallas_call(
-        functools.partial(forward_body, held=len(weights), **common),
-        in_specs=[SMEM_SPEC] + vmem_specs(3 + len(last) + len(weights) + 2),
+        functools.partial(forward_body, **common),
+        in_specs=[SMEM_SPEC] + vmem_specs(3 + len(rest) + 3),
         out_specs=vmem_specs(3),
         out_shape=[
             jax.ShapeDtypeStruct((block, columns), BF16),
@@ -349,7 +337,7 @@
         scratch_shapes=[pltpu.VMEM((1, channels, channels), BF16)] + conv_scratch,
         compiler_params=CONV_PARAMS,
         name="forward",
-    )(where, normed, *on_chip([got_a, got_b] + last), *weights, cotangent, bias)
+    )(where, normed, *on_chip([got_a, got_b]), *rest, weights, cotangent, bias)
 
     tail = slope_rev if whole else slope_rev[block - half :]
     head = slope_rev if whole else slope_rev[:half]
@@ -365,8 +353,8 @@
     for mask in reversed(masks):
         order = order + [p ^ mask for p in order]
     kept, sent, unit_grad, unit_sent = pl.pallas_call(
-        functools.partial(backward_body, scale=scale, order=order, held=len(weights)),
-        in_specs=[SMEM_SPEC] + vmem_specs(6 + len(weights)),
+        functools.partial(backward_body, scale=scale, order=order),
+        in_specs=[SMEM_SPEC] + vmem_specs(7),
         out_specs=vmem_specs(4),
         out_shape=[pltpu.VMEM((members // 2, share, columns), BF16)] * 2
         + [
@@ -382,7 +370,7 @@
         ],
         compiler_params=CONV_PARAMS,
         name="backward",
-    )(where, slope_rev, *on_chip([got_a, got_b]), *weights, cotangent, normed, proj)
+    )(where, slope_rev, *on_chip([got_a, got_b]), weights, cotangent, normed, proj)
 
     got = swap(sent, "tm", 1)
     total = (kept.astype(F32) + got.astype(F32)).astype(BF16)

time: 91.6 us -> 93.9 us (1.025)
  starting transfers between devices: 41.2 us -> 30.7 us
  waiting for transfers between devices: 21.7 us -> 31.8 us
  local copies, waits for them, and re-layouts: 0.25 us -> 1.74 us
  Pallas kernels: 23.9 us -> 25.1 us
    ppermute x27 -> x21, starting transfers between devices: 39.9 us -> 29.4 us  [swap(): return lax.ppermute(values, axis, [(i, i ^ mask) for i in range(count)])]
    ppermute x27 -> x21, waiting for transfers between devices: 21.7 us -> 31.8 us  [swap(): return lax.ppermute(values, axis, [(i, i ^ mask) for i in range(count)])]
    pallas_call x3 -> x4, Pallas kernels: 19.6 us -> 22.8 us  [the longest x1 8.16 us: on_device(): pl.pallas_call(functools.partial(forward_body, **common), in_specs=[SMEM_...]
    pallas_call x1, Pallas kernels: 4.34 us -> 2.25 us  [on_device(): pl.pallas_call(functools.partial(five_body, count=slots, **common), in_sp...]
  transfers between devices with their start and end apart: 29 -> 23, of which waited for: 12 -> 12; matrix products, arithmetic and copies ran while one was open for 3% -> 3% of each run, Pallas kernels for 9% -> 8%
where the time goes in v6:
time: 93.9 us; the launch traced here: 93.6 us
  waiting for transfers between devices  31.8 us (34%)
  starting transfers between devices  30.7 us (33%)
  Pallas kernels  25.1 us (27%)
  other arithmetic  3.42 us (4%)
  local copies, waits for them, and re-layouts  1.74 us (2%)
    ppermute x21, waiting for transfers between devices, swap(): return lax.ppermute(values, axis, [(i, i ^ mask) for i in range(count)])  31.8 us
    ppermute x21, starting transfers between devices, swap(): return lax.ppermute(values, axis, [(i, i ^ mask) for i in range(count)])  29.4 us
    pallas_call x1, Pallas kernels, on_device(): pl.pallas_call(functools.partial(forward_body, **common), in_specs=[SMEM_...  8.16 us
    pallas_call x1, Pallas kernels, on_device(): pl.pallas_call(functools.partial(backward_body, scale=scale, order=order)...  7.84 us
    pallas_call x1, Pallas kernels, on_device(): pl.pallas_call(hold_body, in_specs=[HBM_SPEC], out_specs=vmem_specs(1)[0]...  5.39 us
    pallas_call x1, Pallas kernels, on_device(): pl.pallas_call(functools.partial(five_body, count=slots, **common), in_sp...  2.25 us
  transfers between devices with their start and end apart: 23, of which 12 were waited for; matrix products, arithmetic and copies ran while one was open for 3% of the time, Pallas kernels for 8%

profile of v6, /device:TPU:0, one launch (start us, length us, event | category | flops | bytes accessed | tf_op | source)
XLA Modules:
  0.0 93.6 jit_solution(2793041473203444700)
XLA Ops:
  0.6 0.0 copy-start
  0.6 0.8 copy-done
  1.5 0.1 constant_dynamic-slice_fusion
  1.6 0.9 fusion.1
  2.4 4.1 %collective-permute-start.8 = (bf16[3,32,512]{2,1,0:T(8,128)(2,1)S(1)}, bf16[3,32,512]{2,1,0:T(8,128)(2,1)S(1)}, u32[]{:S(2)}, u32[]{:S(2)}) collective-permute-start(bf16[3,32,512]{2,1,0:T(8,128)(2,1)S(1)} %get-tuple-element.29), channel_id=1, source_target_pairs={{0,16},{2,18},{4,20},{6,22},{8,24},{10,26},{12,28},{14,30},{16,0},... | collective-permute-start | bytes 294920 | tf_op jit(solution)/shard_map/ppermute | solution.py:227
  6.6 1.6 %collective-permute-start.7 = (bf16[3,32,512]{2,1,0:T(8,128)(2,1)S(1)}, bf16[3,32,512]{2,1,0:T(8,128)(2,1)S(1)}, u32[]{:S(2)}, u32[]{:S(2)}) collective-permute-start(bf16[3,32,512]{2,1,0:T(8,128)(2,1)S(1)} %get-tuple-element.29), channel_id=1, source_target_pairs={{0,8},{2,10},{4,12},{6,14},{8,0},{10,2},{12,4},{14,6},{16,24},{18,... | collective-permute-start | bytes 294920 | tf_op jit(solution)/shard_map/ppermute | solution.py:227
  8.1 4.5 %collective-permute-done.8 = bf16[3,32,512]{2,1,0:T(8,128)(2,1)S(1)} collective-permute-done((bf16[3,32,512]{2,1,0:T(8,128)(2,1)S(1)}, bf16[3,32,512]{2,1,0:T(8,128)(2,1)S(1)}, u32[]{:S(2)}, u32[]{:S(2)}) %collective-permute-start.8) | collective-permute-done | bytes 98336 | tf_op jit(solution)/shard_map/ppermute | solution.py:227
  12.6 2.1 %collective-permute-done.9 = bf16[3,32,512]{2,1,0:T(8,128)(2,1)S(1)} collective-permute-done((bf16[3,32,512]{2,1,0:T(8,128)(2,1)S(1)}, bf16[3,32,512]{2,1,0:T(8,128)(2,1)S(1)}, u32[]{:S(2)}, u32[]{:S(2)}) %collective-permute-start.9) | collective-permute-done | bytes 98336 | tf_op jit(solution)/shard_map/ppermute | solution.py:227
  14.7 0.1 pad_maximum_fusion.refs_0_
  14.7 1.5 %collective-permute-start.10 = (bf16[4,3,32,512]{3,2,1,0:T(8,128)(2,1)S(1)}, bf16[4,3,32,512]{3,2,1,0:T(8,128)(2,1)S(1)}, u32[]{:S(2)}, u32[]{:S(2)}) collective-permute-start(bf16[4,3,32,512]{3,2,1,0:T(8,128)(2,1)S(1)} %pad_maximum_fusion.refs_0_), channel_id=1, source_target_pairs={{0,4},{2,6},{4,0},{6,2},{8,12},{10,14},{12,8},{14,10},{16,20},{18,... | collective-permute-start | bytes 1179656 | tf_op jit(solution)/shard_map/ppermute | solution.py:227
  16.3 3.7 %collective-permute-start.2 = (bf16[2,32,512]{2,1,0:T(8,128)(2,1)}, bf16[2,32,512]{2,1,0:T(8,128)(2,1)S(1)}, u32[]{:S(2)}, u32[]{:S(2)}) collective-permute-start(bf16[2,32,512]{2,1,0:T(8,128)(2,1)} %bitcast.35), channel_id=1, source_target_pairs={{0,16},{2,18},{4,20},{6,22},{8,24},{10,26},{12,28},{14,30},{16,0},... | collective-permute-start | bytes 196616 | tf_op jit(solution)/shard_map/ppermute | solution.py:227
  20.0 1.5 %collective-permute-start.3 = (bf16[2,32,512]{2,1,0:T(8,128)(2,1)}, bf16[2,32,512]{2,1,0:T(8,128)(2,1)S(1)}, u32[]{:S(2)}, u32[]{:S(2)}) collective-permute-start(bf16[2,32,512]{2,1,0:T(8,128)(2,1)} %bitcast.37), channel_id=1, source_target_pairs={{0,24},{2,26},{4,28},{6,30},{8,16},{10,18},{12,20},{14,22},{16,8},... | collective-permute-start | bytes 196616 | tf_op jit(solution)/shard_map/ppermute | solution.py:227
  21.4 2.3 %collective-permute-done.2 = bf16[2,32,512]{2,1,0:T(8,128)(2,1)S(1)} collective-permute-done((bf16[2,32,512]{2,1,0:T(8,128)(2,1)}, bf16[2,32,512]{2,1,0:T(8,128)(2,1)S(1)}, u32[]{:S(2)}, u32[]{:S(2)}) %collective-permute-start.2) | collective-permute-done | bytes 65568 | tf_op jit(solution)/shard_map/ppermute | solution.py:227
  23.7 1.4 %collective-permute-done.1 = bf16[2,32,512]{2,1,0:T(8,128)(2,1)S(1)} collective-permute-done((bf16[2,32,512]{2,1,0:T(8,128)(2,1)}, bf16[2,32,512]{2,1,0:T(8,128)(2,1)S(1)}, u32[]{:S(2)}, u32[]{:S(2)}) %collective-permute-start.1) | collective-permute-done | bytes 65568 | tf_op jit(solution)/shard_map/ppermute | solution.py:227
  25.1 1.2 %collective-permute-done.3 = bf16[2,32,512]{2,1,0:T(8,128)(2,1)S(1)} collective-permute-done((bf16[2,32,512]{2,1,0:T(8,128)(2,1)}, bf16[2,32,512]{2,1,0:T(8,128)(2,1)S(1)}, u32[]{:S(2)}, u32[]{:S(2)}) %collective-permute-start.3) | collective-permute-done | bytes 65568 | tf_op jit(solution)/shard_map/ppermute | solution.py:227
  26.3 0.9 pad_maximum_fusion.1.refs_2_
  27.2 0.6 collective-permute-start.4
  27.8 0.5 collective-permute-start.12
  28.3 0.0 collective-permute-start.5
  28.3 5.5 %collective-permute-done.4.refs_3_ = bf16[4,2,32,512]{3,2,1,0:T(8,128)(2,1)S(1)} collective-permute-done((bf16[4,2,32,512]{3,2,1,0:T(8,128)(2,1)S(1)}, bf16[4,2,32,512]{3,2,1,0:T(8,128)(2,1)S(1)}, u32[]{:S(2)}, u32[]{:S(2)}) %collective-permute-start.4) | collective-permute-done | bytes 262176 | tf_op jit(solution)/shard_map/ppermute | solution.py:227
  33.8 1.5 %collective-permute-start = (bf16[128,512]{1,0:T(8,128)(2,1)}, bf16[128,512]{1,0:T(8,128)(2,1)S(1)}, u32[]{:S(2)}, u32[]{:S(2)}) collective-permute-start(bf16[128,512]{1,0:T(8,128)(2,1)} %refs_0_.1), channel_id=1, source_target_pairs={{0,1},{1,0},{2,3},{3,2},{4,5},{5,4},{6,7},{7,6},{8,9},{9,8},{10,11... | collective-permute-start | bytes 393224 | tf_op jit(solution)/shard_map/ppermute | solution.py:227
  35.3 0.1 pad_add_fusion.where
  35.4 4.6 %collective-permute-done.refs_1_ = bf16[128,512]{1,0:T(8,128)(2,1)S(1)} collective-permute-done((bf16[128,512]{1,0:T(8,128)(2,1)}, bf16[128,512]{1,0:T(8,128)(2,1)S(1)}, u32[]{:S(2)}, u32[]{:S(2)}) %collective-permute-start) | collective-permute-done | bytes 131104 | tf_op jit(solution)/shard_map/ppermute | solution.py:227
  40.0 2.3 %five.1.act = bf16[128,512]{1,0:T(8,128)(2,1)S(1)} custom-call(s32[2]{0:T(128)S(1)} %pad_add_fusion.where, bf16[128,512]{1,0:T(8,128)(2,1)} %refs_0_.1, bf16[128,512]{1,0:T(8,128)(2,1)S(1)} %collective-permute-done.refs_1_, bf16[4,2,32,512]{3,2,1,0:T(8,128)(2,1)S(1)} %pad_maximum_fusion.1.refs_2_, ...), custom_call_target="tpu_custom_call" | custom-call | tf_op jit(solution)/shard_map/five/pallas_call | solution.py:295
  42.2 1.4 %six.1 = (bf16[64,512]{1,0:T(8,128)(2,1)S(1)}, f32[32,512]{1,0:T(8,128)S(1)}, f32[32,128]{1,0:T(8,128)S(1)}) custom-call(s32[2]{0:T(128)S(1)} %pad_add_fusion.where, bf16[128,512]{1,0:T(8,128)(2,1)S(1)} %five.1.act, bf16[4,3,32,512]{3,2,1,0:T(8,128)(2,1)S(1)} %pad_maximum_fusion.refs_0_, bf16[4,3,32,512]{3,2,1,0:T(8,128)(2,1)S(1)} %collective-permute-done.10.refs_1_, ...), custom_call_target="tpu_custom_call" | custom-call | tf_op jit(solution)/shard_map/six/pallas_call | solution.py:305
  43.7 0.7 collective-permute-start.14
  44.4 1.9 %collective-permute-start.13 = (bf16[64,512]{1,0:T(8,128)(2,1)S(1)}, bf16[64,512]{1,0:T(8,128)(2,1)S(1)}, u32[]{:S(2)}, u32[]{:S(2)}) collective-permute-start(bf16[64,512]{1,0:T(8,128)(2,1)S(1)} %get-tuple-element.13.normed.refs_2_), channel_id=1, source_target_pairs={{0,2},{2,0},{4,6},{6,4},{8,10},{10,8},{12,14},{14,12},{16,18},{18,... | collective-permute-start | bytes 196616 | tf_op jit(solution)/shard_map/ppermute | solution.py:227
  46.3 0.7 reshape.19.refs_6_
  47.0 5.4 %hold.1.refs_4_.refs_0_ = bf16[4,120,120,128]{3,2,1,0:T(8,128)(2,1)S(1)} custom-call(bf16[4,120,120,128]{3,2,1,0:T(8,128)(2,1)} %bitcast.30), custom_call_target="tpu_custom_call" | custom-call | tf_op jit(solution)/shard_map/hold/pallas_call | solution.py:286
  52.4 8.2 %forward.1 = (bf16[64,480]{1,0:T(8,128)(2,1)}, bf16[64,480]{1,0:T(8,128)(2,1)S(1)}, bf16[512,480]{1,0:T(8,128)(2,1)S(1)}) custom-call(s32[2]{0:T(128)S(1)} %pad_add_fusion.where, bf16[64,512]{1,0:T(8,128)(2,1)S(1)} %get-tuple-element.13.normed.refs_2_, bf16[64,512]{1,0:T(8,128)(2,1)S(1)} %collective-permute-done.13.got_a, ...), custom_call_target="tpu_custom_call" | custom-call | tf_op jit(solution)/shard_map/forward/pallas_call | solution.py:328
  60.6 0.7 collective-permute-start.16
  61.2 3.3 %collective-permute-start.15 = (bf16[64,480]{1,0:T(8,128)(2,1)S(1)}, bf16[64,480]{1,0:T(8,128)(2,1)S(1)}, u32[]{:S(2)}, u32[]{:S(2)}) collective-permute-start(bf16[64,480]{1,0:T(8,128)(2,1)S(1)} %get-tuple-element.16.slope_rev), channel_id=1, source_target_pairs={{0,2},{2,0},{4,6},{6,4},{8,10},{10,8},{12,14},{14,12},{16,18},{18,... | collective-permute-start | bytes 184328 | tf_op jit(solution)/shard_map/ppermute | solution.py:227
  64.6 0.9 collective-permute-done.15.got_a
  65.5 7.8 %backward.1 = (bf16[8,32,480]{2,1,0:T(8,128)(2,1)S(1)}, bf16[8,32,480]{2,1,0:T(8,128)(2,1)S(1)}, f32[32,512]{1,0:T(8,128)S(1)}, bf16[1,32,512]{2,1,0:T(8,128)(2,1)S(1)}) custom-call(s32[2]{0:T(128)S(1)} %pad_add_fusion.where, bf16[64,480]{1,0:T(8,128)(2,1)S(1)} %get-tuple-element.16.slope_rev, bf16[64,480]{1,0:T(8,128)(2,1)S(1)} %collective-permute-done.15.got_a, ...), custom_call_target="tpu_custom_call" | custom-call | tf_op jit(solution)/shard_map/backward/pallas_call | solution.py:355
  73.3 1.0 %collective-permute-start.18 = (bf16[8,32,480]{2,1,0:T(8,128)(2,1)S(1)}, bf16[8,32,480]{2,1,0:T(8,128)(2,1)S(1)}, u32[]{:S(2)}, u32[]{:S(2)}) collective-permute-start(bf16[8,32,480]{2,1,0:T(8,128)(2,1)S(1)} %get-tuple-element.22), channel_id=1, source_target_pairs={{0,2},{2,0},{4,6},{6,4},{8,10},{10,8},{12,14},{14,12},{16,18},{18,... | collective-permute-start | bytes 737288 | tf_op jit(solution)/shard_map/ppermute | solution.py:227
  74.4 1.5 %collective-permute-start.17 = (bf16[32,512]{1,0:T(8,128)(2,1)S(1)}, bf16[32,512]{1,0:T(8,128)(2,1)S(1)}, u32[]{:S(2)}, u32[]{:S(2)}) collective-permute-start(bf16[32,512]{1,0:T(8,128)(2,1)S(1)} %bitcast.29), channel_id=1, source_target_pairs={{0,1},{1,0},{2,3},{3,2},{4,5},{5,4},{6,7},{7,6},{8,9},{9,8},{10,11... | collective-permute-start | bytes 98312 | tf_op jit(solution)/shard_map/ppermute | solution.py:227
  75.9 0.1 slice_reduce_fusion
  76.0 2.3 %collective-permute-done.17 = bf16[32,512]{1,0:T(8,128)(2,1)S(1)} collective-permute-done((bf16[32,512]{1,0:T(8,128)(2,1)S(1)}, bf16[32,512]{1,0:T(8,128)(2,1)S(1)}, u32[]{:S(2)}, u32[]{:S(2)}) %collective-permute-start.17) | collective-permute-done | bytes 32800 | tf_op jit(solution)/shard_map/ppermute | solution.py:227
  78.3 0.1 fusion
  78.4 0.1 add_convert_fusion
  78.5 2.6 %collective-permute-start.19 = (bf16[4,32,480]{2,1,0:T(8,128)(2,1)S(1)}, bf16[4,32,480]{2,1,0:T(8,128)(2,1)S(1)}, u32[]{:S(2)}, u32[]{:S(2)}) collective-permute-start(bf16[4,32,480]{2,1,0:T(8,128)(2,1)S(1)} %slice.29), channel_id=1, source_target_pairs={{0,4},{2,6},{4,0},{6,2},{8,12},{10,14},{12,8},{14,10},{16,20},{18,... | collective-permute-start | bytes 368648 | tf_op jit(solution)/shard_map/ppermute | solution.py:227
  81.1 2.9 %collective-permute-done.19 = bf16[4,32,480]{2,1,0:T(8,128)(2,1)S(1)} collective-permute-done((bf16[4,32,480]{2,1,0:T(8,128)(2,1)S(1)}, bf16[4,32,480]{2,1,0:T(8,128)(2,1)S(1)}, u32[]{:S(2)}, u32[]{:S(2)}) %collective-permute-start.19) | collective-permute-done | bytes 122912 | tf_op jit(solution)/shard_map/ppermute | solution.py:227
  84.1 1.3 %collective-permute-start.20 = (bf16[32,480]{1,0:T(8,128)(2,1)S(1)}, bf16[32,480]{1,0:T(8,128)(2,1)S(1)}, u32[]{:S(2)}, u32[]{:S(2)}) collective-permute-start(bf16[32,480]{1,0:T(8,128)(2,1)S(1)} %get-tuple-element.25), channel_id=1, source_target_pairs={{0,8},{2,10},{4,12},{6,14},{8,0},{10,2},{12,4},{14,6},{16,24},{18,... | collective-permute-start | bytes 92168 | tf_op jit(solution)/shard_map/ppermute | solution.py:227
  85.4 2.7 %collective-permute-start.22 = (bf16[32,480]{1,0:T(8,128)(2,1)S(1)}, bf16[32,480]{1,0:T(8,128)(2,1)S(1)}, u32[]{:S(2)}, u32[]{:S(2)}) collective-permute-start(bf16[32,480]{1,0:T(8,128)(2,1)S(1)} %get-tuple-element.26), channel_id=1, source_target_pairs={{0,24},{2,26},{4,28},{6,30},{8,16},{10,18},{12,20},{14,22},{16,8},... | collective-permute-start | bytes 92168 | tf_op jit(solution)/shard_map/ppermute | solution.py:227
  88.1 0.7 multiply_convert_fusion
  88.8 2.3 %collective-permute-done.22 = bf16[32,480]{1,0:T(8,128)(2,1)S(1)} collective-permute-done((bf16[32,480]{1,0:T(8,128)(2,1)S(1)}, bf16[32,480]{1,0:T(8,128)(2,1)S(1)}, u32[]{:S(2)}, u32[]{:S(2)}) %collective-permute-start.22) | collective-permute-done | bytes 30752 | tf_op jit(solution)/shard_map/ppermute | solution.py:227
  91.1 1.8 %collective-permute-done.21 = bf16[32,480]{1,0:T(8,128)(2,1)S(1)} collective-permute-done((bf16[32,480]{1,0:T(8,128)(2,1)S(1)}, bf16[32,480]{1,0:T(8,128)(2,1)S(1)}, u32[]{:S(2)}, u32[]{:S(2)}) %collective-permute-start.21) | collective-permute-done | bytes 30752 | tf_op jit(solution)/shard_map/ppermute | solution.py:227
  92.9 0.6 convert_add_fusion
  (23 shorter events, 0.1 us)
Async XLA Ops:
  0.6 0.8 copy-start
  2.4 10.2 %collective-permute-start.8 = (bf16[3,32,512]{2,1,0:T(8,128)(2,1)S(1)}, bf16[3,32,512]{2,1,0:T(8,128)(2,1)S(1)}, u32[]{:S(2)}, u32[]{:S(2)}) collective-permute-start(bf16[3,32,512]{2,1,0:T(8,128)(2,1)S(1)} %get-tuple-element.29), channel_id=1, source_target_pairs={{0,16},{2,18},{4,20},{6,22},{8,24},{10,26},{12,28},{14,30},{16,0},... | collective-permute-start | bytes 294920 | tf_op jit(solution)/shard_map/ppermute | solution.py:227
  6.6 6.0 %collective-permute-start.7 = (bf16[3,32,512]{2,1,0:T(8,128)(2,1)S(1)}, bf16[3,32,512]{2,1,0:T(8,128)(2,1)S(1)}, u32[]{:S(2)}, u32[]{:S(2)}) collective-permute-start(bf16[3,32,512]{2,1,0:T(8,128)(2,1)S(1)} %get-tuple-element.29), channel_id=1, source_target_pairs={{0,8},{2,10},{4,12},{6,14},{8,0},{10,2},{12,4},{14,6},{16,24},{18,... | collective-permute-start | bytes 294920 | tf_op jit(solution)/shard_map/ppermute | solution.py:227
  8.1 6.5 %collective-permute-start.9 = (bf16[3,32,512]{2,1,0:T(8,128)(2,1)S(1)}, bf16[3,32,512]{2,1,0:T(8,128)(2,1)S(1)}, u32[]{:S(2)}, u32[]{:S(2)}) collective-permute-start(bf16[3,32,512]{2,1,0:T(8,128)(2,1)S(1)} %get-tuple-element.29), channel_id=1, source_target_pairs={{0,24},{2,26},{4,28},{6,30},{8,16},{10,18},{12,20},{14,22},{16,8},... | collective-permute-start | bytes 294920 | tf_op jit(solution)/shard_map/ppermute | solution.py:227
  14.7 13.1 %collective-permute-start.10 = (bf16[4,3,32,512]{3,2,1,0:T(8,128)(2,1)S(1)}, bf16[4,3,32,512]{3,2,1,0:T(8,128)(2,1)S(1)}, u32[]{:S(2)}, u32[]{:S(2)}) collective-permute-start(bf16[4,3,32,512]{3,2,1,0:T(8,128)(2,1)S(1)} %pad_maximum_fusion.refs_0_), channel_id=1, source_target_pairs={{0,4},{2,6},{4,0},{6,2},{8,12},{10,14},{12,8},{14,10},{16,20},{18,... | collective-permute-start | bytes 1179656 | tf_op jit(solution)/shard_map/ppermute | solution.py:227
  16.3 7.4 %collective-permute-start.2 = (bf16[2,32,512]{2,1,0:T(8,128)(2,1)}, bf16[2,32,512]{2,1,0:T(8,128)(2,1)S(1)}, u32[]{:S(2)}, u32[]{:S(2)}) collective-permute-start(bf16[2,32,512]{2,1,0:T(8,128)(2,1)} %bitcast.35), channel_id=1, source_target_pairs={{0,16},{2,18},{4,20},{6,22},{8,24},{10,26},{12,28},{14,30},{16,0},... | collective-permute-start | bytes 196616 | tf_op jit(solution)/shard_map/ppermute | solution.py:227
  20.0 5.2 %collective-permute-start.1 = (bf16[2,32,512]{2,1,0:T(8,128)(2,1)}, bf16[2,32,512]{2,1,0:T(8,128)(2,1)S(1)}, u32[]{:S(2)}, u32[]{:S(2)}) collective-permute-start(bf16[2,32,512]{2,1,0:T(8,128)(2,1)} %bitcast.36), channel_id=1, source_target_pairs={{0,8},{2,10},{4,12},{6,14},{8,0},{10,2},{12,4},{14,6},{16,24},{18,... | collective-permute-start | bytes 196616 | tf_op jit(solution)/shard_map/ppermute | solution.py:227
  20.0 6.4 %collective-permute-start.3 = (bf16[2,32,512]{2,1,0:T(8,128)(2,1)}, bf16[2,32,512]{2,1,0:T(8,128)(2,1)S(1)}, u32[]{:S(2)}, u32[]{:S(2)}) collective-permute-start(bf16[2,32,512]{2,1,0:T(8,128)(2,1)} %bitcast.37), channel_id=1, source_target_pairs={{0,24},{2,26},{4,28},{6,30},{8,16},{10,18},{12,20},{14,22},{16,8},... | collective-permute-start | bytes 196616 | tf_op jit(solution)/shard_map/ppermute | solution.py:227
  27.2 6.6 %collective-permute-start.4 = (bf16[4,2,32,512]{3,2,1,0:T(8,128)(2,1)S(1)}, bf16[4,2,32,512]{3,2,1,0:T(8,128)(2,1)S(1)}, u32[]{:S(2)}, u32[]{:S(2)}) collective-permute-start(bf16[4,2,32,512]{3,2,1,0:T(8,128)(2,1)S(1)} %pad_maximum_fusion.1.refs_2_), channel_id=1, source_target_pairs={{0,4},{2,6},{4,0},{6,2},{8,12},{10,14},{12,8},{14,10},{16,20},{18,... | collective-permute-start | bytes 786440 | tf_op jit(solution)/shard_map/ppermute | solution.py:227
  27.8 14.4 %collective-permute-start.11 = (bf16[4,3,32,512]{3,2,1,0:T(8,128)(2,1)S(1)}, bf16[4,3,32,512]{3,2,1,0:T(8,128)(2,1)S(1)}, u32[]{:S(2)}, u32[]{:S(2)}) collective-permute-start(bf16[4,3,32,512]{3,2,1,0:T(8,128)(2,1)S(1)} %pad_maximum_fusion.refs_0_), channel_id=1, source_target_pairs={{0,2},{2,0},{4,6},{6,4},{8,10},{10,8},{12,14},{14,12},{16,18},{18,... | collective-permute-start | bytes 1179656 | tf_op jit(solution)/shard_map/ppermute | solution.py:227
  27.8 14.4 %collective-permute-start.12 = (bf16[4,3,32,512]{3,2,1,0:T(8,128)(2,1)S(1)}, bf16[4,3,32,512]{3,2,1,0:T(8,128)(2,1)S(1)}, u32[]{:S(2)}, u32[]{:S(2)}) collective-permute-start(bf16[4,3,32,512]{3,2,1,0:T(8,128)(2,1)S(1)} %collective-permute-done.10.refs_1_), channel_id=1, source_target_pairs={{0,2},{2,0},{4,6},{6,4},{8,10},{10,8},{12,14},{14,12},{16,18},{18,... | collective-permute-start | bytes 1179656 | tf_op jit(solution)/shard_map/ppermute | solution.py:227
  28.3 11.7 %collective-permute-start.5 = (bf16[4,2,32,512]{3,2,1,0:T(8,128)(2,1)S(1)}, bf16[4,2,32,512]{3,2,1,0:T(8,128)(2,1)S(1)}, u32[]{:S(2)}, u32[]{:S(2)}) collective-permute-start(bf16[4,2,32,512]{3,2,1,0:T(8,128)(2,1)S(1)} %pad_maximum_fusion.1.refs_2_), channel_id=1, source_target_pairs={{0,2},{2,0},{4,6},{6,4},{8,10},{10,8},{12,14},{14,12},{16,18},{18,... | collective-permute-start | bytes 786440 | tf_op jit(solution)/shard_map/ppermute | solution.py:227
  33.8 6.1 %collective-permute-start.6 = (bf16[4,2,32,512]{3,2,1,0:T(8,128)(2,1)S(1)}, bf16[4,2,32,512]{3,2,1,0:T(8,128)(2,1)S(1)}, u32[]{:S(2)}, u32[]{:S(2)}) collective-permute-start(bf16[4,2,32,512]{3,2,1,0:T(8,128)(2,1)S(1)} %collective-permute-done.4.refs_3_), channel_id=1, source_target_pairs={{0,2},{2,0},{4,6},{6,4},{8,10},{10,8},{12,14},{14,12},{16,18},{18,... | collective-permute-start | bytes 786440 | tf_op jit(solution)/shard_map/ppermute | solution.py:227
  33.8 6.1 %collective-permute-start = (bf16[128,512]{1,0:T(8,128)(2,1)}, bf16[128,512]{1,0:T(8,128)(2,1)S(1)}, u32[]{:S(2)}, u32[]{:S(2)}) collective-permute-start(bf16[128,512]{1,0:T(8,128)(2,1)} %refs_0_.1), channel_id=1, source_target_pairs={{0,1},{1,0},{2,3},{3,2},{4,5},{5,4},{6,7},{7,6},{8,9},{9,8},{10,11... | collective-permute-start | bytes 393224 | tf_op jit(solution)/shard_map/ppermute | solution.py:227
  43.7 8.7 %collective-permute-start.14 = (bf16[64,512]{1,0:T(8,128)(2,1)S(1)}, bf16[64,512]{1,0:T(8,128)(2,1)S(1)}, u32[]{:S(2)}, u32[]{:S(2)}) collective-permute-start(bf16[64,512]{1,0:T(8,128)(2,1)S(1)} %get-tuple-element.13.normed.refs_2_), channel_id=1, source_target_pairs={{2,4},{6,8},{10,12},{14,16},{18,20},{22,24},{26,28},{4,2},{8,6},{1... | collective-permute-start | bytes 196616 | tf_op jit(solution)/shard_map/ppermute | solution.py:256
  44.4 8.0 %collective-permute-start.13 = (bf16[64,512]{1,0:T(8,128)(2,1)S(1)}, bf16[64,512]{1,0:T(8,128)(2,1)S(1)}, u32[]{:S(2)}, u32[]{:S(2)}) collective-permute-start(bf16[64,512]{1,0:T(8,128)(2,1)S(1)} %get-tuple-element.13.normed.refs_2_), channel_id=1, source_target_pairs={{0,2},{2,0},{4,6},{6,4},{8,10},{10,8},{12,14},{14,12},{16,18},{18,... | collective-permute-start | bytes 196616 | tf_op jit(solution)/shard_map/ppermute | solution.py:227
  47.0 5.4 %copy-start.1 = (bf16[64,480]{1,0:T(8,128)(2,1)S(1)}, bf16[64,480]{1,0:T(8,128)(2,1)}, u32[]{:S(2)}) copy-start(bf16[64,480]{1,0:T(8,128)(2,1)} %refs_1_.1) | copy-start | bytes 184324
  60.6 4.0 %collective-permute-start.16 = (bf16[64,480]{1,0:T(8,128)(2,1)S(1)}, bf16[64,480]{1,0:T(8,128)(2,1)S(1)}, u32[]{:S(2)}, u32[]{:S(2)}) collective-permute-start(bf16[64,480]{1,0:T(8,128)(2,1)S(1)} %get-tuple-element.16.slope_rev), channel_id=1, source_target_pairs={{2,4},{6,8},{10,12},{14,16},{18,20},{22,24},{26,28},{4,2},{8,6},{1... | collective-permute-start | bytes 184328 | tf_op jit(solution)/shard_map/ppermute | solution.py:256
  61.2 4.2 %collective-permute-start.15 = (bf16[64,480]{1,0:T(8,128)(2,1)S(1)}, bf16[64,480]{1,0:T(8,128)(2,1)S(1)}, u32[]{:S(2)}, u32[]{:S(2)}) collective-permute-start(bf16[64,480]{1,0:T(8,128)(2,1)S(1)} %get-tuple-element.16.slope_rev), channel_id=1, source_target_pairs={{0,2},{2,0},{4,6},{6,4},{8,10},{10,8},{12,14},{14,12},{16,18},{18,... | collective-permute-start | bytes 184328 | tf_op jit(solution)/shard_map/ppermute | solution.py:227
  73.3 5.1 %collective-permute-start.18 = (bf16[8,32,480]{2,1,0:T(8,128)(2,1)S(1)}, bf16[8,32,480]{2,1,0:T(8,128)(2,1)S(1)}, u32[]{:S(2)}, u32[]{:S(2)}) collective-permute-start(bf16[8,32,480]{2,1,0:T(8,128)(2,1)S(1)} %get-tuple-element.22), channel_id=1, source_target_pairs={{0,2},{2,0},{4,6},{6,4},{8,10},{10,8},{12,14},{14,12},{16,18},{18,... | collective-permute-start | bytes 737288 | tf_op jit(solution)/shard_map/ppermute | solution.py:227
  74.4 3.9 %collective-permute-start.17 = (bf16[32,512]{1,0:T(8,128)(2,1)S(1)}, bf16[32,512]{1,0:T(8,128)(2,1)S(1)}, u32[]{:S(2)}, u32[]{:S(2)}) collective-permute-start(bf16[32,512]{1,0:T(8,128)(2,1)S(1)} %bitcast.29), channel_id=1, source_target_pairs={{0,1},{1,0},{2,3},{3,2},{4,5},{5,4},{6,7},{7,6},{8,9},{9,8},{10,11... | collective-permute-start | bytes 98312 | tf_op jit(solution)/shard_map/ppermute | solution.py:227
  78.5 5.5 %collective-permute-start.19 = (bf16[4,32,480]{2,1,0:T(8,128)(2,1)S(1)}, bf16[4,32,480]{2,1,0:T(8,128)(2,1)S(1)}, u32[]{:S(2)}, u32[]{:S(2)}) collective-permute-start(bf16[4,32,480]{2,1,0:T(8,128)(2,1)S(1)} %slice.29), channel_id=1, source_target_pairs={{0,4},{2,6},{4,0},{6,2},{8,12},{10,14},{12,8},{14,10},{16,20},{18,... | collective-permute-start | bytes 368648 | tf_op jit(solution)/shard_map/ppermute | solution.py:227
  84.1 4.7 %collective-permute-start.20 = (bf16[32,480]{1,0:T(8,128)(2,1)S(1)}, bf16[32,480]{1,0:T(8,128)(2,1)S(1)}, u32[]{:S(2)}, u32[]{:S(2)}) collective-permute-start(bf16[32,480]{1,0:T(8,128)(2,1)S(1)} %get-tuple-element.25), channel_id=1, source_target_pairs={{0,8},{2,10},{4,12},{6,14},{8,0},{10,2},{12,4},{14,6},{16,24},{18,... | collective-permute-start | bytes 92168 | tf_op jit(solution)/shard_map/ppermute | solution.py:227
  85.4 5.7 %collective-permute-start.22 = (bf16[32,480]{1,0:T(8,128)(2,1)S(1)}, bf16[32,480]{1,0:T(8,128)(2,1)S(1)}, u32[]{:S(2)}, u32[]{:S(2)}) collective-permute-start(bf16[32,480]{1,0:T(8,128)(2,1)S(1)} %get-tuple-element.26), channel_id=1, source_target_pairs={{0,24},{2,26},{4,28},{6,30},{8,16},{10,18},{12,20},{14,22},{16,8},... | collective-permute-start | bytes 92168 | tf_op jit(solution)/shard_map/ppermute | solution.py:227
  88.1 4.8 %collective-permute-start.21 = (bf16[32,480]{1,0:T(8,128)(2,1)S(1)}, bf16[32,480]{1,0:T(8,128)(2,1)S(1)}, u32[]{:S(2)}, u32[]{:S(2)}) collective-permute-start(bf16[32,480]{1,0:T(8,128)(2,1)S(1)} %get-tuple-element.27), channel_id=1, source_target_pairs={{0,16},{2,18},{4,20},{6,22},{8,24},{10,26},{12,28},{14,30},{16,0},... | collective-permute-start | bytes 92168 | tf_op jit(solution)/shard_map/ppermute | solution.py:227

commit v7 on v4

--- a/solution.py
+++ b/solution.py
@@ -248,6 +248,15 @@
     return jnp.stack(pieces), offs
 
 
+def spread_doubling(shard, count):
+    stack, offs = shard[None], [0]
+    for mask in (count // 2, count // 4):
+        got = swap(stack, "tm", mask)
+        stack = jnp.concatenate([stack, got], 0)
+        offs = offs + [o ^ mask for o in offs]
+    return stack, offs
+
+
 def spread_far(stack, offs, count):
     stacks, layout = [stack], [offs]
     mask = count // 8
@@ -267,7 +276,8 @@
     to_b = tail if tail is head else jnp.where(parity == 0, head, tail)
     pairs = [(2 * i + 1, 2 * i + 2) for i in range(count // 2 - 1)]
     got_b = lax.ppermute(to_b, "tm", pairs + [(b, a) for a, b in pairs])
-    return swap(to_a, "tm", 1), got_b
+    got_a = swap(to_a, "tm", 1)
+    return got_a, got_b
 
 
 def on_device(features, weight_five, weight_six, projection, pos_weight, pos_bias, cotangent):
@@ -288,14 +298,14 @@
     proj_half = jnp.pad(proj_half, ((0, 0), (0, channels - columns)))
     five, offs = spread_near(jnp.transpose(weight_five, (0, 2, 1)), members)
     six, _ = spread_near(jnp.transpose(weight_six, (0, 2, 1)), members)
-    last, _ = spread_near(proj_half[None], members)
+    last, last_offs = spread_doubling(proj_half[None], members)
     five, layout = spread_far(five, offs, members)
     six, _ = spread_far(six, offs, members)
-    last, _ = spread_far(last, offs, members)
+    last, last_layout = spread_far(last, last_offs, members)
     common = dict(layout=layout)
     taps_scratch = [pltpu.VMEM((2, channels, channels), BF16)]
 
-    cut = (groups + 1) // 2
+    cut = max(1, groups - 1)
     tap_sems = lambda count: pltpu.SemaphoreType.DMA((count, 5))
     act_five, w_low = pl.pallas_call(
         functools.partial(five_body, count=slots, **common),
@@ -338,7 +348,7 @@
         pltpu.VMEM((groups, half, width), F32),
     ]
     encoded, slope_rev, proj = pl.pallas_call(
-        functools.partial(forward_body, held=len(weights), **common),
+        functools.partial(forward_body, held=len(weights), layout=last_layout),
         in_specs=[SMEM_SPEC] + vmem_specs(3 + len(last) + len(weights) + 2),
         out_specs=vmem_specs(3),
         out_shape=[

time: 91.6 us -> 91.5 us (level)
  starting transfers between devices: 41.2 us -> 37.5 us
  waiting for transfers between devices: 21.7 us -> 25.4 us
    ppermute x27 -> x26, starting transfers between devices: 39.9 us -> 36.2 us  [swap(): return lax.ppermute(values, axis, [(i, i ^ mask) for i in range(count)])]
    ppermute x27 -> x26, waiting for transfers between devices: 21.7 us -> 25.4 us  [swap(): return lax.ppermute(values, axis, [(i, i ^ mask) for i in range(count)])]
    pallas_call x1, Pallas kernels: 4.34 us -> 5.65 us  [on_device(): pl.pallas_call(functools.partial(five_body, count=slots, **common), in_sp...]
    pallas_call x1, Pallas kernels: 3.8 us -> 2.66 us  [on_device(): pl.pallas_call(functools.partial(six_body, count=slots, start=cut if rest...]
  transfers between devices with their start and end apart: 29 -> 28, of which waited for: 12 -> 12; matrix products, arithmetic and copies ran while one was open for 3% -> 3% of each run, Pallas kernels for 9% -> 9%
where the time goes in v7:
time: 91.5 us; the launch traced here: 91.3 us
  starting transfers between devices  37.5 us (41%)
  waiting for transfers between devices  25.4 us (28%)
  Pallas kernels  23.9 us (26%)
  other arithmetic  3.42 us (4%)
    ppermute x26, starting transfers between devices, swap(): return lax.ppermute(values, axis, [(i, i ^ mask) for i in range(count)])  36.2 us
    ppermute x26, waiting for transfers between devices, swap(): return lax.ppermute(values, axis, [(i, i ^ mask) for i in range(count)])  25.4 us
    pallas_call x1, Pallas kernels, on_device(): pl.pallas_call(functools.partial(backward_body, scale=scale, order=order,...  7.86 us
    pallas_call x1, Pallas kernels, on_device(): pl.pallas_call(functools.partial(forward_body, held=len(weights), layout=...  7.78 us
    pallas_call x1, Pallas kernels, on_device(): pl.pallas_call(functools.partial(five_body, count=slots, **common), in_sp...  5.65 us
    pallas_call x1, Pallas kernels, on_device(): pl.pallas_call(functools.partial(six_body, count=slots, start=cut if rest...  2.66 us
  transfers between devices with their start and end apart: 28, of which 12 were waited for; matrix products, arithmetic and copies ran while one was open for 3% of the time, Pallas kernels for 9%

profile of v7, /device:TPU:0, one launch (start us, length us, event | category | flops | bytes accessed | tf_op | source)
XLA Modules:
  0.0 91.3 jit_solution(9318412162691815201)
XLA Ops:
  0.6 5.1 %collective-permute-start.3 = (bf16[2,32,512]{2,1,0:T(8,128)(2,1)}, bf16[2,32,512]{2,1,0:T(8,128)(2,1)S(1)}, u32[]{:S(2)}, u32[]{:S(2)}) collective-permute-start(bf16[2,32,512]{2,1,0:T(8,128)(2,1)} %bitcast.32), channel_id=1, source_target_pairs={{0,24},{2,26},{4,28},{6,30},{8,16},{10,18},{12,20},{14,22},{16,8},... | collective-permute-start | bytes 196616 | tf_op jit(solution)/shard_map/ppermute | solution.py:240
  5.8 0.6 collective-permute-start.1
  6.4 3.7 %collective-permute-start.9 = (bf16[2,32,512]{2,1,0:T(8,128)(2,1)}, bf16[2,32,512]{2,1,0:T(8,128)(2,1)S(1)}, u32[]{:S(2)}, u32[]{:S(2)}) collective-permute-start(bf16[2,32,512]{2,1,0:T(8,128)(2,1)} %bitcast.36), channel_id=1, source_target_pairs={{0,24},{2,26},{4,28},{6,30},{8,16},{10,18},{12,20},{14,22},{16,8},... | collective-permute-start | bytes 196616 | tf_op jit(solution)/shard_map/ppermute | solution.py:240
  10.2 0.1 constant_dynamic-slice_fusion
  10.3 0.9 %collective-permute-start.7 = (bf16[2,32,512]{2,1,0:T(8,128)(2,1)}, bf16[2,32,512]{2,1,0:T(8,128)(2,1)S(1)}, u32[]{:S(2)}, u32[]{:S(2)}) collective-permute-start(bf16[2,32,512]{2,1,0:T(8,128)(2,1)} %bitcast.38), channel_id=1, source_target_pairs={{0,8},{2,10},{4,12},{6,14},{8,0},{10,2},{12,4},{14,6},{16,24},{18,... | collective-permute-start | bytes 196616 | tf_op jit(solution)/shard_map/ppermute | solution.py:240
  11.2 3.5 %collective-permute-done.2 = bf16[2,32,512]{2,1,0:T(8,128)(2,1)S(1)} collective-permute-done((bf16[2,32,512]{2,1,0:T(8,128)(2,1)}, bf16[2,32,512]{2,1,0:T(8,128)(2,1)S(1)}, u32[]{:S(2)}, u32[]{:S(2)}) %collective-permute-start.2) | collective-permute-done | bytes 65568 | tf_op jit(solution)/shard_map/ppermute | solution.py:240
  14.7 0.9 pad_maximum_fusion.refs_2_
  15.6 1.4 %collective-permute-start.4 = (bf16[4,2,32,512]{3,2,1,0:T(8,128)(2,1)S(1)}, bf16[4,2,32,512]{3,2,1,0:T(8,128)(2,1)S(1)}, u32[]{:S(2)}, u32[]{:S(2)}) collective-permute-start(bf16[4,2,32,512]{3,2,1,0:T(8,128)(2,1)S(1)} %pad_maximum_fusion.refs_2_), channel_id=1, source_target_pairs={{0,4},{2,6},{4,0},{6,2},{8,12},{10,14},{12,8},{14,10},{16,20},{18,... | collective-permute-start | bytes 786440 | tf_op jit(solution)/shard_map/ppermute | solution.py:240
  16.9 0.3 collective-permute-done.8
  17.2 0.9 pad_maximum_fusion.1.refs_0_
  18.1 1.6 %collective-permute-start.10 = (bf16[4,2,32,512]{3,2,1,0:T(8,128)(2,1)S(1)}, bf16[4,2,32,512]{3,2,1,0:T(8,128)(2,1)S(1)}, u32[]{:S(2)}, u32[]{:S(2)}) collective-permute-start(bf16[4,2,32,512]{3,2,1,0:T(8,128)(2,1)S(1)} %pad_maximum_fusion.1.refs_0_), channel_id=1, source_target_pairs={{0,4},{2,6},{4,0},{6,2},{8,12},{10,14},{12,8},{14,10},{16,20},{18,... | collective-permute-start | bytes 786440 | tf_op jit(solution)/shard_map/ppermute | solution.py:240
  19.7 1.1 %collective-permute-start.15 = (bf16[1,1,32,512]{3,2,1,0:T(8,128)(2,1)S(1)}, bf16[1,1,32,512]{3,2,1,0:T(8,128)(2,1)S(1)}, u32[]{:S(2)}, u32[]{:S(2)}) collective-permute-start(bf16[1,1,32,512]{3,2,1,0:T(8,128)(2,1)S(1)} %pad_bitcast_fusion), channel_id=1, source_target_pairs={{0,16},{2,18},{4,20},{6,22},{8,24},{10,26},{12,28},{14,30},{16,0},... | collective-permute-start | bytes 98312 | tf_op jit(solution)/shard_map/ppermute | solution.py:240
  20.8 3.8 %collective-permute-done.15 = bf16[1,1,32,512]{3,2,1,0:T(8,128)(2,1)S(1)} collective-permute-done((bf16[1,1,32,512]{3,2,1,0:T(8,128)(2,1)S(1)}, bf16[1,1,32,512]{3,2,1,0:T(8,128)(2,1)S(1)}, u32[]{:S(2)}, u32[]{:S(2)}) %collective-permute-start.15) | collective-permute-done | bytes 32800 | tf_op jit(solution)/shard_map/ppermute | solution.py:240
  24.7 0.3 collective-permute-start.16
  25.0 1.5 %collective-permute-start = (bf16[128,512]{1,0:T(8,128)(2,1)}, bf16[128,512]{1,0:T(8,128)(2,1)S(1)}, u32[]{:S(2)}, u32[]{:S(2)}) collective-permute-start(bf16[128,512]{1,0:T(8,128)(2,1)} %refs_0_.1), channel_id=1, source_target_pairs={{0,1},{1,0},{2,3},{3,2},{4,5},{5,4},{6,7},{7,6},{8,9},{9,8},{10,11... | collective-permute-start | bytes 393224 | tf_op jit(solution)/shard_map/ppermute | solution.py:240
  26.5 2.5 %collective-permute-done.16 = bf16[2,1,32,512]{3,2,1,0:T(8,128)(2,1)S(1)} collective-permute-done((bf16[2,1,32,512]{3,2,1,0:T(8,128)(2,1)S(1)}, bf16[2,1,32,512]{3,2,1,0:T(8,128)(2,1)S(1)}, u32[]{:S(2)}, u32[]{:S(2)}) %collective-permute-start.16) | collective-permute-done | bytes 65568 | tf_op jit(solution)/shard_map/ppermute | solution.py:240
  29.0 0.5 collective-permute-start.6
  29.5 0.1 collective-permute-start.12
  29.6 0.5 collective-permute-done.refs_1_
  30.1 0.5 collective-permute-start.17
  30.6 4.9 %collective-permute-done.17.refs_1_ = bf16[4,1,32,512]{3,2,1,0:T(8,128)(2,1)S(1)} collective-permute-done((bf16[4,1,32,512]{3,2,1,0:T(8,128)(2,1)S(1)}, bf16[4,1,32,512]{3,2,1,0:T(8,128)(2,1)S(1)}, u32[]{:S(2)}, u32[]{:S(2)}) %collective-permute-start.17) | collective-permute-done | bytes 131104 | tf_op jit(solution)/shard_map/ppermute | solution.py:240
  35.5 0.5 collective-permute-start.19
  36.0 0.1 pad_add_fusion.where
  36.1 5.6 %five.1 = (bf16[128,512]{1,0:T(8,128)(2,1)S(1)}, bf16[3,120,120,128]{3,2,1,0:T(8,128)(2,1)S(1)}) custom-call(s32[2]{0:T(128)S(1)} %pad_add_fusion.where, bf16[128,512]{1,0:T(8,128)(2,1)} %refs_0_.1, bf16[128,512]{1,0:T(8,128)(2,1)S(1)} %collective-permute-done.refs_1_, bf16[4,2,32,512]{3,2,1,0:T(8,128)(2,1)S(1)} %pad_maximum_fusion.refs_2_, ...), custom_call_target="tpu_custom_call" | custom-call | tf_op jit(solution)/shard_map/five/pallas_call | solution.py:310
  41.8 2.7 %six.1 = (bf16[64,512]{1,0:T(8,128)(2,1)S(1)}, f32[32,512]{1,0:T(8,128)S(1)}, f32[32,128]{1,0:T(8,128)S(1)}, bf16[1,120,120,128]{3,2,1,0:T(8,128)(2,1)S(1)}) custom-call(s32[2]{0:T(128)S(1)} %pad_add_fusion.where, bf16[128,512]{1,0:T(8,128)(2,1)S(1)} %get-tuple-element.16.act, bf16[4,2,32,512]{3,2,1,0:T(8,128)(2,1)S(1)} %pad_maximum_fusion.1.refs_0_, ...), custom_call_target="tpu_custom_call" | custom-call | tf_op jit(solution)/shard_map/six/pallas_call | solution.py:324
  44.5 0.1 collective-permute-start.13
  44.6 0.7 collective-permute-start.14
  45.3 0.5 collective-permute-done.13.got_a
  45.8 7.8 %forward.1 = (bf16[64,480]{1,0:T(8,128)(2,1)}, bf16[64,480]{1,0:T(8,128)(2,1)S(1)}, bf16[512,480]{1,0:T(8,128)(2,1)S(1)}) custom-call(s32[2]{0:T(128)S(1)} %pad_add_fusion.where, bf16[64,512]{1,0:T(8,128)(2,1)S(1)} %get-tuple-element.17.normed.refs_3_, bf16[64,512]{1,0:T(8,128)(2,1)S(1)} %collective-permute-done.13.got_a, ...), custom_call_target="tpu_custom_call" | custom-call | tf_op jit(solution)/shard_map/forward/pallas_call | solution.py:350
  53.6 4.8 %collective-permute-start.20 = (bf16[64,480]{1,0:T(8,128)(2,1)S(1)}, bf16[64,480]{1,0:T(8,128)(2,1)S(1)}, u32[]{:S(2)}, u32[]{:S(2)}) collective-permute-start(bf16[64,480]{1,0:T(8,128)(2,1)S(1)} %get-tuple-element.22.slope_rev), channel_id=1, source_target_pairs={{0,2},{2,0},{4,6},{6,4},{8,10},{10,8},{12,14},{14,12},{16,18},{18,... | collective-permute-start | bytes 184328 | tf_op jit(solution)/shard_map/ppermute | solution.py:240
  58.4 0.7 collective-permute-start.21
  59.1 0.2 collective-permute-done.20.got_a
  59.3 7.9 %backward.1 = (bf16[8,32,480]{2,1,0:T(8,128)(2,1)S(1)}, bf16[8,32,480]{2,1,0:T(8,128)(2,1)S(1)}, f32[32,512]{1,0:T(8,128)S(1)}, bf16[1,32,512]{2,1,0:T(8,128)(2,1)S(1)}) custom-call(s32[2]{0:T(128)S(1)} %pad_add_fusion.where, bf16[64,480]{1,0:T(8,128)(2,1)S(1)} %get-tuple-element.22.slope_rev, bf16[64,480]{1,0:T(8,128)(2,1)S(1)} %collective-permute-done.20.got_a, ...), custom_call_target="tpu_custom_call" | custom-call | tf_op jit(solution)/shard_map/backward/pallas_call | solution.py:377
  67.2 4.7 %collective-permute-start.23 = (bf16[8,32,480]{2,1,0:T(8,128)(2,1)S(1)}, bf16[8,32,480]{2,1,0:T(8,128)(2,1)S(1)}, u32[]{:S(2)}, u32[]{:S(2)}) collective-permute-start(bf16[8,32,480]{2,1,0:T(8,128)(2,1)S(1)} %get-tuple-element.28), channel_id=1, source_target_pairs={{0,2},{2,0},{4,6},{6,4},{8,10},{10,8},{12,14},{14,12},{16,18},{18,... | collective-permute-start | bytes 737288 | tf_op jit(solution)/shard_map/ppermute | solution.py:240
  71.9 1.5 %collective-permute-start.22 = (bf16[32,512]{1,0:T(8,128)(2,1)S(1)}, bf16[32,512]{1,0:T(8,128)(2,1)S(1)}, u32[]{:S(2)}, u32[]{:S(2)}) collective-permute-start(bf16[32,512]{1,0:T(8,128)(2,1)S(1)} %bitcast.29), channel_id=1, source_target_pairs={{0,1},{1,0},{2,3},{3,2},{4,5},{5,4},{6,7},{7,6},{8,9},{9,8},{10,11... | collective-permute-start | bytes 98312 | tf_op jit(solution)/shard_map/ppermute | solution.py:240
  73.4 0.1 slice_reduce_fusion
  73.5 2.3 %collective-permute-done.22 = bf16[32,512]{1,0:T(8,128)(2,1)S(1)} collective-permute-done((bf16[32,512]{1,0:T(8,128)(2,1)S(1)}, bf16[32,512]{1,0:T(8,128)(2,1)S(1)}, u32[]{:S(2)}, u32[]{:S(2)}) %collective-permute-start.22) | collective-permute-done | bytes 32800 | tf_op jit(solution)/shard_map/ppermute | solution.py:240
  75.8 0.1 fusion
  76.0 0.1 add_convert_fusion
  76.1 2.4 %collective-permute-start.24 = (bf16[4,32,480]{2,1,0:T(8,128)(2,1)S(1)}, bf16[4,32,480]{2,1,0:T(8,128)(2,1)S(1)}, u32[]{:S(2)}, u32[]{:S(2)}) collective-permute-start(bf16[4,32,480]{2,1,0:T(8,128)(2,1)S(1)} %slice.29), channel_id=1, source_target_pairs={{0,4},{2,6},{4,0},{6,2},{8,12},{10,14},{12,8},{14,10},{16,20},{18,... | collective-permute-start | bytes 368648 | tf_op jit(solution)/shard_map/ppermute | solution.py:240
  78.4 2.9 %collective-permute-done.24 = bf16[4,32,480]{2,1,0:T(8,128)(2,1)S(1)} collective-permute-done((bf16[4,32,480]{2,1,0:T(8,128)(2,1)S(1)}, bf16[4,32,480]{2,1,0:T(8,128)(2,1)S(1)}, u32[]{:S(2)}, u32[]{:S(2)}) %collective-permute-start.24) | collective-permute-done | bytes 122912 | tf_op jit(solution)/shard_map/ppermute | solution.py:240
  81.4 4.1 %collective-permute-start.27 = (bf16[32,480]{1,0:T(8,128)(2,1)S(1)}, bf16[32,480]{1,0:T(8,128)(2,1)S(1)}, u32[]{:S(2)}, u32[]{:S(2)}) collective-permute-start(bf16[32,480]{1,0:T(8,128)(2,1)S(1)} %get-tuple-element.32), channel_id=1, source_target_pairs={{0,24},{2,26},{4,28},{6,30},{8,16},{10,18},{12,20},{14,22},{16,8},... | collective-permute-start | bytes 92168 | tf_op jit(solution)/shard_map/ppermute | solution.py:240
  85.6 0.3 collective-permute-start.26
  85.8 0.4 collective-permute-start.25
  86.2 0.7 multiply_convert_fusion
  86.9 0.7 collective-permute-done.27
  87.6 3.1 %collective-permute-done.26 = bf16[32,480]{1,0:T(8,128)(2,1)S(1)} collective-permute-done((bf16[32,480]{1,0:T(8,128)(2,1)S(1)}, bf16[32,480]{1,0:T(8,128)(2,1)S(1)}, u32[]{:S(2)}, u32[]{:S(2)}) %collective-permute-start.26) | collective-permute-done | bytes 30752 | tf_op jit(solution)/shard_map/ppermute | solution.py:240
  90.7 0.6 convert_add_fusion
  (35 shorter events, 0.2 us)
Async XLA Ops:
  0.6 9.6 %copy-start = (bf16[32,960]{1,0:T(8,128)(2,1)S(1)}, bf16[32,960]{1,0:T(8,128)(2,1)}, u32[]{:S(2)}) copy-start(bf16[32,960]{1,0:T(8,128)(2,1)} %param.10) | copy-start | bytes 184324
  0.6 9.6 %collective-permute-start.3 = (bf16[2,32,512]{2,1,0:T(8,128)(2,1)}, bf16[2,32,512]{2,1,0:T(8,128)(2,1)S(1)}, u32[]{:S(2)}, u32[]{:S(2)}) collective-permute-start(bf16[2,32,512]{2,1,0:T(8,128)(2,1)} %bitcast.32), channel_id=1, source_target_pairs={{0,24},{2,26},{4,28},{6,30},{8,16},{10,18},{12,20},{14,22},{16,8},... | collective-permute-start | bytes 196616 | tf_op jit(solution)/shard_map/ppermute | solution.py:240
  5.8 8.9 %collective-permute-start.2 = (bf16[2,32,512]{2,1,0:T(8,128)(2,1)}, bf16[2,32,512]{2,1,0:T(8,128)(2,1)S(1)}, u32[]{:S(2)}, u32[]{:S(2)}) collective-permute-start(bf16[2,32,512]{2,1,0:T(8,128)(2,1)} %bitcast.33), channel_id=1, source_target_pairs={{0,16},{2,18},{4,20},{6,22},{8,24},{10,26},{12,28},{14,30},{16,0},... | collective-permute-start | bytes 196616 | tf_op jit(solution)/shard_map/ppermute | solution.py:240
  5.8 8.9 %collective-permute-start.1 = (bf16[2,32,512]{2,1,0:T(8,128)(2,1)}, bf16[2,32,512]{2,1,0:T(8,128)(2,1)S(1)}, u32[]{:S(2)}, u32[]{:S(2)}) collective-permute-start(bf16[2,32,512]{2,1,0:T(8,128)(2,1)} %bitcast.34), channel_id=1, source_target_pairs={{0,8},{2,10},{4,12},{6,14},{8,0},{10,2},{12,4},{14,6},{16,24},{18,... | collective-permute-start | bytes 196616 | tf_op jit(solution)/shard_map/ppermute | solution.py:240
  6.4 10.5 %collective-permute-start.9 = (bf16[2,32,512]{2,1,0:T(8,128)(2,1)}, bf16[2,32,512]{2,1,0:T(8,128)(2,1)S(1)}, u32[]{:S(2)}, u32[]{:S(2)}) collective-permute-start(bf16[2,32,512]{2,1,0:T(8,128)(2,1)} %bitcast.36), channel_id=1, source_target_pairs={{0,24},{2,26},{4,28},{6,30},{8,16},{10,18},{12,20},{14,22},{16,8},... | collective-permute-start | bytes 196616 | tf_op jit(solution)/shard_map/ppermute | solution.py:240
  10.2 7.0 %collective-permute-start.8 = (bf16[2,32,512]{2,1,0:T(8,128)(2,1)}, bf16[2,32,512]{2,1,0:T(8,128)(2,1)S(1)}, u32[]{:S(2)}, u32[]{:S(2)}) collective-permute-start(bf16[2,32,512]{2,1,0:T(8,128)(2,1)} %bitcast.37), channel_id=1, source_target_pairs={{0,16},{2,18},{4,20},{6,22},{8,24},{10,26},{12,28},{14,30},{16,0},... | collective-permute-start | bytes 196616 | tf_op jit(solution)/shard_map/ppermute | solution.py:240
  10.3 7.0 %collective-permute-start.7 = (bf16[2,32,512]{2,1,0:T(8,128)(2,1)}, bf16[2,32,512]{2,1,0:T(8,128)(2,1)S(1)}, u32[]{:S(2)}, u32[]{:S(2)}) collective-permute-start(bf16[2,32,512]{2,1,0:T(8,128)(2,1)} %bitcast.38), channel_id=1, source_target_pairs={{0,8},{2,10},{4,12},{6,14},{8,0},{10,2},{12,4},{14,6},{16,24},{18,... | collective-permute-start | bytes 196616 | tf_op jit(solution)/shard_map/ppermute | solution.py:240
  15.6 13.4 %collective-permute-start.4 = (bf16[4,2,32,512]{3,2,1,0:T(8,128)(2,1)S(1)}, bf16[4,2,32,512]{3,2,1,0:T(8,128)(2,1)S(1)}, u32[]{:S(2)}, u32[]{:S(2)}) collective-permute-start(bf16[4,2,32,512]{3,2,1,0:T(8,128)(2,1)S(1)} %pad_maximum_fusion.refs_2_), channel_id=1, source_target_pairs={{0,4},{2,6},{4,0},{6,2},{8,12},{10,14},{12,8},{14,10},{16,20},{18,... | collective-permute-start | bytes 786440 | tf_op jit(solution)/shard_map/ppermute | solution.py:240
  18.1 11.4 %collective-permute-start.10 = (bf16[4,2,32,512]{3,2,1,0:T(8,128)(2,1)S(1)}, bf16[4,2,32,512]{3,2,1,0:T(8,128)(2,1)S(1)}, u32[]{:S(2)}, u32[]{:S(2)}) collective-permute-start(bf16[4,2,32,512]{3,2,1,0:T(8,128)(2,1)S(1)} %pad_maximum_fusion.1.refs_0_), channel_id=1, source_target_pairs={{0,4},{2,6},{4,0},{6,2},{8,12},{10,14},{12,8},{14,10},{16,20},{18,... | collective-permute-start | bytes 786440 | tf_op jit(solution)/shard_map/ppermute | solution.py:240
  19.7 5.0 %collective-permute-start.15 = (bf16[1,1,32,512]{3,2,1,0:T(8,128)(2,1)S(1)}, bf16[1,1,32,512]{3,2,1,0:T(8,128)(2,1)S(1)}, u32[]{:S(2)}, u32[]{:S(2)}) collective-permute-start(bf16[1,1,32,512]{3,2,1,0:T(8,128)(2,1)S(1)} %pad_bitcast_fusion), channel_id=1, source_target_pairs={{0,16},{2,18},{4,20},{6,22},{8,24},{10,26},{12,28},{14,30},{16,0},... | collective-permute-start | bytes 98312 | tf_op jit(solution)/shard_map/ppermute | solution.py:240
  24.7 4.3 %collective-permute-start.16 = (bf16[2,1,32,512]{3,2,1,0:T(8,128)(2,1)S(1)}, bf16[2,1,32,512]{3,2,1,0:T(8,128)(2,1)S(1)}, u32[]{:S(2)}, u32[]{:S(2)}) collective-permute-start(bf16[2,1,32,512]{3,2,1,0:T(8,128)(2,1)S(1)} %pad_maximum_fusion.3), channel_id=1, source_target_pairs={{0,8},{2,10},{4,12},{6,14},{8,0},{10,2},{12,4},{14,6},{16,24},{18,... | collective-permute-start | bytes 196616 | tf_op jit(solution)/shard_map/ppermute | solution.py:240
  25.0 5.2 %collective-permute-start = (bf16[128,512]{1,0:T(8,128)(2,1)}, bf16[128,512]{1,0:T(8,128)(2,1)S(1)}, u32[]{:S(2)}, u32[]{:S(2)}) collective-permute-start(bf16[128,512]{1,0:T(8,128)(2,1)} %refs_0_.1), channel_id=1, source_target_pairs={{0,1},{1,0},{2,3},{3,2},{4,5},{5,4},{6,7},{7,6},{8,9},{9,8},{10,11... | collective-permute-start | bytes 393224 | tf_op jit(solution)/shard_map/ppermute | solution.py:240
  26.4 9.1 %collective-permute-start.5 = (bf16[4,2,32,512]{3,2,1,0:T(8,128)(2,1)S(1)}, bf16[4,2,32,512]{3,2,1,0:T(8,128)(2,1)S(1)}, u32[]{:S(2)}, u32[]{:S(2)}) collective-permute-start(bf16[4,2,32,512]{3,2,1,0:T(8,128)(2,1)S(1)} %pad_maximum_fusion.refs_2_), channel_id=1, source_target_pairs={{0,2},{2,0},{4,6},{6,4},{8,10},{10,8},{12,14},{14,12},{16,18},{18,... | collective-permute-start | bytes 786440 | tf_op jit(solution)/shard_map/ppermute | solution.py:240
  29.0 12.8 %collective-permute-start.11 = (bf16[4,2,32,512]{3,2,1,0:T(8,128)(2,1)S(1)}, bf16[4,2,32,512]{3,2,1,0:T(8,128)(2,1)S(1)}, u32[]{:S(2)}, u32[]{:S(2)}) collective-permute-start(bf16[4,2,32,512]{3,2,1,0:T(8,128)(2,1)S(1)} %pad_maximum_fusion.1.refs_0_), channel_id=1, source_target_pairs={{0,2},{2,0},{4,6},{6,4},{8,10},{10,8},{12,14},{14,12},{16,18},{18,... | collective-permute-start | bytes 786440 | tf_op jit(solution)/shard_map/ppermute | solution.py:240
  29.0 7.1 %collective-permute-start.6 = (bf16[4,2,32,512]{3,2,1,0:T(8,128)(2,1)S(1)}, bf16[4,2,32,512]{3,2,1,0:T(8,128)(2,1)S(1)}, u32[]{:S(2)}, u32[]{:S(2)}) collective-permute-start(bf16[4,2,32,512]{3,2,1,0:T(8,128)(2,1)S(1)} %collective-permute-done.4.refs_3_), channel_id=1, source_target_pairs={{0,2},{2,0},{4,6},{6,4},{8,10},{10,8},{12,14},{14,12},{16,18},{18,... | collective-permute-start | bytes 786440 | tf_op jit(solution)/shard_map/ppermute | solution.py:240
  29.5 12.3 %collective-permute-start.12 = (bf16[4,2,32,512]{3,2,1,0:T(8,128)(2,1)S(1)}, bf16[4,2,32,512]{3,2,1,0:T(8,128)(2,1)S(1)}, u32[]{:S(2)}, u32[]{:S(2)}) collective-permute-start(bf16[4,2,32,512]{3,2,1,0:T(8,128)(2,1)S(1)} %collective-permute-done.10.refs_1_), channel_id=1, source_target_pairs={{0,2},{2,0},{4,6},{6,4},{8,10},{10,8},{12,14},{14,12},{16,18},{18,... | collective-permute-start | bytes 786440 | tf_op jit(solution)/shard_map/ppermute | solution.py:240
  30.1 5.4 %collective-permute-start.17 = (bf16[4,1,32,512]{3,2,1,0:T(8,128)(2,1)S(1)}, bf16[4,1,32,512]{3,2,1,0:T(8,128)(2,1)S(1)}, u32[]{:S(2)}, u32[]{:S(2)}) collective-permute-start(bf16[4,1,32,512]{3,2,1,0:T(8,128)(2,1)S(1)} %pad_maximum_fusion.2.refs_0_), channel_id=1, source_target_pairs={{0,4},{2,6},{4,0},{6,2},{8,12},{10,14},{12,8},{14,10},{16,20},{18,... | collective-permute-start | bytes 393224 | tf_op jit(solution)/shard_map/ppermute | solution.py:240
  35.5 9.7 %collective-permute-start.18 = (bf16[4,1,32,512]{3,2,1,0:T(8,128)(2,1)S(1)}, bf16[4,1,32,512]{3,2,1,0:T(8,128)(2,1)S(1)}, u32[]{:S(2)}, u32[]{:S(2)}) collective-permute-start(bf16[4,1,32,512]{3,2,1,0:T(8,128)(2,1)S(1)} %pad_maximum_fusion.2.refs_0_), channel_id=1, source_target_pairs={{0,2},{2,0},{4,6},{6,4},{8,10},{10,8},{12,14},{14,12},{16,18},{18,... | collective-permute-start | bytes 393224 | tf_op jit(solution)/shard_map/ppermute | solution.py:240
  35.5 9.7 %collective-permute-start.19 = (bf16[4,1,32,512]{3,2,1,0:T(8,128)(2,1)S(1)}, bf16[4,1,32,512]{3,2,1,0:T(8,128)(2,1)S(1)}, u32[]{:S(2)}, u32[]{:S(2)}) collective-permute-start(bf16[4,1,32,512]{3,2,1,0:T(8,128)(2,1)S(1)} %collective-permute-done.17.refs_1_), channel_id=1, source_target_pairs={{0,2},{2,0},{4,6},{6,4},{8,10},{10,8},{12,14},{14,12},{16,18},{18,... | collective-permute-start | bytes 393224 | tf_op jit(solution)/shard_map/ppermute | solution.py:240
  41.8 3.5 %copy-start.2 = (bf16[480]{0:T(512)(128)(2,1)S(1)}, bf16[480]{0:T(512)(128)(2,1)}, u32[]{:S(2)}) copy-start(bf16[480]{0:T(512)(128)(2,1)} %param.12) | copy-start | bytes 2884
  41.8 4.0 %copy-start.1 = (bf16[64,480]{1,0:T(8,128)(2,1)S(1)}, bf16[64,480]{1,0:T(8,128)(2,1)}, u32[]{:S(2)}) copy-start(bf16[64,480]{1,0:T(8,128)(2,1)} %refs_2_.1) | copy-start | bytes 184324
  44.5 1.3 %collective-permute-start.13 = (bf16[64,512]{1,0:T(8,128)(2,1)S(1)}, bf16[64,512]{1,0:T(8,128)(2,1)S(1)}, u32[]{:S(2)}, u32[]{:S(2)}) collective-permute-start(bf16[64,512]{1,0:T(8,128)(2,1)S(1)} %get-tuple-element.17.normed.refs_3_), channel_id=1, source_target_pairs={{0,2},{2,0},{4,6},{6,4},{8,10},{10,8},{12,14},{14,12},{16,18},{18,... | collective-permute-start | bytes 196616 | tf_op jit(solution)/shard_map/ppermute | solution.py:240
  44.6 1.2 %collective-permute-start.14 = (bf16[64,512]{1,0:T(8,128)(2,1)S(1)}, bf16[64,512]{1,0:T(8,128)(2,1)S(1)}, u32[]{:S(2)}, u32[]{:S(2)}) collective-permute-start(bf16[64,512]{1,0:T(8,128)(2,1)S(1)} %get-tuple-element.17.normed.refs_3_), channel_id=1, source_target_pairs={{2,4},{6,8},{10,12},{14,16},{18,20},{22,24},{26,28},{4,2},{8,6},{1... | collective-permute-start | bytes 196616 | tf_op jit(solution)/shard_map/ppermute | solution.py:278
  53.6 5.7 %collective-permute-start.20 = (bf16[64,480]{1,0:T(8,128)(2,1)S(1)}, bf16[64,480]{1,0:T(8,128)(2,1)S(1)}, u32[]{:S(2)}, u32[]{:S(2)}) collective-permute-start(bf16[64,480]{1,0:T(8,128)(2,1)S(1)} %get-tuple-element.22.slope_rev), channel_id=1, source_target_pairs={{0,2},{2,0},{4,6},{6,4},{8,10},{10,8},{12,14},{14,12},{16,18},{18,... | collective-permute-start | bytes 184328 | tf_op jit(solution)/shard_map/ppermute | solution.py:240
  58.4 0.9 collective-permute-start.21
  67.2 8.8 %collective-permute-start.23 = (bf16[8,32,480]{2,1,0:T(8,128)(2,1)S(1)}, bf16[8,32,480]{2,1,0:T(8,128)(2,1)S(1)}, u32[]{:S(2)}, u32[]{:S(2)}) collective-permute-start(bf16[8,32,480]{2,1,0:T(8,128)(2,1)S(1)} %get-tuple-element.28), channel_id=1, source_target_pairs={{0,2},{2,0},{4,6},{6,4},{8,10},{10,8},{12,14},{14,12},{16,18},{18,... | collective-permute-start | bytes 737288 | tf_op jit(solution)/shard_map/ppermute | solution.py:240
  71.9 3.9 %collective-permute-start.22 = (bf16[32,512]{1,0:T(8,128)(2,1)S(1)}, bf16[32,512]{1,0:T(8,128)(2,1)S(1)}, u32[]{:S(2)}, u32[]{:S(2)}) collective-permute-start(bf16[32,512]{1,0:T(8,128)(2,1)S(1)} %bitcast.29), channel_id=1, source_target_pairs={{0,1},{1,0},{2,3},{3,2},{4,5},{5,4},{6,7},{7,6},{8,9},{9,8},{10,11... | collective-permute-start | bytes 98312 | tf_op jit(solution)/shard_map/ppermute | solution.py:240
  76.1 5.3 %collective-permute-start.24 = (bf16[4,32,480]{2,1,0:T(8,128)(2,1)S(1)}, bf16[4,32,480]{2,1,0:T(8,128)(2,1)S(1)}, u32[]{:S(2)}, u32[]{:S(2)}) collective-permute-start(bf16[4,32,480]{2,1,0:T(8,128)(2,1)S(1)} %slice.29), channel_id=1, source_target_pairs={{0,4},{2,6},{4,0},{6,2},{8,12},{10,14},{12,8},{14,10},{16,20},{18,... | collective-permute-start | bytes 368648 | tf_op jit(solution)/shard_map/ppermute | solution.py:240
  81.4 6.2 %collective-permute-start.27 = (bf16[32,480]{1,0:T(8,128)(2,1)S(1)}, bf16[32,480]{1,0:T(8,128)(2,1)S(1)}, u32[]{:S(2)}, u32[]{:S(2)}) collective-permute-start(bf16[32,480]{1,0:T(8,128)(2,1)S(1)} %get-tuple-element.32), channel_id=1, source_target_pairs={{0,24},{2,26},{4,28},{6,30},{8,16},{10,18},{12,20},{14,22},{16,8},... | collective-permute-start | bytes 92168 | tf_op jit(solution)/shard_map/ppermute | solution.py:240
  85.6 5.1 %collective-permute-start.26 = (bf16[32,480]{1,0:T(8,128)(2,1)S(1)}, bf16[32,480]{1,0:T(8,128)(2,1)S(1)}, u32[]{:S(2)}, u32[]{:S(2)}) collective-permute-start(bf16[32,480]{1,0:T(8,128)(2,1)S(1)} %get-tuple-element.33), channel_id=1, source_target_pairs={{0,16},{2,18},{4,20},{6,22},{8,24},{10,26},{12,28},{14,30},{16,0},... | collective-permute-start | bytes 92168 | tf_op jit(solution)/shard_map/ppermute | solution.py:240
  85.8 4.8 %collective-permute-start.25 = (bf16[32,480]{1,0:T(8,128)(2,1)S(1)}, bf16[32,480]{1,0:T(8,128)(2,1)S(1)}, u32[]{:S(2)}, u32[]{:S(2)}) collective-permute-start(bf16[32,480]{1,0:T(8,128)(2,1)S(1)} %get-tuple-element.31), channel_id=1, source_target_pairs={{0,8},{2,10},{4,12},{6,14},{8,0},{10,2},{12,4},{14,6},{16,24},{18,... | collective-permute-start | bytes 92168 | tf_op jit(solution)/shard_map/ppermute | solution.py:240

commit v8 on v7

--- a/solution.py
+++ b/solution.py
@@ -245,7 +245,8 @@
     pieces = [shard]
     for n in (1, 2, 3):
         pieces.append(swap(shard, "tm", offs[n]))
-    return jnp.stack(pieces), offs
+    stack = jnp.stack(pieces)
+    return stack, offs
 
 
 def spread_doubling(shard, count):
@@ -305,7 +306,7 @@
     common = dict(layout=layout)
     taps_scratch = [pltpu.VMEM((2, channels, channels), BF16)]
 
-    cut = max(1, groups - 1)
+    cut = (groups + 1) // 2
     tap_sems = lambda count: pltpu.SemaphoreType.DMA((count, 5))
     act_five, w_low = pl.pallas_call(
         functools.partial(five_body, count=slots, **common),

time: 91.5 us -> 91.5 us (level)
    pallas_call x1, Pallas kernels: 5.65 us -> 4.34 us  [on_device(): pl.pallas_call(functools.partial(five_body, count=slots, **common), in_sp...]
    pallas_call x1, Pallas kernels: 2.66 us -> 3.8 us  [on_device(): pl.pallas_call(functools.partial(six_body, count=slots, start=cut if rest...]
where the time goes in v8:
time: 91.5 us; the launch traced here: 91.3 us
  starting transfers between devices  37.5 us (41%)
  waiting for transfers between devices  25.4 us (28%)
  Pallas kernels  23.9 us (26%)
  other arithmetic  3.42 us (4%)
    ppermute x26, starting transfers between devices, swap(): return lax.ppermute(values, axis, [(i, i ^ mask) for i in range(count)])  36.2 us
    ppermute x26, waiting for transfers between devices, swap(): return lax.ppermute(values, axis, [(i, i ^ mask) for i in range(count)])  25.4 us
    pallas_call x1, Pallas kernels, on_device(): pl.pallas_call(functools.partial(forward_body, held=len(weights), layout=...  8.04 us
    pallas_call x1, Pallas kernels, on_device(): pl.pallas_call(functools.partial(backward_body, scale=scale, order=order,...  7.75 us
    pallas_call x1, Pallas kernels, on_device(): pl.pallas_call(functools.partial(five_body, count=slots, **common), in_sp...  4.34 us
    pallas_call x1, Pallas kernels, on_device(): pl.pallas_call(functools.partial(six_body, count=slots, start=cut if rest...  3.8 us
  transfers between devices with their start and end apart: 28, of which 12 were waited for; matrix products, arithmetic and copies ran while one was open for 3% of the time, Pallas kernels for 9%

profile of v8, /device:TPU:0, one launch (start us, length us, event | category | flops | bytes accessed | tf_op | source)
XLA Modules:
  0.0 91.3 jit_solution(18017316671178948067)
XLA Ops:
  0.6 5.1 %collective-permute-start.3 = (bf16[2,32,512]{2,1,0:T(8,128)(2,1)}, bf16[2,32,512]{2,1,0:T(8,128)(2,1)S(1)}, u32[]{:S(2)}, u32[]{:S(2)}) collective-permute-start(bf16[2,32,512]{2,1,0:T(8,128)(2,1)} %bitcast.32), channel_id=1, source_target_pairs={{0,24},{2,26},{4,28},{6,30},{8,16},{10,18},{12,20},{14,22},{16,8},... | collective-permute-start | bytes 196616 | tf_op jit(solution)/shard_map/ppermute | solution.py:240
  5.8 0.6 collective-permute-start.1
  6.4 3.7 %collective-permute-start.9 = (bf16[2,32,512]{2,1,0:T(8,128)(2,1)}, bf16[2,32,512]{2,1,0:T(8,128)(2,1)S(1)}, u32[]{:S(2)}, u32[]{:S(2)}) collective-permute-start(bf16[2,32,512]{2,1,0:T(8,128)(2,1)} %bitcast.36), channel_id=1, source_target_pairs={{0,24},{2,26},{4,28},{6,30},{8,16},{10,18},{12,20},{14,22},{16,8},... | collective-permute-start | bytes 196616 | tf_op jit(solution)/shard_map/ppermute | solution.py:240
  10.2 0.1 constant_dynamic-slice_fusion
  10.3 0.9 %collective-permute-start.7 = (bf16[2,32,512]{2,1,0:T(8,128)(2,1)}, bf16[2,32,512]{2,1,0:T(8,128)(2,1)S(1)}, u32[]{:S(2)}, u32[]{:S(2)}) collective-permute-start(bf16[2,32,512]{2,1,0:T(8,128)(2,1)} %bitcast.38), channel_id=1, source_target_pairs={{0,8},{2,10},{4,12},{6,14},{8,0},{10,2},{12,4},{14,6},{16,24},{18,... | collective-permute-start | bytes 196616 | tf_op jit(solution)/shard_map/ppermute | solution.py:240
  11.2 3.5 %collective-permute-done.2 = bf16[2,32,512]{2,1,0:T(8,128)(2,1)S(1)} collective-permute-done((bf16[2,32,512]{2,1,0:T(8,128)(2,1)}, bf16[2,32,512]{2,1,0:T(8,128)(2,1)S(1)}, u32[]{:S(2)}, u32[]{:S(2)}) %collective-permute-start.2) | collective-permute-done | bytes 65568 | tf_op jit(solution)/shard_map/ppermute | solution.py:240
  14.7 0.9 pad_maximum_fusion.refs_2_
  15.6 1.4 %collective-permute-start.4 = (bf16[4,2,32,512]{3,2,1,0:T(8,128)(2,1)S(1)}, bf16[4,2,32,512]{3,2,1,0:T(8,128)(2,1)S(1)}, u32[]{:S(2)}, u32[]{:S(2)}) collective-permute-start(bf16[4,2,32,512]{3,2,1,0:T(8,128)(2,1)S(1)} %pad_maximum_fusion.refs_2_), channel_id=1, source_target_pairs={{0,4},{2,6},{4,0},{6,2},{8,12},{10,14},{12,8},{14,10},{16,20},{18,... | collective-permute-start | bytes 786440 | tf_op jit(solution)/shard_map/ppermute | solution.py:240
  16.9 0.3 collective-permute-done.8
  17.2 0.9 pad_maximum_fusion.1.refs_0_
  18.1 1.6 %collective-permute-start.10 = (bf16[4,2,32,512]{3,2,1,0:T(8,128)(2,1)S(1)}, bf16[4,2,32,512]{3,2,1,0:T(8,128)(2,1)S(1)}, u32[]{:S(2)}, u32[]{:S(2)}) collective-permute-start(bf16[4,2,32,512]{3,2,1,0:T(8,128)(2,1)S(1)} %pad_maximum_fusion.1.refs_0_), channel_id=1, source_target_pairs={{0,4},{2,6},{4,0},{6,2},{8,12},{10,14},{12,8},{14,10},{16,20},{18,... | collective-permute-start | bytes 786440 | tf_op jit(solution)/shard_map/ppermute | solution.py:240
  19.7 1.1 %collective-permute-start.15 = (bf16[1,1,32,512]{3,2,1,0:T(8,128)(2,1)S(1)}, bf16[1,1,32,512]{3,2,1,0:T(8,128)(2,1)S(1)}, u32[]{:S(2)}, u32[]{:S(2)}) collective-permute-start(bf16[1,1,32,512]{3,2,1,0:T(8,128)(2,1)S(1)} %pad_bitcast_fusion), channel_id=1, source_target_pairs={{0,16},{2,18},{4,20},{6,22},{8,24},{10,26},{12,28},{14,30},{16,0},... | collective-permute-start | bytes 98312 | tf_op jit(solution)/shard_map/ppermute | solution.py:240
  20.8 3.8 %collective-permute-done.15 = bf16[1,1,32,512]{3,2,1,0:T(8,128)(2,1)S(1)} collective-permute-done((bf16[1,1,32,512]{3,2,1,0:T(8,128)(2,1)S(1)}, bf16[1,1,32,512]{3,2,1,0:T(8,128)(2,1)S(1)}, u32[]{:S(2)}, u32[]{:S(2)}) %collective-permute-start.15) | collective-permute-done | bytes 32800 | tf_op jit(solution)/shard_map/ppermute | solution.py:240
  24.7 0.3 collective-permute-start.16
  25.0 1.5 %collective-permute-start = (bf16[128,512]{1,0:T(8,128)(2,1)}, bf16[128,512]{1,0:T(8,128)(2,1)S(1)}, u32[]{:S(2)}, u32[]{:S(2)}) collective-permute-start(bf16[128,512]{1,0:T(8,128)(2,1)} %refs_0_.1), channel_id=1, source_target_pairs={{0,1},{1,0},{2,3},{3,2},{4,5},{5,4},{6,7},{7,6},{8,9},{9,8},{10,11... | collective-permute-start | bytes 393224 | tf_op jit(solution)/shard_map/ppermute | solution.py:240
  26.5 2.5 %collective-permute-done.16 = bf16[2,1,32,512]{3,2,1,0:T(8,128)(2,1)S(1)} collective-permute-done((bf16[2,1,32,512]{3,2,1,0:T(8,128)(2,1)S(1)}, bf16[2,1,32,512]{3,2,1,0:T(8,128)(2,1)S(1)}, u32[]{:S(2)}, u32[]{:S(2)}) %collective-permute-start.16) | collective-permute-done | bytes 65568 | tf_op jit(solution)/shard_map/ppermute | solution.py:240
  29.0 0.5 collective-permute-start.6
  29.5 0.1 collective-permute-start.12
  29.6 0.5 collective-permute-done.refs_1_
  30.1 0.5 collective-permute-start.17
  30.6 4.9 %collective-permute-done.17.refs_1_ = bf16[4,1,32,512]{3,2,1,0:T(8,128)(2,1)S(1)} collective-permute-done((bf16[4,1,32,512]{3,2,1,0:T(8,128)(2,1)S(1)}, bf16[4,1,32,512]{3,2,1,0:T(8,128)(2,1)S(1)}, u32[]{:S(2)}, u32[]{:S(2)}) %collective-permute-start.17) | collective-permute-done | bytes 131104 | tf_op jit(solution)/shard_map/ppermute | solution.py:240
  35.5 0.5 collective-permute-start.19
  36.0 0.1 pad_add_fusion.where
  36.1 4.3 %five.1 = (bf16[128,512]{1,0:T(8,128)(2,1)S(1)}, bf16[2,120,120,128]{3,2,1,0:T(8,128)(2,1)S(1)}) custom-call(s32[2]{0:T(128)S(1)} %pad_add_fusion.where, bf16[128,512]{1,0:T(8,128)(2,1)} %refs_0_.1, bf16[128,512]{1,0:T(8,128)(2,1)S(1)} %collective-permute-done.refs_1_, bf16[4,2,32,512]{3,2,1,0:T(8,128)(2,1)S(1)} %pad_maximum_fusion.refs_2_, ...), custom_call_target="tpu_custom_call" | custom-call | tf_op jit(solution)/shard_map/five/pallas_call | solution.py:311
  40.5 3.8 %six.1 = (bf16[64,512]{1,0:T(8,128)(2,1)S(1)}, f32[32,512]{1,0:T(8,128)S(1)}, f32[32,128]{1,0:T(8,128)S(1)}, bf16[2,120,120,128]{3,2,1,0:T(8,128)(2,1)S(1)}) custom-call(s32[2]{0:T(128)S(1)} %pad_add_fusion.where, bf16[128,512]{1,0:T(8,128)(2,1)S(1)} %get-tuple-element.16.act, bf16[4,2,32,512]{3,2,1,0:T(8,128)(2,1)S(1)} %pad_maximum_fusion.1.refs_0_, ...), custom_call_target="tpu_custom_call" | custom-call | tf_op jit(solution)/shard_map/six/pallas_call | solution.py:325
  44.3 0.1 collective-permute-start.13
  44.4 0.7 collective-permute-start.14
  45.1 0.5 collective-permute-done.13.got_a
  45.7 8.0 %forward.1 = (bf16[64,480]{1,0:T(8,128)(2,1)}, bf16[64,480]{1,0:T(8,128)(2,1)S(1)}, bf16[512,480]{1,0:T(8,128)(2,1)S(1)}) custom-call(s32[2]{0:T(128)S(1)} %pad_add_fusion.where, bf16[64,512]{1,0:T(8,128)(2,1)S(1)} %get-tuple-element.17.normed.refs_3_, bf16[64,512]{1,0:T(8,128)(2,1)S(1)} %collective-permute-done.13.got_a, ...), custom_call_target="tpu_custom_call" | custom-call | tf_op jit(solution)/shard_map/forward/pallas_call | solution.py:351
  53.7 4.8 %collective-permute-start.20 = (bf16[64,480]{1,0:T(8,128)(2,1)S(1)}, bf16[64,480]{1,0:T(8,128)(2,1)S(1)}, u32[]{:S(2)}, u32[]{:S(2)}) collective-permute-start(bf16[64,480]{1,0:T(8,128)(2,1)S(1)} %get-tuple-element.22.slope_rev), channel_id=1, source_target_pairs={{0,2},{2,0},{4,6},{6,4},{8,10},{10,8},{12,14},{14,12},{16,18},{18,... | collective-permute-start | bytes 184328 | tf_op jit(solution)/shard_map/ppermute | solution.py:240
  58.5 0.7 collective-permute-start.21
  59.2 0.2 collective-permute-done.20.got_a
  59.4 7.8 %backward.1 = (bf16[8,32,480]{2,1,0:T(8,128)(2,1)S(1)}, bf16[8,32,480]{2,1,0:T(8,128)(2,1)S(1)}, f32[32,512]{1,0:T(8,128)S(1)}, bf16[1,32,512]{2,1,0:T(8,128)(2,1)S(1)}) custom-call(s32[2]{0:T(128)S(1)} %pad_add_fusion.where, bf16[64,480]{1,0:T(8,128)(2,1)S(1)} %get-tuple-element.22.slope_rev, bf16[64,480]{1,0:T(8,128)(2,1)S(1)} %collective-permute-done.20.got_a, ...), custom_call_target="tpu_custom_call" | custom-call | tf_op jit(solution)/shard_map/backward/pallas_call | solution.py:378
  67.2 4.7 %collective-permute-start.23 = (bf16[8,32,480]{2,1,0:T(8,128)(2,1)S(1)}, bf16[8,32,480]{2,1,0:T(8,128)(2,1)S(1)}, u32[]{:S(2)}, u32[]{:S(2)}) collective-permute-start(bf16[8,32,480]{2,1,0:T(8,128)(2,1)S(1)} %get-tuple-element.28), channel_id=1, source_target_pairs={{0,2},{2,0},{4,6},{6,4},{8,10},{10,8},{12,14},{14,12},{16,18},{18,... | collective-permute-start | bytes 737288 | tf_op jit(solution)/shard_map/ppermute | solution.py:240
  71.9 1.5 %collective-permute-start.22 = (bf16[32,512]{1,0:T(8,128)(2,1)S(1)}, bf16[32,512]{1,0:T(8,128)(2,1)S(1)}, u32[]{:S(2)}, u32[]{:S(2)}) collective-permute-start(bf16[32,512]{1,0:T(8,128)(2,1)S(1)} %bitcast.29), channel_id=1, source_target_pairs={{0,1},{1,0},{2,3},{3,2},{4,5},{5,4},{6,7},{7,6},{8,9},{9,8},{10,11... | collective-permute-start | bytes 98312 | tf_op jit(solution)/shard_map/ppermute | solution.py:240
  73.4 0.1 slice_reduce_fusion
  73.5 2.3 %collective-permute-done.22 = bf16[32,512]{1,0:T(8,128)(2,1)S(1)} collective-permute-done((bf16[32,512]{1,0:T(8,128)(2,1)S(1)}, bf16[32,512]{1,0:T(8,128)(2,1)S(1)}, u32[]{:S(2)}, u32[]{:S(2)}) %collective-permute-start.22) | collective-permute-done | bytes 32800 | tf_op jit(solution)/shard_map/ppermute | solution.py:240
  75.8 0.1 fusion
  76.0 0.1 add_convert_fusion
  76.0 2.4 %collective-permute-start.24 = (bf16[4,32,480]{2,1,0:T(8,128)(2,1)S(1)}, bf16[4,32,480]{2,1,0:T(8,128)(2,1)S(1)}, u32[]{:S(2)}, u32[]{:S(2)}) collective-permute-start(bf16[4,32,480]{2,1,0:T(8,128)(2,1)S(1)} %slice.29), channel_id=1, source_target_pairs={{0,4},{2,6},{4,0},{6,2},{8,12},{10,14},{12,8},{14,10},{16,20},{18,... | collective-permute-start | bytes 368648 | tf_op jit(solution)/shard_map/ppermute | solution.py:240
  78.4 2.9 %collective-permute-done.24 = bf16[4,32,480]{2,1,0:T(8,128)(2,1)S(1)} collective-permute-done((bf16[4,32,480]{2,1,0:T(8,128)(2,1)S(1)}, bf16[4,32,480]{2,1,0:T(8,128)(2,1)S(1)}, u32[]{:S(2)}, u32[]{:S(2)}) %collective-permute-start.24) | collective-permute-done | bytes 122912 | tf_op jit(solution)/shard_map/ppermute | solution.py:240
  81.4 4.1 %collective-permute-start.27 = (bf16[32,480]{1,0:T(8,128)(2,1)S(1)}, bf16[32,480]{1,0:T(8,128)(2,1)S(1)}, u32[]{:S(2)}, u32[]{:S(2)}) collective-permute-start(bf16[32,480]{1,0:T(8,128)(2,1)S(1)} %get-tuple-element.32), channel_id=1, source_target_pairs={{0,24},{2,26},{4,28},{6,30},{8,16},{10,18},{12,20},{14,22},{16,8},... | collective-permute-start | bytes 92168 | tf_op jit(solution)/shard_map/ppermute | solution.py:240
  85.5 0.3 collective-permute-start.26
  85.8 0.4 collective-permute-start.25
  86.2 0.7 multiply_convert_fusion
  86.9 0.7 collective-permute-done.27
  87.6 3.1 %collective-permute-done.26 = bf16[32,480]{1,0:T(8,128)(2,1)S(1)} collective-permute-done((bf16[32,480]{1,0:T(8,128)(2,1)S(1)}, bf16[32,480]{1,0:T(8,128)(2,1)S(1)}, u32[]{:S(2)}, u32[]{:S(2)}) %collective-permute-start.26) | collective-permute-done | bytes 30752 | tf_op jit(solution)/shard_map/ppermute | solution.py:240
  90.6 0.6 convert_add_fusion
  (35 shorter events, 0.2 us)
Async XLA Ops:
  0.6 9.6 %copy-start = (bf16[32,960]{1,0:T(8,128)(2,1)S(1)}, bf16[32,960]{1,0:T(8,128)(2,1)}, u32[]{:S(2)}) copy-start(bf16[32,960]{1,0:T(8,128)(2,1)} %param.10) | copy-start | bytes 184324
  0.6 9.6 %collective-permute-start.3 = (bf16[2,32,512]{2,1,0:T(8,128)(2,1)}, bf16[2,32,512]{2,1,0:T(8,128)(2,1)S(1)}, u32[]{:S(2)}, u32[]{:S(2)}) collective-permute-start(bf16[2,32,512]{2,1,0:T(8,128)(2,1)} %bitcast.32), channel_id=1, source_target_pairs={{0,24},{2,26},{4,28},{6,30},{8,16},{10,18},{12,20},{14,22},{16,8},... | collective-permute-start | bytes 196616 | tf_op jit(solution)/shard_map/ppermute | solution.py:240
  5.8 8.9 %collective-permute-start.2 = (bf16[2,32,512]{2,1,0:T(8,128)(2,1)}, bf16[2,32,512]{2,1,0:T(8,128)(2,1)S(1)}, u32[]{:S(2)}, u32[]{:S(2)}) collective-permute-start(bf16[2,32,512]{2,1,0:T(8,128)(2,1)} %bitcast.33), channel_id=1, source_target_pairs={{0,16},{2,18},{4,20},{6,22},{8,24},{10,26},{12,28},{14,30},{16,0},... | collective-permute-start | bytes 196616 | tf_op jit(solution)/shard_map/ppermute | solution.py:240
  5.8 8.9 %collective-permute-start.1 = (bf16[2,32,512]{2,1,0:T(8,128)(2,1)}, bf16[2,32,512]{2,1,0:T(8,128)(2,1)S(1)}, u32[]{:S(2)}, u32[]{:S(2)}) collective-permute-start(bf16[2,32,512]{2,1,0:T(8,128)(2,1)} %bitcast.34), channel_id=1, source_target_pairs={{0,8},{2,10},{4,12},{6,14},{8,0},{10,2},{12,4},{14,6},{16,24},{18,... | collective-permute-start | bytes 196616 | tf_op jit(solution)/shard_map/ppermute | solution.py:240
  6.4 10.5 %collective-permute-start.9 = (bf16[2,32,512]{2,1,0:T(8,128)(2,1)}, bf16[2,32,512]{2,1,0:T(8,128)(2,1)S(1)}, u32[]{:S(2)}, u32[]{:S(2)}) collective-permute-start(bf16[2,32,512]{2,1,0:T(8,128)(2,1)} %bitcast.36), channel_id=1, source_target_pairs={{0,24},{2,26},{4,28},{6,30},{8,16},{10,18},{12,20},{14,22},{16,8},... | collective-permute-start | bytes 196616 | tf_op jit(solution)/shard_map/ppermute | solution.py:240
  10.2 7.0 %collective-permute-start.8 = (bf16[2,32,512]{2,1,0:T(8,128)(2,1)}, bf16[2,32,512]{2,1,0:T(8,128)(2,1)S(1)}, u32[]{:S(2)}, u32[]{:S(2)}) collective-permute-start(bf16[2,32,512]{2,1,0:T(8,128)(2,1)} %bitcast.37), channel_id=1, source_target_pairs={{0,16},{2,18},{4,20},{6,22},{8,24},{10,26},{12,28},{14,30},{16,0},... | collective-permute-start | bytes 196616 | tf_op jit(solution)/shard_map/ppermute | solution.py:240
  10.3 7.0 %collective-permute-start.7 = (bf16[2,32,512]{2,1,0:T(8,128)(2,1)}, bf16[2,32,512]{2,1,0:T(8,128)(2,1)S(1)}, u32[]{:S(2)}, u32[]{:S(2)}) collective-permute-start(bf16[2,32,512]{2,1,0:T(8,128)(2,1)} %bitcast.38), channel_id=1, source_target_pairs={{0,8},{2,10},{4,12},{6,14},{8,0},{10,2},{12,4},{14,6},{16,24},{18,... | collective-permute-start | bytes 196616 | tf_op jit(solution)/shard_map/ppermute | solution.py:240
  15.6 13.4 %collective-permute-start.4 = (bf16[4,2,32,512]{3,2,1,0:T(8,128)(2,1)S(1)}, bf16[4,2,32,512]{3,2,1,0:T(8,128)(2,1)S(1)}, u32[]{:S(2)}, u32[]{:S(2)}) collective-permute-start(bf16[4,2,32,512]{3,2,1,0:T(8,128)(2,1)S(1)} %pad_maximum_fusion.refs_2_), channel_id=1, source_target_pairs={{0,4},{2,6},{4,0},{6,2},{8,12},{10,14},{12,8},{14,10},{16,20},{18,... | collective-permute-start | bytes 786440 | tf_op jit(solution)/shard_map/ppermute | solution.py:240
  18.1 11.4 %collective-permute-start.10 = (bf16[4,2,32,512]{3,2,1,0:T(8,128)(2,1)S(1)}, bf16[4,2,32,512]{3,2,1,0:T(8,128)(2,1)S(1)}, u32[]{:S(2)}, u32[]{:S(2)}) collective-permute-start(bf16[4,2,32,512]{3,2,1,0:T(8,128)(2,1)S(1)} %pad_maximum_fusion.1.refs_0_), channel_id=1, source_target_pairs={{0,4},{2,6},{4,0},{6,2},{8,12},{10,14},{12,8},{14,10},{16,20},{18,... | collective-permute-start | bytes 786440 | tf_op jit(solution)/shard_map/ppermute | solution.py:240
  19.7 5.0 %collective-permute-start.15 = (bf16[1,1,32,512]{3,2,1,0:T(8,128)(2,1)S(1)}, bf16[1,1,32,512]{3,2,1,0:T(8,128)(2,1)S(1)}, u32[]{:S(2)}, u32[]{:S(2)}) collective-permute-start(bf16[1,1,32,512]{3,2,1,0:T(8,128)(2,1)S(1)} %pad_bitcast_fusion), channel_id=1, source_target_pairs={{0,16},{2,18},{4,20},{6,22},{8,24},{10,26},{12,28},{14,30},{16,0},... | collective-permute-start | bytes 98312 | tf_op jit(solution)/shard_map/ppermute | solution.py:240
  24.7 4.3 %collective-permute-start.16 = (bf16[2,1,32,512]{3,2,1,0:T(8,128)(2,1)S(1)}, bf16[2,1,32,512]{3,2,1,0:T(8,128)(2,1)S(1)}, u32[]{:S(2)}, u32[]{:S(2)}) collective-permute-start(bf16[2,1,32,512]{3,2,1,0:T(8,128)(2,1)S(1)} %pad_maximum_fusion.3), channel_id=1, source_target_pairs={{0,8},{2,10},{4,12},{6,14},{8,0},{10,2},{12,4},{14,6},{16,24},{18,... | collective-permute-start | bytes 196616 | tf_op jit(solution)/shard_map/ppermute | solution.py:240
  25.0 5.2 %collective-permute-start = (bf16[128,512]{1,0:T(8,128)(2,1)}, bf16[128,512]{1,0:T(8,128)(2,1)S(1)}, u32[]{:S(2)}, u32[]{:S(2)}) collective-permute-start(bf16[128,512]{1,0:T(8,128)(2,1)} %refs_0_.1), channel_id=1, source_target_pairs={{0,1},{1,0},{2,3},{3,2},{4,5},{5,4},{6,7},{7,6},{8,9},{9,8},{10,11... | collective-permute-start | bytes 393224 | tf_op jit(solution)/shard_map/ppermute | solution.py:240
  26.4 9.1 %collective-permute-start.5 = (bf16[4,2,32,512]{3,2,1,0:T(8,128)(2,1)S(1)}, bf16[4,2,32,512]{3,2,1,0:T(8,128)(2,1)S(1)}, u32[]{:S(2)}, u32[]{:S(2)}) collective-permute-start(bf16[4,2,32,512]{3,2,1,0:T(8,128)(2,1)S(1)} %pad_maximum_fusion.refs_2_), channel_id=1, source_target_pairs={{0,2},{2,0},{4,6},{6,4},{8,10},{10,8},{12,14},{14,12},{16,18},{18,... | collective-permute-start | bytes 786440 | tf_op jit(solution)/shard_map/ppermute | solution.py:240
  29.0 11.5 %collective-permute-start.11 = (bf16[4,2,32,512]{3,2,1,0:T(8,128)(2,1)S(1)}, bf16[4,2,32,512]{3,2,1,0:T(8,128)(2,1)S(1)}, u32[]{:S(2)}, u32[]{:S(2)}) collective-permute-start(bf16[4,2,32,512]{3,2,1,0:T(8,128)(2,1)S(1)} %pad_maximum_fusion.1.refs_0_), channel_id=1, source_target_pairs={{0,2},{2,0},{4,6},{6,4},{8,10},{10,8},{12,14},{14,12},{16,18},{18,... | collective-permute-start | bytes 786440 | tf_op jit(solution)/shard_map/ppermute | solution.py:240
  29.0 7.1 %collective-permute-start.6 = (bf16[4,2,32,512]{3,2,1,0:T(8,128)(2,1)S(1)}, bf16[4,2,32,512]{3,2,1,0:T(8,128)(2,1)S(1)}, u32[]{:S(2)}, u32[]{:S(2)}) collective-permute-start(bf16[4,2,32,512]{3,2,1,0:T(8,128)(2,1)S(1)} %collective-permute-done.4.refs_3_), channel_id=1, source_target_pairs={{0,2},{2,0},{4,6},{6,4},{8,10},{10,8},{12,14},{14,12},{16,18},{18,... | collective-permute-start | bytes 786440 | tf_op jit(solution)/shard_map/ppermute | solution.py:240
  29.5 11.0 %collective-permute-start.12 = (bf16[4,2,32,512]{3,2,1,0:T(8,128)(2,1)S(1)}, bf16[4,2,32,512]{3,2,1,0:T(8,128)(2,1)S(1)}, u32[]{:S(2)}, u32[]{:S(2)}) collective-permute-start(bf16[4,2,32,512]{3,2,1,0:T(8,128)(2,1)S(1)} %collective-permute-done.10.refs_1_), channel_id=1, source_target_pairs={{0,2},{2,0},{4,6},{6,4},{8,10},{10,8},{12,14},{14,12},{16,18},{18,... | collective-permute-start | bytes 786440 | tf_op jit(solution)/shard_map/ppermute | solution.py:240
  30.1 5.4 %collective-permute-start.17 = (bf16[4,1,32,512]{3,2,1,0:T(8,128)(2,1)S(1)}, bf16[4,1,32,512]{3,2,1,0:T(8,128)(2,1)S(1)}, u32[]{:S(2)}, u32[]{:S(2)}) collective-permute-start(bf16[4,1,32,512]{3,2,1,0:T(8,128)(2,1)S(1)} %pad_maximum_fusion.2.refs_0_), channel_id=1, source_target_pairs={{0,4},{2,6},{4,0},{6,2},{8,12},{10,14},{12,8},{14,10},{16,20},{18,... | collective-permute-start | bytes 393224 | tf_op jit(solution)/shard_map/ppermute | solution.py:240
  35.5 9.6 %collective-permute-start.18 = (bf16[4,1,32,512]{3,2,1,0:T(8,128)(2,1)S(1)}, bf16[4,1,32,512]{3,2,1,0:T(8,128)(2,1)S(1)}, u32[]{:S(2)}, u32[]{:S(2)}) collective-permute-start(bf16[4,1,32,512]{3,2,1,0:T(8,128)(2,1)S(1)} %pad_maximum_fusion.2.refs_0_), channel_id=1, source_target_pairs={{0,2},{2,0},{4,6},{6,4},{8,10},{10,8},{12,14},{14,12},{16,18},{18,... | collective-permute-start | bytes 393224 | tf_op jit(solution)/shard_map/ppermute | solution.py:240
  35.5 9.6 %collective-permute-start.19 = (bf16[4,1,32,512]{3,2,1,0:T(8,128)(2,1)S(1)}, bf16[4,1,32,512]{3,2,1,0:T(8,128)(2,1)S(1)}, u32[]{:S(2)}, u32[]{:S(2)}) collective-permute-start(bf16[4,1,32,512]{3,2,1,0:T(8,128)(2,1)S(1)} %collective-permute-done.17.refs_1_), channel_id=1, source_target_pairs={{0,2},{2,0},{4,6},{6,4},{8,10},{10,8},{12,14},{14,12},{16,18},{18,... | collective-permute-start | bytes 393224 | tf_op jit(solution)/shard_map/ppermute | solution.py:240
  40.5 4.6 %copy-start.2 = (bf16[480]{0:T(512)(128)(2,1)S(1)}, bf16[480]{0:T(512)(128)(2,1)}, u32[]{:S(2)}) copy-start(bf16[480]{0:T(512)(128)(2,1)} %param.12) | copy-start | bytes 2884
  40.5 5.1 %copy-start.1 = (bf16[64,480]{1,0:T(8,128)(2,1)S(1)}, bf16[64,480]{1,0:T(8,128)(2,1)}, u32[]{:S(2)}) copy-start(bf16[64,480]{1,0:T(8,128)(2,1)} %refs_2_.1) | copy-start | bytes 184324
  44.3 1.3 %collective-permute-start.13 = (bf16[64,512]{1,0:T(8,128)(2,1)S(1)}, bf16[64,512]{1,0:T(8,128)(2,1)S(1)}, u32[]{:S(2)}, u32[]{:S(2)}) collective-permute-start(bf16[64,512]{1,0:T(8,128)(2,1)S(1)} %get-tuple-element.17.normed.refs_3_), channel_id=1, source_target_pairs={{0,2},{2,0},{4,6},{6,4},{8,10},{10,8},{12,14},{14,12},{16,18},{18,... | collective-permute-start | bytes 196616 | tf_op jit(solution)/shard_map/ppermute | solution.py:240
  44.4 1.2 %collective-permute-start.14 = (bf16[64,512]{1,0:T(8,128)(2,1)S(1)}, bf16[64,512]{1,0:T(8,128)(2,1)S(1)}, u32[]{:S(2)}, u32[]{:S(2)}) collective-permute-start(bf16[64,512]{1,0:T(8,128)(2,1)S(1)} %get-tuple-element.17.normed.refs_3_), channel_id=1, source_target_pairs={{2,4},{6,8},{10,12},{14,16},{18,20},{22,24},{26,28},{4,2},{8,6},{1... | collective-permute-start | bytes 196616 | tf_op jit(solution)/shard_map/ppermute | solution.py:279
  53.7 5.7 %collective-permute-start.20 = (bf16[64,480]{1,0:T(8,128)(2,1)S(1)}, bf16[64,480]{1,0:T(8,128)(2,1)S(1)}, u32[]{:S(2)}, u32[]{:S(2)}) collective-permute-start(bf16[64,480]{1,0:T(8,128)(2,1)S(1)} %get-tuple-element.22.slope_rev), channel_id=1, source_target_pairs={{0,2},{2,0},{4,6},{6,4},{8,10},{10,8},{12,14},{14,12},{16,18},{18,... | collective-permute-start | bytes 184328 | tf_op jit(solution)/shard_map/ppermute | solution.py:240
  58.5 0.9 collective-permute-start.21
  67.2 8.8 %collective-permute-start.23 = (bf16[8,32,480]{2,1,0:T(8,128)(2,1)S(1)}, bf16[8,32,480]{2,1,0:T(8,128)(2,1)S(1)}, u32[]{:S(2)}, u32[]{:S(2)}) collective-permute-start(bf16[8,32,480]{2,1,0:T(8,128)(2,1)S(1)} %get-tuple-element.28), channel_id=1, source_target_pairs={{0,2},{2,0},{4,6},{6,4},{8,10},{10,8},{12,14},{14,12},{16,18},{18,... | collective-permute-start | bytes 737288 | tf_op jit(solution)/shard_map/ppermute | solution.py:240
  71.9 3.9 %collective-permute-start.22 = (bf16[32,512]{1,0:T(8,128)(2,1)S(1)}, bf16[32,512]{1,0:T(8,128)(2,1)S(1)}, u32[]{:S(2)}, u32[]{:S(2)}) collective-permute-start(bf16[32,512]{1,0:T(8,128)(2,1)S(1)} %bitcast.29), channel_id=1, source_target_pairs={{0,1},{1,0},{2,3},{3,2},{4,5},{5,4},{6,7},{7,6},{8,9},{9,8},{10,11... | collective-permute-start | bytes 98312 | tf_op jit(solution)/shard_map/ppermute | solution.py:240
  76.0 5.3 %collective-permute-start.24 = (bf16[4,32,480]{2,1,0:T(8,128)(2,1)S(1)}, bf16[4,32,480]{2,1,0:T(8,128)(2,1)S(1)}, u32[]{:S(2)}, u32[]{:S(2)}) collective-permute-start(bf16[4,32,480]{2,1,0:T(8,128)(2,1)S(1)} %slice.29), channel_id=1, source_target_pairs={{0,4},{2,6},{4,0},{6,2},{8,12},{10,14},{12,8},{14,10},{16,20},{18,... | collective-permute-start | bytes 368648 | tf_op jit(solution)/shard_map/ppermute | solution.py:240
  81.4 6.2 %collective-permute-start.27 = (bf16[32,480]{1,0:T(8,128)(2,1)S(1)}, bf16[32,480]{1,0:T(8,128)(2,1)S(1)}, u32[]{:S(2)}, u32[]{:S(2)}) collective-permute-start(bf16[32,480]{1,0:T(8,128)(2,1)S(1)} %get-tuple-element.32), channel_id=1, source_target_pairs={{0,24},{2,26},{4,28},{6,30},{8,16},{10,18},{12,20},{14,22},{16,8},... | collective-permute-start | bytes 92168 | tf_op jit(solution)/shard_map/ppermute | solution.py:240
  85.5 5.1 %collective-permute-start.26 = (bf16[32,480]{1,0:T(8,128)(2,1)S(1)}, bf16[32,480]{1,0:T(8,128)(2,1)S(1)}, u32[]{:S(2)}, u32[]{:S(2)}) collective-permute-start(bf16[32,480]{1,0:T(8,128)(2,1)S(1)} %get-tuple-element.33), channel_id=1, source_target_pairs={{0,16},{2,18},{4,20},{6,22},{8,24},{10,26},{12,28},{14,30},{16,0},... | collective-permute-start | bytes 92168 | tf_op jit(solution)/shard_map/ppermute | solution.py:240
  85.8 4.8 %collective-permute-start.25 = (bf16[32,480]{1,0:T(8,128)(2,1)S(1)}, bf16[32,480]{1,0:T(8,128)(2,1)S(1)}, u32[]{:S(2)}, u32[]{:S(2)}) collective-permute-start(bf16[32,480]{1,0:T(8,128)(2,1)S(1)} %get-tuple-element.31), channel_id=1, source_target_pairs={{0,8},{2,10},{4,12},{6,14},{8,0},{10,2},{12,4},{14,6},{16,24},{18,... | collective-permute-start | bytes 92168 | tf_op jit(solution)/shard_map/ppermute | solution.py:240
